TPU v7x, 32 devices: a whole 2x2x4 slice. The times are simulated.
32 devices in a mesh: ctx: 8 (over y, x, core), fsdp: 4 (over z).
Axes of the slice: x: 2, y: 2, z: 4, core: 2. Of those that a mesh axis runs over, the one named last changes fastest.
Arguments:
- tokens: bfloat16 [4, 4096, 2048], P('fsdp', 'ctx'), may hold values from -6 to 6
- cotangent: bfloat16 [4, 4096, 2048], P('fsdp', 'ctx'), may hold values from -6 to 6
- kv_cotangent: bfloat16 [4, 4096, 256], P('fsdp', 'ctx'), may hold values from -6 to 6
- lengths: int32 [4], P('fsdp'), may hold values from 1024 to 4096, as said below
- block_order: int32 [4, 16], P('fsdp'), may hold values from 0 to 15, each once within a row
- w_query: bfloat16 [2048, 2048], P('fsdp'), may hold values from -0.125 to 0.125
- w_kv: bfloat16 [2048, 256], P('fsdp'), may hold values from -0.25 to 0.25
- w_out: bfloat16 [2048, 2048], P('fsdp'), may hold values from -0.375 to 0.375
- gain_attn: bfloat16 [2048], P('fsdp'), may hold values from 0.5 to 1.5
- gain_ffn: bfloat16 [2048], P('fsdp'), may hold values from 0.5 to 1.5
- w_gate: bfloat16 [2048, 5632], P(None, 'fsdp'), may hold values from -0.125 to 0.125
- w_up: bfloat16 [2048, 5632], P(None, 'fsdp'), may hold values from -0.125 to 0.125
- w_down: bfloat16 [2048, 5632], P(None, 'fsdp'), may hold values from -0.078125 to 0.078125
Outputs:
- output: bfloat16 [4, 4096, 2048], P('fsdp', 'ctx')
- input_grad: bfloat16 [4, 4096, 2048], P('fsdp', 'ctx')
- grad_w_query: float32 [2048, 2048], P(('ctx', 'fsdp'))
- grad_w_kv: float32 [2048, 256], P(('ctx', 'fsdp'))
- grad_w_out: float32 [2048, 2048], P(('ctx', 'fsdp'))
- grad_gain_attn: float32 [2048], P(('ctx', 'fsdp'))
- grad_gain_ffn: float32 [2048], P(('ctx', 'fsdp'))
- grad_w_gate: float32 [2048, 5632], P('ctx', 'fsdp')
- grad_w_up: float32 [2048, 5632], P('ctx', 'fsdp')
- grad_w_down: float32 [2048, 5632], P('ctx', 'fsdp')
Inputs may be any that keep to these rules, and one draw needn't show every extreme that they name: Slot s holds one sequence of lengths[s] tokens; in every draw some slot is full. Each row is a permutation: stored block j of slot s, its tokens j * 256 to (j + 1) * 256 - 1, holds positions block_order[s, j] * 256 onward.
All inputs are finite; a program needn't handle non-finite values.
Results may differ from a plain program's by a relative error of at most 0.025.
Values may be sent and summed in bfloat16 or wider, within the bound.
No kernel may reach another device: no remote copies, remote signals or barrier semaphores. Data moves between devices by JAX's collectives and lax.ppermute only.
A program may use at most 448 MiB of HBM per device.

v0:
```python
import jax
import jax.numpy as jnp
from jax import lax
from jax.sharding import PartitionSpec as P

H = 16
HD = 128


EPSILON = 1e-05
ROPE_BASE = 10000.0
MASKED = -1e30


def angles(positions, head_dim):
    half_dim = head_dim // 2
    frequency = ROPE_BASE ** (-2.0 * jnp.arange(half_dim, dtype=jnp.float32) / head_dim)
    phase_angle = positions.astype(jnp.float32)[:, None] * frequency[None, :]
    return (jnp.cos(phase_angle), jnp.sin(phase_angle))


def rotate(vectors, cosine, sine_vals):
    half_dim = cosine.shape[-1]
    first_half = vectors[..., :half_dim]
    second_half = vectors[..., half_dim:]
    return jnp.concatenate(
        [
            first_half * cosine - second_half * sine_vals,
            second_half * cosine + first_half * sine_vals,
        ],
        axis=-1,
    )


def contract_rows(left, right):
    return lax.dot_general(
        left, right, (((0,), (0,)), ((), ())), preferred_element_type=jnp.float32
    )


def contract_cols(left, right):
    return lax.dot_general(
        left, right, (((1,), (1,)), ((), ())), preferred_element_type=jnp.float32
    )


def score_block(query_rows, row_pos, keys_all, key_pos, length, offset_at, block_width):
    key_part = lax.dynamic_slice_in_dim(keys_all, offset_at, block_width, 0)
    pos_part = lax.dynamic_slice_in_dim(key_pos, offset_at, block_width, 0)
    scores = contract_cols(query_rows, key_part)
    allowed = (pos_part[None, :] <= row_pos[:, None]) & (pos_part[None, :] < length)
    return jnp.where(allowed, scores, MASKED)


def attention_forward(query_rot, kv_slot, query_pos, key_pos, length):
    local_len, head_count, head_dim = query_rot.shape
    rows_total = local_len * head_count
    query_rows = query_rot.reshape(rows_total, head_dim)
    row_pos = jnp.repeat(query_pos, head_count)
    keys_all = kv_slot[:, :head_dim]
    values_all = kv_slot[:, head_dim:]
    block_width = min(512, kv_slot.shape[0])
    steps_count = kv_slot.shape[0] // block_width

    def stat_update(carried, offset_at):
        maximum, running_sum = carried
        scores = score_block(query_rows, row_pos, keys_all, key_pos, length, offset_at, block_width)
        new_max = jnp.maximum(maximum, jnp.max(scores, axis=1))
        summed = running_sum * jnp.exp(maximum - new_max) + jnp.sum(
            jnp.exp(scores - new_max[:, None]), axis=1
        )
        return (new_max, summed)

    def stat_step(carried, step_index):
        offset_at = step_index * block_width
        carried = stat_update(carried, offset_at)
        return (carried, None)

    initial = (jnp.full((rows_total,), MASKED, jnp.float32), jnp.zeros((rows_total,), jnp.float32))
    (maximum, running_sum), unused = lax.scan(
        stat_step, initial, jnp.arange(steps_count, dtype=jnp.int32)
    )
    log_total = maximum + jnp.log(running_sum)

    def value_update(accumulated, offset_at):
        scores = score_block(query_rows, row_pos, keys_all, key_pos, length, offset_at, block_width)
        weights_low = jnp.exp(scores - log_total[:, None]).astype(jnp.bfloat16)
        value_part = lax.dynamic_slice_in_dim(values_all, offset_at, block_width, 0)
        return accumulated + jnp.dot(weights_low, value_part, preferred_element_type=jnp.float32)

    def value_step(accumulated, step_index):
        offset_at = step_index * block_width
        accumulated = value_update(accumulated, offset_at)
        return (accumulated, None)

    attention, unused = lax.scan(
        value_step,
        jnp.zeros((rows_total, head_dim), jnp.float32),
        jnp.arange(steps_count, dtype=jnp.int32),
    )
    return (attention.reshape(local_len, head_count * head_dim), log_total)


def attention_backward(
    query_rot, kv_slot, query_pos, key_pos, length, log_total, grad_attn, row_delta
):
    local_len, head_count, head_dim = query_rot.shape
    rows_total = local_len * head_count
    query_rows = query_rot.reshape(rows_total, head_dim)
    grad_rows = grad_attn.reshape(rows_total, head_dim)
    row_pos = jnp.repeat(query_pos, head_count)
    keys_all = kv_slot[:, :head_dim]
    values_all = kv_slot[:, head_dim:]
    block_width = min(512, kv_slot.shape[0])
    steps_count = kv_slot.shape[0] // block_width

    def grad_update(grad_query, offset_at):
        scores = score_block(query_rows, row_pos, keys_all, key_pos, length, offset_at, block_width)
        probability = jnp.exp(scores - log_total[:, None])
        key_part = lax.dynamic_slice_in_dim(keys_all, offset_at, block_width, 0)
        value_part = lax.dynamic_slice_in_dim(values_all, offset_at, block_width, 0)
        grad_prob = contract_cols(grad_rows, value_part)
        grad_score = (probability * (grad_prob - row_delta[:, None])).astype(jnp.bfloat16)
        grad_key = contract_rows(grad_score, query_rows)
        grad_value = contract_rows(probability.astype(jnp.bfloat16), grad_rows)
        updated = grad_query + jnp.dot(grad_score, key_part, preferred_element_type=jnp.float32)
        return (updated, jnp.concatenate([grad_key, grad_value], axis=1))

    def grad_step(grad_query, step_index):
        offset_at = step_index * block_width
        return grad_update(grad_query, offset_at)

    grad_query, key_grads = lax.scan(
        grad_step,
        jnp.zeros((rows_total, head_dim), jnp.float32),
        jnp.arange(steps_count, dtype=jnp.int32),
    )
    return (
        grad_query.reshape(local_len, head_count, head_dim),
        key_grads.reshape(steps_count * block_width, 2 * head_dim),
    )


def swiglu_back(gate_proj, up_proj, grad_hidden):
    sigmoid_gate = jax.nn.sigmoid(gate_proj)
    grad_float = grad_hidden.astype(jnp.float32)
    grad_gate = (
        grad_float * up_proj * sigmoid_gate * (1.0 + gate_proj * (1.0 - sigmoid_gate))
    ).astype(jnp.bfloat16)
    grad_up = (grad_float * (gate_proj * sigmoid_gate)).astype(jnp.bfloat16)
    return (grad_gate, grad_up)


def split_term(left, right, ctx_count, fsdp_count):
    left_split = left.reshape(left.shape[0], ctx_count, left.shape[1] // ctx_count)
    right_split = right.reshape(right.shape[0], fsdp_count, right.shape[1] // fsdp_count)
    grad_term = jnp.einsum(
        "tcd,tfk->cfdk", left_split, right_split, preferred_element_type=jnp.float32
    )
    return grad_term.reshape(ctx_count * fsdp_count * grad_term.shape[2], grad_term.shape[3])


def shards(
    tokens,
    cotangent,
    kv_cotangent,
    lengths,
    block_order,
    w_query,
    w_kv,
    w_out,
    gain_attn,
    gain_ffn,
    w_gate,
    w_up,
    w_down,
):
    slots_here, local_len, model_dim = tokens.shape
    ctx_count = lax.axis_size("ctx")
    fsdp_count = lax.axis_size("fsdp")
    head_dim = HD
    head_count = H
    block_len = local_len // 2
    slot_len = local_len * ctx_count
    local_rows = slots_here * local_len
    offsets = jnp.arange(slot_len, dtype=jnp.int32) % block_len
    key_pos = jnp.repeat(block_order, block_len, axis=1) * block_len + offsets[None, :]
    query_pos = lax.dynamic_slice_in_dim(key_pos, lax.axis_index("ctx") * local_len, local_len, 1)
    live_rows = (query_pos < lengths[:, None]).reshape(local_rows, 1)
    query_full, kv_full, out_full, gain_one, gain_two = (
        lax.all_gather(w_query, "fsdp", axis=0, tiled=True),
        lax.all_gather(w_kv, "fsdp", axis=0, tiled=True),
        lax.all_gather(w_out, "fsdp", axis=0, tiled=True),
        lax.all_gather(gain_attn, "fsdp", axis=0, tiled=True),
        lax.all_gather(gain_ffn, "fsdp", axis=0, tiled=True),
    )
    tokens_flat = tokens.reshape(local_rows, model_dim).astype(jnp.float32)
    inverse_one = lax.rsqrt(jnp.mean(tokens_flat * tokens_flat, axis=1, keepdims=True) + EPSILON)
    unit_one = tokens_flat * inverse_one
    normed_attn = (unit_one * gain_one.astype(jnp.float32)).astype(jnp.bfloat16)
    queries = jnp.dot(normed_attn, query_full, preferred_element_type=jnp.float32).reshape(
        local_rows, head_count, head_dim
    )
    key_value = jnp.dot(normed_attn, kv_full, preferred_element_type=jnp.float32)
    cosine, sine_vals = angles(query_pos.reshape(local_rows), head_dim)
    query_rot = (
        rotate(queries, cosine[:, None, :], sine_vals[:, None, :]) * head_dim ** (-0.5)
    ).astype(jnp.bfloat16)
    key_rot = rotate(key_value[:, :head_dim], cosine, sine_vals).astype(jnp.bfloat16)
    local_kv = jnp.concatenate([key_rot, key_value[:, head_dim:].astype(jnp.bfloat16)], axis=1)
    slot_kv = lax.all_gather(
        local_kv.reshape(slots_here, local_len, 2 * head_dim), "ctx", axis=1, tiled=True
    )
    slot_queries = query_rot.reshape(slots_here, local_len, head_count, head_dim)

    def slot_forward(inputs):
        query_slot, kv_slot, pos_query, pos_key, length, order_row = inputs
        return attention_forward(query_slot, kv_slot, pos_query, pos_key, length)

    attention, log_total = lax.map(
        slot_forward, (slot_queries, slot_kv, query_pos, key_pos, lengths, block_order)
    )
    attention = attention.reshape(local_rows, head_count * head_dim)
    attn_low = attention.astype(jnp.bfloat16)
    residual = tokens_flat + jnp.dot(attn_low, out_full, preferred_element_type=jnp.float32)
    inverse_two = lax.rsqrt(jnp.mean(residual * residual, axis=1, keepdims=True) + EPSILON)
    unit_two = residual * inverse_two
    normed_ffn = (unit_two * gain_two.astype(jnp.float32)).astype(jnp.bfloat16)
    grad_out = jnp.where(
        live_rows, cotangent.reshape(local_rows, model_dim), jnp.zeros((), jnp.bfloat16)
    )
    gate_full, up_full, down_full = (
        lax.all_gather(w_gate, "fsdp", axis=1, tiled=True),
        lax.all_gather(w_up, "fsdp", axis=1, tiled=True),
        lax.all_gather(w_down, "fsdp", axis=1, tiled=True),
    )
    gate_proj = jnp.dot(normed_ffn, gate_full, preferred_element_type=jnp.float32)
    up_proj = jnp.dot(normed_ffn, up_full, preferred_element_type=jnp.float32)
    hidden = (jax.nn.silu(gate_proj) * up_proj).astype(jnp.bfloat16)
    ffn_out = contract_cols(hidden, down_full)
    grad_hidden = jnp.dot(grad_out, down_full, preferred_element_type=jnp.float32).astype(
        jnp.bfloat16
    )
    grad_gate, grad_up = swiglu_back(gate_proj, up_proj, grad_hidden)
    grad_normed = contract_cols(grad_gate, gate_full) + contract_cols(grad_up, up_full)
    ffn_grads = (
        lax.psum_scatter(
            split_term(normed_ffn, grad_gate, ctx_count, fsdp_count),
            ("ctx", "fsdp"),
            scatter_dimension=0,
            tiled=True,
        ),
        lax.psum_scatter(
            split_term(normed_ffn, grad_up, ctx_count, fsdp_count),
            ("ctx", "fsdp"),
            scatter_dimension=0,
            tiled=True,
        ),
        lax.psum_scatter(
            split_term(grad_out, hidden, ctx_count, fsdp_count),
            ("ctx", "fsdp"),
            scatter_dimension=0,
            tiled=True,
        ),
    )
    output = jnp.where(live_rows, residual + ffn_out, 0.0)
    grad_gain_two = jnp.sum(grad_normed * unit_two, axis=0)
    scaled_two = grad_normed * gain_two.astype(jnp.float32)
    grad_residual = grad_out.astype(jnp.float32) + inverse_two * (
        scaled_two - unit_two * jnp.mean(scaled_two * unit_two, axis=1, keepdims=True)
    )
    grad_branch = grad_residual.astype(jnp.bfloat16)
    grad_attn = contract_cols(grad_branch, out_full).astype(jnp.bfloat16)
    row_delta = jnp.sum(
        grad_attn.astype(jnp.float32).reshape(local_rows, head_count, head_dim)
        * attention.reshape(local_rows, head_count, head_dim),
        axis=2,
    )

    def slot_backward(inputs):
        (
            query_slot,
            kv_slot,
            pos_query,
            pos_key,
            length,
            log_slot,
            grad_slot,
            delta_slot,
            order_row,
        ) = inputs
        grad_query_slot, key_grads = attention_backward(
            query_slot, kv_slot, pos_query, pos_key, length, log_slot, grad_slot, delta_slot
        )
        return (grad_query_slot, key_grads)

    grad_query_rot, key_terms = lax.map(
        slot_backward,
        (
            slot_queries,
            slot_kv,
            query_pos,
            key_pos,
            lengths,
            log_total,
            grad_attn.reshape(slots_here, local_len, head_count, head_dim),
            row_delta.reshape(slots_here, local_len * head_count),
            block_order,
        ),
    )
    key_sums = lax.psum_scatter(
        key_terms.astype(jnp.bfloat16), "ctx", scatter_dimension=1, tiled=True
    ).astype(jnp.float32)
    kv_total = key_sums + jnp.where(
        live_rows.reshape(slots_here, local_len, 1), kv_cotangent.astype(jnp.float32), 0.0
    )
    grad_kv_low = kv_total.reshape(local_rows, 2 * head_dim).astype(jnp.bfloat16)
    grad_key = rotate(grad_kv_low[:, :head_dim].astype(jnp.float32), cosine, -sine_vals)
    grad_kv = jnp.concatenate(
        [grad_key, grad_kv_low[:, head_dim:].astype(jnp.float32)], axis=1
    ).astype(jnp.bfloat16)
    grad_qrot = (
        grad_query_rot.reshape(local_rows, head_count, head_dim)
        .astype(jnp.bfloat16)
        .astype(jnp.float32)
    )
    grad_query = (
        (rotate(grad_qrot, cosine[:, None, :], -sine_vals[:, None, :]) * head_dim ** (-0.5))
        .reshape(local_rows, head_count * head_dim)
        .astype(jnp.bfloat16)
    )
    grad_normed_one = contract_cols(grad_query, query_full) + contract_cols(grad_kv, kv_full)
    grad_gain_one = jnp.sum(grad_normed_one * unit_one, axis=0)
    scaled_one = grad_normed_one * gain_one.astype(jnp.float32)
    grad_tokens = grad_residual + inverse_one * (
        scaled_one - unit_one * jnp.mean(scaled_one * unit_one, axis=1, keepdims=True)
    )
    attn_grads = (
        lax.psum_scatter(
            contract_rows(normed_attn, grad_query), ("ctx", "fsdp"), scatter_dimension=0, tiled=True
        ),
        lax.psum_scatter(
            contract_rows(normed_attn, grad_kv), ("ctx", "fsdp"), scatter_dimension=0, tiled=True
        ),
        lax.psum_scatter(
            contract_rows(attn_low, grad_branch), ("ctx", "fsdp"), scatter_dimension=0, tiled=True
        ),
        lax.psum_scatter(grad_gain_one, ("ctx", "fsdp"), scatter_dimension=0, tiled=True),
        lax.psum_scatter(grad_gain_two, ("ctx", "fsdp"), scatter_dimension=0, tiled=True),
    )
    return (
        output.reshape(tokens.shape).astype(jnp.bfloat16),
        grad_tokens.reshape(tokens.shape).astype(jnp.bfloat16),
        attn_grads[0],
        attn_grads[1],
        attn_grads[2],
        attn_grads[3],
        attn_grads[4],
        ffn_grads[0],
        ffn_grads[1],
        ffn_grads[2],
    )


def solution(mesh):
    return jax.shard_map(
        shards,
        mesh=mesh,
        in_specs=(
            P("fsdp", "ctx", None),
            P("fsdp", "ctx", None),
            P("fsdp", "ctx", None),
            P("fsdp"),
            P("fsdp", None),
            P("fsdp", None),
            P("fsdp", None),
            P("fsdp", None),
            P("fsdp"),
            P("fsdp"),
            P(None, "fsdp"),
            P(None, "fsdp"),
            P(None, "fsdp"),
        ),
        out_specs=(
            P("fsdp", "ctx", None),
            P("fsdp", "ctx", None),
            P(("ctx", "fsdp"), None),
            P(("ctx", "fsdp"), None),
            P(("ctx", "fsdp"), None),
            P(("ctx", "fsdp")),
            P(("ctx", "fsdp")),
            P("ctx", "fsdp"),
            P("ctx", "fsdp"),
            P("ctx", "fsdp"),
        ),
        check_vma=False,
    )
```

profile of v0, /device:TPU:0, one launch (start us, length us, event | category | flops | bytes accessed | tf_op | source)
XLA Modules:
  0.0 5839.8 jit_solution(3675595155620998251)
XLA Ops:
  8.6 13.5 all-gather.1
  26.3 14.0 all-gather.11.cloned.1.call-done
  47.8 12.4 all-gather.2
  60.2 12.0 all-gather.23.cloned.1.call-done
  75.9 147.6 %all-gather.13.cloned.1.call-done = bf16[2048,2048]{1,0:T(8,128)(2,1)} async-done(((bf16[512,2048]{1,0:T(8,128)(2,1)}), bf16[2048,2048]{1,0:T(8,128)(2,1)}) %all-gather.13.cloned.1.call-update) | async-done | bytes 8388624 | tf_op jit(solution)/shard_map/all_gather | solution.py:191
  223.5 12.6 copy.58
  258.7 154.5 %while.58 = (s32[]{:T(128)}, f32[8192]{0:T(1024)S(1)}, f32[8192]{0:T(1024)S(1)}, s32[8]{0:T(128)S(1)}, s32[4096]{0:T(1024)S(1)}, /*index=5*/s32[]{:T(128)}, bf16...) while((s32[]{:T(128)}, f32[8192]{0:T(1024)S(1)}, ...), condition=%wide.region_4.5_spmd.clone, body=%wide.region_1.4_spmd.clone.sunk | while | flops 1111532032 | bytes 36384468 | solution.py:80
  374.0 10.1 fusion.159
  384.1 10.2 exponential_reduce_fusion.2
  413.8 110.1 %while.59 = (s32[]{:T(128)}, f32[8192,128]{1,0:T(8,128)}, s32[8]{0:T(128)S(1)}, s32[4096]{0:T(1024)S(1)}, s32[]{:T(128)}, /*index=5*/bf16[4096,128]{1,0:T(8,128)...) while((s32[]{:T(128)}, f32[8192,128]{1,0:T(8,128)}, ...), condition=%wide.region_6.7_spmd.clone, body=%wide.region_5.6_spmd.clone.sunk | while | flops 2170552832 | bytes 10922712 | solution.py:96
  416.2 10.3 convolution_add_fusion.6
  428.8 11.7 convolution_add_fusion.6
  442.7 11.7 convolution_add_fusion.6
  456.7 11.7 convolution_add_fusion.6
  470.6 11.7 convolution_add_fusion.6
  484.5 11.7 convolution_add_fusion.6
  498.4 11.7 convolution_add_fusion.6
  512.3 11.7 convolution_add_fusion.6
  533.0 9.3 multiply_reduce_fusion.3
  546.1 217.5 %all-gather.17.cloned.1.call-done = bf16[2048,5632]{1,0:T(8,128)(2,1)} async-done(((bf16[2048,1408]{1,0:T(8,128)(2,1)}), bf16[2048,5632]{1,0:T(8,128)(2,1)}) %all-gather.17.cloned.1.call-update) | async-done | bytes 23068688 | tf_op jit(solution)/shard_map/all_gather | solution.py:233
  763.6 20.2 fusion.102
  783.8 370.7 %all-gather.21.cloned.1.call-done = bf16[2048,5632]{1,0:T(8,128)(2,1)} async-done(((bf16[2048,1408]{1,0:T(8,128)(2,1)}), bf16[2048,5632]{1,0:T(8,128)(2,1)}) %all-gather.21.cloned.1.call-update) | async-done | bytes 23068688 | tf_op jit(solution)/shard_map/all_gather | solution.py:235
  1154.5 18.4 convolution_convert_fusion
  1172.9 372.6 %all-gather.19.cloned.1.call-done = bf16[2048,5632]{1,0:T(8,128)(2,1)} async-done(((bf16[2048,1408]{1,0:T(8,128)(2,1)}), bf16[2048,5632]{1,0:T(8,128)(2,1)}) %all-gather.19.cloned.1.call-update) | async-done | bytes 23068688 | tf_op jit(solution)/shard_map/all_gather | solution.py:234
  1545.5 26.8 fusion.34
  1572.4 19.5 fusion.103
  1591.9 19.4 multiply_reduce_fusion
  1615.0 9.2 convolution_convert_fusion.1
  1632.7 354.5 %while.60 = (s32[]{:T(128)}, f32[8192,128]{1,0:T(8,128)}, bf16[8,512,256]{1,2,0:T(8,128)(2,1)}, s32[8]{0:T(128)S(1)}, s32[4096]{0:T(1024)}, /*index=5*/s32[]{:T(...) while((s32[]{:T(128)}, f32[8192,128]{1,0:T(8,128)}, ...), condition=%wide.region_11.12_spmd.clone, body=%wide.region_10.11_spmd.clone.sunk | while | flops 5404885504 | bytes 127214928 | solution.py:133
  1636.0 10.4 fusion.174
  1646.4 9.5 fusion.175
  1679.2 10.4 fusion.174
  1689.6 9.5 fusion.175
  1723.6 10.4 fusion.174
  1734.0 9.5 fusion.175
  1768.0 10.4 fusion.174
  1778.4 9.5 fusion.175
  1787.9 9.1 convolution_add_fusion.7
  1812.4 10.4 fusion.174
  1822.8 9.5 fusion.175
  1856.9 10.4 fusion.174
  1867.3 9.5 fusion.175
  1901.3 10.4 fusion.174
  1911.7 9.5 fusion.175
  1945.7 10.4 fusion.174
  1956.1 9.5 fusion.175
  1996.2 39.3 reduce-scatter.8.cloned.1.call-done
  2039.7 13.2 fusion.65
  2084.4 11.2 reshape.367
  2095.6 20.8 convolution_bitcast_fusion.2
  2116.4 33.3 copy.72
  2150.2 11.1 reshape.370
  2161.3 20.9 convolution_bitcast_fusion.1
  2182.1 33.6 copy.75
  2221.8 11.1 reshape.372
  2232.8 20.8 convolution_bitcast_fusion
  2253.6 33.4 copy.78
  2287.0 19.9 fusion.59
  2318.9 43.8 all-reduce.2
  2369.7 174.0 %reduce-scatter.14.cloned.1.call-done = f32[64,2048]{1,0:T(8,128)} async-done(((f32[2048,2048]{1,0:T(8,128)}), f32[64,2048]{1,0:T(8,128)}) %reduce-scatter.14.cloned.1.call-update) | async-done | bytes 524304 | tf_op jit(solution)/shard_map/reduce_scatter | solution.py:345
  2543.7 365.1 %reduce-scatter.10.cloned.1.call-done = f32[64,2048]{1,0:T(8,128)} async-done(((f32[2048,2048]{1,0:T(8,128)}), f32[64,2048]{1,0:T(8,128)}) %reduce-scatter.10.cloned.1.call-update) | async-done | bytes 524304 | tf_op jit(solution)/shard_map/reduce_scatter | solution.py:339
  2908.8 973.1 %reduce-scatter.16.cloned.1.call-done = f32[256,1408]{1,0:T(8,128)} async-done(((f32[8192,1408]{1,0:T(8,128)}), f32[256,1408]{1,0:T(8,128)}) %reduce-scatter.16.cloned.1.call-update) | async-done | bytes 1441808 | tf_op jit(solution)/shard_map/reduce_scatter | solution.py:247
  3881.8 975.7 %reduce-scatter.18.cloned.1.call-done = f32[256,1408]{1,0:T(8,128)} async-done(((f32[8192,1408]{1,0:T(8,128)}), f32[256,1408]{1,0:T(8,128)}) %reduce-scatter.18.cloned.1.call-update) | async-done | bytes 1441808 | tf_op jit(solution)/shard_map/reduce_scatter | solution.py:253
  4857.5 975.5 %reduce-scatter.20.cloned.1.call-done = f32[256,1408]{1,0:T(8,128)} async-done(((f32[8192,1408]{1,0:T(8,128)}), f32[256,1408]{1,0:T(8,128)}) %reduce-scatter.20.cloned.1.call-update) | async-done | bytes 1441808 | tf_op jit(solution)/shard_map/reduce_scatter | solution.py:259
  (406 shorter events, 454.8 us)
Async XLA Ops:
  7.2 33.1 all-gather.11.cloned.1.call-start
  7.9 64.3 %all-gather.23.cloned.1.call-start = ((), (), s32[]{:S(2)}) async-start(), calls=%async_computation.20 | async-start | bytes 2359296 | tf_op jit(solution)/shard_map/all_gather | solution.py:211
  22.2 213.9 %copy-start.28 = (f32[4,1,512]{2,1,0:T(1,128)}, f32[4,1,512]{2,1,0:T(1,128)S(1)}, u32[]{:S(2)}) copy-start(f32[4,1,512]{2,1,0:T(1,128)S(1)} %convert_element_type.188) | copy-start | bytes 24580
  24.2 20.2 copy-start.32
  24.2 20.2 copy-start.41
  26.3 209.9 %copy-start.34 = (f32[512]{0:T(512)}, f32[512]{0:T(512)S(1)}, u32[]{:S(2)}) copy-start(f32[512]{0:T(512)S(1)} %add_rsqrt_fusion.1) | copy-start | bytes 6148
  43.6 199.7 %copy-start.15 = (f32[512,64]{0,1:T(8,128)}, f32[512,64]{0,1:T(8,128)S(1)}, u32[]{:S(2)}) copy-start(f32[512,64]{0,1:T(8,128)S(1)} %get-tuple-element.548) | copy-start | bytes 393220
  44.4 179.1 %all-gather.13.cloned.1.call-start = ((), (), s32[]{:S(2)}) async-start(), calls=%async_computation.8 | async-start | bytes 10485760 | tf_op jit(solution)/shard_map/all_gather | solution.py:191
  45.1 487.9 %all-gather.15.cloned.1.call-start = ((), (), s32[]{:S(2)}) async-start(), calls=%async_computation.9 | async-start | bytes 10485760 | tf_op jit(solution)/shard_map/all_gather | solution.py:193
  45.7 717.9 %all-gather.17.cloned.1.call-start = ((), (), s32[]{:S(2)}) async-start(), calls=%async_computation.10 | async-start | bytes 28835840 | tf_op jit(solution)/shard_map/all_gather | solution.py:233
  46.3 1108.2 %all-gather.21.cloned.1.call-start = ((), (), s32[]{:S(2)}) async-start(), calls=%async_computation.12 | async-start | bytes 28835840 | tf_op jit(solution)/shard_map/all_gather | solution.py:235
  46.9 1498.6 %all-gather.19.cloned.1.call-start = ((), (), s32[]{:S(2)}) async-start(), calls=%async_computation.11 | async-start | bytes 28835840 | tf_op jit(solution)/shard_map/all_gather | solution.py:234
  47.6 1987.9 %reduce-scatter.8.cloned.1.call-start = ((), (), s32[]{:S(2)}) async-start(), calls=%async_computation.13 | async-start | bytes 2359296 | tf_op jit(solution)/shard_map/reduce_scatter | solution.py:311
  223.5 12.6 copy-start.2
  523.9 9.0 copy-start
  523.9 9.0 copy-start.12
  524.0 9.0 copy-start.18
  524.0 9.0 copy-start.27
  546.1 608.4 %copy-start.9 = (bf16[1,512,2048]{2,1,0:T(8,128)(2,1)S(1)}, bf16[1,512,2048]{2,1,0:T(8,128)(2,1)}, u32[]{:S(2)}) copy-start(bf16[1,512,2048]{2,1,0:T(8,128)(2,1)} %param.20) | copy-start | bytes 6291460
  546.1 608.4 %copy-start.37 = (pred[512]{0:T(512)(128)(4,1)S(1)}, pred[512]{0:T(512)(128)(4,1)}, u32[]{:S(2)}) copy-start(pred[512]{0:T(512)(128)(4,1)} %get-tuple-element.526) | copy-start | bytes 1540
  1591.9 19.5 copy-start.7
  1655.9 16.7 slice-start
  1663.8 8.8 slice-start.1
  1663.8 8.8 copy-start.1
  1699.1 17.9 slice-start
  1708.2 8.8 slice-start.1
  1708.2 8.8 copy-start.1
  1743.5 17.9 slice-start
  1752.6 8.8 slice-start.1
  1752.6 8.8 copy-start.1
  1787.9 17.9 slice-start
  1797.0 8.8 slice-start.1
  1797.0 8.8 copy-start.1
  1832.3 17.9 slice-start
  1841.4 8.8 slice-start.1
  1841.5 8.8 copy-start.1
  1876.7 17.9 slice-start
  1885.9 8.8 slice-start.1
  1885.9 8.8 copy-start.1
  1921.2 17.9 slice-start
  1930.3 8.8 slice-start.1
  1930.3 8.8 copy-start.1
  1965.6 17.9 slice-start
  1974.7 8.8 slice-start.1
  1974.7 8.8 copy-start.1
  1991.4 44.1 copy-start.38
  1991.4 45.2 copy-start.33
  1991.4 45.2 copy-start.42
  1991.4 45.8 copy-start.3
  1991.4 45.8 copy-start.29
  1991.4 45.8 copy-start.35
  1995.8 373.9 %reduce-scatter.12.cloned.1.call-start = ((), (), s32[]{:S(2)}) async-start(), calls=%async_computation.15 | async-start | bytes 2162688 | tf_op jit(solution)/shard_map/reduce_scatter | solution.py:342
  2039.7 504.0 %reduce-scatter.14.cloned.1.call-start = ((), (), s32[]{:S(2)}) async-start(), calls=%async_computation.16 | async-start | bytes 17301504 | tf_op jit(solution)/shard_map/reduce_scatter | solution.py:345
  2053.0 855.8 %reduce-scatter.10.cloned.1.call-start = ((), (), s32[]{:S(2)}) async-start(), calls=%async_computation.14 | async-start | bytes 17301504 | tf_op jit(solution)/shard_map/reduce_scatter | solution.py:339
  2080.3 1801.5 %reduce-scatter.16.cloned.1.call-start = ((), (), s32[]{:S(2)}) async-start(), calls=%async_computation.17 | async-start | bytes 47579136 | tf_op jit(solution)/shard_map/reduce_scatter | solution.py:247
  2084.4 11.2 copy-start.14
  2149.7 2707.8 %reduce-scatter.18.cloned.1.call-start = ((), (), s32[]{:S(2)}) async-start(), calls=%async_computation.18 | async-start | bytes 47579136 | tf_op jit(solution)/shard_map/reduce_scatter | solution.py:253
  2215.8 3617.3 %reduce-scatter.20.cloned.1.call-start = ((), (), s32[]{:S(2)}) async-start(), calls=%async_computation.19 | async-start | bytes 47579136 | tf_op jit(solution)/shard_map/reduce_scatter | solution.py:259
  2306.9 8.1 copy-start.17
  2306.9 8.1 copy-start.21
  2306.9 8.1 copy-start.23
  2306.9 8.1 copy-start.25
  2306.9 8.1 copy-start.30
  2306.9 8.1 copy-start.36
  (17 other events, 41.8 us)
Sparse Core Ops, SparseCore 0:
  9.6 30.6 all-gather.10
  44.5 27.6 all-gather.22
  73.8 149.6 all-gather.12
  224.9 147.8 all-gather.14
  374.3 389.3 all-gather.16
  765.1 389.3 all-gather.20
  1156.1 389.3 all-gather.18
  1995.9 39.5 reduce-scatter.7
  2039.8 138.3 reduce-scatter.11
  2180.9 362.8 reduce-scatter.13
  2546.6 362.1 reduce-scatter.9
  2911.5 970.2 reduce-scatter.15
  3884.7 972.7 reduce-scatter.17
  4860.3 972.7 reduce-scatter.19
where the time goes:
time: 5850 us; the launch traced here: 5840 us
  waiting for transfers between devices  4640 us (79%)
  matrix products  733 us (13%)
  local copies, waits for them, and re-layouts  224 us (4%)
  other arithmetic  138 us (2%)
  blocking collectives  69.7 us (1%)
    reduce_scatter x1, waiting for transfers between devices, shards(): lax.psum_scatter(split_term(normed_ffn, grad_up, ctx_count, fsdp_count),...  976 us
    reduce_scatter x1, waiting for transfers between devices, shards(): lax.psum_scatter(split_term(grad_out, hidden, ctx_count, fsdp_count), ('c...  976 us
    reduce_scatter x1, waiting for transfers between devices, shards(): lax.psum_scatter(split_term(normed_ffn, grad_gate, ctx_count, fsdp_count)...  973 us
    all_gather x1, waiting for transfers between devices, shards(): lax.all_gather(w_up, 'fsdp', axis=1, tiled=True)  373 us
    all_gather x1, waiting for transfers between devices, shards(): lax.all_gather(w_down, 'fsdp', axis=1, tiled=True)  371 us
    reduce_scatter x1, waiting for transfers between devices, shards(): lax.psum_scatter(contract_rows(normed_attn, grad_query), ('ctx', 'fsdp'),...  365 us
    dot_general x30, matrix products, contract_cols(): lax.dot_general(left, right, (((1,), (1,)), ((), ())), preferred_element_...  304 us
    all_gather x1, waiting for transfers between devices, shards(): lax.all_gather(w_gate, 'fsdp', axis=1, tiled=True)  217 us
  transfers between devices with their start and end apart: 14, of which 12 were waited for; matrix products, arithmetic and copies ran while one was open for 11% of the time, Pallas kernels for 0%

commit v1 on v0

v1 whole, which is shorter than its diff:
```python
import functools
import jax
import jax.numpy as jnp
from jax import lax
from jax.experimental import pallas as pl
from jax.experimental.pallas import tpu as pltpu
from jax.sharding import Mesh
from jax.sharding import PartitionSpec as P

H = 16
HD = 128
MASKED = -1e30
LN2 = 0.6931471805599453

def block_places(order_ref, place_ref, own, count):
    for stored in range(count):
        relative = ((stored // 2) ^ own) * 2 + stored % 2
        place_ref[order_ref[stored]] = relative


def attend_forward(group, blk, scal_ref, order_ref, q_ref, kv_ref, out_ref, lse_ref, place_ref, qt_ref, vt_ref, acc_ref, max_ref, sum_ref):
    row_block, head_group = pl.program_id(0), pl.program_id(1)
    own, length = scal_ref[0], scal_ref[1]
    count = order_ref.shape[0]

    @pl.when((row_block == 0) & (head_group == 0))
    def _():
        block_places(order_ref, place_ref, own, count)
        for piece in range(count):
            vt_ref[:, piece * blk:(piece + 1) * blk] = kv_ref[piece * blk:(piece + 1) * blk, HD:].T

    mine = order_ref[2 * (own ^ (row_block // 2)) + row_block % 2]
    for head in range(group):
        qt_ref[:, head * blk:(head + 1) * blk] = q_ref[:, head * HD:(head + 1) * HD].T
    max_ref[...] = jnp.full(max_ref.shape, MASKED, jnp.float32)
    sum_ref[...] = jnp.zeros(sum_ref.shape, jnp.float32)
    acc_ref[...] = jnp.zeros(acc_ref.shape, jnp.float32)

    def step(place, masked):
        start = pl.multiple_of(place * blk, blk)
        scores = jnp.dot(kv_ref[pl.ds(start, blk), :HD], qt_ref[...], preferred_element_type=jnp.float32)
        if masked:
            keys = lax.broadcasted_iota(jnp.int32, (blk, blk), 0)
            rows = lax.broadcasted_iota(jnp.int32, (blk, blk), 1)
            scores = jnp.where(jnp.concatenate([keys <= rows] * group, axis=1), scores, MASKED)
        old = max_ref[...]
        new = jnp.maximum(old, jnp.max(scores, axis=0, keepdims=True))
        weights = jnp.exp2(scores - new)
        scale = jnp.exp2(old - new)
        max_ref[...] = new
        sum_ref[...] = sum_ref[...] * scale + jnp.sum(weights, axis=0, keepdims=True)
        acc_ref[...] = acc_ref[...] * scale + jnp.dot(
            vt_ref[:, pl.ds(start, blk)], weights.astype(jnp.bfloat16), preferred_element_type=jnp.float32)

    @pl.when(mine * blk < length)
    def _():
        step(place_ref[mine], True)

        def body(j, carried):
            step(place_ref[j], False)
            return carried
        lax.fori_loop(0, mine, body, 0)
        total = sum_ref[...]
        result = acc_ref[...] * (1.0 / total)
        for head in range(group):
            out_ref[:, head * HD:(head + 1) * HD] = result[:, head * blk:(head + 1) * blk].T.astype(jnp.bfloat16)
        lse_ref[0] = max_ref[...] + jnp.log2(total)

    @pl.when(mine * blk >= length)
    def _():
        out_ref[...] = jnp.zeros(out_ref.shape, jnp.bfloat16)
        lse_ref[...] = jnp.zeros(lse_ref.shape, jnp.float32)


def attention_forward(scalars, order, queries, keys_values, group, blk):
    rows, width = queries.shape
    span = keys_values.shape[0]
    row_blocks, head_groups = rows // blk, width // (group * HD)
    return pl.pallas_call(
        functools.partial(attend_forward, group, blk),
        grid_spec=pltpu.PrefetchScalarGridSpec(
            num_scalar_prefetch=2,
            grid=(row_blocks, head_groups),
            in_specs=[
                pl.BlockSpec((blk, group * HD), lambda i, g, *_: (i, g)),
                pl.BlockSpec((span, 2 * HD), lambda i, g, *_: (0, 0)),
            ],
            out_specs=[
                pl.BlockSpec((blk, group * HD), lambda i, g, *_: (i, g)),
                pl.BlockSpec((1, 1, group * blk), lambda i, g, *_: (i * head_groups + g, 0, 0)),
            ],
            scratch_shapes=[
                pltpu.SMEM((order.shape[0],), jnp.int32),
                pltpu.VMEM((HD, group * blk), jnp.bfloat16),
                pltpu.VMEM((HD, span), jnp.bfloat16),
                pltpu.VMEM((HD, group * blk), jnp.float32),
                pltpu.VMEM((1, group * blk), jnp.float32),
                pltpu.VMEM((1, group * blk), jnp.float32),
            ],
        ),
        out_shape=[
            jax.ShapeDtypeStruct((rows, width), jnp.bfloat16),
            jax.ShapeDtypeStruct((row_blocks * head_groups, 1, group * blk), jnp.float32),
        ],
        compiler_params=pltpu.CompilerParams(vmem_limit_bytes=40 * 2**20),
        cost_estimate=pl.CostEstimate(flops=3 * rows * width * span, bytes_accessed=4 * rows * width + 4 * span * HD, transcendentals=rows * span * width // HD),
        name="attend_forward",
    )(scalars, order, queries, keys_values)


def attend_backward(group, blk, scal_ref, order_ref, q_ref, g_ref, a_ref, lse_ref, kv_ref, dq_ref, dkv_ref, place_ref, qt_ref, gt_ref, qs_ref, gs_ref, kt_ref, acc_ref, delta_ref):
    row_block, head_group = pl.program_id(0), pl.program_id(1)
    own, length = scal_ref[0], scal_ref[1]
    count = order_ref.shape[0]

    @pl.when((row_block == 0) & (head_group == 0))
    def _():
        block_places(order_ref, place_ref, own, count)
        for piece in range(count):
            kt_ref[:, piece * blk:(piece + 1) * blk] = kv_ref[piece * blk:(piece + 1) * blk, :HD].T
        dkv_ref[...] = jnp.zeros(dkv_ref.shape, jnp.float32)

    mine = order_ref[2 * (own ^ (row_block // 2)) + row_block % 2]

    def step(place, masked):
        start = pl.multiple_of(place * blk, blk)
        scores = jnp.dot(kv_ref[pl.ds(start, blk), :HD], qt_ref[...], preferred_element_type=jnp.float32)
        weights = jnp.exp2(scores - lse_ref[0])
        if masked:
            keys = lax.broadcasted_iota(jnp.int32, (blk, blk), 0)
            rows = lax.broadcasted_iota(jnp.int32, (blk, blk), 1)
            weights = jnp.where(jnp.concatenate([keys <= rows] * group, axis=1), weights, 0.0)
        grads = jnp.dot(kv_ref[pl.ds(start, blk), HD:], gt_ref[...], preferred_element_type=jnp.float32)
        dscores = (weights * (grads - delta_ref[...])).astype(jnp.bfloat16)
        dkv_ref[pl.ds(start, blk), HD:] += jnp.dot(weights.astype(jnp.bfloat16), gs_ref[...], preferred_element_type=jnp.float32)
        dkv_ref[pl.ds(start, blk), :HD] += jnp.dot(dscores, qs_ref[...], preferred_element_type=jnp.float32)
        acc_ref[...] += jnp.dot(kt_ref[:, pl.ds(start, blk)], dscores, preferred_element_type=jnp.float32)

    @pl.when(mine * blk < length)
    def _():
        for head in range(group):
            lanes = slice(head * HD, (head + 1) * HD)
            cells = slice(head * blk, (head + 1) * blk)
            query, grad = q_ref[:, lanes], g_ref[:, lanes]
            qt_ref[:, cells] = query.T
            gt_ref[:, cells] = grad.T
            qs_ref[cells, :] = query
            gs_ref[cells, :] = grad
            product = grad.astype(jnp.float32) * a_ref[:, lanes].astype(jnp.float32)
            delta_ref[:, cells] = jnp.sum(product.T, axis=0, keepdims=True)
        acc_ref[...] = jnp.zeros(acc_ref.shape, jnp.float32)
        step(place_ref[mine], True)

        def body(j, carried):
            step(place_ref[j], False)
            return carried
        lax.fori_loop(0, mine, body, 0)
        for head in range(group):
            dq_ref[:, head * HD:(head + 1) * HD] = acc_ref[:, head * blk:(head + 1) * blk].T.astype(jnp.bfloat16)

    @pl.when(mine * blk >= length)
    def _():
        dq_ref[...] = jnp.zeros(dq_ref.shape, jnp.bfloat16)


def attention_backward(scalars, order, queries, grads, attended, lse, keys_values, group, blk):
    rows, width = queries.shape
    span = keys_values.shape[0]
    row_blocks, head_groups = rows // blk, width // (group * HD)
    rowspec = pl.BlockSpec((blk, group * HD), lambda i, g, *_: (i, g))
    return pl.pallas_call(
        functools.partial(attend_backward, group, blk),
        grid_spec=pltpu.PrefetchScalarGridSpec(
            num_scalar_prefetch=2,
            grid=(row_blocks, head_groups),
            in_specs=[
                rowspec, rowspec, rowspec,
                pl.BlockSpec((1, 1, group * blk), lambda i, g, *_: (i * head_groups + g, 0, 0)),
                pl.BlockSpec((span, 2 * HD), lambda i, g, *_: (0, 0)),
            ],
            out_specs=[rowspec, pl.BlockSpec((span, 2 * HD), lambda i, g, *_: (0, 0))],
            scratch_shapes=[
                pltpu.SMEM((order.shape[0],), jnp.int32),
                pltpu.VMEM((HD, group * blk), jnp.bfloat16),
                pltpu.VMEM((HD, group * blk), jnp.bfloat16),
                pltpu.VMEM((group * blk, HD), jnp.bfloat16),
                pltpu.VMEM((group * blk, HD), jnp.bfloat16),
                pltpu.VMEM((HD, span), jnp.bfloat16),
                pltpu.VMEM((HD, group * blk), jnp.float32),
                pltpu.VMEM((1, group * blk), jnp.float32),
            ],
        ),
        out_shape=[
            jax.ShapeDtypeStruct((rows, width), jnp.bfloat16),
            jax.ShapeDtypeStruct((span, 2 * HD), jnp.float32),
        ],
        compiler_params=pltpu.CompilerParams(vmem_limit_bytes=48 * 2**20),
        cost_estimate=pl.CostEstimate(flops=7 * rows * width * span, bytes_accessed=8 * rows * width + 12 * span * HD, transcendentals=rows * span * width // HD),
        name="attend_backward",
    )(scalars, order, queries, grads, attended, lse, keys_values)


EPSILON = 1e-05
ROPE_BASE = 10000.0
LOG2E = 1.4426950408889634
BF16 = jnp.bfloat16
F32 = jnp.float32


def angles(positions):
    half_dim = HD // 2
    frequency = ROPE_BASE ** (-2.0 * jnp.arange(half_dim, dtype=F32) / HD)
    phase_angle = positions.astype(F32)[:, None] * frequency[None, :]
    return (jnp.cos(phase_angle), jnp.sin(phase_angle))


def rotate(vectors, cosine, sine_vals):
    half_dim = cosine.shape[-1]
    first_half = vectors[..., :half_dim]
    second_half = vectors[..., half_dim:]
    return jnp.concatenate(
        [
            first_half * cosine - second_half * sine_vals,
            second_half * cosine + first_half * sine_vals,
        ],
        axis=-1,
    )


def matmul(left, right):
    return jnp.dot(left, right, preferred_element_type=F32)


def contract_rows(left, right):
    return lax.dot_general(left, right, (((0,), (0,)), ((), ())), preferred_element_type=F32)


def contract_cols(left, right):
    return lax.dot_general(left, right, (((1,), (1,)), ((), ())), preferred_element_type=F32)


def exchange(value, axis, distance):
    size = lax.axis_size(axis)
    return lax.ppermute(value, axis, [(i, i ^ distance) for i in range(size)])


def swap_core(value):
    return exchange(value, "core", 1)


def gather_chips(value):
    chips = lax.axis_size("chip")
    if chips != 4:
        return [value] + [exchange(value, "chip", k) for k in range(1, chips)]
    half = value.shape[0] // 2
    first, second = exchange(value, "chip", 1), exchange(value, "chip", 2)
    far = jnp.concatenate(
        [exchange(first[:half], "chip", 2), exchange(second[half:], "chip", 1)], axis=0
    )
    return [value, first, second, far]


def gather_ctx(value):
    return [piece for chunk in gather_chips(value) for piece in (chunk, swap_core(chunk))]


def reduce_chips(parts):
    chips = lax.axis_size("chip")
    if chips != 4:
        total = parts[0].astype(F32)
        for k in range(1, chips):
            total = total + exchange(parts[k].astype(BF16), "chip", k).astype(F32)
        return total
    half = parts[0].shape[0] // 2
    far = parts[3].astype(BF16)
    for_second = exchange(far[:half], "chip", 1).astype(F32)
    for_first = exchange(far[half:], "chip", 2).astype(F32)
    first = jnp.concatenate(
        [parts[1][:half].astype(F32), parts[1][half:].astype(F32) + for_first], axis=0
    ).astype(BF16)
    second = jnp.concatenate(
        [parts[2][:half].astype(F32) + for_second, parts[2][half:].astype(F32)], axis=0
    ).astype(BF16)
    return (
        parts[0].astype(F32)
        + exchange(first, "chip", 1).astype(F32)
        + exchange(second, "chip", 2).astype(F32)
    )


def reduce_depth(pieces_of):
    total = pieces_of(0).astype(F32)
    for k in range(1, lax.axis_size("fsdp")):
        total = total + exchange(pieces_of(k).astype(BF16), "fsdp", k).astype(F32)
    return total


def reduce_ctx(term_of, chips):
    order = [3, 1, 2, 0] if chips == 4 else list(range(chips))
    parts = [None] * chips
    for k in order:
        other = swap_core(term_of(2 * k + 1).astype(BF16))
        parts[k] = (term_of(2 * k) + other.astype(F32)).astype(BF16)
    return reduce_chips(parts)


def at(value, index):
    return lax.dynamic_index_in_dim(value, index, 0, keepdims=False)


def lay_columns(chunks, chip, width):
    rows = chunks[0].shape[0]
    whole = jnp.zeros((rows, width * len(chunks)), chunks[0].dtype)
    for k, chunk in enumerate(chunks):
        whole = lax.dynamic_update_slice(whole, chunk, (0, (chip ^ k) * width))
    return whole


def shards(
    tokens,
    cotangent,
    kv_cotangent,
    lengths,
    block_order,
    w_query,
    w_kv,
    w_out,
    gain_attn,
    gain_ffn,
    w_gate,
    w_up,
    w_down,
):
    local_len, model_dim = tokens.shape[1:]
    chips, planes = lax.axis_size("chip"), lax.axis_size("fsdp")
    chip, core, plane = lax.axis_index("chip"), lax.axis_index("core"), lax.axis_index("fsdp")
    own = chip * 2 + core
    places = chips * 2
    blk = local_len // 2
    order, length = block_order[0], lengths[0]
    depth = w_query.shape[0]

    kv_rows = depth // chips
    small = jnp.concatenate(
        [
            lax.dynamic_slice_in_dim(w_kv, chip * kv_rows, kv_rows, 0),
            jnp.concatenate([gain_attn, gain_ffn]).reshape(-1, 2 * HD),
        ],
        axis=0,
    )
    gain_rows = depth // (2 * HD)
    small_all = lax.all_gather(small, "fsdp", axis=0)
    gain_one = small_all[:, kv_rows : kv_rows + gain_rows].reshape(model_dim).astype(F32)
    gain_two = small_all[:, kv_rows + gain_rows :].reshape(model_dim).astype(F32)
    kv_chunks = gather_chips(small_all[:, :kv_rows])
    kv_full = jnp.zeros((planes, chips, kv_rows, 2 * HD), BF16)
    for k, chunk in enumerate(kv_chunks):
        kv_full = lax.dynamic_update_slice(kv_full, chunk[:, None], (0, chip ^ k, 0, 0))
    kv_full = kv_full.reshape(model_dim, 2 * HD)

    part = depth // 2
    wide = part * planes
    query_piece = lax.dynamic_slice(w_query, (0, chip * 2 * part + core * part), (depth, part))
    query_half = lay_columns(
        gather_chips(lax.all_gather(query_piece, "fsdp", axis=0, tiled=True)), chip, part
    )
    out_cols = model_dim // chips
    out_piece = lax.dynamic_slice(w_out, (core * part, chip * out_cols), (part, out_cols))
    out_half = lay_columns(
        gather_chips(lax.all_gather(out_piece, "fsdp", axis=0, tiled=True)), chip, out_cols
    )

    offsets = jnp.arange(blk, dtype=jnp.int32)
    mine = lax.dynamic_slice_in_dim(order, own * 2, 2, 0)
    theirs = lax.dynamic_slice_in_dim(order, (own ^ 1) * 2, 2, 0)
    both_pos = (jnp.concatenate([mine, theirs])[:, None] * blk + offsets[None, :]).reshape(-1)
    live_rows = (both_pos[:local_len] < length)[:, None]
    cosine, sine_vals = angles(both_pos)

    tokens_low = tokens[0]
    tokens_flat = tokens_low.astype(F32)
    both_tokens = jnp.concatenate([tokens_low, swap_core(tokens_low)], axis=0).astype(F32)
    both_inverse = lax.rsqrt(jnp.mean(both_tokens * both_tokens, axis=1, keepdims=True) + EPSILON)
    both_normed = (both_tokens * both_inverse * gain_one).astype(BF16)
    inverse_one = both_inverse[:local_len]

    key_value = matmul(both_normed[:local_len], kv_full)
    key_rot = rotate(key_value[:, :HD], cosine[:local_len], sine_vals[:local_len])
    local_kv = jnp.concatenate([key_rot, key_value[:, HD:]], axis=1).astype(BF16)
    slot_kv = jnp.concatenate(gather_ctx(local_kv), axis=0)

    heads = wide // HD
    queries = matmul(both_normed, query_half).reshape(2 * local_len, heads, HD)
    query_rot = rotate(queries, cosine[:, None, :], sine_vals[:, None, :]) * (
        LOG2E * HD ** (-0.5)
    )
    query_rot = query_rot.astype(BF16).reshape(2 * local_len, wide)

    scalars = jnp.stack([own, length]).astype(jnp.int32)
    attended, lse = attention_forward(scalars, order, query_rot, slot_kv, heads, blk)

    branch_other = swap_core(matmul(attended[local_len:], out_half).astype(BF16))
    residual = tokens_flat + matmul(attended[:local_len], out_half) + branch_other.astype(F32)
    inverse_two = lax.rsqrt(jnp.mean(residual * residual, axis=1, keepdims=True) + EPSILON)
    unit_two = residual * inverse_two
    normed_ffn = (unit_two * gain_two).astype(BF16)
    grad_out = jnp.where(live_rows, cotangent[0], jnp.zeros((), BF16))

    share = w_gate.shape[1] // places

    def hidden_rows(weight):
        piece = lax.dynamic_slice(weight, (0, own * share), (model_dim, share)).T
        return lax.all_gather(piece, "fsdp", axis=0, tiled=True)

    gate_rows, up_rows, down_rows = hidden_rows(w_gate), hidden_rows(w_up), hidden_rows(w_down)
    grad_chunks = gather_ctx(grad_out)
    normed_chunks = gather_ctx(normed_ffn)
    hidden_chunks, gate_chunks, up_chunks = [], [], []
    for normed, grad in zip(normed_chunks, grad_chunks):
        grad_hidden = contract_cols(grad, down_rows).astype(BF16).astype(F32)
        gate_proj = contract_cols(normed, gate_rows)
        up_proj = contract_cols(normed, up_rows)
        sigmoid_gate = jax.nn.sigmoid(gate_proj)
        silu_gate = gate_proj * sigmoid_gate
        hidden_chunks.append((silu_gate * up_proj).astype(BF16))
        gate_chunks.append(
            (grad_hidden * up_proj * sigmoid_gate * (1.0 + gate_proj * (1.0 - sigmoid_gate))).astype(BF16)
        )
        up_chunks.append((grad_hidden * silu_gate).astype(BF16))

    grad_normed = reduce_ctx(
        lambda i: matmul(gate_chunks[i], gate_rows) + matmul(up_chunks[i], up_rows), chips
    )
    ffn_out = reduce_ctx(lambda i: matmul(hidden_chunks[i], down_rows), chips)
    output = jnp.where(live_rows, residual + ffn_out, 0.0).astype(BF16)

    normed_all = jnp.concatenate(normed_chunks, axis=0)
    grad_all = jnp.concatenate(grad_chunks, axis=0)

    def ffn_gradient(left_chunks, right):
        term = contract_rows(jnp.concatenate(left_chunks, axis=0), right).astype(BF16)
        return lax.psum_scatter(term, "fsdp", scatter_dimension=0, tiled=True)

    ffn_terms = jnp.stack(
        [
            ffn_gradient(gate_chunks, normed_all),
            ffn_gradient(up_chunks, normed_all),
            ffn_gradient(hidden_chunks, grad_all),
        ]
    )
    ffn_terms = ffn_terms.reshape(3, share, places, model_dim // places)
    ffn_terms = lax.all_to_all(ffn_terms, ("chip", "core"), 2, 0, tiled=False)
    ffn_grads = ffn_terms.transpose(1, 3, 0, 2).reshape(3, model_dim // places, places * share)
    ffn_grads = ffn_grads.astype(F32)

    grad_gain_two = jnp.sum(grad_normed * unit_two, axis=0)
    scaled_two = grad_normed * gain_two
    grad_residual = grad_out.astype(F32) + inverse_two * (
        scaled_two - unit_two * jnp.mean(scaled_two * unit_two, axis=1, keepdims=True)
    )
    grad_branch = grad_residual.astype(BF16)
    both_branch = jnp.concatenate([grad_branch, swap_core(grad_branch)], axis=0)
    grad_attn = contract_cols(both_branch, out_half).astype(BF16)
    grad_query_rot, kv_terms = attention_backward(
        scalars, order, query_rot, grad_attn, attended, lse, slot_kv, heads, blk
    )

    out_terms = contract_rows(attended, both_branch).astype(BF16).reshape(planes, part, model_dim)
    out_sum = reduce_chips([at(out_terms, chip ^ k) for k in range(chips)])
    out_sum = out_sum.reshape(planes, part // planes, model_dim)
    grad_w_out = reduce_depth(lambda k: at(out_sum, plane ^ k))

    kv_terms = jnp.concatenate([kv_terms[:, :HD] * LN2, kv_terms[:, HD:]], axis=1)
    kv_terms = kv_terms.reshape(places, local_len, 2 * HD)
    kv_total = reduce_ctx(lambda i: kv_terms[i], chips) + jnp.where(
        live_rows, kv_cotangent[0].astype(F32), 0.0
    )
    kv_low = kv_total.astype(BF16).astype(F32)
    grad_key = rotate(kv_low[:, :HD], cosine[:local_len], -sine_vals[:local_len])
    grad_kv = jnp.concatenate([grad_key, kv_low[:, HD:]], axis=1).astype(BF16)
    both_grad_kv = jnp.concatenate([grad_kv, swap_core(grad_kv)], axis=0)
    kv_half = lax.dynamic_slice_in_dim(both_grad_kv, core * HD, HD, 1)
    grad_qrot = grad_query_rot.astype(F32).reshape(2 * local_len, heads, HD)
    grad_query = rotate(grad_qrot, cosine[:, None, :], -sine_vals[:, None, :]) * HD ** (-0.5)
    grad_query = grad_query.reshape(2 * local_len, wide).astype(BF16)

    kv_weight_half = lax.dynamic_slice_in_dim(kv_full, core * HD, HD, 1)

    def normed_one_term(rows):
        return contract_cols(grad_query[rows], query_half) + contract_cols(kv_half[rows], kv_weight_half)

    other_one = swap_core(normed_one_term(slice(local_len, None)).astype(BF16))
    grad_normed_one = normed_one_term(slice(0, local_len)) + other_one.astype(F32)
    unit_one = tokens_flat * inverse_one
    grad_gain_one = jnp.sum(grad_normed_one * unit_one, axis=0)
    scaled_one = grad_normed_one * gain_one
    grad_tokens = grad_residual + inverse_one * (
        scaled_one - unit_one * jnp.mean(scaled_one * unit_one, axis=1, keepdims=True)
    )

    def attn_gradient(terms):
        terms = terms.astype(BF16).reshape(chips, places * planes // chips * (depth // places), -1)
        total = reduce_chips([at(terms, chip ^ k) for k in range(chips)])
        total = total.reshape(2, planes, depth // places, -1)
        total = reduce_depth(lambda k: lax.dynamic_index_in_dim(total, plane ^ k, 1, keepdims=False))
        return at(total, core), swap_core(at(total, core ^ 1))

    def by_core(kept, other):
        return jnp.where(core == 0, jnp.stack([kept, other], -2), jnp.stack([other, kept], -2))

    kept, other = attn_gradient(contract_rows(both_normed, grad_query))
    rows = kept.shape[0]
    grad_w_query = by_core(
        kept.reshape(rows, planes, part), other.reshape(rows, planes, part)
    ).reshape(rows, model_dim)
    gains = jnp.stack([grad_gain_one, grad_gain_two], axis=1)
    kept, other = attn_gradient(
        jnp.concatenate(
            [contract_rows(both_normed, kv_half), jnp.pad(gains, ((0, 0), (0, HD - 2)))], axis=1
        )
    )
    grad_w_kv = by_core(kept[:, :HD], other[:, :HD]).reshape(rows, 2 * HD)
    gain_sums = kept[:, HD : HD + 2] + other[:, HD : HD + 2]
    return (
        output[None],
        grad_tokens.astype(BF16)[None],
        grad_w_query,
        grad_w_kv,
        grad_w_out,
        gain_sums[:, 0],
        gain_sums[:, 1],
        ffn_grads[0],
        ffn_grads[1],
        ffn_grads[2],
    )


def solution(mesh):
    ctx, planes = mesh.shape["ctx"], mesh.shape["fsdp"]
    split = Mesh(mesh.devices.reshape(ctx // 2, 2, planes), ("chip", "core", "fsdp"))
    ctx_axes = ("chip", "core")
    return jax.shard_map(
        shards,
        mesh=split,
        in_specs=(
            P("fsdp", ctx_axes, None),
            P("fsdp", ctx_axes, None),
            P("fsdp", ctx_axes, None),
            P("fsdp"),
            P("fsdp", None),
            P("fsdp", None),
            P("fsdp", None),
            P("fsdp", None),
            P("fsdp"),
            P("fsdp"),
            P(None, "fsdp"),
            P(None, "fsdp"),
            P(None, "fsdp"),
        ),
        out_specs=(
            P("fsdp", ctx_axes, None),
            P("fsdp", ctx_axes, None),
            P(("chip", "core", "fsdp"), None),
            P(("chip", "core", "fsdp"), None),
            P(("chip", "core", "fsdp"), None),
            P(("chip", "core", "fsdp")),
            P(("chip", "core", "fsdp")),
            P(ctx_axes, "fsdp"),
            P(ctx_axes, "fsdp"),
            P(ctx_axes, "fsdp"),
        ),
        check_vma=False,
    )
```

time: 5850 us -> 1040 us (0.18)
  waiting for transfers between devices: 4640 us -> 316 us
  matrix products: 733 us -> 287 us
  starting transfers between devices: 1.14 us -> 103 us
  local copies, waits for them, and re-layouts: 224 us -> 128 us
  Pallas kernels: 0 us -> 83.4 us
  other arithmetic: 138 us -> 74.3 us
    reduce_scatter x7 -> x3, waiting for transfers between devices: 3500 us -> 0.06 us  [ffn_gradient(): return lax.psum_scatter(term, 'fsdp', scatter_dimension=0, tiled=True)]
    all_gather x7 -> x5, waiting for transfers between devices: 1130 us -> 0.01 us  [the longest x3 0.01 us: hidden_rows(): return lax.all_gather(piece, 'fsdp', axis=0, tiled=True)]
    ppermute x0 -> x88, waiting for transfers between devices: none -> 316 us  [exchange(): return lax.ppermute(value, axis, [(i, i ^ distance) for i in range(size)])]
    dot_general x25 -> x28, matrix products: 311 us -> 101 us  [matmul(): return jnp.dot(left, right, preferred_element_type=F32)]
    dot_general x30 -> x29, matrix products: 304 us -> 123 us  [contract_cols(): lax.dot_general(left, right, (((1,), (1,)), ((), ())), preferred_element_...]
    transpose x3 -> x0, local copies, waits for them, and re-layouts: 100 us -> none  [split_term(): jnp.einsum('tcd,tfk->cfdk', left_split, right_split, preferred_element_ty...]
    ppermute x0 -> x88, starting transfers between devices: none -> 97.7 us  [exchange(): return lax.ppermute(value, axis, [(i, i ^ distance) for i in range(size)])]
    pallas_call x0 -> x2, Pallas kernels: none -> 83.4 us  [the longest x1 51.1 us: attention_backward(): pl.pallas_call(functools.partial(attend_backward, group, blk), grid_spec=...]
  transfers between devices with their start and end apart: 14 -> 97, of which waited for: 12 -> 23; matrix products, arithmetic and copies ran while one was open for 11% -> 45% of each run, Pallas kernels for 0% -> 8%
where the time goes in v1:
time: 1040 us; the launch traced here: 1030 us
  waiting for transfers between devices  316 us (30%)
  matrix products  287 us (28%)
  local copies, waits for them, and re-layouts  128 us (12%)
  starting transfers between devices  103 us (10%)
  Pallas kernels  83.4 us (8%)
  other arithmetic  74.3 us (7%)
  blocking collectives  18.6 us (2%)
  between operations  17.6 us (2%)
    ppermute x88, waiting for transfers between devices, exchange(): return lax.ppermute(value, axis, [(i, i ^ distance) for i in range(size)])  316 us
    dot_general x29, matrix products, contract_cols(): lax.dot_general(left, right, (((1,), (1,)), ((), ())), preferred_element_...  123 us
    dot_general x28, matrix products, matmul(): return jnp.dot(left, right, preferred_element_type=F32)  101 us
    ppermute x88, starting transfers between devices, exchange(): return lax.ppermute(value, axis, [(i, i ^ distance) for i in range(size)])  97.7 us
    unnamed x263, local copies, waits for them, and re-layouts  71.8 us
    dot_general x6, matrix products, contract_rows(): lax.dot_general(left, right, (((0,), (0,)), ((), ())), preferred_element_...  63.4 us
    pallas_call x1, Pallas kernels, attention_backward(): pl.pallas_call(functools.partial(attend_backward, group, blk), grid_spec=...  51.1 us
    pallas_call x1, Pallas kernels, attention_forward(): pl.pallas_call(functools.partial(attend_forward, group, blk), grid_spec=p...  32.3 us
  transfers between devices with their start and end apart: 97, of which 23 were waited for; matrix products, arithmetic and copies ran while one was open for 45% of the time, Pallas kernels for 8%

profile of v1, /device:TPU:0, one launch (start us, length us, event | category | flops | bytes accessed | tf_op | source)
XLA Modules:
  0.0 1027.9 jit_solution(3075333016273071204)
XLA Ops:
  17.8 18.6 %all-gather.1 = bf16[4,132,256]{2,1,0:T(8,128)(2,1)S(1)} all-gather(bf16[1,132,256]{2,1,0:T(8,128)(2,1)S(1)} %maximum_bitcast_fusion.1), channel_id=2, replica_groups=mesh['chip'=4,'core'=2,'fsdp'=4] {'fsdp'}, dimensions={0}, use_global_device_ids=true | all-gather | bytes 337920 | tf_op jit(solution)/shard_map/all_gather | solution.py:352
  41.1 4.1 constant_dynamic-update-slice_fusion.54
  63.3 33.0 %collective-permute-done.8 = bf16[2,128,256]{2,1,0:T(8,128)(2,1)S(1)} collective-permute-done((bf16[2,128,256]{2,1,0:T(8,128)(2,1)S(1)}, bf16[2,128,256]{2,1,0:T(8,128)(2,1)S(1)}, u32[]{:S(2)}, u32[]{:S(2)}) %collective-permute-start.8) | collective-permute-done | bytes 131104 | tf_op jit(solution)/shard_map/ppermute | solution.py:244
  104.9 4.3 fusion.2
  117.5 10.2 collective-permute-done.10
  138.6 16.1 %collective-permute-done.14 = bf16[256,256]{1,0:T(8,128)(2,1)S(1)} collective-permute-done((bf16[256,256]{1,0:T(8,128)(2,1)S(1)}, bf16[256,256]{1,0:T(8,128)(2,1)S(1)}, u32[]{:S(2)}, u32[]{:S(2)}) %collective-permute-start.14) | collective-permute-done | bytes 131104 | tf_op jit(solution)/shard_map/ppermute | solution.py:244
  164.6 16.2 %collective-permute-done.17 = bf16[1024,512]{1,0:T(8,128)(2,1)S(1)} collective-permute-done((bf16[1024,512]{1,0:T(8,128)(2,1)S(1)}, bf16[1024,512]{1,0:T(8,128)(2,1)S(1)}, u32[]{:S(2)}, u32[]{:S(2)}) %collective-permute-start.17) | collective-permute-done | bytes 1048608 | tf_op jit(solution)/shard_map/ppermute | solution.py:244
  185.6 26.5 %collective-permute-done.3 = bf16[1024,256]{1,0:T(8,128)(2,1)S(1)} collective-permute-done((bf16[1024,256]{1,0:T(8,128)(2,1)S(1)}, bf16[1024,256]{1,0:T(8,128)(2,1)S(1)}, u32[]{:S(2)}, u32[]{:S(2)}) %collective-permute-start.3) | collective-permute-done | bytes 524320 | tf_op jit(solution)/shard_map/ppermute | solution.py:244
  215.2 6.4 fusion.155
  224.2 3.9 copy.89
  228.1 3.9 copy.90
  232.0 4.5 multiply_subtract_fusion.1
  241.9 32.3 %attend_forward.1 = (bf16[1024,1024]{1,0:T(8,128)(2,1)S(1)}, f32[4,1,2048]{2,1,0:T(1,128)S(1)}) custom-call(s32[2]{0:T(128)S(1)} %pad_add_fusion.scal_ref, s32[16]{0:T(128)S(1)} %bitcast.338, bf16[1024,1024]{1,0:T(8,128)(2,1)S(1)} %bitcast.336, bf16[4096,256]{1,0:T(8,128)(2,1)S(1)} %constant_dynamic-update-slice_fusion.kv_ref), custom_call_target="tpu_custom_call" | custom-call | flops 12884901888 | bytes 6291456 | tf_op jit(solution)/shard_map/attend_forward/pallas_call | solution.py:79
  292.1 5.2 convolution_convert_fusion.14
  297.3 4.1 convolution_convert_fusion.18
  301.4 4.1 convolution_convert_fusion.17
  305.6 4.1 convolution_convert_fusion.16
  313.0 4.3 convolution_convert_fusion.12
  326.5 5.2 fusion.156
  331.7 7.7 constant_dynamic-update-slice_fusion.20
  342.8 4.2 convolution_convert_fusion.13
  347.0 25.2 %collective-permute-done.24 = bf16[512,2048]{1,0:T(8,128)(2,1)} collective-permute-done((bf16[512,2048]{1,0:T(8,128)(2,1)}, bf16[512,2048]{1,0:T(8,128)(2,1)}, u32[]{:S(2)}, u32[]{:S(2)}) %collective-permute-start.24) | collective-permute-done | bytes 2097184 | tf_op jit(solution)/shard_map/ppermute | solution.py:244
  377.5 5.6 constant_dynamic-update-slice_fusion.19
  392.2 6.1 constant_dynamic-update-slice_fusion.18
  416.3 5.1 constant_dynamic-update-slice_fusion.17
  426.7 3.9 constant_dynamic-update-slice_fusion.16
  430.6 5.0 constant_dynamic-update-slice_fusion.15
  442.3 3.9 constant_dynamic-update-slice_fusion.14
  451.9 4.2 fusion.171
  459.4 4.6 add_convert_fusion.2
  473.1 15.2 %convolution_convert_fusion.4 = bf16[704,2048]{1,0:T(8,128)(2,1)} fusion(bf16[4096,704]{0,1:T(8,128)(2,1)} %get-tuple-element.42, bf16[4096,2048]{1,0:T(8,128)(2,1)S(1)} %constant_dynamic-update-slice_fusion.21), kind=kOutput, calls=%fused_computation.64 | convolution fusion | flops 11812601856 | bytes 25427968 | tf_op jit(solution)/shard_map/dot_general | solution.py:235
  489.4 4.4 add_convert_fusion.11
  505.6 15.7 %convolution_convert_fusion.3 = bf16[704,2048]{1,0:T(8,128)(2,1)} fusion(bf16[4096,704]{0,1:T(8,128)(2,1)} %get-tuple-element.128, bf16[4096,2048]{1,0:T(8,128)(2,1)S(1)} %bitcast.381), kind=kOutput, calls=%fused_computation.63 | convolution fusion | flops 11812601856 | bytes 25427968 | tf_op jit(solution)/shard_map/dot_general | solution.py:235
  521.4 18.8 %convolution_convert_fusion.2 = bf16[704,2048]{1,0:T(8,128)(2,1)} fusion(bf16[4096,704]{0,1:T(8,128)(2,1)} %get-tuple-element.112, bf16[4096,2048]{1,0:T(8,128)(2,1)} %constant_dynamic-update-slice_fusion.46), kind=kOutput, calls=%fused_computation.62 | convolution fusion | flops 11812601856 | bytes 25427968 | tf_op jit(solution)/shard_map/dot_general | solution.py:235
  540.2 5.3 convolution_convert_fusion.7
  546.1 5.2 add_convert_fusion.5
  551.3 4.6 add_convert_fusion.1
  558.4 6.1 add_convert_fusion.3
  572.2 18.6 %collective-permute-done.48 = bf16[256,2048]{1,0:T(8,128)(2,1)S(1)} collective-permute-done((bf16[256,2048]{1,0:T(8,128)(2,1)S(1)}, bf16[256,2048]{1,0:T(8,128)(2,1)S(1)}, u32[]{:S(2)}, u32[]{:S(2)}) %collective-permute-start.48) | collective-permute-done | bytes 1048608 | tf_op jit(solution)/shard_map/ppermute | solution.py:244
  594.2 18.2 %collective-permute-done.32 = bf16[256,2048]{1,0:T(8,128)(2,1)S(1)} collective-permute-done((bf16[256,2048]{1,0:T(8,128)(2,1)S(1)}, bf16[256,2048]{1,0:T(8,128)(2,1)S(1)}, u32[]{:S(2)}, u32[]{:S(2)}) %collective-permute-start.32) | collective-permute-done | bytes 1048608 | tf_op jit(solution)/shard_map/ppermute | solution.py:244
  626.3 35.5 %collective-permute-done.49 = bf16[512,2048]{1,0:T(8,128)(2,1)S(1)} collective-permute-done((bf16[512,2048]{1,0:T(8,128)(2,1)S(1)}, bf16[512,2048]{1,0:T(8,128)(2,1)S(1)}, u32[]{:S(2)}, u32[]{:S(2)}) %collective-permute-start.49) | collective-permute-done | bytes 2097184 | tf_op jit(solution)/shard_map/ppermute | solution.py:244
  661.9 5.8 multiply_reduce_fusion
  667.8 36.6 %collective-permute-done.33 = bf16[512,2048]{1,0:T(8,128)(2,1)S(1)} collective-permute-done((bf16[512,2048]{1,0:T(8,128)(2,1)}, bf16[512,2048]{1,0:T(8,128)(2,1)S(1)}, u32[]{:S(2)}, u32[]{:S(2)}) %collective-permute-start.33) | collective-permute-done | bytes 2097184 | tf_op jit(solution)/shard_map/ppermute | solution.py:244
  704.3 7.7 fusion.146
  718.0 4.6 all-to-all-start
  722.6 9.4 fusion.25.g_ref
  732.0 51.1 %attend_backward.1 = (bf16[1024,1024]{1,0:T(8,128)(2,1)S(1)}, f32[4096,256]{1,0:T(8,128)}) custom-call(s32[2]{0:T(128)S(1)} %pad_add_fusion.scal_ref, s32[16]{0:T(128)S(1)} %bitcast.339, bf16[1024,1024]{1,0:T(8,128)(2,1)S(1)} %bitcast.337, bf16[1024,1024]{1,0:T(8,128)(2,1)} %fusion.25.g_ref, bf16[1024,1024]{1,0:T(8,128)(2,1)} %copy-done.6, ...), custom_call_target="tpu_custom_call" | custom-call | flops 30064771072 | bytes 14680064 | tf_op jit(solution)/shard_map/attend_backward/pallas_call | solution.py:171
  788.9 6.7 fusion.68
  798.3 7.1 convolution_convert_fusion
  809.8 5.2 convolution_convert_fusion.1
  846.0 9.9 collective-permute-done.67
  867.0 5.9 add_convert_fusion
  873.1 3.9 fusion.98
  878.4 25.8 %collective-permute-done.66 = bf16[512,1024]{1,0:T(8,128)(2,1)S(1)} collective-permute-done((bf16[512,1024]{1,0:T(8,128)(2,1)S(1)}, bf16[512,1024]{1,0:T(8,128)(2,1)S(1)}, u32[]{:S(2)}, u32[]{:S(2)}) %collective-permute-start.66) | collective-permute-done | bytes 1048608 | tf_op jit(solution)/shard_map/ppermute | solution.py:244
  904.9 29.2 %collective-permute-start.70 = (bf16[2,64,1024]{2,1,0:T(8,128)(2,1)S(1)}, bf16[2,64,1024]{2,1,0:T(8,128)(2,1)S(1)}, u32[]{:S(2)}, u32[]{:S(2)}) collective-permute-start(bf16[2,64,1024]{2,1,0:T(8,128)(2,1)S(1)} %get-tuple-element.141), channel_id=1, source_target_pairs={{0,2},{1,3},{2,0},{3,1},{4,6},{5,7},{6,4},{7,5},{8,10},{9,11},{10,... | collective-permute-start | bytes 786440 | tf_op jit(solution)/shard_map/ppermute | solution.py:244
  937.6 5.9 collective-permute-start.86
  943.5 9.2 collective-permute-done.70
  952.7 8.9 collective-permute-start.87
  962.8 12.0 %collective-permute-done.86 = bf16[64,2048]{1,0:T(8,128)(2,1)} collective-permute-done((bf16[64,2048]{1,0:T(8,128)(2,1)}, bf16[64,2048]{1,0:T(8,128)(2,1)}, u32[]{:S(2)}, u32[]{:S(2)}) %collective-permute-start.86) | collective-permute-done | bytes 262176 | tf_op jit(solution)/shard_map/ppermute | solution.py:244
  982.0 7.4 fusion.11
  991.2 4.3 collective-permute-done.73
  997.7 6.0 fusion.18
  1004.0 4.4 collective-permute-start.77
  1012.5 5.6 collective-permute-done.78
  (622 shorter events, 307.4 us)
Async XLA Ops:
  7.2 89.8 %all-gather.8.cloned.1.call-start = ((), (), s32[]{:S(2)}) async-start(), calls=%async_computation.4 | async-start | bytes 1310720 | tf_op jit(solution)/shard_map/all_gather | solution.py:365
  9.5 91.7 %all-gather.10.cloned.1.call-start = ((), (), s32[]{:S(2)}) async-start(), calls=%async_computation.5 | async-start | bytes 1310720 | tf_op jit(solution)/shard_map/all_gather | solution.py:370
  11.3 280.8 %all-gather.16.cloned.1.call-start = ((), (), s32[]{:S(2)}) async-start(), calls=%async_computation.8 | async-start | bytes 3604480 | tf_op jit(solution)/shard_map/all_gather | solution.py:413
  15.6 310.9 %all-gather.14.cloned.1.call-start = ((), (), s32[]{:S(2)}) async-start(), calls=%async_computation.7 | async-start | bytes 3604480 | tf_op jit(solution)/shard_map/all_gather | solution.py:413
  16.9 314.8 %all-gather.12.cloned.1.call-start = ((), (), s32[]{:S(2)}) async-start(), calls=%async_computation.6 | async-start | bytes 3604480 | tf_op jit(solution)/shard_map/all_gather | solution.py:413
  45.2 68.6 %collective-permute-start.38 = (bf16[512,2048]{1,0:T(8,128)(2,1)}, bf16[512,2048]{1,0:T(8,128)(2,1)}, u32[]{:S(2)}, u32[]{:S(2)}) collective-permute-start(bf16[512,2048]{1,0:T(8,128)(2,1)} %get-tuple-element.61), channel_id=1, source_target_pairs={{0,4},{4,0},{1,5},{5,1},{2,6},{6,2},{3,7},{7,3},{8,12},{12,8},{9,1... | collective-permute-start | bytes 6291464 | tf_op jit(solution)/shard_map/ppermute | solution.py:244
  45.2 83.0 %collective-permute-start.40 = (bf16[512,2048]{1,0:T(8,128)(2,1)}, bf16[512,2048]{1,0:T(8,128)(2,1)}, u32[]{:S(2)}, u32[]{:S(2)}) collective-permute-start(bf16[512,2048]{1,0:T(8,128)(2,1)} %get-tuple-element.61), channel_id=1, source_target_pairs={{0,8},{8,0},{16,24},{24,16},{1,9},{9,1},{17,25},{25,17},{2,10},{10... | collective-permute-start | bytes 6291464 | tf_op jit(solution)/shard_map/ppermute | solution.py:244
  45.8 56.9 %collective-permute-start = (bf16[512,2048]{1,0:T(8,128)(2,1)S(1)}, bf16[512,2048]{1,0:T(8,128)(2,1)}, u32[]{:S(2)}, u32[]{:S(2)}) collective-permute-start(bf16[512,2048]{1,0:T(8,128)(2,1)S(1)} %bitcast.341), channel_id=1, source_target_pairs={{0,4},{4,0},{1,5},{5,1},{2,6},{6,2},{3,7},{7,3},{8,12},{12,8},{9,1... | collective-permute-start | bytes 6291464 | tf_op jit(solution)/shard_map/ppermute | solution.py:244
  49.1 663.0 %reduce-scatter.4.cloned.1.call-start = ((), (), s32[]{:S(2)}) async-start(), calls=%async_computation.9 | async-start | bytes 3604480 | tf_op jit(solution)/shard_map/reduce_scatter | solution.py:442
  56.9 39.4 %collective-permute-start.8 = (bf16[2,128,256]{2,1,0:T(8,128)(2,1)S(1)}, bf16[2,128,256]{2,1,0:T(8,128)(2,1)S(1)}, u32[]{:S(2)}, u32[]{:S(2)}) collective-permute-start(bf16[2,128,256]{2,1,0:T(8,128)(2,1)S(1)} %slice.444), channel_id=1, source_target_pairs={{0,8},{8,0},{16,24},{24,16},{1,9},{9,1},{17,25},{25,17},{2,10},{10... | collective-permute-start | bytes 393224 | tf_op jit(solution)/shard_map/ppermute | solution.py:244
  61.8 66.6 %collective-permute-start.44 = (bf16[512,2048]{1,0:T(8,128)(2,1)}, bf16[512,2048]{1,0:T(8,128)(2,1)}, u32[]{:S(2)}, u32[]{:S(2)}) collective-permute-start(bf16[512,2048]{1,0:T(8,128)(2,1)} %get-tuple-element.61), channel_id=1, source_target_pairs={{0,16},{8,24},{16,0},{24,8},{1,17},{9,25},{17,1},{25,9},{2,18},{10... | collective-permute-start | bytes 6291464 | tf_op jit(solution)/shard_map/ppermute | solution.py:244
  97.0 62.0 %collective-permute-start.1 = (bf16[2048,256]{1,0:T(8,128)(2,1)}, bf16[2048,256]{1,0:T(8,128)(2,1)}, u32[]{:S(2)}, u32[]{:S(2)}) collective-permute-start(bf16[2048,256]{1,0:T(8,128)(2,1)} %all-gather.8.cloned.1.call-done), channel_id=1, source_target_pairs={{0,8},{8,0},{16,24},{24,16},{1,9},{9,1},{17,25},{25,17},{2,10},{10... | collective-permute-start | bytes 3145736 | tf_op jit(solution)/shard_map/ppermute | solution.py:244
  127.7 33.8 %collective-permute-start.2 = (bf16[2048,256]{1,0:T(8,128)(2,1)S(1)}, bf16[2048,256]{1,0:T(8,128)(2,1)S(1)}, u32[]{:S(2)}, u32[]{:S(2)}) collective-permute-start(bf16[2048,256]{1,0:T(8,128)(2,1)S(1)} %copy-done.58), channel_id=1, source_target_pairs={{0,16},{8,24},{16,0},{24,8},{1,17},{9,25},{17,1},{25,9},{2,18},{10... | collective-permute-start | bytes 3145736 | tf_op jit(solution)/shard_map/ppermute | solution.py:244
  128.4 26.3 %collective-permute-start.14 = (bf16[256,256]{1,0:T(8,128)(2,1)S(1)}, bf16[256,256]{1,0:T(8,128)(2,1)S(1)}, u32[]{:S(2)}, u32[]{:S(2)}) collective-permute-start(bf16[256,256]{1,0:T(8,128)(2,1)S(1)} %slice.450), channel_id=1, source_target_pairs={{0,16},{8,24},{16,0},{24,8},{1,17},{9,25},{17,1},{25,9},{2,18},{10... | collective-permute-start | bytes 393224 | tf_op jit(solution)/shard_map/ppermute | solution.py:244
  129.9 25.9 %collective-permute-start.11 = (bf16[512,256]{1,0:T(8,128)(2,1)S(1)}, bf16[512,256]{1,0:T(8,128)(2,1)S(1)}, u32[]{:S(2)}, u32[]{:S(2)}) collective-permute-start(bf16[512,256]{1,0:T(8,128)(2,1)S(1)} %collective-permute-done.10), channel_id=1, source_target_pairs={{0,4},{4,0},{1,5},{5,1},{2,6},{6,2},{3,7},{7,3},{8,12},{12,8},{9,1... | collective-permute-start | bytes 786440 | tf_op jit(solution)/shard_map/ppermute | solution.py:244
  154.7 26.1 %collective-permute-start.17 = (bf16[1024,512]{1,0:T(8,128)(2,1)S(1)}, bf16[1024,512]{1,0:T(8,128)(2,1)S(1)}, u32[]{:S(2)}, u32[]{:S(2)}) collective-permute-start(bf16[1024,512]{1,0:T(8,128)(2,1)S(1)} %copy-done.59), channel_id=1, source_target_pairs={{0,8},{8,0},{16,24},{24,16},{1,9},{9,1},{17,25},{25,17},{2,10},{10... | collective-permute-start | bytes 3145736 | tf_op jit(solution)/shard_map/ppermute | solution.py:244
  155.3 26.2 %collective-permute-start.18 = (bf16[1024,512]{1,0:T(8,128)(2,1)S(1)}, bf16[1024,512]{1,0:T(8,128)(2,1)S(1)}, u32[]{:S(2)}, u32[]{:S(2)}) collective-permute-start(bf16[1024,512]{1,0:T(8,128)(2,1)S(1)} %copy-done.59), channel_id=1, source_target_pairs={{0,16},{8,24},{16,0},{24,8},{1,17},{9,25},{17,1},{25,9},{2,18},{10... | collective-permute-start | bytes 3145736 | tf_op jit(solution)/shard_map/ppermute | solution.py:244
  157.4 128.6 %collective-permute-start.43 = (bf16[256,2048]{1,0:T(8,128)(2,1)}, bf16[256,2048]{1,0:T(8,128)(2,1)}, u32[]{:S(2)}, u32[]{:S(2)}) collective-permute-start(bf16[256,2048]{1,0:T(8,128)(2,1)} %slice.465), channel_id=1, source_target_pairs={{0,16},{8,24},{16,0},{24,8},{1,17},{9,25},{17,1},{25,9},{2,18},{10... | collective-permute-start | bytes 3145736 | tf_op jit(solution)/shard_map/ppermute | solution.py:244
  159.0 129.8 %collective-permute-start.45 = (bf16[256,2048]{1,0:T(8,128)(2,1)}, bf16[256,2048]{1,0:T(8,128)(2,1)}, u32[]{:S(2)}, u32[]{:S(2)}) collective-permute-start(bf16[256,2048]{1,0:T(8,128)(2,1)} %slice.466), channel_id=1, source_target_pairs={{0,8},{8,0},{16,24},{24,16},{1,9},{9,1},{17,25},{25,17},{2,10},{10... | collective-permute-start | bytes 3145736 | tf_op jit(solution)/shard_map/ppermute | solution.py:244
  161.6 50.5 %collective-permute-start.3 = (bf16[1024,256]{1,0:T(8,128)(2,1)S(1)}, bf16[1024,256]{1,0:T(8,128)(2,1)S(1)}, u32[]{:S(2)}, u32[]{:S(2)}) collective-permute-start(bf16[1024,256]{1,0:T(8,128)(2,1)S(1)} %slice.437), channel_id=1, source_target_pairs={{0,16},{8,24},{16,0},{24,8},{1,17},{9,25},{17,1},{25,9},{2,18},{10... | collective-permute-start | bytes 1572872 | tf_op jit(solution)/shard_map/ppermute | solution.py:244
  180.8 31.8 %collective-permute-start.4 = (bf16[1024,256]{1,0:T(8,128)(2,1)S(1)}, bf16[1024,256]{1,0:T(8,128)(2,1)S(1)}, u32[]{:S(2)}, u32[]{:S(2)}) collective-permute-start(bf16[1024,256]{1,0:T(8,128)(2,1)S(1)} %slice.438), channel_id=1, source_target_pairs={{0,8},{8,0},{16,24},{24,16},{1,9},{9,1},{17,25},{25,17},{2,10},{10... | collective-permute-start | bytes 1572872 | tf_op jit(solution)/shard_map/ppermute | solution.py:244
  185.1 92.9 %collective-permute-start.41 = (bf16[512,2048]{1,0:T(8,128)(2,1)}, bf16[512,2048]{1,0:T(8,128)(2,1)}, u32[]{:S(2)}, u32[]{:S(2)}) collective-permute-start(bf16[512,2048]{1,0:T(8,128)(2,1)} %collective-permute-done.40), channel_id=1, source_target_pairs={{0,4},{4,0},{1,5},{5,1},{2,6},{6,2},{3,7},{7,3},{8,12},{12,8},{9,1... | collective-permute-start | bytes 6291464 | tf_op jit(solution)/shard_map/ppermute | solution.py:244
  212.1 26.1 %collective-permute-start.19 = (bf16[512,512]{1,0:T(8,128)(2,1)}, bf16[512,512]{1,0:T(8,128)(2,1)}, u32[]{:S(2)}, u32[]{:S(2)}) collective-permute-start(bf16[512,512]{1,0:T(8,128)(2,1)} %slice.452), channel_id=1, source_target_pairs={{0,16},{8,24},{16,0},{24,8},{1,17},{9,25},{17,1},{25,9},{2,18},{10... | collective-permute-start | bytes 1572872 | tf_op jit(solution)/shard_map/ppermute | solution.py:244
  238.2 46.1 %collective-permute-start.50 = (bf16[512,2048]{1,0:T(8,128)(2,1)}, bf16[512,2048]{1,0:T(8,128)(2,1)S(1)}, u32[]{:S(2)}, u32[]{:S(2)}) collective-permute-start(bf16[512,2048]{1,0:T(8,128)(2,1)} %collective-permute-done.44), channel_id=1, source_target_pairs={{0,4},{4,0},{1,5},{5,1},{2,6},{6,2},{3,7},{7,3},{8,12},{12,8},{9,1... | collective-permute-start | bytes 6291464 | tf_op jit(solution)/shard_map/ppermute | solution.py:244
  278.0 39.3 %collective-permute-start.21 = (bf16[512,2048]{1,0:T(8,128)(2,1)}, bf16[512,2048]{1,0:T(8,128)(2,1)S(1)}, u32[]{:S(2)}, u32[]{:S(2)}) collective-permute-start(bf16[512,2048]{1,0:T(8,128)(2,1)} %convolution_convert_fusion.5), channel_id=1, source_target_pairs={{0,4},{4,0},{1,5},{5,1},{2,6},{6,2},{3,7},{7,3},{8,12},{12,8},{9,1... | collective-permute-start | bytes 6291464 | tf_op jit(solution)/shard_map/ppermute | solution.py:244
  291.6 47.9 %collective-permute-start.46 = (bf16[512,2048]{1,0:T(8,128)(2,1)}, bf16[512,2048]{1,0:T(8,128)(2,1)}, u32[]{:S(2)}, u32[]{:S(2)}) collective-permute-start(bf16[512,2048]{1,0:T(8,128)(2,1)} %get-tuple-element.161), channel_id=1, source_target_pairs={{0,4},{4,0},{1,5},{5,1},{2,6},{6,2},{3,7},{7,3},{8,12},{12,8},{9,1... | collective-permute-start | bytes 6291464 | tf_op jit(solution)/shard_map/ppermute | solution.py:244
  323.8 50.2 %collective-permute-start.22 = (bf16[512,2048]{1,0:T(8,128)(2,1)}, bf16[512,2048]{1,0:T(8,128)(2,1)}, u32[]{:S(2)}, u32[]{:S(2)}) collective-permute-start(bf16[512,2048]{1,0:T(8,128)(2,1)} %get-tuple-element.59), channel_id=1, source_target_pairs={{0,4},{4,0},{1,5},{5,1},{2,6},{6,2},{3,7},{7,3},{8,12},{12,8},{9,1... | collective-permute-start | bytes 6291464 | tf_op jit(solution)/shard_map/ppermute | solution.py:244
  323.8 48.3 %collective-permute-start.24 = (bf16[512,2048]{1,0:T(8,128)(2,1)}, bf16[512,2048]{1,0:T(8,128)(2,1)}, u32[]{:S(2)}, u32[]{:S(2)}) collective-permute-start(bf16[512,2048]{1,0:T(8,128)(2,1)} %get-tuple-element.59), channel_id=1, source_target_pairs={{0,8},{8,0},{16,24},{24,16},{1,9},{9,1},{17,25},{25,17},{2,10},{10... | collective-permute-start | bytes 6291464 | tf_op jit(solution)/shard_map/ppermute | solution.py:244
  323.8 49.7 %collective-permute-start.28 = (bf16[512,2048]{1,0:T(8,128)(2,1)}, bf16[512,2048]{1,0:T(8,128)(2,1)S(1)}, u32[]{:S(2)}, u32[]{:S(2)}) collective-permute-start(bf16[512,2048]{1,0:T(8,128)(2,1)} %get-tuple-element.59), channel_id=1, source_target_pairs={{0,16},{8,24},{16,0},{24,8},{1,17},{9,25},{17,1},{25,9},{2,18},{10... | collective-permute-start | bytes 6291464 | tf_op jit(solution)/shard_map/ppermute | solution.py:244
  373.5 39.4 %collective-permute-start.27 = (bf16[256,2048]{1,0:T(8,128)(2,1)S(1)}, bf16[256,2048]{1,0:T(8,128)(2,1)S(1)}, u32[]{:S(2)}, u32[]{:S(2)}) collective-permute-start(bf16[256,2048]{1,0:T(8,128)(2,1)S(1)} %slice.457), channel_id=1, source_target_pairs={{0,16},{8,24},{16,0},{24,8},{1,17},{9,25},{17,1},{25,9},{2,18},{10... | collective-permute-start | bytes 3145736 | tf_op jit(solution)/shard_map/ppermute | solution.py:244
  373.7 39.4 %collective-permute-start.29 = (bf16[256,2048]{1,0:T(8,128)(2,1)S(1)}, bf16[256,2048]{1,0:T(8,128)(2,1)S(1)}, u32[]{:S(2)}, u32[]{:S(2)}) collective-permute-start(bf16[256,2048]{1,0:T(8,128)(2,1)S(1)} %slice.458), channel_id=1, source_target_pairs={{0,8},{8,0},{16,24},{24,16},{1,9},{9,1},{17,25},{25,17},{2,10},{10... | collective-permute-start | bytes 3145736 | tf_op jit(solution)/shard_map/ppermute | solution.py:244
  388.2 232.3 %collective-permute-start.39 = (bf16[512,2048]{1,0:T(8,128)(2,1)}, bf16[512,2048]{1,0:T(8,128)(2,1)}, u32[]{:S(2)}, u32[]{:S(2)}) collective-permute-start(bf16[512,2048]{1,0:T(8,128)(2,1)} %add_convert_fusion.8), channel_id=1, source_target_pairs={{0,4},{4,0},{1,5},{5,1},{2,6},{6,2},{3,7},{7,3},{8,12},{12,8},{9,1... | collective-permute-start | bytes 6291464 | tf_op jit(solution)/shard_map/ppermute | solution.py:244
  411.5 256.2 %collective-permute-start.23 = (bf16[512,2048]{1,0:T(8,128)(2,1)}, bf16[512,2048]{1,0:T(8,128)(2,1)}, u32[]{:S(2)}, u32[]{:S(2)}) collective-permute-start(bf16[512,2048]{1,0:T(8,128)(2,1)} %convolution_convert_fusion.9), channel_id=1, source_target_pairs={{0,4},{4,0},{1,5},{5,1},{2,6},{6,2},{3,7},{7,3},{8,12},{12,8},{9,1... | collective-permute-start | bytes 6291464 | tf_op jit(solution)/shard_map/ppermute | solution.py:244
  413.4 50.6 %collective-permute-start.30 = (bf16[512,2048]{1,0:T(8,128)(2,1)S(1)}, bf16[512,2048]{1,0:T(8,128)(2,1)S(1)}, u32[]{:S(2)}, u32[]{:S(2)}) collective-permute-start(bf16[512,2048]{1,0:T(8,128)(2,1)S(1)} %get-tuple-element.157), channel_id=1, source_target_pairs={{0,4},{4,0},{1,5},{5,1},{2,6},{6,2},{3,7},{7,3},{8,12},{12,8},{9,1... | collective-permute-start | bytes 6291464 | tf_op jit(solution)/shard_map/ppermute | solution.py:244
  424.5 64.0 %collective-permute-start.26 = (bf16[512,2048]{1,0:T(8,128)(2,1)}, bf16[512,2048]{1,0:T(8,128)(2,1)}, u32[]{:S(2)}, u32[]{:S(2)}) collective-permute-start(bf16[512,2048]{1,0:T(8,128)(2,1)} %convolution_convert_fusion.8), channel_id=1, source_target_pairs={{0,4},{4,0},{1,5},{5,1},{2,6},{6,2},{3,7},{7,3},{8,12},{12,8},{9,1... | collective-permute-start | bytes 6291464 | tf_op jit(solution)/shard_map/ppermute | solution.py:244
  438.7 55.1 %collective-permute-start.35 = (bf16[512,2048]{1,0:T(8,128)(2,1)}, bf16[512,2048]{1,0:T(8,128)(2,1)}, u32[]{:S(2)}, u32[]{:S(2)}) collective-permute-start(bf16[512,2048]{1,0:T(8,128)(2,1)} %convolution_convert_fusion.6), channel_id=1, source_target_pairs={{0,4},{4,0},{1,5},{5,1},{2,6},{6,2},{3,7},{7,3},{8,12},{12,8},{9,1... | collective-permute-start | bytes 6291464 | tf_op jit(solution)/shard_map/ppermute | solution.py:244
  463.9 81.6 %collective-permute-start.42 = (bf16[512,2048]{1,0:T(8,128)(2,1)}, bf16[512,2048]{1,0:T(8,128)(2,1)}, u32[]{:S(2)}, u32[]{:S(2)}) collective-permute-start(bf16[512,2048]{1,0:T(8,128)(2,1)} %add_convert_fusion.6), channel_id=1, source_target_pairs={{0,4},{4,0},{1,5},{5,1},{2,6},{6,2},{3,7},{7,3},{8,12},{12,8},{9,1... | collective-permute-start | bytes 6291464 | tf_op jit(solution)/shard_map/ppermute | solution.py:244
  488.3 225.3 %reduce-scatter.6.cloned.1.call-start = ((), (), s32[]{:S(2)}) async-start(), calls=%async_computation.10 | async-start | bytes 3604480 | tf_op jit(solution)/shard_map/reduce_scatter | solution.py:442
  488.5 62.8 %collective-permute-start.51 = (bf16[512,2048]{1,0:T(8,128)(2,1)}, bf16[512,2048]{1,0:T(8,128)(2,1)}, u32[]{:S(2)}, u32[]{:S(2)}) collective-permute-start(bf16[512,2048]{1,0:T(8,128)(2,1)} %add_convert_fusion.2), channel_id=1, source_target_pairs={{0,4},{4,0},{1,5},{5,1},{2,6},{6,2},{3,7},{7,3},{8,12},{12,8},{9,1... | collective-permute-start | bytes 6291464 | tf_op jit(solution)/shard_map/ppermute | solution.py:244
  505.6 51.8 %collective-permute-start.47 = (bf16[512,2048]{1,0:T(8,128)(2,1)}, bf16[512,2048]{1,0:T(8,128)(2,1)}, u32[]{:S(2)}, u32[]{:S(2)}) collective-permute-start(bf16[512,2048]{1,0:T(8,128)(2,1)} %add_convert_fusion.4), channel_id=1, source_target_pairs={{0,4},{4,0},{1,5},{5,1},{2,6},{6,2},{3,7},{7,3},{8,12},{12,8},{9,1... | collective-permute-start | bytes 6291464 | tf_op jit(solution)/shard_map/ppermute | solution.py:244
  521.3 193.7 %reduce-scatter.8.cloned.1.call-start = ((), (), s32[]{:S(2)}) async-start(), calls=%async_computation.11 | async-start | bytes 3604480 | tf_op jit(solution)/shard_map/reduce_scatter | solution.py:442
  564.7 26.1 %collective-permute-start.48 = (bf16[256,2048]{1,0:T(8,128)(2,1)S(1)}, bf16[256,2048]{1,0:T(8,128)(2,1)S(1)}, u32[]{:S(2)}, u32[]{:S(2)}) collective-permute-start(bf16[256,2048]{1,0:T(8,128)(2,1)S(1)} %get-tuple-element.148), channel_id=1, source_target_pairs={{0,16},{8,24},{16,0},{24,8},{1,17},{9,25},{17,1},{25,9},{2,18},{10... | collective-permute-start | bytes 3145736 | tf_op jit(solution)/shard_map/ppermute | solution.py:244
  566.7 26.3 %collective-permute-start.52 = (bf16[256,2048]{1,0:T(8,128)(2,1)S(1)}, bf16[256,2048]{1,0:T(8,128)(2,1)S(1)}, u32[]{:S(2)}, u32[]{:S(2)}) collective-permute-start(bf16[256,2048]{1,0:T(8,128)(2,1)S(1)} %get-tuple-element.149), channel_id=1, source_target_pairs={{0,8},{8,0},{16,24},{24,16},{1,9},{9,1},{17,25},{25,17},{2,10},{10... | collective-permute-start | bytes 3145736 | tf_op jit(solution)/shard_map/ppermute | solution.py:244
  571.9 40.5 %collective-permute-start.32 = (bf16[256,2048]{1,0:T(8,128)(2,1)S(1)}, bf16[256,2048]{1,0:T(8,128)(2,1)S(1)}, u32[]{:S(2)}, u32[]{:S(2)}) collective-permute-start(bf16[256,2048]{1,0:T(8,128)(2,1)S(1)} %get-tuple-element.150), channel_id=1, source_target_pairs={{0,16},{8,24},{16,0},{24,8},{1,17},{9,25},{17,1},{25,9},{2,18},{10... | collective-permute-start | bytes 3145736 | tf_op jit(solution)/shard_map/ppermute | solution.py:244
  590.8 26.1 %collective-permute-start.36 = (bf16[256,2048]{1,0:T(8,128)(2,1)S(1)}, bf16[256,2048]{1,0:T(8,128)(2,1)S(1)}, u32[]{:S(2)}, u32[]{:S(2)}) collective-permute-start(bf16[256,2048]{1,0:T(8,128)(2,1)S(1)} %get-tuple-element.151), channel_id=1, source_target_pairs={{0,8},{8,0},{16,24},{24,16},{1,9},{9,1},{17,25},{25,17},{2,10},{10... | collective-permute-start | bytes 3145736 | tf_op jit(solution)/shard_map/ppermute | solution.py:244
  593.0 68.8 %collective-permute-start.49 = (bf16[512,2048]{1,0:T(8,128)(2,1)S(1)}, bf16[512,2048]{1,0:T(8,128)(2,1)S(1)}, u32[]{:S(2)}, u32[]{:S(2)}) collective-permute-start(bf16[512,2048]{1,0:T(8,128)(2,1)S(1)} %pad_maximum_fusion.8), channel_id=1, source_target_pairs={{0,8},{8,0},{16,24},{24,16},{1,9},{9,1},{17,25},{25,17},{2,10},{10... | collective-permute-start | bytes 6291464 | tf_op jit(solution)/shard_map/ppermute | solution.py:244
  612.4 49.4 %collective-permute-start.53 = (bf16[512,2048]{1,0:T(8,128)(2,1)S(1)}, bf16[512,2048]{1,0:T(8,128)(2,1)S(1)}, u32[]{:S(2)}, u32[]{:S(2)}) collective-permute-start(bf16[512,2048]{1,0:T(8,128)(2,1)S(1)} %pad_maximum_fusion.9), channel_id=1, source_target_pairs={{0,16},{8,24},{16,0},{24,8},{1,17},{9,25},{17,1},{25,9},{2,18},{10... | collective-permute-start | bytes 6291464 | tf_op jit(solution)/shard_map/ppermute | solution.py:244
  616.9 87.4 %collective-permute-start.33 = (bf16[512,2048]{1,0:T(8,128)(2,1)}, bf16[512,2048]{1,0:T(8,128)(2,1)S(1)}, u32[]{:S(2)}, u32[]{:S(2)}) collective-permute-start(bf16[512,2048]{1,0:T(8,128)(2,1)} %pad_maximum_fusion.6), channel_id=1, source_target_pairs={{0,8},{8,0},{16,24},{24,16},{1,9},{9,1},{17,25},{25,17},{2,10},{10... | collective-permute-start | bytes 6291464 | tf_op jit(solution)/shard_map/ppermute | solution.py:244
  620.6 83.7 %collective-permute-start.37 = (bf16[512,2048]{1,0:T(8,128)(2,1)}, bf16[512,2048]{1,0:T(8,128)(2,1)S(1)}, u32[]{:S(2)}, u32[]{:S(2)}) collective-permute-start(bf16[512,2048]{1,0:T(8,128)(2,1)} %pad_maximum_fusion.7), channel_id=1, source_target_pairs={{0,16},{8,24},{16,0},{24,8},{1,17},{9,25},{17,1},{25,9},{2,18},{10... | collective-permute-start | bytes 6291464 | tf_op jit(solution)/shard_map/ppermute | solution.py:244
  718.0 102.2 %all-to-all-start = ((bf16[1,3,176,8,256]{4,2,1,0,3:T(8,128)(2,1)}), bf16[1,3,176,8,256]{4,2,1,0,3:T(8,128)(2,1)}, u32[]{:S(2)}, u32[]{:S(2)}) async-start(bf16[1,3,176,8,256]{4,2,1,0,3:T(8,128)(2,1)} %pad_maximum_fusion.5), calls=%async_computation.3 | async-start | bytes 4325376 | tf_op jit(solution)/shard_map/all_to_all | solution.py:452
  797.9 59.9 %collective-permute-start.55 = (bf16[512,256]{1,0:T(8,128)(2,1)}, bf16[512,256]{1,0:T(8,128)(2,1)}, u32[]{:S(2)}, u32[]{:S(2)}) collective-permute-start(bf16[512,256]{1,0:T(8,128)(2,1)} %get-tuple-element.144), channel_id=1, source_target_pairs={{0,4},{4,0},{1,5},{5,1},{2,6},{6,2},{3,7},{7,3},{8,12},{12,8},{9,1... | collective-permute-start | bytes 786440 | tf_op jit(solution)/shard_map/ppermute | solution.py:244
  806.8 34.3 %collective-permute-start.81 = (bf16[128,2048]{1,0:T(8,128)(2,1)}, bf16[128,2048]{1,0:T(8,128)(2,1)}, u32[]{:S(2)}, u32[]{:S(2)}) collective-permute-start(bf16[128,2048]{1,0:T(8,128)(2,1)} %get-tuple-element.93), channel_id=1, source_target_pairs={{0,16},{8,24},{16,0},{24,8},{1,17},{9,25},{17,1},{25,9},{2,18},{10... | collective-permute-start | bytes 1572872 | tf_op jit(solution)/shard_map/ppermute | solution.py:244
  816.4 26.5 %collective-permute-start.83 = (bf16[128,2048]{1,0:T(8,128)(2,1)}, bf16[128,2048]{1,0:T(8,128)(2,1)}, u32[]{:S(2)}, u32[]{:S(2)}) collective-permute-start(bf16[128,2048]{1,0:T(8,128)(2,1)} %get-tuple-element.95), channel_id=1, source_target_pairs={{0,8},{8,0},{16,24},{24,16},{1,9},{9,1},{17,25},{25,17},{2,10},{10... | collective-permute-start | bytes 1572872 | tf_op jit(solution)/shard_map/ppermute | solution.py:244
  816.4 29.2 %collective-permute-start.65 = (bf16[256,1024]{1,0:T(8,128)(2,1)}, bf16[256,1024]{1,0:T(8,128)(2,1)}, u32[]{:S(2)}, u32[]{:S(2)}) collective-permute-start(bf16[256,1024]{1,0:T(8,128)(2,1)} %get-tuple-element.99), channel_id=1, source_target_pairs={{0,16},{8,24},{16,0},{24,8},{1,17},{9,25},{17,1},{25,9},{2,18},{10... | collective-permute-start | bytes 1572872 | tf_op jit(solution)/shard_map/ppermute | solution.py:244
  845.6 88.6 %collective-permute-start.82 = (bf16[256,2048]{1,0:T(8,128)(2,1)S(1)}, bf16[256,2048]{1,0:T(8,128)(2,1)S(1)}, u32[]{:S(2)}, u32[]{:S(2)}) collective-permute-start(bf16[256,2048]{1,0:T(8,128)(2,1)S(1)} %pad_maximum_fusion.14), channel_id=1, source_target_pairs={{0,8},{8,0},{16,24},{24,16},{1,9},{9,1},{17,25},{25,17},{2,10},{10... | collective-permute-start | bytes 3145736 | tf_op jit(solution)/shard_map/ppermute | solution.py:244
  855.8 78.4 %collective-permute-start.84 = (bf16[256,2048]{1,0:T(8,128)(2,1)S(1)}, bf16[256,2048]{1,0:T(8,128)(2,1)S(1)}, u32[]{:S(2)}, u32[]{:S(2)}) collective-permute-start(bf16[256,2048]{1,0:T(8,128)(2,1)S(1)} %pad_maximum_fusion.15), channel_id=1, source_target_pairs={{0,16},{8,24},{16,0},{24,8},{1,17},{9,25},{17,1},{25,9},{2,18},{10... | collective-permute-start | bytes 3145736 | tf_op jit(solution)/shard_map/ppermute | solution.py:244
  863.2 41.0 %collective-permute-start.66 = (bf16[512,1024]{1,0:T(8,128)(2,1)S(1)}, bf16[512,1024]{1,0:T(8,128)(2,1)S(1)}, u32[]{:S(2)}, u32[]{:S(2)}) collective-permute-start(bf16[512,1024]{1,0:T(8,128)(2,1)S(1)} %pad_maximum_fusion.12), channel_id=1, source_target_pairs={{0,8},{8,0},{16,24},{24,16},{1,9},{9,1},{17,25},{25,17},{2,10},{10... | collective-permute-start | bytes 3145736 | tf_op jit(solution)/shard_map/ppermute | solution.py:244
  863.6 40.6 %collective-permute-start.68 = (bf16[512,1024]{1,0:T(8,128)(2,1)S(1)}, bf16[512,1024]{1,0:T(8,128)(2,1)S(1)}, u32[]{:S(2)}, u32[]{:S(2)}) collective-permute-start(bf16[512,1024]{1,0:T(8,128)(2,1)S(1)} %pad_maximum_fusion.13), channel_id=1, source_target_pairs={{0,16},{8,24},{16,0},{24,8},{1,17},{9,25},{17,1},{25,9},{2,18},{10... | collective-permute-start | bytes 3145736 | tf_op jit(solution)/shard_map/ppermute | solution.py:244
  873.0 109.0 %collective-permute-start.64 = (bf16[512,2048]{1,0:T(8,128)(2,1)}, bf16[512,2048]{1,0:T(8,128)(2,1)}, u32[]{:S(2)}, u32[]{:S(2)}) collective-permute-start(bf16[512,2048]{1,0:T(8,128)(2,1)} %add_convert_fusion), channel_id=1, source_target_pairs={{0,4},{4,0},{1,5},{5,1},{2,6},{6,2},{3,7},{7,3},{8,12},{12,8},{9,1... | collective-permute-start | bytes 6291464 | tf_op jit(solution)/shard_map/ppermute | solution.py:244
  904.9 32.7 %collective-permute-start.69 = (bf16[2,64,1024]{2,1,0:T(8,128)(2,1)S(1)}, bf16[2,64,1024]{2,1,0:T(8,128)(2,1)S(1)}, u32[]{:S(2)}, u32[]{:S(2)}) collective-permute-start(bf16[2,64,1024]{2,1,0:T(8,128)(2,1)S(1)} %get-tuple-element.139), channel_id=1, source_target_pairs={{0,1},{1,0},{2,3},{3,2},{4,5},{5,4},{6,7},{7,6},{8,9},{9,8},{10,11... | collective-permute-start | bytes 786440 | tf_op jit(solution)/shard_map/ppermute | solution.py:244
  904.9 47.8 %collective-permute-start.70 = (bf16[2,64,1024]{2,1,0:T(8,128)(2,1)S(1)}, bf16[2,64,1024]{2,1,0:T(8,128)(2,1)S(1)}, u32[]{:S(2)}, u32[]{:S(2)}) collective-permute-start(bf16[2,64,1024]{2,1,0:T(8,128)(2,1)S(1)} %get-tuple-element.141), channel_id=1, source_target_pairs={{0,2},{1,3},{2,0},{3,1},{4,6},{5,7},{6,4},{7,5},{8,10},{9,11},{10,... | collective-permute-start | bytes 786440 | tf_op jit(solution)/shard_map/ppermute | solution.py:244
  934.2 27.4 %collective-permute-start.71 = (bf16[2,64,1024]{2,1,0:T(8,128)(2,1)S(1)}, bf16[2,64,1024]{2,1,0:T(8,128)(2,1)S(1)}, u32[]{:S(2)}, u32[]{:S(2)}) collective-permute-start(bf16[2,64,1024]{2,1,0:T(8,128)(2,1)S(1)} %get-tuple-element.140), channel_id=1, source_target_pairs={{0,3},{1,2},{2,1},{3,0},{4,7},{5,6},{6,5},{7,4},{8,11},{9,10},{10,... | collective-permute-start | bytes 786440 | tf_op jit(solution)/shard_map/ppermute | solution.py:244
  937.0 25.8 %collective-permute-start.85 = (bf16[64,2048]{1,0:T(8,128)(2,1)}, bf16[64,2048]{1,0:T(8,128)(2,1)}, u32[]{:S(2)}, u32[]{:S(2)}) collective-permute-start(bf16[64,2048]{1,0:T(8,128)(2,1)} %get-tuple-element.136), channel_id=1, source_target_pairs={{0,1},{1,0},{2,3},{3,2},{4,5},{5,4},{6,7},{7,6},{8,9},{9,8},{10,11... | collective-permute-start | bytes 786440 | tf_op jit(solution)/shard_map/ppermute | solution.py:244
  937.6 37.3 %collective-permute-start.86 = (bf16[64,2048]{1,0:T(8,128)(2,1)}, bf16[64,2048]{1,0:T(8,128)(2,1)}, u32[]{:S(2)}, u32[]{:S(2)}) collective-permute-start(bf16[64,2048]{1,0:T(8,128)(2,1)} %get-tuple-element.138), channel_id=1, source_target_pairs={{0,2},{1,3},{2,0},{3,1},{4,6},{5,7},{6,4},{7,5},{8,10},{9,11},{10,... | collective-permute-start | bytes 786440 | tf_op jit(solution)/shard_map/ppermute | solution.py:244
  (147 other events, 2331.9 us)
Sparse Core Ops, SparseCore 0:
  10.2 35.6 all-gather.7
  48.0 26.8 all-gather.9
  76.5 58.6 all-gather.15
  137.2 57.8 all-gather.13
  196.5 57.8 all-gather.11
  488.4 67.5 reduce-scatter.3
  558.3 56.0 reduce-scatter.5
  616.7 56.0 reduce-scatter.7

commit v2 on v1

v2 whole, which is shorter than its diff:
```python
import functools

import jax
import jax.numpy as jnp
from jax import lax
from jax.experimental import pallas as pl
from jax.experimental.layout import Layout, with_layout_constraint
from jax.experimental.pallas import tpu as pltpu
from jax.sharding import Mesh
from jax.sharding import PartitionSpec as P

H = 16
HD = 128
HALF = HD // 2
MASKED = -1e30
LN2 = 0.6931471805599453
LOG2E = 1.4426950408889634
EPSILON = 1e-05
ROPE_BASE = 10000.0
BF16 = jnp.bfloat16
F32 = jnp.float32


def block_places(order_ref, place_ref, own):
    count = order_ref.shape[0]
    for stored in range(count):
        relative = (stored // 2) ^ own
        place_ref[order_ref[stored]] = (relative % 2 * (count // 4) + relative // 2) * 2 + stored % 2


def causal(blk, group):
    keys = lax.broadcasted_iota(jnp.int32, (blk, blk), 0)
    rows = lax.broadcasted_iota(jnp.int32, (blk, blk), 1)
    return jnp.concatenate([keys <= rows] * group, axis=1)


def row_position(order_ref, own, row_block):
    return order_ref[2 * (own ^ (row_block // 2)) + row_block % 2]


def attend_forward(group, blk, scal_ref, order_ref, q_ref, cos_ref, sin_ref, kv_ref, out_ref, lse_ref, qt_ref, place_ref, vt_ref, acc_ref, max_ref, sum_ref):
    row_block = pl.program_id(0)
    own, length = scal_ref[0], scal_ref[1]

    @pl.when(row_block == 0)
    def _():
        block_places(order_ref, place_ref, own)
        for piece in range(order_ref.shape[0]):
            cells = slice(piece * blk, (piece + 1) * blk)
            vt_ref[:, cells] = kv_ref[cells, HD:].T

    mine = row_position(order_ref, own, row_block)

    def step(place, masked):
        start = pl.multiple_of(place * blk, blk)
        scores = jnp.dot(kv_ref[pl.ds(start, blk), :HD], qt_ref[0], preferred_element_type=F32)
        if masked:
            scores = jnp.where(causal(blk, group), scores, MASKED)
        old = max_ref[...]
        new = jnp.maximum(old, jnp.max(scores, axis=0, keepdims=True))
        weights = jnp.exp2(scores - new)
        scale = jnp.exp2(old - new)
        max_ref[...] = new
        sum_ref[...] = sum_ref[...] * scale + jnp.sum(weights, axis=0, keepdims=True)
        acc_ref[...] = acc_ref[...] * scale + jnp.dot(
            vt_ref[:, pl.ds(start, blk)], weights.astype(BF16), preferred_element_type=F32
        )

    @pl.when(mine * blk < length)
    def _():
        cosine, sine = cos_ref[...], sin_ref[...]
        for head in range(group):
            query = q_ref[:, head * HD : (head + 1) * HD].T
            first, second = query[:HALF], query[HALF:]
            turned = jnp.concatenate(
                [first * cosine - second * sine, second * cosine + first * sine], axis=0
            )
            qt_ref[0, :, head * blk : (head + 1) * blk] = (turned * (LOG2E * HD**-0.5)).astype(BF16)
        max_ref[...] = jnp.full(max_ref.shape, MASKED, F32)
        sum_ref[...] = jnp.zeros(sum_ref.shape, F32)
        acc_ref[...] = jnp.zeros(acc_ref.shape, F32)
        step(place_ref[mine], True)

        def body(j, carried):
            step(place_ref[j], False)
            return carried

        lax.fori_loop(0, mine, body, 0)
        total = sum_ref[...]
        result = acc_ref[...] * (1.0 / total)
        for head in range(group):
            out_ref[:, head * HD : (head + 1) * HD] = (
                result[:, head * blk : (head + 1) * blk].T.astype(BF16)
            )
        lse_ref[0] = max_ref[...] + jnp.log2(total)

    @pl.when(mine * blk >= length)
    def _():
        out_ref[...] = jnp.zeros(out_ref.shape, BF16)
        lse_ref[...] = jnp.zeros(lse_ref.shape, F32)
        qt_ref[...] = jnp.zeros(qt_ref.shape, BF16)


def attention_forward(scalars, order, queries, cosine, sine, keys_values, blk):
    rows, width = queries.shape
    span = keys_values.shape[0]
    row_blocks, heads = rows // blk, width // HD
    table = pl.BlockSpec((HALF, blk), lambda i, *_: (0, i))
    per_block = lambda *dims: pl.BlockSpec((1,) + dims, lambda i, *_: (i, 0, 0))
    return pl.pallas_call(
        functools.partial(attend_forward, heads, blk),
        grid_spec=pltpu.PrefetchScalarGridSpec(
            num_scalar_prefetch=2,
            grid=(row_blocks,),
            in_specs=[
                pl.BlockSpec((blk, width), lambda i, *_: (i, 0)),
                table,
                table,
                pl.BlockSpec((span, 2 * HD), lambda i, *_: (0, 0)),
            ],
            out_specs=[
                pl.BlockSpec((blk, width), lambda i, *_: (i, 0)),
                per_block(1, heads * blk),
                per_block(HD, heads * blk),
            ],
            scratch_shapes=[
                pltpu.SMEM((order.shape[0],), jnp.int32),
                pltpu.VMEM((HD, span), BF16),
                pltpu.VMEM((HD, heads * blk), F32),
                pltpu.VMEM((1, heads * blk), F32),
                pltpu.VMEM((1, heads * blk), F32),
            ],
        ),
        out_shape=[
            jax.ShapeDtypeStruct((rows, width), BF16),
            jax.ShapeDtypeStruct((row_blocks, 1, heads * blk), F32),
            jax.ShapeDtypeStruct((row_blocks, HD, heads * blk), BF16),
        ],
        compiler_params=pltpu.CompilerParams(vmem_limit_bytes=40 * 2**20),
        cost_estimate=pl.CostEstimate(flops=2**20, bytes_accessed=2**16, transcendentals=0),
        name="attend_forward",
    )(scalars, order, queries, cosine, sine, keys_values)


def attend_backward(group, blk, scal_ref, order_ref, qt_ref, g_ref, a_ref, lse_ref, cos_ref, sin_ref, kv_ref, dq_ref, dkv_ref, place_ref, gt_ref, qs_ref, gs_ref, kt_ref, acc_ref, delta_ref):
    row_block = pl.program_id(0)
    own, length = scal_ref[0], scal_ref[1]

    @pl.when(row_block == 0)
    def _():
        block_places(order_ref, place_ref, own)
        for piece in range(order_ref.shape[0]):
            cells = slice(piece * blk, (piece + 1) * blk)
            kt_ref[:, cells] = kv_ref[cells, :HD].T
        dkv_ref[...] = jnp.zeros(dkv_ref.shape, F32)

    mine = row_position(order_ref, own, row_block)

    def step(place, masked):
        start = pl.multiple_of(place * blk, blk)
        scores = jnp.dot(kv_ref[pl.ds(start, blk), :HD], qt_ref[0], preferred_element_type=F32)
        weights = jnp.exp2(scores - lse_ref[0])
        if masked:
            weights = jnp.where(causal(blk, group), weights, 0.0)
        grads = jnp.dot(kv_ref[pl.ds(start, blk), HD:], gt_ref[...], preferred_element_type=F32)
        dscores = (weights * (grads - delta_ref[...])).astype(BF16)
        dkv_ref[pl.ds(start, blk), HD:] += jnp.dot(
            weights.astype(BF16), gs_ref[...], preferred_element_type=F32
        )
        dkv_ref[pl.ds(start, blk), :HD] += jnp.dot(dscores, qs_ref[...], preferred_element_type=F32)
        acc_ref[...] += jnp.dot(kt_ref[:, pl.ds(start, blk)], dscores, preferred_element_type=F32)

    @pl.when(mine * blk < length)
    def _():
        for head in range(group):
            lanes = slice(head * HD, (head + 1) * HD)
            cells = slice(head * blk, (head + 1) * blk)
            grad = g_ref[:, lanes]
            gt_ref[:, cells] = grad.T
            qs_ref[cells, :] = qt_ref[0, :, cells].T
            gs_ref[cells, :] = grad
            product = grad.astype(F32) * a_ref[:, lanes].astype(F32)
            delta_ref[:, cells] = jnp.sum(product.T, axis=0, keepdims=True)
        acc_ref[...] = jnp.zeros(acc_ref.shape, F32)
        step(place_ref[mine], True)

        def body(j, carried):
            step(place_ref[j], False)
            return carried

        lax.fori_loop(0, mine, body, 0)
        cosine, sine = cos_ref[...], sin_ref[...]
        for head in range(group):
            turned = acc_ref[:, head * blk : (head + 1) * blk].astype(BF16).astype(F32)
            first, second = turned[:HALF], turned[HALF:]
            grad = jnp.concatenate(
                [first * cosine + second * sine, second * cosine - first * sine], axis=0
            )
            dq_ref[:, head * HD : (head + 1) * HD] = (grad * HD**-0.5).T.astype(BF16)

    @pl.when(mine * blk >= length)
    def _():
        dq_ref[...] = jnp.zeros(dq_ref.shape, BF16)


def attention_backward(scalars, order, turned, grads, attended, lse, cosine, sine, keys_values, blk, group, which):
    rows = grads.shape[0]
    span = keys_values.shape[0]
    row_blocks = rows // blk
    table = pl.BlockSpec((HALF, blk), lambda i, *_: (0, i))
    rowspec = pl.BlockSpec((blk, group * HD), lambda i, *_: (i, which))
    per_block = lambda *dims: pl.BlockSpec((1,) + dims, lambda i, *_: (i, 0, which))
    return pl.pallas_call(
        functools.partial(attend_backward, group, blk),
        grid_spec=pltpu.PrefetchScalarGridSpec(
            num_scalar_prefetch=2,
            grid=(row_blocks,),
            in_specs=[
                per_block(HD, group * blk),
                rowspec,
                rowspec,
                per_block(1, group * blk),
                table,
                table,
                pl.BlockSpec((span, 2 * HD), lambda i, *_: (0, 0)),
            ],
            out_specs=[
                pl.BlockSpec((blk, group * HD), lambda i, *_: (i, 0)),
                pl.BlockSpec((span, 2 * HD), lambda i, *_: (0, 0)),
            ],
            scratch_shapes=[
                pltpu.SMEM((order.shape[0],), jnp.int32),
                pltpu.VMEM((HD, group * blk), BF16),
                pltpu.VMEM((group * blk, HD), BF16),
                pltpu.VMEM((group * blk, HD), BF16),
                pltpu.VMEM((HD, span), BF16),
                pltpu.VMEM((HD, group * blk), F32),
                pltpu.VMEM((1, group * blk), F32),
            ],
        ),
        out_shape=[
            jax.ShapeDtypeStruct((rows, group * HD), BF16),
            jax.ShapeDtypeStruct((span, 2 * HD), F32),
        ],
        compiler_params=pltpu.CompilerParams(vmem_limit_bytes=48 * 2**20),
        cost_estimate=pl.CostEstimate(flops=2**20, bytes_accessed=2**16, transcendentals=0),
        name="attend_backward",
    )(scalars, order, turned, grads, attended, lse, cosine, sine, keys_values)


def ffn_rows(count, tiles, place_ref, xa_ref, xb_ref, ga_ref, gb_ref, gate_ref, up_ref, down_ref, *rest):
    back_a, back_b, out_a, out_b, x_all, g_all, hidden_all, dgate_all, dup_all = rest[count:]
    units = gate_ref.shape[0] * gate_ref.shape[2]
    gate_rows, up_rows, down_rows = (ref[...].reshape(units, -1) for ref in (gate_ref, up_ref, down_ref))
    nt = (((1,), (1,)), ((), ()))
    early = pl.program_id(0) < tiles
    x = jnp.where(early, xa_ref[...], xb_ref[...])
    grad = jnp.where(early, ga_ref[...], gb_ref[...])
    gate = lax.dot_general(x, gate_rows, nt, preferred_element_type=F32)
    up = lax.dot_general(x, up_rows, nt, preferred_element_type=F32)
    dhidden = lax.dot_general(grad, down_rows, nt, preferred_element_type=F32)
    dhidden = dhidden.astype(BF16).astype(F32)
    sigmoid = jax.nn.sigmoid(gate)
    silu = gate * sigmoid
    hidden = (silu * up).astype(BF16)
    dgate = (dhidden * up * sigmoid * (1.0 + gate * (1.0 - sigmoid))).astype(BF16)
    dup = (dhidden * silu).astype(BF16)
    back = (
        jnp.dot(dgate, gate_rows, preferred_element_type=F32)
        + jnp.dot(dup, up_rows, preferred_element_type=F32)
    ).astype(BF16)
    out = jnp.dot(hidden, down_rows, preferred_element_type=F32).astype(BF16)
    x_all[...] = x
    g_all[...] = grad
    hidden_all[...] = hidden
    dgate_all[...] = dgate
    dup_all[...] = dup

    @pl.when(early)
    def _():
        back_a[...] = back
        out_a[...] = out

    @pl.when(jnp.logical_not(early))
    def _():
        back_b[...] = back
        out_b[...] = out


def ffn_pair(place, pairs, xa, xb, ga, gb, weights, kept):
    rows, model_dim = xa.shape
    planes, _, share, _ = weights.shape
    units = planes * share
    tile = min(256, rows)
    tiles = rows // tile
    weight = lambda which: pl.BlockSpec(
        (planes, 1, share, model_dim), lambda i, *_: (0, which, 0, 0), pipeline_mode=pl.Buffered(1)
    )
    turn_a = lambda i: jnp.minimum(i, tiles - 1)
    turn_b = lambda i: jnp.maximum(i - tiles, 0)
    block = lambda index: pl.BlockSpec((tile, model_dim), index)
    here_a, here_b = block(lambda i, *_: (turn_a(i), 0)), block(lambda i, *_: (turn_b(i), 0))
    out_a = block(lambda i, place_ref: (place_ref[0] * tiles + turn_a(i), 0))
    out_b = block(lambda i, place_ref: (place_ref[0] * tiles + turn_b(i), 0))
    there = lambda wide: pl.BlockSpec((tile, wide), lambda i, place_ref: (place_ref[0] * 2 * tiles + i, 0))
    count = len(kept)
    shape = lambda tall, wide: jax.ShapeDtypeStruct((tall, wide), BF16)
    return pl.pallas_call(
        functools.partial(ffn_rows, count, tiles),
        grid_spec=pltpu.PrefetchScalarGridSpec(
            num_scalar_prefetch=1,
            grid=(2 * tiles,),
            in_specs=[here_a, here_b, out_a, out_b, weight(0), weight(1), weight(2)]
            + [pl.BlockSpec(memory_space=pl.ANY)] * count,
            out_specs=[here_a, here_b, out_a, out_b] + [there(model_dim)] * 2 + [there(units)] * 3,
        ),
        out_shape=[shape(rows, model_dim)] * 2
        + [shape(pairs * rows, model_dim)] * 2
        + [shape(pairs * 2 * rows, model_dim)] * 2
        + [shape(pairs * 2 * rows, units)] * 3,
        input_output_aliases={8 + i: 2 + i for i in range(count)},
        compiler_params=pltpu.CompilerParams(vmem_limit_bytes=52 * 2**20),
        cost_estimate=pl.CostEstimate(flops=2**20, bytes_accessed=2**16, transcendentals=0),
        name="ffn_pair",
    )(place, xa, xb, ga, gb, weights, weights, weights, *kept)


def angles(positions):
    frequency = ROPE_BASE ** (-2.0 * jnp.arange(HALF, dtype=F32) / HD)
    phase_angle = frequency[:, None] * positions.astype(F32)[None, :]
    return (jnp.cos(phase_angle), jnp.sin(phase_angle))


def rotate(vectors, cosine, sine_vals):
    first_half = vectors[..., :HALF]
    second_half = vectors[..., HALF:]
    return jnp.concatenate(
        [
            first_half * cosine - second_half * sine_vals,
            second_half * cosine + first_half * sine_vals,
        ],
        axis=-1,
    )


def matmul(left, right):
    return jnp.dot(left, right, preferred_element_type=F32)


def contract_rows(left, right):
    return lax.dot_general(left, right, (((0,), (0,)), ((), ())), preferred_element_type=F32)


def contract_cols(left, right):
    return lax.dot_general(left, right, (((1,), (1,)), ((), ())), preferred_element_type=F32)


def after(value, *earlier):
    return lax.optimization_barrier((value, earlier))[0]


def exchange(value, axis, distance):
    size = lax.axis_size(axis)
    return lax.ppermute(value, axis, [(i, i ^ distance) for i in range(size)])


def swap_core(value):
    return exchange(value, "core", 1)


def spread_chips(value):
    return [value] + [exchange(value, "chip", k) for k in range(1, lax.axis_size("chip"))]


def gather_near(value):
    if lax.axis_size("chip") != 4:
        return spread_chips(value)
    return [value, exchange(value, "chip", 1), exchange(value, "chip", 2)]


def send_far(near):
    if lax.axis_size("chip") != 4:
        return ()
    value, first, second = near
    half = value.shape[0] // 2
    return exchange(first[:half], "chip", 2), exchange(second[half:], "chip", 1)


def gather_far(near):
    halves = send_far(near)
    return near + [jnp.concatenate(halves, axis=0)] if halves else near


def gather_chips(value):
    return gather_far(gather_near(value))


def add_cores(terms, terms_of_other):
    return (terms.astype(F32) + swap_core(terms_of_other.astype(BF16)).astype(F32)).astype(BF16)


def deal(terms, axis):
    dealt = lax.all_to_all(terms.astype(BF16), axis, 0, 0, tiled=False)
    return jnp.sum(dealt.astype(F32), axis=0)


def at(value, index, axis=0):
    return lax.dynamic_index_in_dim(value, index, axis, keepdims=False)


def sum_planes(terms, plane):
    total = at(terms, plane).astype(F32)
    for k in range(1, lax.axis_size("fsdp")):
        total = total + exchange(at(terms, plane ^ k).astype(BF16), "fsdp", k).astype(F32)
    return total


def reduce_far(last):
    half = last.shape[0] // 2
    return exchange(last[:half], "chip", 1), exchange(last[half:], "chip", 2)


def add_half(term, passing, which):
    half = passing.shape[0]
    first, second = term[:half].astype(F32), term[half:].astype(F32)
    if which == 0:
        first = first + passing.astype(F32)
    else:
        second = second + passing.astype(F32)
    return jnp.concatenate([first, second], axis=0).astype(BF16)


def lay_columns(chunks, chip):
    rows, width = chunks[0].shape
    whole = jnp.zeros((rows, width * len(chunks)), chunks[0].dtype)
    for k, chunk in enumerate(chunks):
        whole = lax.dynamic_update_slice(whole, chunk, (0, (chip ^ k) * width))
    return whole


def shards(
    tokens,
    cotangent,
    kv_cotangent,
    lengths,
    block_order,
    w_query,
    w_kv,
    w_out,
    gain_attn,
    gain_ffn,
    w_gate,
    w_up,
    w_down,
):
    local_len, model_dim = tokens.shape[1:]
    chips, planes = lax.axis_size("chip"), lax.axis_size("fsdp")
    chip, core, plane = lax.axis_index("chip"), lax.axis_index("core"), lax.axis_index("fsdp")
    own = chip * 2 + core
    places = chips * 2
    blk = local_len // 2
    order, length = block_order[0], lengths[0]
    depth = w_query.shape[0]

    part = depth // 2
    wide = part * planes
    out_cols = model_dim // chips
    kv_rows = depth // chips
    gain_rows = depth // (2 * HD)
    narrow = lambda value: value.reshape(-1, 2 * HD)
    pieces = [
        lax.dynamic_slice(w_query, (0, chip * 2 * part + core * part), (depth, part)),
        lax.dynamic_slice(w_out, (core * part, chip * out_cols), (part, out_cols)),
        lax.dynamic_slice_in_dim(w_kv, chip * kv_rows, kv_rows, 0),
        gain_attn,
        gain_ffn,
    ]
    heights = [piece.size // (2 * HD) for piece in pieces]
    packed = jnp.concatenate([narrow(piece) for piece in pieces], axis=0)
    packed = lax.all_gather(packed, "fsdp", axis=0)
    bounds = [sum(heights[: i + 1]) for i in range(4)]
    query_piece, out_piece, kv_piece, gain_one, gain_two = jnp.split(packed, bounds, axis=1)
    share = w_gate.shape[1] // places
    pieces = jnp.stack(
        [
            lax.dynamic_slice(weight, (0, own * share), (model_dim, share)).T
            for weight in (w_gate, w_up, w_down)
        ]
    )
    ffn_weights = lax.all_gather(pieces, "fsdp", axis=0)
    query_piece = query_piece.reshape(model_dim, part)
    out_piece = out_piece.reshape(wide, out_cols)
    gain_one = gain_one.reshape(model_dim).astype(F32)
    gain_two = gain_two.reshape(model_dim).astype(F32)
    kv_full = jnp.zeros((planes, chips, kv_rows, 2 * HD), BF16)
    kv_chunks = gather_chips(kv_piece)
    for k, chunk in enumerate(kv_chunks):
        kv_full = lax.dynamic_update_slice(kv_full, chunk[:, None], (0, chip ^ k, 0, 0))
    kv_full = with_layout_constraint(kv_full.reshape(model_dim, 2 * HD), Layout((0, 1)))

    own_pos = jnp.repeat(lax.dynamic_slice_in_dim(order, own * 2, 2, 0) * blk, blk) + (
        jnp.arange(local_len, dtype=jnp.int32) % blk
    )
    live_rows = (own_pos < length)[:, None]
    grad_out = jnp.where(live_rows, cotangent[0], jnp.zeros((), BF16))
    grad_near = after(gather_near(grad_out), pieces)
    query_piece = after(query_piece, kv_chunks, grad_near)
    query_half = lay_columns(gather_chips(query_piece), chip)
    out_chunks = spread_chips(after(out_piece, query_half))
    grad_far = send_far(after(grad_near, query_half))

    offsets = jnp.arange(blk, dtype=jnp.int32)
    mine = lax.dynamic_slice_in_dim(order, own * 2, 2, 0)
    theirs = lax.dynamic_slice_in_dim(order, (own ^ 1) * 2, 2, 0)
    both_pos = (jnp.concatenate([mine, theirs])[:, None] * blk + offsets[None, :]).reshape(-1)
    cosine, sine_vals = angles(both_pos)
    own_cosine, own_sine = cosine[:, :local_len].T, sine_vals[:, :local_len].T

    tokens_low = tokens[0]
    tokens_flat = tokens_low.astype(F32)
    both_tokens = jnp.concatenate([tokens_low, swap_core(tokens_low)], axis=0).astype(F32)
    both_inverse = lax.rsqrt(jnp.mean(both_tokens * both_tokens, axis=1, keepdims=True) + EPSILON)
    both_normed = (both_tokens * both_inverse * gain_one).astype(BF16)
    inverse_one = both_inverse[:local_len]

    key_value = matmul(both_normed[:local_len], kv_full)
    key_rot = rotate(key_value[:, :HD], own_cosine, own_sine)
    local_kv = jnp.concatenate([key_rot, key_value[:, HD:]], axis=1).astype(BF16)
    slot_kv = jnp.concatenate(gather_chips(local_kv), axis=0)
    slot_kv = jnp.concatenate([slot_kv, swap_core(slot_kv)], axis=0)

    heads = wide // HD
    queries = matmul(both_normed, query_half)
    scalars = jnp.stack([own, length]).astype(jnp.int32)
    attended, lse, turned = attention_forward(
        scalars, order, queries, cosine, sine_vals, slot_kv, blk
    )

    attended, lse, turned, out_chunks, grad_far = lax.optimization_barrier(
        (attended, lse, turned, out_chunks, grad_far)
    )
    grad_mine = jnp.concatenate(list(grad_near) + ([jnp.concatenate(grad_far, axis=0)] if grad_far else []), axis=0)
    grad_other = swap_core(grad_mine)
    out_half = lay_columns(out_chunks, chip)
    branch_other = swap_core(matmul(attended[local_len:], out_half).astype(BF16))
    residual = tokens_flat + matmul(attended[:local_len], out_half) + branch_other.astype(F32)
    inverse_two = lax.rsqrt(jnp.mean(residual * residual, axis=1, keepdims=True) + EPSILON)
    unit_two = residual * inverse_two
    normed_ffn = (unit_two * gain_two).astype(BF16)
    def pair(at_place, chunk, kept):
        result = ffn_pair(
            jnp.full((1,), at_place, jnp.int32),
            chips,
            chunk,
            swap_core(chunk),
            grad_mine,
            grad_other,
            ffn_weights,
            kept,
        )
        return result[0], result[1], tuple(result[2:])

    normed_near = gather_near(normed_ffn)
    back_own, back_other, kept = pair(0, normed_near[0], ())
    back_other = swap_core(back_other)
    if chips == 4:
        normed_near = after(normed_near, back_own)
        normed_far = send_far(normed_near)
        own_first, other_first, kept = pair(1, normed_near[1], kept)
        normed_far = after(normed_far, own_first)
        own_last, other_last, kept = pair(3, jnp.concatenate(normed_far, axis=0), kept)
        last = add_cores(own_last, other_last)
        first = add_cores(own_first, other_first)
        kept = after(kept, last, first)
        passing = reduce_far(last)
        own_second, other_second, kept = pair(2, normed_near[2], kept)
        passing, own_second, other_second, kept = lax.optimization_barrier(
            (passing, own_second, other_second, kept)
        )
        first = add_half(first, passing[1], 1)
        second = add_half(add_cores(own_second, other_second), passing[0], 0)
        kept = after(kept, first, second)
        arrived = [exchange(first, "chip", 1), exchange(second, "chip", 2), back_other]
    else:
        normed_chunks = gather_far(after(normed_near, back_own))
        arrived = [back_other]
        for k in range(1, chips):
            own_term, other_term, kept = pair(k, normed_chunks[k], kept)
            arrived.append(exchange(add_cores(own_term, other_term), "chip", k))

    out_own, out_other, normed_all, grad_all, hidden_all, dgate_all, dup_all = kept
    down_term = contract_rows(hidden_all, grad_all).astype(BF16)
    out_parts = add_cores(out_own, out_other).reshape(chips, local_len, model_dim)
    gate_term = contract_rows(dgate_all, normed_all).astype(BF16)
    arrived = after(arrived, down_term, out_parts, gate_term)
    grad_normed = back_own.astype(F32)
    for term in arrived:
        grad_normed = grad_normed + term.astype(F32)
    out_parts = after(out_parts, arrived)

    def over_planes(term):
        return lax.psum_scatter(term, "fsdp", scatter_dimension=0, tiled=True)

    gate_term, down_term = over_planes(gate_term), over_planes(down_term)

    grad_gain_two = jnp.sum(grad_normed * unit_two, axis=0)
    scaled_two = grad_normed * gain_two
    grad_residual = grad_out.astype(F32) + inverse_two * (
        scaled_two - unit_two * jnp.mean(scaled_two * unit_two, axis=1, keepdims=True)
    )
    grad_branch = grad_residual.astype(BF16)
    both_branch = jnp.concatenate([grad_branch, swap_core(grad_branch)], axis=0)
    grad_attn = contract_cols(both_branch, out_half).astype(BF16)
    branch_terms = contract_rows(attended, both_branch).astype(BF16)
    branch_terms = branch_terms.reshape(planes, part, model_dim)
    grad_attn = after(grad_attn, branch_terms)
    group = heads // 2

    def backward(grads, which):
        return attention_backward(
            scalars, order, turned, grads, attended, lse, cosine, sine_vals, slot_kv, blk, group, which
        )

    def deal_rows(terms):
        terms = terms.reshape(chips, 2 * planes * (depth // places), -1)
        return lax.all_to_all(terms, "chip", 0, 0, tiled=False)

    def by_plane(dealt):
        total = jnp.sum(dealt.astype(F32), axis=0)
        return total.reshape(2, planes, depth // places, -1).swapaxes(0, 1)

    branch_dealt = lax.all_to_all(branch_terms, "chip", 0, 0, tiled=False)
    up_term = contract_rows(*after((dup_all, normed_all), branch_terms)).astype(BF16)
    if chips == 4:
        out_passing = reduce_far(out_parts[3])
    else:
        out_passing = ()
    grad_query_a, kv_terms_a = backward(after(grad_attn, up_term), 0)
    grad_query_a, kv_terms_a, out_passing, branch_dealt = lax.optimization_barrier(
        (grad_query_a, kv_terms_a, out_passing, branch_dealt)
    )
    branch_sum = jnp.sum(branch_dealt.astype(F32), axis=0)
    query_terms_a = contract_rows(both_normed, grad_query_a).astype(BF16)
    if chips == 4:
        out_near = (add_half(out_parts[1], out_passing[1], 1), add_half(out_parts[2], out_passing[0], 0))
    else:
        out_near = tuple(out_parts[k] for k in range(1, chips))
    branch_sum = branch_sum.reshape(planes, part // planes, model_dim)
    grad_query_b, kv_terms_b = backward(after(grad_attn, out_near, query_terms_a, branch_sum), 1)
    out_arrived = [exchange(term, "chip", k + 1) for k, term in enumerate(out_near)]
    grad_w_out = sum_planes(branch_sum, plane)
    query_sums_a = deal_rows(query_terms_a)
    ffn_terms = [gate_term, over_planes(up_term), down_term]
    grad_query_b, kv_terms_b, out_arrived, grad_w_out, query_sums_a, ffn_terms = lax.optimization_barrier(
        (grad_query_b, kv_terms_b, out_arrived, grad_w_out, query_sums_a, ffn_terms)
    )
    kv_terms = kv_terms_a + kv_terms_b
    kv_terms = jnp.concatenate([kv_terms[:, :HD] * LN2, kv_terms[:, HD:]], axis=1)
    kv_terms = kv_terms.reshape(2, chips * local_len, 2 * HD)
    kv_parts = add_cores(kv_terms[0], kv_terms[1]).reshape(chips, local_len, 2 * HD)
    kv_arrived = [exchange(kv_parts[k], "chip", k) for k in range(1, chips)]
    query_terms_b = contract_rows(*after((both_normed, grad_query_b), kv_parts)).astype(BF16)
    kv_arrived = after(kv_arrived, query_terms_b)
    ffn_terms = jnp.stack(ffn_terms).reshape(3, share, places, model_dim // places)
    ffn_terms = lax.all_to_all(ffn_terms, ("chip", "core"), 2, 0, tiled=False)
    kv_arrived, ffn_terms = lax.optimization_barrier((kv_arrived, ffn_terms))
    query_sums_b = deal_rows(after(query_terms_b, kv_arrived))
    kv_total = kv_parts[0].astype(F32)
    for term in kv_arrived:
        kv_total = kv_total + term.astype(F32)
    kv_total = kv_total + jnp.where(live_rows, kv_cotangent[0].astype(F32), 0.0)
    kv_low = kv_total.astype(BF16).astype(F32)
    grad_key = rotate(kv_low[:, :HD], own_cosine, -own_sine)
    grad_kv = jnp.concatenate([grad_key, kv_low[:, HD:]], axis=1).astype(BF16)
    both_grad_kv = jnp.concatenate([grad_kv, swap_core(grad_kv)], axis=0)
    kv_half = lax.dynamic_slice_in_dim(both_grad_kv, core * HD, HD, 1)
    kv_weight_half = lax.dynamic_slice_in_dim(kv_full, core * HD, HD, 1)
    both_query = jnp.concatenate([grad_query_a, grad_query_b], axis=1)

    def normed_one_term(rows):
        return contract_cols(both_query[rows], query_half) + contract_cols(kv_half[rows], kv_weight_half)

    other_one = swap_core(normed_one_term(slice(local_len, None)).astype(BF16))
    gains = jnp.pad(grad_gain_two[:, None], ((0, 0), (0, HD - 1)))
    kv_grads = jnp.concatenate([contract_rows(both_normed, kv_half), gains], axis=1).astype(BF16)
    kv_grads = kv_grads.reshape(chips, 2 * planes * (depth // places), 2 * HD)
    kv_sent = [exchange(at(kv_grads, chip ^ k), "chip", k) for k in range(1, chips)]

    query_sums_b = after(query_sums_b, kv_grads)
    query_sums = jnp.concatenate([by_plane(query_sums_a), by_plane(query_sums_b)], axis=3)
    query_sums = sum_planes(query_sums, plane)

    grad_normed_one = normed_one_term(slice(0, local_len)) + other_one.astype(F32)
    unit_one = tokens_flat * inverse_one
    scaled_one = grad_normed_one * gain_one
    grad_tokens = grad_residual + inverse_one * (
        scaled_one - unit_one * jnp.mean(scaled_one * unit_one, axis=1, keepdims=True)
    )
    grad_tokens = grad_tokens.astype(BF16)
    ffn_out = out_parts[0].astype(F32)
    for term in out_arrived:
        ffn_out = ffn_out + term.astype(F32)
    output = jnp.where(live_rows, residual + ffn_out, 0.0).astype(BF16)

    kv_sent = after(kv_sent, grad_tokens)
    kv_sums = at(kv_grads, chip).astype(F32)
    for term in kv_sent:
        kv_sums = kv_sums + term.astype(F32)
    kv_sums = kv_sums.reshape(2, planes, depth // places, 2 * HD).swapaxes(0, 1)
    kv_sums = sum_planes(kv_sums, plane)

    rows = depth // places
    own_rows = [((chip * 2 + j) * planes + plane) * rows for j in range(2)]
    gain_sums = jnp.stack(
        [
            jnp.sum(lax.dynamic_slice_in_dim(query_half, row, rows, 0).astype(F32) * query_sums[j], axis=1)
            + jnp.sum(
                lax.dynamic_slice_in_dim(kv_weight_half, row, rows, 0).astype(F32) * kv_sums[j, :, :HD],
                axis=1,
            )
            for j, row in enumerate(own_rows)
        ]
    )
    kv_sums = lax.dynamic_update_slice(kv_sums, gain_sums[:, :, None], (0, 0, HD + 1))

    def by_core(sums):
        kept, other = at(sums, core), swap_core(at(sums, core ^ 1))
        return jnp.where(core == 0, kept, other), jnp.where(core == 0, other, kept)

    first, second = by_core(query_sums)
    grad_w_query = jnp.stack(
        [first.reshape(rows, planes, part), second.reshape(rows, planes, part)], axis=2
    ).reshape(rows, model_dim)
    first, second = by_core(kv_sums)
    grad_w_kv = jnp.concatenate([first[:, :HD], second[:, :HD]], axis=1)
    gain_sums = first[:, HD : HD + 2] + second[:, HD : HD + 2]
    grad_gain_two = gain_sums[:, 0]
    grad_gain_one = gain_sums[:, 1] / lax.dynamic_slice_in_dim(gain_one, (own * planes + plane) * rows, rows, 0)
    ffn_grads = ffn_terms.transpose(1, 3, 0, 2).reshape(3, model_dim // places, places * share)
    ffn_grads = ffn_grads.astype(F32)
    return (
        output[None],
        grad_tokens.astype(BF16)[None],
        grad_w_query,
        grad_w_kv,
        grad_w_out,
        grad_gain_one,
        grad_gain_two,
        ffn_grads[0],
        ffn_grads[1],
        ffn_grads[2],
    )


def solution(mesh):
    ctx, planes = mesh.shape["ctx"], mesh.shape["fsdp"]
    split = Mesh(mesh.devices.reshape(ctx // 2, 2, planes), ("chip", "core", "fsdp"))
    ctx_axes = ("chip", "core")
    return jax.shard_map(
        shards,
        mesh=split,
        in_specs=(
            P("fsdp", ctx_axes, None),
            P("fsdp", ctx_axes, None),
            P("fsdp", ctx_axes, None),
            P("fsdp"),
            P("fsdp", None),
            P("fsdp", None),
            P("fsdp", None),
            P("fsdp", None),
            P("fsdp"),
            P("fsdp"),
            P(None, "fsdp"),
            P(None, "fsdp"),
            P(None, "fsdp"),
        ),
        out_specs=(
            P("fsdp", ctx_axes, None),
            P("fsdp", ctx_axes, None),
            P(("chip", "core", "fsdp"), None),
            P(("chip", "core", "fsdp"), None),
            P(("chip", "core", "fsdp"), None),
            P(("chip", "core", "fsdp")),
            P(("chip", "core", "fsdp")),
            P(ctx_axes, "fsdp"),
            P(ctx_axes, "fsdp"),
            P(ctx_axes, "fsdp"),
        ),
        check_vma=False,
    )
```

time: 1040 us -> 824 us (0.79)
  matrix products: 287 us -> 106 us
  waiting for transfers between devices: 316 us -> 225 us
  Pallas kernels: 83.4 us -> 173 us
  local copies, waits for them, and re-layouts: 128 us -> 98.7 us
  other arithmetic: 74.3 us -> 102 us
  blocking collectives: 18.6 us -> 0 us
    pallas_call x1 -> x5, Pallas kernels: 32.3 us -> 142 us  [the longest x4 129 us: ffn_pair(): pl.pallas_call(functools.partial(ffn_rows, count, tiles), grid_spec=pltpu...]
    ppermute x88 -> x65, waiting for transfers between devices: 316 us -> 207 us  [exchange(): return lax.ppermute(value, axis, [(i, i ^ distance) for i in range(size)])]
    dot_general x29 -> x5, matrix products: 123 us -> 19.3 us  [contract_cols(): lax.dot_general(left, right, (((1,), (1,)), ((), ())), preferred_element_...]
    dot_general x28 -> x4, matrix products: 101 us -> 12.3 us  [matmul(): return jnp.dot(left, right, preferred_element_type=F32)]
    unnamed x263 -> x203, local copies, waits for them, and re-layouts: 71.8 us -> 46.9 us
    convert_element_type x3 -> x8, other arithmetic: 2.53 us -> 24.3 us  [the longest x5 16.5 us: add_cores(): (terms.astype(F32) + swap_core(terms_of_other.astype(BF16)).astype(F32))....]
    ppermute x88 -> x65, starting transfers between devices: 97.7 us -> 76.8 us  [exchange(): return lax.ppermute(value, axis, [(i, i ^ distance) for i in range(size)])]
    pallas_call x1 -> x2, Pallas kernels: 51.1 us -> 31.1 us  [attention_backward(): pl.pallas_call(functools.partial(attend_backward, group, blk), grid_spec=...]
  transfers between devices with their start and end apart: 97 -> 74, of which waited for: 23 -> 28; matrix products, arithmetic and copies ran while one was open for 45% -> 32% of each run, Pallas kernels for 8% -> 17%
where the time goes in v2:
time: 824 us; the launch traced here: 816 us
  waiting for transfers between devices  225 us (27%)
  Pallas kernels  173 us (21%)
  matrix products  106 us (13%)
  other arithmetic  102 us (12%)
  local copies, waits for them, and re-layouts  98.7 us (12%)
  starting transfers between devices  95.5 us (12%)
  between operations  16.5 us (2%)
    ppermute x65, waiting for transfers between devices, exchange(): return lax.ppermute(value, axis, [(i, i ^ distance) for i in range(size)])  207 us
    pallas_call x4, Pallas kernels, ffn_pair(): pl.pallas_call(functools.partial(ffn_rows, count, tiles), grid_spec=pltpu...  129 us
    ppermute x65, starting transfers between devices, exchange(): return lax.ppermute(value, axis, [(i, i ^ distance) for i in range(size)])  76.8 us
    dot_general x7, matrix products, contract_rows(): lax.dot_general(left, right, (((0,), (0,)), ((), ())), preferred_element_...  74.5 us
    unnamed x203, local copies, waits for them, and re-layouts  46.9 us
    pallas_call x2, Pallas kernels, attention_backward(): pl.pallas_call(functools.partial(attend_backward, group, blk), grid_spec=...  31.1 us
    dot_general x5, matrix products, contract_cols(): lax.dot_general(left, right, (((1,), (1,)), ((), ())), preferred_element_...  19.3 us
    all_to_all x2, waiting for transfers between devices, deal_rows(): return lax.all_to_all(terms, 'chip', 0, 0, tiled=False)  16.9 us
  transfers between devices with their start and end apart: 74, of which 28 were waited for; matrix products, arithmetic and copies ran while one was open for 32% of the time, Pallas kernels for 17%

profile of v2, /device:TPU:0, one launch (start us, length us, event | category | flops | bytes accessed | tf_op | source)
XLA Modules:
  0.0 816.1 jit_solution(13541588992682626194)
XLA Ops:
  15.2 3.1 bitcast_select_fusion
  18.3 2.9 collective-permute-start.5
  22.8 4.1 constant_dynamic-slice_fusion.1
  35.4 2.9 pad_maximum_fusion.4
  38.8 3.0 multiply_sine_fusion
  43.5 23.7 %collective-permute-done.5 = bf16[512,2048]{1,0:T(8,128)(2,1)} collective-permute-done((bf16[512,2048]{1,0:T(8,128)(2,1)}, bf16[512,2048]{1,0:T(8,128)(2,1)}, u32[]{:S(2)}, u32[]{:S(2)}) %collective-permute-start.5) | collective-permute-done | bytes 2097184 | tf_op jit(solution)/shard_map/ppermute | solution.py:364
  70.9 3.2 constant_dynamic-update-slice_fusion.17
  78.0 4.3 fusion.2
  96.1 3.7 collective-permute-done.11
  103.9 18.3 %collective-permute-done.13 = bf16[256,256]{1,0:T(8,128)(2,1)S(1)} collective-permute-done((bf16[256,256]{1,0:T(8,128)(2,1)S(1)}, bf16[256,256]{1,0:T(8,128)(2,1)S(1)}, u32[]{:S(2)}, u32[]{:S(2)}) %collective-permute-start.13) | collective-permute-done | bytes 131104 | tf_op jit(solution)/shard_map/ppermute | solution.py:364
  123.5 3.2 constant_dynamic-update-slice_fusion.16
  126.7 3.2 constant_dynamic-update-slice_fusion.15
  142.5 7.0 collective-permute-done.10
  160.0 4.5 fusion.106.q_ref
  164.5 13.0 %attend_forward.1 = (bf16[1024,1024]{1,0:T(8,128)(2,1)S(1)}, f32[4,1,2048]{2,1,0:T(1,128)S(1)}, bf16[4,128,2048]{2,1,0:T(8,128)(2,1)S(1)}) custom-call(s32[2]{0:T(128)S(1)} %pad_add_fusion.scal_ref, s32[16]{0:T(128)S(1)} %bitcast.271, f32[1024,1024]{1,0:T(8,128)S(1)} %fusion.106.q_ref, f32[64,1024]{1,0:T(8,128)S(1)} %copy.130.cos_ref, ...), custom_call_target="tpu_custom_call" | custom-call | flops 1048576 | bytes 65536 | tf_op jit(solution)/shard_map/attend_forward/pallas_call | solution.py:110
  180.2 41.7 %collective-permute-done.19 = bf16[256,2048]{1,0:T(8,128)(2,1)S(1)} collective-permute-done((bf16[256,2048]{1,0:T(8,128)(2,1)S(1)}, bf16[256,2048]{1,0:T(8,128)(2,1)S(1)}, u32[]{:S(2)}, u32[]{:S(2)}) %collective-permute-start.19) | collective-permute-done | bytes 1048608 | tf_op jit(solution)/shard_map/ppermute | solution.py:364
  230.7 10.7 %collective-permute-done.21 = bf16[512,2048]{1,0:T(8,128)(2,1)S(1)} collective-permute-done((bf16[512,2048]{1,0:T(8,128)(2,1)S(1)}, bf16[512,2048]{1,0:T(8,128)(2,1)S(1)}, u32[]{:S(2)}, u32[]{:S(2)}) %collective-permute-start.21) | collective-permute-done | bytes 2097184 | tf_op jit(solution)/shard_map/ppermute | solution.py:364
  241.4 4.7 multiply_reduce_fusion.2
  253.2 32.4 %ffn_pair.4 = (bf16[512,2048]{1,0:T(8,128)(2,1)}, bf16[512,2048]{1,0:T(8,128)(2,1)}, bf16[2048,2048]{1,0:T(8,128)(2,1)}, bf16[2048,2048]{1,0:T(8,128)(2,1)}, bf1...) custom-call(s32[1]{0:T(128)} %constant.163.clone.1.place_ref, ...), custom_call_target="tpu_custom_call" | custom-call | flops 1048576 | bytes 65536 | tf_op jit(solution)/shard_map/ffn_pair/pallas_call | solution.py:308
  285.6 11.4 %collective-permute-done.22.xa_ref = bf16[512,2048]{1,0:T(8,128)(2,1)} collective-permute-done((bf16[512,2048]{1,0:T(8,128)(2,1)S(1)}, bf16[512,2048]{1,0:T(8,128)(2,1)}, u32[]{:S(2)}, u32[]{:S(2)}) %collective-permute-start.22) | collective-permute-done | bytes 2097184 | tf_op jit(solution)/shard_map/ppermute | solution.py:364
  304.0 31.9 %ffn_pair.5 = (bf16[512,2048]{1,0:T(8,128)(2,1)}, bf16[512,2048]{1,0:T(8,128)(2,1)}, bf16[2048,2048]{1,0:T(8,128)(2,1)}, bf16[2048,2048]{1,0:T(8,128)(2,1)}, bf1...) custom-call(s32[1]{0:T(128)} %constant.164.clone.1.place_ref, ...), custom_call_target="tpu_custom_call", output_to_operand_aliasing={{2}: (8, {}), {3}: (9, {}), {4}: (10, {}), {5}: (11, {}), {... | custom-call | flops 1048576 | bytes 65536 | tf_op jit(solution)/shard_map/ffn_pair/pallas_call | solution.py:308
  336.3 4.1 collective-permute-done.29.xb_ref
  341.8 32.2 %ffn_pair.6 = (bf16[512,2048]{1,0:T(8,128)(2,1)}, bf16[512,2048]{1,0:T(8,128)(2,1)}, bf16[2048,2048]{1,0:T(8,128)(2,1)}, bf16[2048,2048]{1,0:T(8,128)(2,1)}, bf1...) custom-call(s32[1]{0:T(128)} %constant.162.clone.1.place_ref, ...), custom_call_target="tpu_custom_call", output_to_operand_aliasing={{2}: (8, {}), {3}: (9, {}), {4}: (10, {}), {5}: (11, {}), {... | custom-call | flops 1048576 | bytes 65536 | tf_op jit(solution)/shard_map/ffn_pair/pallas_call | solution.py:308
  374.6 3.7 collective-permute-done.30
  386.9 32.1 %ffn_pair.7 = (bf16[512,2048]{1,0:T(8,128)(2,1)}, bf16[512,2048]{1,0:T(8,128)(2,1)}, bf16[2048,2048]{1,0:T(8,128)(2,1)}, bf16[2048,2048]{1,0:T(8,128)(2,1)}, bf1...) custom-call(s32[1]{0:T(128)} %constant.165.clone.1.place_ref, ...), custom_call_target="tpu_custom_call", output_to_operand_aliasing={{2}: (8, {}), {3}: (9, {}), {4}: (10, {}), {5}: (11, {}), {... | custom-call | flops 1048576 | bytes 65536 | tf_op jit(solution)/shard_map/ffn_pair/pallas_call | solution.py:308
  428.6 16.6 %convolution_convert_fusion.2 = bf16[704,2048]{1,0:T(8,128)(2,1)} fusion(bf16[4096,704]{1,0:T(8,128)(2,1)} %get-tuple-element.214, bf16[4096,2048]{1,0:T(8,128)(2,1)S(1)} %copy-done.16), kind=kOutput, calls=%fused_computation.50 | convolution fusion | flops 11812601856 | bytes 25427968 | tf_op jit(solution)/shard_map/dot_general | solution.py:351
  445.3 19.1 %convolution_convert_fusion.3 = bf16[704,2048]{1,0:T(8,128)(2,1)} fusion(bf16[4096,704]{1,0:T(8,128)(2,1)} %get-tuple-element.212, bf16[4096,2048]{1,0:T(8,128)(2,1)} %get-tuple-element.213), kind=kOutput, calls=%fused_computation.51 | convolution fusion | flops 11812601856 | bytes 25427968 | tf_op jit(solution)/shard_map/dot_general | solution.py:351
  464.4 10.7 %add_convert_fusion = bf16[2048,2048]{1,0:T(8,128)(2,1)} fusion(bf16[2048,2048]{1,0:T(8,128)(2,1)} %collective-permute-done.36, bf16[2048,2048]{1,0:T(8,128)(2,1)} %get-tuple-element.209), kind=kLoop, calls=%fused_computation | loop fusion | flops 16777216 | bytes 25165824 | tf_op jit(solution)/shard_map/convert_element_type | solution.py:399
  475.2 5.3 multiply_reduce_fusion
  480.5 7.5 fusion.99
  488.3 4.2 collective-permute-done.40
  492.5 8.4 %convolution_convert_fusion = bf16[1024,2048]{1,0:T(8,128)(2,1)} fusion(bf16[1024,1024]{1,0:T(8,128)(2,1)S(1)} %copy-done.5, bf16[512,2048]{1,0:T(8,128)(2,1)} %collective-permute-done.40, bf16[512,2048]{1,0:T(8,128)(2,1)} %get-tuple-element.300), kind=kOutput, calls=%fused_computation.40 | convolution fusion | flops 4305453056 | bytes 10485760 | tf_op jit(solution)/shard_map/dot_general | solution.py:351
  500.8 4.9 all-to-all-start
  505.8 19.4 %convolution_convert_fusion.1 = bf16[704,2048]{1,0:T(8,128)(2,1)} fusion(bf16[4096,704]{1,0:T(8,128)(2,1)} %get-tuple-element.223, bf16[4096,2048]{1,0:T(8,128)(2,1)} %get-tuple-element.224), kind=kOutput, calls=%fused_computation.49 | convolution fusion | flops 11812601856 | bytes 25427968 | tf_op jit(solution)/shard_map/dot_general | solution.py:351
  525.2 4.1 slice_bitcast_fusion
  532.7 7.0 fusion.25.g_ref
  539.7 15.7 %attend_backward.2 = (bf16[1024,512]{1,0:T(8,128)(2,1)S(1)}, f32[4096,256]{1,0:T(8,128)}) custom-call(s32[2]{0:T(128)S(1)} %pad_add_fusion.scal_ref, s32[16]{0:T(128)S(1)} %bitcast.272, bf16[4,128,2048]{2,1,0:T(8,128)(2,1)S(1)} %copy-done.7, bf16[1024,1024]{1,0:T(8,128)(2,1)S(1)} %fusion.25.g_ref, bf16[1024,1024]{1,0:T(8,128)(2,1)} %copy-done.3, ...), custom_call_target="tpu_custom_call" | custom-call | flops 1048576 | bytes 65536 | tf_op jit(solution)/shard_map/attend_backward/pallas_call | solution.py:213
  556.4 19.8 %collective-permute-done.41 = bf16[256,2048]{1,0:T(8,128)(2,1)S(1)} collective-permute-done((bf16[256,2048]{1,0:T(8,128)(2,1)S(1)}, bf16[256,2048]{1,0:T(8,128)(2,1)S(1)}, u32[]{:S(2)}, u32[]{:S(2)}) %collective-permute-start.41) | collective-permute-done | bytes 1048608 | tf_op jit(solution)/shard_map/ppermute | solution.py:364
  577.2 3.2 fusion.23
  585.7 3.7 convolution_convert_fusion.5
  589.4 4.5 all-to-all-start.1
  593.9 3.3 convert_reduce_fusion
  600.6 7.2 collective-permute-start.46
  612.0 15.4 %attend_backward.3 = (bf16[1024,512]{1,0:T(8,128)(2,1)S(1)}, f32[4096,256]{1,0:T(8,128)}) custom-call(s32[2]{0:T(128)S(1)} %pad_add_fusion.scal_ref, s32[16]{0:T(128)S(1)} %bitcast.273, bf16[4,128,2048]{2,1,0:T(8,128)(2,1)S(1)} %copy-done.7, bf16[1024,1024]{1,0:T(8,128)(2,1)S(1)} %copy-done.9, bf16[1024,1024]{1,0:T(8,128)(2,1)} %copy-done.3, ...), custom_call_target="tpu_custom_call" | custom-call | flops 1048576 | bytes 65536 | tf_op jit(solution)/shard_map/attend_backward/pallas_call | solution.py:213
  628.4 7.6 collective-permute-done.47
  638.2 16.5 %all-to-all-done.1 = bf16[4,512,512]{2,1,0:T(8,128)(2,1)} async-done(((bf16[4,512,512]{2,1,0:T(8,128)(2,1)}), bf16[4,512,512]{2,1,0:T(8,128)(2,1)}, u32[]{:S(2)}, u32[]{:S(2)}) %all-to-all-start.1) | async-done | bytes 2097184 | tf_op jit(solution)/shard_map/all_to_all | solution.py:626
  654.8 4.0 add.410
  664.8 4.5 all-to-all-start.2
  669.3 7.2 fusion.16
  682.8 3.8 convolution_convert_fusion.4
  686.6 15.2 %collective-permute-done.49 = bf16[512,256]{1,0:T(8,128)(2,1)S(1)} collective-permute-done((bf16[512,256]{1,0:T(8,128)(2,1)S(1)}, bf16[512,256]{1,0:T(8,128)(2,1)S(1)}, u32[]{:S(2)}, u32[]{:S(2)}) %collective-permute-start.49) | collective-permute-done | bytes 262176 | tf_op jit(solution)/shard_map/ppermute | solution.py:364
  701.8 6.1 collective-permute-done.51
  717.5 4.5 all-to-all-start.3
  726.0 4.9 add_convert_fusion.1
  734.0 2.9 copy.147
  736.9 2.9 copy.148
  741.3 3.5 convolution_convert_fusion.7
  751.9 7.0 collective-permute-start.55
  762.6 4.5 collective-permute-done.55
  768.6 8.9 %collective-permute-done.56 = bf16[2,64,1024]{2,1,0:T(8,128)(2,1)S(1)} collective-permute-done((bf16[2,64,1024]{2,1,0:T(8,128)(2,1)S(1)}, bf16[2,64,1024]{2,1,0:T(8,128)(2,1)S(1)}, u32[]{:S(2)}, u32[]{:S(2)}) %collective-permute-start.56) | collective-permute-done | bytes 262176 | tf_op jit(solution)/shard_map/ppermute | solution.py:364
  777.9 4.9 fusion.5
  782.8 5.1 fusion.9
  789.1 5.2 collective-permute-start.61
  799.5 3.6 collective-permute-done.63
  (451 shorter events, 191.6 us)
Async XLA Ops:
  7.2 66.9 %all-gather.8.cloned.1.call-start = ((), (), s32[]{:S(2)}) async-start(), calls=%async_computation.11 | async-start | bytes 2969600 | tf_op jit(solution)/shard_map/all_gather | solution.py:480
  13.7 239.5 %all-gather.6.cloned.1.call-start = ((), (), s32[]{:S(2)}) async-start(), calls=%async_computation.10 | async-start | bytes 10813440 | tf_op jit(solution)/shard_map/all_gather | solution.py:490
  18.3 48.9 %collective-permute-start.5 = (bf16[512,2048]{1,0:T(8,128)(2,1)}, bf16[512,2048]{1,0:T(8,128)(2,1)}, u32[]{:S(2)}, u32[]{:S(2)}) collective-permute-start(bf16[512,2048]{1,0:T(8,128)(2,1)} %bitcast_select_fusion), channel_id=1, source_target_pairs={{0,8},{8,0},{16,24},{24,16},{1,9},{9,1},{17,25},{25,17},{2,10},{10... | collective-permute-start | bytes 6291464 | tf_op jit(solution)/shard_map/ppermute | solution.py:364
  21.3 47.4 %collective-permute-start.6 = (bf16[512,2048]{1,0:T(8,128)(2,1)}, bf16[512,2048]{1,0:T(8,128)(2,1)}, u32[]{:S(2)}, u32[]{:S(2)}) collective-permute-start(bf16[512,2048]{1,0:T(8,128)(2,1)} %bitcast_select_fusion), channel_id=1, source_target_pairs={{0,16},{8,24},{16,0},{24,8},{1,17},{9,25},{17,1},{25,9},{2,18},{10... | collective-permute-start | bytes 6291464 | tf_op jit(solution)/shard_map/ppermute | solution.py:364
  22.8 45.9 %collective-permute-start = (bf16[512,2048]{1,0:T(8,128)(2,1)S(1)}, bf16[512,2048]{1,0:T(8,128)(2,1)}, u32[]{:S(2)}, u32[]{:S(2)}) collective-permute-start(bf16[512,2048]{1,0:T(8,128)(2,1)S(1)} %bitcast.289), channel_id=1, source_target_pairs={{0,4},{4,0},{1,5},{5,1},{2,6},{6,2},{3,7},{7,3},{8,12},{12,8},{9,1... | collective-permute-start | bytes 6291464 | tf_op jit(solution)/shard_map/ppermute | solution.py:364
  38.3 599.9 %reduce-scatter.4.cloned.1.call-start = ((), (), s32[]{:S(2)}) async-start(), calls=%async_computation.7 | async-start | bytes 3604480 | tf_op jit(solution)/shard_map/reduce_scatter | solution.py:602
  75.1 7.4 collective-permute-start.1
  75.5 8.1 collective-permute-start.2
  90.5 9.2 %collective-permute-start.11 = (bf16[512,256]{1,0:T(8,128)(2,1)S(1)}, bf16[512,256]{1,0:T(8,128)(2,1)S(1)}, u32[]{:S(2)}, u32[]{:S(2)}) collective-permute-start(bf16[512,256]{1,0:T(8,128)(2,1)S(1)} %get-tuple-element.303), channel_id=1, source_target_pairs={{0,8},{8,0},{16,24},{24,16},{1,9},{9,1},{17,25},{25,17},{2,10},{10... | collective-permute-start | bytes 786440 | tf_op jit(solution)/shard_map/ppermute | solution.py:364
  91.5 9.2 %collective-permute-start.12 = (bf16[512,256]{1,0:T(8,128)(2,1)S(1)}, bf16[512,256]{1,0:T(8,128)(2,1)S(1)}, u32[]{:S(2)}, u32[]{:S(2)}) collective-permute-start(bf16[512,256]{1,0:T(8,128)(2,1)S(1)} %get-tuple-element.303), channel_id=1, source_target_pairs={{0,16},{8,24},{16,0},{24,8},{1,17},{9,25},{17,1},{25,9},{2,18},{10... | collective-permute-start | bytes 786440 | tf_op jit(solution)/shard_map/ppermute | solution.py:364
  94.5 42.1 %collective-permute-start.7 = (bf16[2048,256]{1,0:T(8,128)(2,1)}, bf16[2048,256]{1,0:T(8,128)(2,1)}, u32[]{:S(2)}, u32[]{:S(2)}) collective-permute-start(bf16[2048,256]{1,0:T(8,128)(2,1)} %bitcast.6), channel_id=1, source_target_pairs={{0,8},{8,0},{16,24},{24,16},{1,9},{9,1},{17,25},{25,17},{2,10},{10... | collective-permute-start | bytes 3145736 | tf_op jit(solution)/shard_map/ppermute | solution.py:364
  95.0 39.0 %collective-permute-start.8 = (bf16[2048,256]{1,0:T(8,128)(2,1)}, bf16[2048,256]{1,0:T(8,128)(2,1)}, u32[]{:S(2)}, u32[]{:S(2)}) collective-permute-start(bf16[2048,256]{1,0:T(8,128)(2,1)} %bitcast.6), channel_id=1, source_target_pairs={{0,16},{8,24},{16,0},{24,8},{1,17},{9,25},{17,1},{25,9},{2,18},{10... | collective-permute-start | bytes 3145736 | tf_op jit(solution)/shard_map/ppermute | solution.py:364
  99.7 22.4 %collective-permute-start.13 = (bf16[256,256]{1,0:T(8,128)(2,1)S(1)}, bf16[256,256]{1,0:T(8,128)(2,1)S(1)}, u32[]{:S(2)}, u32[]{:S(2)}) collective-permute-start(bf16[256,256]{1,0:T(8,128)(2,1)S(1)} %slice.290), channel_id=1, source_target_pairs={{0,16},{8,24},{16,0},{24,8},{1,17},{9,25},{17,1},{25,9},{2,18},{10... | collective-permute-start | bytes 393224 | tf_op jit(solution)/shard_map/ppermute | solution.py:364
  100.8 22.1 %collective-permute-start.14 = (bf16[256,256]{1,0:T(8,128)(2,1)S(1)}, bf16[256,256]{1,0:T(8,128)(2,1)S(1)}, u32[]{:S(2)}, u32[]{:S(2)}) collective-permute-start(bf16[256,256]{1,0:T(8,128)(2,1)S(1)} %slice.291), channel_id=1, source_target_pairs={{0,8},{8,0},{16,24},{24,16},{1,9},{9,1},{17,25},{25,17},{2,10},{10... | collective-permute-start | bytes 393224 | tf_op jit(solution)/shard_map/ppermute | solution.py:364
  123.5 17.5 %collective-permute-start.15 = (bf16[2048,256]{1,0:T(8,128)(2,1)}, bf16[2048,256]{1,0:T(8,128)(2,1)}, u32[]{:S(2)}, u32[]{:S(2)}) collective-permute-start(bf16[2048,256]{1,0:T(8,128)(2,1)} %get-tuple-element.352), channel_id=1, source_target_pairs={{0,4},{4,0},{1,5},{5,1},{2,6},{6,2},{3,7},{7,3},{8,12},{12,8},{9,1... | collective-permute-start | bytes 3145736 | tf_op jit(solution)/shard_map/ppermute | solution.py:364
  135.1 14.4 %collective-permute-start.10 = (bf16[1024,256]{1,0:T(8,128)(2,1)S(1)}, bf16[1024,256]{1,0:T(8,128)(2,1)S(1)}, u32[]{:S(2)}, u32[]{:S(2)}) collective-permute-start(bf16[1024,256]{1,0:T(8,128)(2,1)S(1)} %slice.283), channel_id=1, source_target_pairs={{0,8},{8,0},{16,24},{24,16},{1,9},{9,1},{17,25},{25,17},{2,10},{10... | collective-permute-start | bytes 1572872 | tf_op jit(solution)/shard_map/ppermute | solution.py:364
  137.7 14.1 %collective-permute-start.9 = (bf16[1024,256]{1,0:T(8,128)(2,1)S(1)}, bf16[1024,256]{1,0:T(8,128)(2,1)S(1)}, u32[]{:S(2)}, u32[]{:S(2)}) collective-permute-start(bf16[1024,256]{1,0:T(8,128)(2,1)S(1)} %slice.282), channel_id=1, source_target_pairs={{0,16},{8,24},{16,0},{24,8},{1,17},{9,25},{17,1},{25,9},{2,18},{10... | collective-permute-start | bytes 1572872 | tf_op jit(solution)/shard_map/ppermute | solution.py:364
  152.0 69.9 %collective-permute-start.16 = (bf16[1024,512]{1,0:T(8,128)(2,1)S(1)}, bf16[1024,512]{1,0:T(8,128)(2,1)S(1)}, u32[]{:S(2)}, u32[]{:S(2)}) collective-permute-start(bf16[1024,512]{1,0:T(8,128)(2,1)S(1)} %copy-done.37), channel_id=1, source_target_pairs={{0,8},{8,0},{16,24},{24,16},{1,9},{9,1},{17,25},{25,17},{2,10},{10... | collective-permute-start | bytes 3145736 | tf_op jit(solution)/shard_map/ppermute | solution.py:364
  152.6 69.2 %collective-permute-start.17 = (bf16[1024,512]{1,0:T(8,128)(2,1)S(1)}, bf16[1024,512]{1,0:T(8,128)(2,1)S(1)}, u32[]{:S(2)}, u32[]{:S(2)}) collective-permute-start(bf16[1024,512]{1,0:T(8,128)(2,1)S(1)} %copy-done.37), channel_id=1, source_target_pairs={{0,16},{8,24},{16,0},{24,8},{1,17},{9,25},{17,1},{25,9},{2,18},{10... | collective-permute-start | bytes 3145736 | tf_op jit(solution)/shard_map/ppermute | solution.py:364
  153.7 68.2 %collective-permute-start.18 = (bf16[1024,512]{1,0:T(8,128)(2,1)S(1)}, bf16[1024,512]{1,0:T(8,128)(2,1)S(1)}, u32[]{:S(2)}, u32[]{:S(2)}) collective-permute-start(bf16[1024,512]{1,0:T(8,128)(2,1)S(1)} %copy-done.37), channel_id=1, source_target_pairs={{0,24},{8,16},{16,8},{24,0},{1,25},{9,17},{17,9},{25,1},{2,26},{10... | collective-permute-start | bytes 3145736 | tf_op jit(solution)/shard_map/ppermute | solution.py:364
  156.8 65.0 %collective-permute-start.19 = (bf16[256,2048]{1,0:T(8,128)(2,1)S(1)}, bf16[256,2048]{1,0:T(8,128)(2,1)S(1)}, u32[]{:S(2)}, u32[]{:S(2)}) collective-permute-start(bf16[256,2048]{1,0:T(8,128)(2,1)S(1)} %slice.230), channel_id=1, source_target_pairs={{0,16},{8,24},{16,0},{24,8},{1,17},{9,25},{17,1},{25,9},{2,18},{10... | collective-permute-start | bytes 3145736 | tf_op jit(solution)/shard_map/ppermute | solution.py:364
  158.7 63.1 %collective-permute-start.20 = (bf16[256,2048]{1,0:T(8,128)(2,1)S(1)}, bf16[256,2048]{1,0:T(8,128)(2,1)S(1)}, u32[]{:S(2)}, u32[]{:S(2)}) collective-permute-start(bf16[256,2048]{1,0:T(8,128)(2,1)S(1)} %slice.231), channel_id=1, source_target_pairs={{0,8},{8,0},{16,24},{24,16},{1,9},{9,1},{17,25},{25,17},{2,10},{10... | collective-permute-start | bytes 3145736 | tf_op jit(solution)/shard_map/ppermute | solution.py:364
  225.3 27.9 %collective-permute-start.25 = (bf16[2048,2048]{1,0:T(8,128)(2,1)}, bf16[2048,2048]{1,0:T(8,128)(2,1)}, u32[]{:S(2)}, u32[]{:S(2)}) collective-permute-start(bf16[2048,2048]{1,0:T(8,128)(2,1)} %constant_dynamic-update-slice_fusion.13.ga_ref), channel_id=1, source_target_pairs={{0,4},{4,0},{1,5},{5,1},{2,6},{6,2},{3,7},{7,3},{8,12},{12,8},{9,1... | collective-permute-start | bytes 25165832 | tf_op jit(solution)/shard_map/ppermute | solution.py:364
  230.2 11.3 %collective-permute-start.21 = (bf16[512,2048]{1,0:T(8,128)(2,1)S(1)}, bf16[512,2048]{1,0:T(8,128)(2,1)S(1)}, u32[]{:S(2)}, u32[]{:S(2)}) collective-permute-start(bf16[512,2048]{1,0:T(8,128)(2,1)S(1)} %convolution_convert_fusion.6), channel_id=1, source_target_pairs={{0,4},{4,0},{1,5},{5,1},{2,6},{6,2},{3,7},{7,3},{8,12},{12,8},{9,1... | collective-permute-start | bytes 6291464 | tf_op jit(solution)/shard_map/ppermute | solution.py:364
  249.0 48.0 %collective-permute-start.22 = (bf16[512,2048]{1,0:T(8,128)(2,1)S(1)}, bf16[512,2048]{1,0:T(8,128)(2,1)}, u32[]{:S(2)}, u32[]{:S(2)}) collective-permute-start(bf16[512,2048]{1,0:T(8,128)(2,1)S(1)} %multiply_convert_fusion.xa_ref), channel_id=1, source_target_pairs={{0,8},{8,0},{16,24},{24,16},{1,9},{9,1},{17,25},{25,17},{2,10},{10... | collective-permute-start | bytes 6291464 | tf_op jit(solution)/shard_map/ppermute | solution.py:364
  250.5 47.7 %collective-permute-start.23 = (bf16[512,2048]{1,0:T(8,128)(2,1)S(1)}, bf16[512,2048]{1,0:T(8,128)(2,1)}, u32[]{:S(2)}, u32[]{:S(2)}) collective-permute-start(bf16[512,2048]{1,0:T(8,128)(2,1)S(1)} %multiply_convert_fusion.xa_ref), channel_id=1, source_target_pairs={{0,16},{8,24},{16,0},{24,8},{1,17},{9,25},{17,1},{25,9},{2,18},{10... | collective-permute-start | bytes 6291464 | tf_op jit(solution)/shard_map/ppermute | solution.py:364
  299.5 36.4 %collective-permute-start.26 = (bf16[256,2048]{1,0:T(8,128)(2,1)S(1)}, bf16[256,2048]{1,0:T(8,128)(2,1)S(1)}, u32[]{:S(2)}, u32[]{:S(2)}) collective-permute-start(bf16[256,2048]{1,0:T(8,128)(2,1)S(1)} %slice.234), channel_id=1, source_target_pairs={{0,16},{8,24},{16,0},{24,8},{1,17},{9,25},{17,1},{25,9},{2,18},{10... | collective-permute-start | bytes 3145736 | tf_op jit(solution)/shard_map/ppermute | solution.py:364
  301.4 34.5 %collective-permute-start.27 = (bf16[256,2048]{1,0:T(8,128)(2,1)S(1)}, bf16[256,2048]{1,0:T(8,128)(2,1)S(1)}, u32[]{:S(2)}, u32[]{:S(2)}) collective-permute-start(bf16[256,2048]{1,0:T(8,128)(2,1)S(1)} %slice.235), channel_id=1, source_target_pairs={{0,8},{8,0},{16,24},{24,16},{1,9},{9,1},{17,25},{25,17},{2,10},{10... | collective-permute-start | bytes 3145736 | tf_op jit(solution)/shard_map/ppermute | solution.py:364
  374.1 10.6 %collective-permute-start.34 = (bf16[512,2048]{1,0:T(8,128)(2,1)}, bf16[512,2048]{1,0:T(8,128)(2,1)S(1)}, u32[]{:S(2)}, u32[]{:S(2)}) collective-permute-start(bf16[512,2048]{1,0:T(8,128)(2,1)} %get-tuple-element.181), channel_id=1, source_target_pairs={{0,4},{4,0},{1,5},{5,1},{2,6},{6,2},{3,7},{7,3},{8,12},{12,8},{9,1... | collective-permute-start | bytes 6291464 | tf_op jit(solution)/shard_map/ppermute | solution.py:364
  374.5 11.1 %collective-permute-start.33 = (bf16[512,2048]{1,0:T(8,128)(2,1)}, bf16[512,2048]{1,0:T(8,128)(2,1)S(1)}, u32[]{:S(2)}, u32[]{:S(2)}) collective-permute-start(bf16[512,2048]{1,0:T(8,128)(2,1)} %collective-permute-done.23.xa_ref), channel_id=1, source_target_pairs={{0,4},{4,0},{1,5},{5,1},{2,6},{6,2},{3,7},{7,3},{8,12},{12,8},{9,1... | collective-permute-start | bytes 6291464 | tf_op jit(solution)/shard_map/ppermute | solution.py:364
  382.3 36.7 %collective-permute-start.31 = (bf16[256,2048]{1,0:T(8,128)(2,1)}, bf16[256,2048]{1,0:T(8,128)(2,1)S(1)}, u32[]{:S(2)}, u32[]{:S(2)}) collective-permute-start(bf16[256,2048]{1,0:T(8,128)(2,1)} %get-tuple-element.328), channel_id=1, source_target_pairs={{0,8},{8,0},{16,24},{24,16},{1,9},{9,1},{17,25},{25,17},{2,10},{10... | collective-permute-start | bytes 3145736 | tf_op jit(solution)/shard_map/ppermute | solution.py:364
  383.2 35.8 %collective-permute-start.32 = (bf16[256,2048]{1,0:T(8,128)(2,1)}, bf16[256,2048]{1,0:T(8,128)(2,1)}, u32[]{:S(2)}, u32[]{:S(2)}) collective-permute-start(bf16[256,2048]{1,0:T(8,128)(2,1)} %get-tuple-element.327), channel_id=1, source_target_pairs={{0,16},{8,24},{16,0},{24,8},{1,17},{9,25},{17,1},{25,9},{2,18},{10... | collective-permute-start | bytes 3145736 | tf_op jit(solution)/shard_map/ppermute | solution.py:364
  426.4 38.0 %collective-permute-start.36 = (bf16[2048,2048]{1,0:T(8,128)(2,1)}, bf16[2048,2048]{1,0:T(8,128)(2,1)}, u32[]{:S(2)}, u32[]{:S(2)}) collective-permute-start(bf16[2048,2048]{1,0:T(8,128)(2,1)} %get-tuple-element.210), channel_id=1, source_target_pairs={{0,4},{4,0},{1,5},{5,1},{2,6},{6,2},{3,7},{7,3},{8,12},{12,8},{9,1... | collective-permute-start | bytes 25165832 | tf_op jit(solution)/shard_map/ppermute | solution.py:364
  426.5 48.6 %collective-permute-start.39 = (bf16[512,2048]{1,0:T(8,128)(2,1)}, bf16[512,2048]{1,0:T(8,128)(2,1)S(1)}, u32[]{:S(2)}, u32[]{:S(2)}) collective-permute-start(bf16[512,2048]{1,0:T(8,128)(2,1)} %get-tuple-element.211), channel_id=1, source_target_pairs={{0,4},{4,0},{1,5},{5,1},{2,6},{6,2},{3,7},{7,3},{8,12},{12,8},{9,1... | collective-permute-start | bytes 6291464 | tf_op jit(solution)/shard_map/ppermute | solution.py:364
  426.9 48.2 %collective-permute-start.37 = (bf16[512,2048]{1,0:T(8,128)(2,1)}, bf16[512,2048]{1,0:T(8,128)(2,1)}, u32[]{:S(2)}, u32[]{:S(2)}) collective-permute-start(bf16[512,2048]{1,0:T(8,128)(2,1)} %pad_maximum_fusion.7), channel_id=1, source_target_pairs={{0,8},{8,0},{16,24},{24,16},{1,9},{9,1},{17,25},{25,17},{2,10},{10... | collective-permute-start | bytes 6291464 | tf_op jit(solution)/shard_map/ppermute | solution.py:364
  427.4 47.7 %collective-permute-start.38 = (bf16[512,2048]{1,0:T(8,128)(2,1)}, bf16[512,2048]{1,0:T(8,128)(2,1)}, u32[]{:S(2)}, u32[]{:S(2)}) collective-permute-start(bf16[512,2048]{1,0:T(8,128)(2,1)} %pad_maximum_fusion.8), channel_id=1, source_target_pairs={{0,16},{8,24},{16,0},{24,8},{1,17},{9,25},{17,1},{25,9},{2,18},{10... | collective-permute-start | bytes 6291464 | tf_op jit(solution)/shard_map/ppermute | solution.py:364
  445.2 193.0 %reduce-scatter.8.cloned.1.call-start = ((), (), s32[]{:S(2)}) async-start(), calls=%async_computation.9 | async-start | bytes 3604480 | tf_op jit(solution)/shard_map/reduce_scatter | solution.py:602
  500.8 76.3 %all-to-all-start = ((bf16[4,256,2048]{2,1,0:T(8,128)(2,1)}), bf16[4,256,2048]{2,1,0:T(8,128)(2,1)}, u32[]{:S(2)}, u32[]{:S(2)}) async-start(bf16[4,256,2048]{2,1,0:T(8,128)(2,1)} %bitcast.308), calls=%async_computation | async-start | bytes 8388608 | tf_op jit(solution)/shard_map/all_to_all | solution.py:632
  505.7 149.0 %reduce-scatter.6.cloned.1.call-start = ((), (), s32[]{:S(2)}) async-start(), calls=%async_computation.8 | async-start | bytes 3604480 | tf_op jit(solution)/shard_map/reduce_scatter | solution.py:602
  529.3 46.9 %collective-permute-start.41 = (bf16[256,2048]{1,0:T(8,128)(2,1)S(1)}, bf16[256,2048]{1,0:T(8,128)(2,1)S(1)}, u32[]{:S(2)}, u32[]{:S(2)}) collective-permute-start(bf16[256,2048]{1,0:T(8,128)(2,1)S(1)} %get-tuple-element.310), channel_id=1, source_target_pairs={{0,8},{8,0},{16,24},{24,16},{1,9},{9,1},{17,25},{25,17},{2,10},{10... | collective-permute-start | bytes 3145736 | tf_op jit(solution)/shard_map/ppermute | solution.py:364
  531.2 46.0 %collective-permute-start.42 = (bf16[256,2048]{1,0:T(8,128)(2,1)S(1)}, bf16[256,2048]{1,0:T(8,128)(2,1)}, u32[]{:S(2)}, u32[]{:S(2)}) collective-permute-start(bf16[256,2048]{1,0:T(8,128)(2,1)S(1)} %get-tuple-element.309), channel_id=1, source_target_pairs={{0,16},{8,24},{16,0},{24,8},{1,17},{9,25},{17,1},{25,9},{2,18},{10... | collective-permute-start | bytes 3145736 | tf_op jit(solution)/shard_map/ppermute | solution.py:364
  582.0 72.7 %collective-permute-start.44 = (bf16[512,2048]{1,0:T(8,128)(2,1)}, bf16[512,2048]{1,0:T(8,128)(2,1)}, u32[]{:S(2)}, u32[]{:S(2)}) collective-permute-start(bf16[512,2048]{1,0:T(8,128)(2,1)} %pad_maximum_fusion.10), channel_id=1, source_target_pairs={{0,16},{8,24},{16,0},{24,8},{1,17},{9,25},{17,1},{25,9},{2,18},{10... | collective-permute-start | bytes 6291464 | tf_op jit(solution)/shard_map/ppermute | solution.py:364
  585.1 69.7 %collective-permute-start.43 = (bf16[512,2048]{1,0:T(8,128)(2,1)}, bf16[512,2048]{1,0:T(8,128)(2,1)}, u32[]{:S(2)}, u32[]{:S(2)}) collective-permute-start(bf16[512,2048]{1,0:T(8,128)(2,1)} %pad_maximum_fusion.9), channel_id=1, source_target_pairs={{0,8},{8,0},{16,24},{24,16},{1,9},{9,1},{17,25},{25,17},{2,10},{10... | collective-permute-start | bytes 6291464 | tf_op jit(solution)/shard_map/ppermute | solution.py:364
  589.4 65.3 %all-to-all-start.1 = ((bf16[4,512,512]{2,1,0:T(8,128)(2,1)}), bf16[4,512,512]{2,1,0:T(8,128)(2,1)}, u32[]{:S(2)}, u32[]{:S(2)}) async-start(bf16[4,512,512]{2,1,0:T(8,128)(2,1)} %bitcast.317), calls=%async_computation.1 | async-start | bytes 4194304 | tf_op jit(solution)/shard_map/all_to_all | solution.py:626
  598.7 29.7 %collective-permute-start.45 = (bf16[64,2048]{1,0:T(8,128)(2,1)S(1)}, bf16[64,2048]{1,0:T(8,128)(2,1)}, u32[]{:S(2)}, u32[]{:S(2)}) collective-permute-start(bf16[64,2048]{1,0:T(8,128)(2,1)S(1)} %get-tuple-element.324), channel_id=1, source_target_pairs={{0,1},{1,0},{2,3},{3,2},{4,5},{5,4},{6,7},{7,6},{8,9},{9,8},{10,11... | collective-permute-start | bytes 786440 | tf_op jit(solution)/shard_map/ppermute | solution.py:364
  600.6 27.8 %collective-permute-start.46 = (bf16[64,2048]{1,0:T(8,128)(2,1)S(1)}, bf16[64,2048]{1,0:T(8,128)(2,1)}, u32[]{:S(2)}, u32[]{:S(2)}) collective-permute-start(bf16[64,2048]{1,0:T(8,128)(2,1)S(1)} %get-tuple-element.326), channel_id=1, source_target_pairs={{0,2},{1,3},{2,0},{3,1},{4,6},{5,7},{6,4},{7,5},{8,10},{9,11},{10,... | collective-permute-start | bytes 786440 | tf_op jit(solution)/shard_map/ppermute | solution.py:364
  607.8 28.2 %collective-permute-start.47 = (bf16[64,2048]{1,0:T(8,128)(2,1)S(1)}, bf16[64,2048]{1,0:T(8,128)(2,1)}, u32[]{:S(2)}, u32[]{:S(2)}) collective-permute-start(bf16[64,2048]{1,0:T(8,128)(2,1)S(1)} %get-tuple-element.325), channel_id=1, source_target_pairs={{0,3},{1,2},{2,1},{3,0},{4,7},{5,6},{6,5},{7,4},{8,11},{9,10},{10,... | collective-permute-start | bytes 786440 | tf_op jit(solution)/shard_map/ppermute | solution.py:364
  660.2 16.4 %collective-permute-start.48 = (bf16[2048,256]{1,0:T(8,128)(2,1)}, bf16[2048,256]{1,0:T(8,128)(2,1)}, u32[]{:S(2)}, u32[]{:S(2)}) collective-permute-start(bf16[2048,256]{1,0:T(8,128)(2,1)} %fusion.20), channel_id=1, source_target_pairs={{0,4},{4,0},{1,5},{5,1},{2,6},{6,2},{3,7},{7,3},{8,12},{12,8},{9,1... | collective-permute-start | bytes 3145736 | tf_op jit(solution)/shard_map/ppermute | solution.py:364
  664.8 43.8 %all-to-all-start.2 = ((bf16[1,3,176,8,256]{4,2,1,0,3:T(8,128)(2,1)}), bf16[1,3,176,8,256]{4,2,1,0,3:T(8,128)(2,1)}, u32[]{:S(2)}, u32[]{:S(2)}) async-start(bf16[1,3,176,8,256]{4,2,1,0,3:T(8,128)(2,1)} %pad_maximum_fusion.5), calls=%async_computation.5 | async-start | bytes 4325376 | tf_op jit(solution)/shard_map/all_to_all | solution.py:665
  679.2 22.6 %collective-permute-start.49 = (bf16[512,256]{1,0:T(8,128)(2,1)S(1)}, bf16[512,256]{1,0:T(8,128)(2,1)S(1)}, u32[]{:S(2)}, u32[]{:S(2)}) collective-permute-start(bf16[512,256]{1,0:T(8,128)(2,1)S(1)} %get-tuple-element.338), channel_id=1, source_target_pairs={{0,8},{8,0},{16,24},{24,16},{1,9},{9,1},{17,25},{25,17},{2,10},{10... | collective-permute-start | bytes 786440 | tf_op jit(solution)/shard_map/ppermute | solution.py:364
  681.2 20.6 %collective-permute-start.50 = (bf16[512,256]{1,0:T(8,128)(2,1)S(1)}, bf16[512,256]{1,0:T(8,128)(2,1)S(1)}, u32[]{:S(2)}, u32[]{:S(2)}) collective-permute-start(bf16[512,256]{1,0:T(8,128)(2,1)S(1)} %get-tuple-element.337), channel_id=1, source_target_pairs={{0,16},{8,24},{16,0},{24,8},{1,17},{9,25},{17,1},{25,9},{2,18},{10... | collective-permute-start | bytes 786440 | tf_op jit(solution)/shard_map/ppermute | solution.py:364
  682.7 25.2 %collective-permute-start.51 = (bf16[512,256]{1,0:T(8,128)(2,1)S(1)}, bf16[512,256]{1,0:T(8,128)(2,1)S(1)}, u32[]{:S(2)}, u32[]{:S(2)}) collective-permute-start(bf16[512,256]{1,0:T(8,128)(2,1)S(1)} %get-tuple-element.336), channel_id=1, source_target_pairs={{0,24},{8,16},{16,8},{24,0},{1,25},{9,17},{17,9},{25,1},{2,26},{10... | collective-permute-start | bytes 786440 | tf_op jit(solution)/shard_map/ppermute | solution.py:364
  714.4 7.7 collective-permute-start.52
  717.5 30.4 %all-to-all-start.3 = ((bf16[4,512,512]{2,1,0:T(8,128)(2,1)}), bf16[4,512,512]{2,1,0:T(8,128)(2,1)}, u32[]{:S(2)}, u32[]{:S(2)}) async-start(bf16[4,512,512]{2,1,0:T(8,128)(2,1)} %bitcast.318), calls=%async_computation.6 | async-start | bytes 4194304 | tf_op jit(solution)/shard_map/all_to_all | solution.py:626
  731.0 46.8 %collective-permute-start.53 = (bf16[512,2048]{1,0:T(8,128)(2,1)}, bf16[512,2048]{1,0:T(8,128)(2,1)}, u32[]{:S(2)}, u32[]{:S(2)}) collective-permute-start(bf16[512,2048]{1,0:T(8,128)(2,1)} %add_convert_fusion.1), channel_id=1, source_target_pairs={{0,4},{4,0},{1,5},{5,1},{2,6},{6,2},{3,7},{7,3},{8,12},{12,8},{9,1... | collective-permute-start | bytes 6291464 | tf_op jit(solution)/shard_map/ppermute | solution.py:364
  745.8 42.1 %collective-permute-start.58 = (bf16[512,256]{1,0:T(8,128)(2,1)}, bf16[512,256]{1,0:T(8,128)(2,1)}, u32[]{:S(2)}, u32[]{:S(2)}) collective-permute-start(bf16[512,256]{1,0:T(8,128)(2,1)} %get-tuple-element.334), channel_id=1, source_target_pairs={{0,8},{8,0},{16,24},{24,16},{1,9},{9,1},{17,25},{25,17},{2,10},{10... | collective-permute-start | bytes 786440 | tf_op jit(solution)/shard_map/ppermute | solution.py:364
  750.0 11.0 %collective-permute-start.54 = (bf16[2,64,1024]{2,1,0:T(8,128)(2,1)S(1)}, bf16[2,64,1024]{2,1,0:T(8,128)(2,1)S(1)}, u32[]{:S(2)}, u32[]{:S(2)}) collective-permute-start(bf16[2,64,1024]{2,1,0:T(8,128)(2,1)S(1)} %get-tuple-element.321), channel_id=1, source_target_pairs={{0,1},{1,0},{2,3},{3,2},{4,5},{5,4},{6,7},{7,6},{8,9},{9,8},{10,11... | collective-permute-start | bytes 786440 | tf_op jit(solution)/shard_map/ppermute | solution.py:364
  751.9 15.3 %collective-permute-start.55 = (bf16[2,64,1024]{2,1,0:T(8,128)(2,1)S(1)}, bf16[2,64,1024]{2,1,0:T(8,128)(2,1)S(1)}, u32[]{:S(2)}, u32[]{:S(2)}) collective-permute-start(bf16[2,64,1024]{2,1,0:T(8,128)(2,1)S(1)} %get-tuple-element.322), channel_id=1, source_target_pairs={{0,2},{1,3},{2,0},{3,1},{4,6},{5,7},{6,4},{7,5},{8,10},{9,11},{10,... | collective-permute-start | bytes 786440 | tf_op jit(solution)/shard_map/ppermute | solution.py:364
  758.9 18.6 %collective-permute-start.56 = (bf16[2,64,1024]{2,1,0:T(8,128)(2,1)S(1)}, bf16[2,64,1024]{2,1,0:T(8,128)(2,1)S(1)}, u32[]{:S(2)}, u32[]{:S(2)}) collective-permute-start(bf16[2,64,1024]{2,1,0:T(8,128)(2,1)S(1)} %get-tuple-element.323), channel_id=1, source_target_pairs={{0,3},{1,2},{2,1},{3,0},{4,7},{5,6},{6,5},{7,4},{8,11},{9,10},{10,... | collective-permute-start | bytes 786440 | tf_op jit(solution)/shard_map/ppermute | solution.py:364
  761.1 26.8 %collective-permute-start.59 = (bf16[512,256]{1,0:T(8,128)(2,1)S(1)}, bf16[512,256]{1,0:T(8,128)(2,1)S(1)}, u32[]{:S(2)}, u32[]{:S(2)}) collective-permute-start(bf16[512,256]{1,0:T(8,128)(2,1)S(1)} %copy-done.78), channel_id=1, source_target_pairs={{0,16},{8,24},{16,0},{24,8},{1,17},{9,25},{17,1},{25,9},{2,18},{10... | collective-permute-start | bytes 786440 | tf_op jit(solution)/shard_map/ppermute | solution.py:364
  767.2 20.8 %collective-permute-start.60 = (bf16[512,256]{1,0:T(8,128)(2,1)S(1)}, bf16[512,256]{1,0:T(8,128)(2,1)S(1)}, u32[]{:S(2)}, u32[]{:S(2)}) collective-permute-start(bf16[512,256]{1,0:T(8,128)(2,1)S(1)} %copy-done.77), channel_id=1, source_target_pairs={{0,24},{8,16},{16,8},{24,0},{1,25},{9,17},{17,9},{25,1},{2,26},{10... | collective-permute-start | bytes 786440 | tf_op jit(solution)/shard_map/ppermute | solution.py:364
  777.7 19.9 %collective-permute-start.57 = (f32[64,1024]{1,0:T(8,128)S(1)}, f32[64,1024]{1,0:T(8,128)S(1)}, u32[]{:S(2)}, u32[]{:S(2)}) collective-permute-start(f32[64,1024]{1,0:T(8,128)S(1)} %dynamic-slice_bitcast_fusion), channel_id=1, source_target_pairs={{0,4},{4,0},{1,5},{5,1},{2,6},{6,2},{3,7},{7,3},{8,12},{12,8},{9,1... | collective-permute-start | bytes 786440 | tf_op jit(solution)/shard_map/ppermute | solution.py:364
  789.1 9.4 %collective-permute-start.61 = (bf16[2,64,256]{2,1,0:T(8,128)(2,1)S(1)}, bf16[2,64,256]{2,1,0:T(8,128)(2,1)S(1)}, u32[]{:S(2)}, u32[]{:S(2)}) collective-permute-start(bf16[2,64,256]{2,1,0:T(8,128)(2,1)S(1)} %get-tuple-element.343), channel_id=1, source_target_pairs={{0,1},{1,0},{2,3},{3,2},{4,5},{5,4},{6,7},{7,6},{8,9},{9,8},{10,11... | collective-permute-start | bytes 196616 | tf_op jit(solution)/shard_map/ppermute | solution.py:364
  796.3 6.9 collective-permute-start.63
  (99 other events, 715.3 us)
Sparse Core Ops, SparseCore 0:
  13.8 53.4 all-gather.7
  68.8 152.7 all-gather.5
  445.3 56.7 reduce-scatter.3
  504.3 56.0 reduce-scatter.7
  562.5 67.9 reduce-scatter.5

commit v3 on v2

--- a/solution.py
+++ b/solution.py
@@ -24,8 +24,8 @@
 def block_places(order_ref, place_ref, own):
     count = order_ref.shape[0]
     for stored in range(count):
-        relative = (stored // 2) ^ own
-        place_ref[order_ref[stored]] = (relative % 2 * (count // 4) + relative // 2) * 2 + stored % 2
+        device = stored // 2
+        place_ref[order_ref[stored]] = ((device ^ own) % 2 * (count // 4) + device // 2) * 2 + stored % 2
 
 
 def causal(blk, group):
@@ -142,7 +142,11 @@
     )(scalars, order, queries, cosine, sine, keys_values)
 
 
-def attend_backward(group, blk, scal_ref, order_ref, qt_ref, g_ref, a_ref, lse_ref, cos_ref, sin_ref, kv_ref, dq_ref, dkv_ref, place_ref, gt_ref, qs_ref, gs_ref, kt_ref, acc_ref, delta_ref):
+def attend_backward(group, blk, last, scal_ref, order_ref, qt_ref, g_ref, a_ref, lse_ref, cos_ref, sin_ref, kv_ref, *rest):
+    if last:
+        before_ref, dq_ref, mine_ref, other_ref, place_ref, gt_ref, qs_ref, gs_ref, kt_ref, acc_ref, delta_ref, dkv_ref = rest
+    else:
+        dq_ref, dkv_ref, place_ref, gt_ref, qs_ref, gs_ref, kt_ref, acc_ref, delta_ref = rest
     row_block = pl.program_id(0)
     own, length = scal_ref[0], scal_ref[1]
 
@@ -152,7 +156,7 @@
         for piece in range(order_ref.shape[0]):
             cells = slice(piece * blk, (piece + 1) * blk)
             kt_ref[:, cells] = kv_ref[cells, :HD].T
-        dkv_ref[...] = jnp.zeros(dkv_ref.shape, F32)
+        dkv_ref[...] = before_ref[...] if last else jnp.zeros(dkv_ref.shape, F32)
 
     mine = row_position(order_ref, own, row_block)
 
@@ -202,16 +206,27 @@
     def _():
         dq_ref[...] = jnp.zeros(dq_ref.shape, BF16)
 
-
-def attention_backward(scalars, order, turned, grads, attended, lse, cosine, sine, keys_values, blk, group, which):
+    if last:
+
+        @pl.when(row_block == pl.num_programs(0) - 1)
+        def _():
+            half = mine_ref.shape[0]
+            for total_ref, rows in ((mine_ref, slice(0, half)), (other_ref, slice(half, 2 * half))):
+                total_ref[:, :HD] = (dkv_ref[rows, :HD] * LN2).astype(BF16)
+                total_ref[:, HD:] = dkv_ref[rows, HD:].astype(BF16)
+
+
+def attention_backward(scalars, order, turned, grads, attended, lse, cosine, sine, keys_values, blk, group, which, before=None):
+    last = before is not None
     rows = grads.shape[0]
     span = keys_values.shape[0]
     row_blocks = rows // blk
+    whole = pl.BlockSpec((span, 2 * HD), lambda i, *_: (0, 0))
     table = pl.BlockSpec((HALF, blk), lambda i, *_: (0, i))
     rowspec = pl.BlockSpec((blk, group * HD), lambda i, *_: (i, which))
     per_block = lambda *dims: pl.BlockSpec((1,) + dims, lambda i, *_: (i, 0, which))
     return pl.pallas_call(
-        functools.partial(attend_backward, group, blk),
+        functools.partial(attend_backward, group, blk, last),
         grid_spec=pltpu.PrefetchScalarGridSpec(
             num_scalar_prefetch=2,
             grid=(row_blocks,),
@@ -222,12 +237,13 @@
                 per_block(1, group * blk),
                 table,
                 table,
-                pl.BlockSpec((span, 2 * HD), lambda i, *_: (0, 0)),
-            ],
+                whole,
+            ]
+            + [whole] * last,
             out_specs=[
                 pl.BlockSpec((blk, group * HD), lambda i, *_: (i, 0)),
-                pl.BlockSpec((span, 2 * HD), lambda i, *_: (0, 0)),
-            ],
+            ]
+            + ([pl.BlockSpec((span // 2, 2 * HD), lambda i, *_: (0, 0))] * 2 if last else [whole]),
             scratch_shapes=[
                 pltpu.SMEM((order.shape[0],), jnp.int32),
                 pltpu.VMEM((HD, group * blk), BF16),
@@ -236,16 +252,21 @@
                 pltpu.VMEM((HD, span), BF16),
                 pltpu.VMEM((HD, group * blk), F32),
                 pltpu.VMEM((1, group * blk), F32),
-            ],
+            ]
+            + [pltpu.VMEM((span, 2 * HD), F32)] * last,
         ),
         out_shape=[
             jax.ShapeDtypeStruct((rows, group * HD), BF16),
-            jax.ShapeDtypeStruct((span, 2 * HD), F32),
-        ],
+        ]
+        + (
+            [jax.ShapeDtypeStruct((span // 2, 2 * HD), BF16)] * 2
+            if last
+            else [jax.ShapeDtypeStruct((span, 2 * HD), F32)]
+        ),
         compiler_params=pltpu.CompilerParams(vmem_limit_bytes=48 * 2**20),
         cost_estimate=pl.CostEstimate(flops=2**20, bytes_accessed=2**16, transcendentals=0),
         name="attend_backward",
-    )(scalars, order, turned, grads, attended, lse, cosine, sine, keys_values)
+    )(scalars, order, turned, grads, attended, lse, cosine, sine, keys_values, *([before] if last else []))
 
 
 def ffn_rows(count, tiles, place_ref, xa_ref, xb_ref, ga_ref, gb_ref, gate_ref, up_ref, down_ref, *rest):
@@ -265,11 +286,18 @@
     hidden = (silu * up).astype(BF16)
     dgate = (dhidden * up * sigmoid * (1.0 + gate * (1.0 - sigmoid))).astype(BF16)
     dup = (dhidden * silu).astype(BF16)
-    back = (
-        jnp.dot(dgate, gate_rows, preferred_element_type=F32)
-        + jnp.dot(dup, up_rows, preferred_element_type=F32)
-    ).astype(BF16)
     out = jnp.dot(hidden, down_rows, preferred_element_type=F32).astype(BF16)
+    step = 512 if x.shape[1] % 512 == 0 else x.shape[1]
+    back = jnp.concatenate(
+        [
+            (
+                jnp.dot(dgate, gate_rows[:, at_col : at_col + step], preferred_element_type=F32)
+                + jnp.dot(dup, up_rows[:, at_col : at_col + step], preferred_element_type=F32)
+            ).astype(BF16)
+            for at_col in range(0, x.shape[1], step)
+        ],
+        axis=1,
+    )
     x_all[...] = x
     g_all[...] = grad
     hidden_all[...] = hidden
@@ -310,7 +338,7 @@
         grid_spec=pltpu.PrefetchScalarGridSpec(
             num_scalar_prefetch=1,
             grid=(2 * tiles,),
-            in_specs=[here_a, here_b, out_a, out_b, weight(0), weight(1), weight(2)]
+            in_specs=[here_a, here_b, here_a, here_b, weight(0), weight(1), weight(2)]
             + [pl.BlockSpec(memory_space=pl.ANY)] * count,
             out_specs=[here_a, here_b, out_a, out_b] + [there(model_dim)] * 2 + [there(units)] * 3,
         ),
@@ -325,6 +353,62 @@
     )(place, xa, xb, ga, gb, weights, weights, weights, *kept)
 
 
+def pack_columns(*refs):
+    out_ref = refs[-1]
+    columns = out_ref.shape[3]
+    for which, in_ref in enumerate(refs[:-1]):
+        for place in range(out_ref.shape[0]):
+            out_ref[place, which] = in_ref[:, place * columns : (place + 1) * columns]
+
+
+def pack_units(terms, places):
+    share, columns = terms[0].shape
+    if share % 16:
+        return jnp.stack(terms).reshape(len(terms), share, places, columns // places).transpose(2, 0, 1, 3)
+    return pl.pallas_call(
+        pack_columns,
+        out_shape=jax.ShapeDtypeStruct((places, len(terms), share, columns // places), BF16),
+        compiler_params=pltpu.CompilerParams(vmem_limit_bytes=32 * 2**20),
+        cost_estimate=pl.CostEstimate(flops=2**16, bytes_accessed=len(terms) * terms[0].size * 4, transcendentals=0),
+        name="pack_units",
+    )(*terms)
+
+
+def turn_rows(in_ref, *out_refs):
+    for which, out_ref in enumerate(out_refs):
+        out_ref[...] = in_ref[:, which].reshape(out_ref.shape[1], out_ref.shape[0]).T.astype(F32)
+
+
+def turn_units(terms):
+    places, count, share, columns = terms.shape
+    if share % 16:
+        turned = terms.transpose(1, 3, 0, 2).reshape(count, columns, places * share).astype(F32)
+        return [turned[which] for which in range(count)]
+    return pl.pallas_call(
+        turn_rows,
+        out_shape=[jax.ShapeDtypeStruct((columns, places * share), F32)] * count,
+        compiler_params=pltpu.CompilerParams(vmem_limit_bytes=32 * 2**20),
+        cost_estimate=pl.CostEstimate(flops=2**20, bytes_accessed=terms.size * 6, transcendentals=0),
+        name="turn_units",
+    )(terms)
+
+
+def alternate_columns(part, first_ref, second_ref, out_ref):
+    for at_col in range(0, first_ref.shape[1], part):
+        out_ref[:, 2 * at_col : 2 * at_col + part] = first_ref[:, at_col : at_col + part]
+        out_ref[:, 2 * at_col + part : 2 * at_col + 2 * part] = second_ref[:, at_col : at_col + part]
+
+
+def alternate(first, second, part):
+    rows, width = first.shape
+    return pl.pallas_call(
+        functools.partial(alternate_columns, part),
+        out_shape=jax.ShapeDtypeStruct((rows, 2 * width), F32),
+        cost_estimate=pl.CostEstimate(flops=2**16, bytes_accessed=first.size * 16, transcendentals=0),
+        name="alternate",
+    )(first, second)
+
+
 def angles(positions):
     frequency = ROPE_BASE ** (-2.0 * jnp.arange(HALF, dtype=F32) / HD)
     phase_angle = frequency[:, None] * positions.astype(F32)[None, :]
@@ -369,19 +453,21 @@
 
 
 def spread_chips(value):
-    return [value] + [exchange(value, "chip", k) for k in range(1, lax.axis_size("chip"))]
+    chips = lax.axis_size("chip")
+    copies = jnp.broadcast_to(value[None], (chips,) + value.shape)
+    return lax.all_to_all(copies, "chip", 0, 0, tiled=False)
 
 
 def gather_near(value):
     if lax.axis_size("chip") != 4:
-        return spread_chips(value)
+        return [value] + [exchange(value, "chip", k) for k in range(1, lax.axis_size("chip"))]
     return [value, exchange(value, "chip", 1), exchange(value, "chip", 2)]
 
 
 def send_far(near):
     if lax.axis_size("chip") != 4:
         return ()
-    value, first, second = near
+    value, first, second = lax.optimization_barrier(near)
     half = value.shape[0] // 2
     return exchange(first[:half], "chip", 2), exchange(second[half:], "chip", 1)
 
@@ -421,13 +507,9 @@
 
 
 def add_half(term, passing, which):
-    half = passing.shape[0]
-    first, second = term[:half].astype(F32), term[half:].astype(F32)
-    if which == 0:
-        first = first + passing.astype(F32)
-    else:
-        second = second + passing.astype(F32)
-    return jnp.concatenate([first, second], axis=0).astype(BF16)
+    start = which * passing.shape[0]
+    half = term[start : start + passing.shape[0]].astype(F32) + passing.astype(F32)
+    return lax.dynamic_update_slice(term, half.astype(BF16), (start, 0))
 
 
 def lay_columns(chunks, chip):
@@ -480,6 +562,9 @@
     packed = lax.all_gather(packed, "fsdp", axis=0)
     bounds = [sum(heights[: i + 1]) for i in range(4)]
     query_piece, out_piece, kv_piece, gain_one, gain_two = jnp.split(packed, bounds, axis=1)
+    out_piece = out_piece.reshape(wide, out_cols)
+    gain_one = gain_one.reshape(model_dim).astype(F32)
+    gain_two = gain_two.reshape(model_dim).astype(F32)
     share = w_gate.shape[1] // places
     pieces = jnp.stack(
         [
@@ -487,27 +572,22 @@
             for weight in (w_gate, w_up, w_down)
         ]
     )
-    ffn_weights = lax.all_gather(pieces, "fsdp", axis=0)
     query_piece = query_piece.reshape(model_dim, part)
-    out_piece = out_piece.reshape(wide, out_cols)
-    gain_one = gain_one.reshape(model_dim).astype(F32)
-    gain_two = gain_two.reshape(model_dim).astype(F32)
-    kv_full = jnp.zeros((planes, chips, kv_rows, 2 * HD), BF16)
-    kv_chunks = gather_chips(kv_piece)
-    for k, chunk in enumerate(kv_chunks):
-        kv_full = lax.dynamic_update_slice(kv_full, chunk[:, None], (0, chip ^ k, 0, 0))
-    kv_full = with_layout_constraint(kv_full.reshape(model_dim, 2 * HD), Layout((0, 1)))
-
     own_pos = jnp.repeat(lax.dynamic_slice_in_dim(order, own * 2, 2, 0) * blk, blk) + (
         jnp.arange(local_len, dtype=jnp.int32) % blk
     )
     live_rows = (own_pos < length)[:, None]
     grad_out = jnp.where(live_rows, cotangent[0], jnp.zeros((), BF16))
     grad_near = after(gather_near(grad_out), pieces)
-    query_piece = after(query_piece, kv_chunks, grad_near)
-    query_half = lay_columns(gather_chips(query_piece), chip)
-    out_chunks = spread_chips(after(out_piece, query_half))
-    grad_far = send_far(after(grad_near, query_half))
+    grad_far = send_far(grad_near)
+    kv_full = spread_chips(after(kv_piece, grad_near)).swapaxes(0, 1).reshape(model_dim, 2 * HD)
+    kv_full = with_layout_constraint(kv_full, Layout((0, 1)))
+    query_near = gather_near(after(query_piece, grad_far))
+    query_half = lay_columns(gather_far(query_near), chip)
+    grad_others = [swap_core(chunk) for chunk in after(grad_near, query_near)]
+    out_piece = after(out_piece, query_half)
+    out_chunks = [out_piece] + [exchange(out_piece, "chip", k) for k in range(1, chips)]
+    ffn_weights = lax.all_gather(pieces, "fsdp", axis=0)
 
     offsets = jnp.arange(blk, dtype=jnp.int32)
     mine = lax.dynamic_slice_in_dim(order, own * 2, 2, 0)
@@ -526,21 +606,21 @@
     key_value = matmul(both_normed[:local_len], kv_full)
     key_rot = rotate(key_value[:, :HD], own_cosine, own_sine)
     local_kv = jnp.concatenate([key_rot, key_value[:, HD:]], axis=1).astype(BF16)
-    slot_kv = jnp.concatenate(gather_chips(local_kv), axis=0)
+    slot_kv = spread_chips(local_kv).reshape(-1, 2 * HD)
     slot_kv = jnp.concatenate([slot_kv, swap_core(slot_kv)], axis=0)
 
     heads = wide // HD
     queries = matmul(both_normed, query_half)
-    scalars = jnp.stack([own, length]).astype(jnp.int32)
+    scalars = after(jnp.stack([own, length]).astype(jnp.int32), grad_others)
     attended, lse, turned = attention_forward(
         scalars, order, queries, cosine, sine_vals, slot_kv, blk
     )
 
-    attended, lse, turned, out_chunks, grad_far = lax.optimization_barrier(
-        (attended, lse, turned, out_chunks, grad_far)
-    )
-    grad_mine = jnp.concatenate(list(grad_near) + ([jnp.concatenate(grad_far, axis=0)] if grad_far else []), axis=0)
-    grad_other = swap_core(grad_mine)
+    attended, lse, turned, out_chunks = lax.optimization_barrier((attended, lse, turned, out_chunks))
+    grad_mine = list(grad_near)
+    if grad_far:
+        grad_mine.append(jnp.concatenate(grad_far, axis=0))
+        grad_others.append(swap_core(grad_mine[3]))
     out_half = lay_columns(out_chunks, chip)
     branch_other = swap_core(matmul(attended[local_len:], out_half).astype(BF16))
     residual = tokens_flat + matmul(attended[:local_len], out_half) + branch_other.astype(F32)
@@ -553,8 +633,8 @@
             chips,
             chunk,
             swap_core(chunk),
-            grad_mine,
-            grad_other,
+            grad_mine[at_place],
+            grad_others[at_place],
             ffn_weights,
             kept,
         )
@@ -590,7 +670,12 @@
 
     out_own, out_other, normed_all, grad_all, hidden_all, dgate_all, dup_all = kept
     down_term = contract_rows(hidden_all, grad_all).astype(BF16)
-    out_parts = add_cores(out_own, out_other).reshape(chips, local_len, model_dim)
+    out_other = swap_core(out_other)
+    cuts = [0, 1, 2, 3, 3.5, 4] if chips == 4 else range(chips + 1)
+    out_parts = [
+        (out_own[int(a * local_len) : int(b * local_len)].astype(F32) + out_other[int(a * local_len) : int(b * local_len)].astype(F32)).astype(BF16)
+        for a, b in zip(cuts[:-1], cuts[1:])
+    ]
     gate_term = contract_rows(dgate_all, normed_all).astype(BF16)
     arrived = after(arrived, down_term, out_parts, gate_term)
     grad_normed = back_own.astype(F32)
@@ -616,23 +701,22 @@
     grad_attn = after(grad_attn, branch_terms)
     group = heads // 2
 
-    def backward(grads, which):
+    def backward(grads, which, before=None):
         return attention_backward(
-            scalars, order, turned, grads, attended, lse, cosine, sine_vals, slot_kv, blk, group, which
+            scalars, order, turned, grads, attended, lse, cosine, sine_vals, slot_kv, blk, group, which, before
         )
 
     def deal_rows(terms):
-        terms = terms.reshape(chips, 2 * planes * (depth // places), -1)
-        return lax.all_to_all(terms, "chip", 0, 0, tiled=False)
+        return lax.all_to_all(terms.reshape(places, planes * (depth // places), -1), ("chip", "core"), 0, 0, tiled=False)
 
     def by_plane(dealt):
-        total = jnp.sum(dealt.astype(F32), axis=0)
-        return total.reshape(2, planes, depth // places, -1).swapaxes(0, 1)
+        total = jnp.sum(dealt.astype(F32).reshape(chips, 2, planes, depth // places, -1), axis=0)
+        return total.swapaxes(0, 1).astype(BF16)
 
     branch_dealt = lax.all_to_all(branch_terms, "chip", 0, 0, tiled=False)
     up_term = contract_rows(*after((dup_all, normed_all), branch_terms)).astype(BF16)
     if chips == 4:
-        out_passing = reduce_far(out_parts[3])
+        out_passing = exchange(out_parts[3], "chip", 1), exchange(out_parts[4], "chip", 2)
     else:
         out_passing = ()
     grad_query_a, kv_terms_a = backward(after(grad_attn, up_term), 0)
@@ -646,25 +730,27 @@
     else:
         out_near = tuple(out_parts[k] for k in range(1, chips))
     branch_sum = branch_sum.reshape(planes, part // planes, model_dim)
-    grad_query_b, kv_terms_b = backward(after(grad_attn, out_near, query_terms_a, branch_sum), 1)
+    grad_query_b, kv_mine, kv_other = backward(
+        after(grad_attn, out_near, query_terms_a, branch_sum), 1, kv_terms_a
+    )
     out_arrived = [exchange(term, "chip", k + 1) for k, term in enumerate(out_near)]
     grad_w_out = sum_planes(branch_sum, plane)
     query_sums_a = deal_rows(query_terms_a)
     ffn_terms = [gate_term, over_planes(up_term), down_term]
-    grad_query_b, kv_terms_b, out_arrived, grad_w_out, query_sums_a, ffn_terms = lax.optimization_barrier(
-        (grad_query_b, kv_terms_b, out_arrived, grad_w_out, query_sums_a, ffn_terms)
-    )
-    kv_terms = kv_terms_a + kv_terms_b
-    kv_terms = jnp.concatenate([kv_terms[:, :HD] * LN2, kv_terms[:, HD:]], axis=1)
-    kv_terms = kv_terms.reshape(2, chips * local_len, 2 * HD)
-    kv_parts = add_cores(kv_terms[0], kv_terms[1]).reshape(chips, local_len, 2 * HD)
+    grad_query_b, kv_mine, kv_other, out_arrived, grad_w_out, ffn_terms, query_sums_a = lax.optimization_barrier(
+        (grad_query_b, kv_mine, kv_other, out_arrived, grad_w_out, ffn_terms, query_sums_a)
+    )
+    kv_parts = with_layout_constraint(add_cores(kv_mine, kv_other), Layout((0, 1)))
+    kv_parts = kv_parts.reshape(chips, local_len, 2 * HD)
+    kv_parts = [at(kv_parts, chip ^ k) for k in range(chips)]
     kv_arrived = [exchange(kv_parts[k], "chip", k) for k in range(1, chips)]
-    query_terms_b = contract_rows(*after((both_normed, grad_query_b), kv_parts)).astype(BF16)
+    out_arrived, ffn_terms, grad_query_b, query_sums_a = after(
+        (out_arrived, ffn_terms, grad_query_b, query_sums_a), kv_parts
+    )
+    query_terms_b = contract_rows(both_normed, grad_query_b).astype(BF16)
     kv_arrived = after(kv_arrived, query_terms_b)
-    ffn_terms = jnp.stack(ffn_terms).reshape(3, share, places, model_dim // places)
-    ffn_terms = lax.all_to_all(ffn_terms, ("chip", "core"), 2, 0, tiled=False)
-    kv_arrived, ffn_terms = lax.optimization_barrier((kv_arrived, ffn_terms))
-    query_sums_b = deal_rows(after(query_terms_b, kv_arrived))
+    ffn_terms = pack_units(after(ffn_terms, query_sums_a), places)
+    ffn_terms = lax.all_to_all(ffn_terms, ("chip", "core"), 0, 0, tiled=False)
     kv_total = kv_parts[0].astype(F32)
     for term in kv_arrived:
         kv_total = kv_total + term.astype(F32)
@@ -675,20 +761,28 @@
     both_grad_kv = jnp.concatenate([grad_kv, swap_core(grad_kv)], axis=0)
     kv_half = lax.dynamic_slice_in_dim(both_grad_kv, core * HD, HD, 1)
     kv_weight_half = lax.dynamic_slice_in_dim(kv_full, core * HD, HD, 1)
+    rows = depth // places
+    first_row = (own * planes + plane) * rows
+    other_row = ((own ^ 1) * planes + plane) * rows
+    kept_rows = lax.dynamic_slice_in_dim(query_half, first_row, rows, 0)
+    sent_rows = swap_core(lax.dynamic_slice_in_dim(query_half, other_row, rows, 0))
+    own_query_rows = jnp.where(
+        core == 0, jnp.stack([kept_rows, sent_rows]), jnp.stack([sent_rows, kept_rows])
+    )
+    own_kv_rows = lax.dynamic_slice_in_dim(kv_full, first_row, rows, 0)
     both_query = jnp.concatenate([grad_query_a, grad_query_b], axis=1)
 
     def normed_one_term(rows):
         return contract_cols(both_query[rows], query_half) + contract_cols(kv_half[rows], kv_weight_half)
 
-    other_one = swap_core(normed_one_term(slice(local_len, None)).astype(BF16))
     gains = jnp.pad(grad_gain_two[:, None], ((0, 0), (0, HD - 1)))
     kv_grads = jnp.concatenate([contract_rows(both_normed, kv_half), gains], axis=1).astype(BF16)
-    kv_grads = kv_grads.reshape(chips, 2 * planes * (depth // places), 2 * HD)
-    kv_sent = [exchange(at(kv_grads, chip ^ k), "chip", k) for k in range(1, chips)]
-
-    query_sums_b = after(query_sums_b, kv_grads)
-    query_sums = jnp.concatenate([by_plane(query_sums_a), by_plane(query_sums_b)], axis=3)
-    query_sums = sum_planes(query_sums, plane)
+    last_terms = jnp.concatenate([query_terms_b, kv_grads], axis=1)
+    last_terms = with_layout_constraint(last_terms, Layout((0, 1)))
+    last_dealt = deal_rows(after(last_terms, ffn_terms))
+    query_sums_a = sum_planes(by_plane(after(query_sums_a, last_terms)), plane)
+    both_query = after(both_query, last_terms)
+    other_one = swap_core(normed_one_term(slice(local_len, None)).astype(BF16))
 
     grad_normed_one = normed_one_term(slice(0, local_len)) + other_one.astype(F32)
     unit_one = tokens_flat * inverse_one
@@ -697,47 +791,30 @@
         scaled_one - unit_one * jnp.mean(scaled_one * unit_one, axis=1, keepdims=True)
     )
     grad_tokens = grad_tokens.astype(BF16)
+    out_arrived = after(out_arrived, last_terms)
     ffn_out = out_parts[0].astype(F32)
     for term in out_arrived:
         ffn_out = ffn_out + term.astype(F32)
     output = jnp.where(live_rows, residual + ffn_out, 0.0).astype(BF16)
 
-    kv_sent = after(kv_sent, grad_tokens)
-    kv_sums = at(kv_grads, chip).astype(F32)
-    for term in kv_sent:
-        kv_sums = kv_sums + term.astype(F32)
-    kv_sums = kv_sums.reshape(2, planes, depth // places, 2 * HD).swapaxes(0, 1)
-    kv_sums = sum_planes(kv_sums, plane)
-
-    rows = depth // places
-    own_rows = [((chip * 2 + j) * planes + plane) * rows for j in range(2)]
-    gain_sums = jnp.stack(
-        [
-            jnp.sum(lax.dynamic_slice_in_dim(query_half, row, rows, 0).astype(F32) * query_sums[j], axis=1)
-            + jnp.sum(
-                lax.dynamic_slice_in_dim(kv_weight_half, row, rows, 0).astype(F32) * kv_sums[j, :, :HD],
-                axis=1,
-            )
-            for j, row in enumerate(own_rows)
-        ]
-    )
-    kv_sums = lax.dynamic_update_slice(kv_sums, gain_sums[:, :, None], (0, 0, HD + 1))
-
-    def by_core(sums):
-        kept, other = at(sums, core), swap_core(at(sums, core ^ 1))
-        return jnp.where(core == 0, kept, other), jnp.where(core == 0, other, kept)
-
-    first, second = by_core(query_sums)
-    grad_w_query = jnp.stack(
-        [first.reshape(rows, planes, part), second.reshape(rows, planes, part)], axis=2
-    ).reshape(rows, model_dim)
-    first, second = by_core(kv_sums)
-    grad_w_kv = jnp.concatenate([first[:, :HD], second[:, :HD]], axis=1)
-    gain_sums = first[:, HD : HD + 2] + second[:, HD : HD + 2]
-    grad_gain_two = gain_sums[:, 0]
-    grad_gain_one = gain_sums[:, 1] / lax.dynamic_slice_in_dim(gain_one, (own * planes + plane) * rows, rows, 0)
-    ffn_grads = ffn_terms.transpose(1, 3, 0, 2).reshape(3, model_dim // places, places * share)
-    ffn_grads = ffn_grads.astype(F32)
+    ffn_grads = turn_units(after(ffn_terms, last_terms))
+    last_dealt = after(last_dealt, grad_tokens, output, query_sums_a, ffn_grads)
+    last_planes = by_plane(last_dealt)
+    last_arrived = [exchange(at(last_planes, plane ^ k), "fsdp", k) for k in range(1, planes)]
+    last_sums = at(last_planes, plane).astype(F32)
+    for term in last_arrived:
+        last_sums = last_sums + term.astype(F32)
+    query_sums = jnp.concatenate([query_sums_a, last_sums[:, :, : -2 * HD]], axis=2)
+    kv_sums = last_sums[:, :, -2 * HD :]
+
+    own_gain = lax.dynamic_slice_in_dim(gain_one, first_row, rows, 0)
+    grad_gain_one = (
+        jnp.sum(own_query_rows.astype(F32) * query_sums, axis=(0, 2))
+        + jnp.sum(own_kv_rows.astype(F32) * jnp.concatenate([kv_sums[0, :, :HD], kv_sums[1, :, :HD]], axis=1), axis=1)
+    ) / own_gain
+    grad_gain_two = kv_sums[0, :, HD] + kv_sums[1, :, HD]
+    grad_w_query = alternate(query_sums[0], query_sums[1], part)
+    grad_w_kv = jnp.concatenate([kv_sums[0, :, :HD], kv_sums[1, :, :HD]], axis=1)
     return (
         output[None],
         grad_tokens.astype(BF16)[None],

time: 824 us -> 806 us (0.978)
  starting transfers between devices: 95.5 us -> 113 us
  waiting for transfers between devices: 225 us -> 210 us
  local copies, waits for them, and re-layouts: 98.7 us -> 86.4 us
  Pallas kernels: 173 us -> 161 us
    ppermute x65 -> x56, waiting for transfers between devices: 207 us -> 181 us  [exchange(): return lax.ppermute(value, axis, [(i, i ^ distance) for i in range(size)])]
    convert_element_type x2 -> x3, other arithmetic: 0.6 us -> 19.5 us  [the longest x2 12.4 us: shards(): (out_own[int(a * local_len):int(b * local_len)].astype(F32) + out_other[i...]
    unnamed x203 -> x165, local copies, waits for them, and re-layouts: 46.9 us -> 29.3 us
    all_to_all x3 -> x5, waiting for transfers between devices: 16.9 us -> 28.3 us  [the longest x2 14.5 us: deal_rows(): lax.all_to_all(terms.reshape(places, planes * (depth // places), -1), ('c...]
    dynamic_update_slice x0 -> x4, other arithmetic: none -> 11.3 us  [add_half(): return lax.dynamic_update_slice(term, half.astype(BF16), (start, 0))]
    another operation x9 -> x3, other arithmetic: 10 us -> 0.17 us
    ppermute x65 -> x56, starting transfers between devices: 76.8 us -> 85.7 us  [exchange(): return lax.ppermute(value, axis, [(i, i ^ distance) for i in range(size)])]
    all_to_all x3 -> x5, starting transfers between devices: 13.4 us -> 21.4 us  [the longest x2 9.07 us: deal_rows(): lax.all_to_all(terms.reshape(places, planes * (depth // places), -1), ('c...]
  transfers between devices with their start and end apart: 74 -> 67, of which waited for: 28 -> 25; matrix products, arithmetic and copies ran while one was open for 32% -> 31% of each run, Pallas kernels for 17% -> 16%
where the time goes in v3:
time: 806 us; the launch traced here: 801 us
  waiting for transfers between devices  210 us (26%)
  Pallas kernels  161 us (20%)
  starting transfers between devices  113 us (14%)
  matrix products  110 us (14%)
  other arithmetic  105 us (13%)
  local copies, waits for them, and re-layouts  86.4 us (11%)
  between operations  16.3 us (2%)
    ppermute x56, waiting for transfers between devices, exchange(): return lax.ppermute(value, axis, [(i, i ^ distance) for i in range(size)])  181 us
    pallas_call x4, Pallas kernels, ffn_pair(): pl.pallas_call(functools.partial(ffn_rows, count, tiles), grid_spec=pltpu...  123 us
    ppermute x56, starting transfers between devices, exchange(): return lax.ppermute(value, axis, [(i, i ^ distance) for i in range(size)])  85.7 us
    dot_general x7, matrix products, contract_rows(): lax.dot_general(left, right, (((0,), (0,)), ((), ())), preferred_element_...  74.1 us
    unnamed x165, local copies, waits for them, and re-layouts  29.3 us
    pallas_call x2, Pallas kernels, attention_backward(): pl.pallas_call(functools.partial(attend_backward, group, blk, last), grid...  24.1 us
    dot_general x5, matrix products, contract_cols(): lax.dot_general(left, right, (((1,), (1,)), ((), ())), preferred_element_...  21.6 us
  transfers between devices with their start and end apart: 67, of which 25 were waited for; matrix products, arithmetic and copies ran while one was open for 31% of the time, Pallas kernels for 16%

profile of v3, /device:TPU:0, one launch (start us, length us, event | category | flops | bytes accessed | tf_op | source)
XLA Modules:
  0.0 801.0 jit_solution(11413955180712547612)
XLA Ops:
  15.2 3.1 bitcast_select_fusion.ga_ref
  18.3 2.9 collective-permute-start
  22.8 4.5 constant_dynamic-slice_fusion.8
  30.9 2.8 constant_dynamic-slice_fusion.10
  35.9 3.0 pad_maximum_fusion.4
  39.2 28.0 %collective-permute-done.ga_ref = bf16[512,2048]{1,0:T(8,128)(2,1)} collective-permute-done((bf16[512,2048]{1,0:T(8,128)(2,1)}, bf16[512,2048]{1,0:T(8,128)(2,1)}, u32[]{:S(2)}, u32[]{:S(2)}) %collective-permute-start) | collective-permute-done | bytes 2097184 | tf_op jit(solution)/shard_map/ppermute | solution.py:448
  81.0 4.2 all-to-all-start
  85.2 3.0 fusion.68
  88.2 10.7 %collective-permute-done.2 = bf16[256,2048]{1,0:T(8,128)(2,1)} collective-permute-done((bf16[256,2048]{1,0:T(8,128)(2,1)}, bf16[256,2048]{1,0:T(8,128)(2,1)}, u32[]{:S(2)}, u32[]{:S(2)}) %collective-permute-start.2) | collective-permute-done | bytes 1048608 | tf_op jit(solution)/shard_map/ppermute | solution.py:448
  103.4 6.1 fusion.2
  109.5 2.9 all-to-all-done
  117.1 15.1 %collective-permute-done.4 = bf16[2048,256]{1,0:T(8,128)(2,1)} collective-permute-done((bf16[2048,256]{1,0:T(8,128)(2,1)}, bf16[2048,256]{1,0:T(8,128)(2,1)}, u32[]{:S(2)}, u32[]{:S(2)}) %collective-permute-start.4) | collective-permute-done | bytes 1048608 | tf_op jit(solution)/shard_map/ppermute | solution.py:448
  133.5 4.2 all-to-all-start.1
  141.9 10.9 %all-to-all-done.1 = bf16[4,512,256]{2,1,0:T(8,128)(2,1)} async-done(((bf16[4,512,256]{2,1,0:T(8,128)(2,1)}), bf16[4,512,256]{2,1,0:T(8,128)(2,1)}, u32[]{:S(2)}, u32[]{:S(2)}) %all-to-all-start.1) | async-done | bytes 1048608 | tf_op jit(solution)/shard_map/all_to_all | solution.py:458
  175.1 6.3 fusion.70.q_ref
  185.8 9.7 %attend_forward.1 = (bf16[1024,1024]{1,0:T(8,128)(2,1)S(1)}, f32[4,1,2048]{2,1,0:T(1,128)S(1)}, bf16[4,128,2048]{2,1,0:T(8,128)(2,1)S(1)}) custom-call(s32[2]{0:T(128)S(1)} %pad_add_fusion.scal_ref, s32[16]{0:T(128)S(1)} %bitcast.149, f32[1024,1024]{1,0:T(8,128)S(1)} %fusion.70.q_ref, f32[64,1024]{1,0:T(8,128)S(1)} %get-tuple-element.349.cos_ref, ...), custom_call_target="tpu_custom_call" | custom-call | flops 1048576 | bytes 65536 | tf_op jit(solution)/shard_map/attend_forward/pallas_call | solution.py:110
  197.6 22.3 %collective-permute-done.14 = bf16[1024,512]{1,0:T(8,128)(2,1)S(1)} collective-permute-done((bf16[1024,512]{1,0:T(8,128)(2,1)S(1)}, bf16[1024,512]{1,0:T(8,128)(2,1)S(1)}, u32[]{:S(2)}, u32[]{:S(2)}) %collective-permute-start.14) | collective-permute-done | bytes 1048608 | tf_op jit(solution)/shard_map/ppermute | solution.py:448
  223.7 4.1 collective-permute-done.16
  227.8 2.9 multiply_reduce_fusion.2
  237.5 30.8 %ffn_pair.4 = (bf16[512,2048]{1,0:T(8,128)(2,1)}, bf16[512,2048]{1,0:T(8,128)(2,1)}, bf16[2048,2048]{1,0:T(8,128)(2,1)}, bf16[2048,2048]{1,0:T(8,128)(2,1)}, bf1...) custom-call(s32[1]{0:T(128)} %constant.126.clone.1.place_ref, ...), custom_call_target="tpu_custom_call" | custom-call | flops 1048576 | bytes 65536 | tf_op jit(solution)/shard_map/ffn_pair/pallas_call | solution.py:336
  268.3 13.1 %collective-permute-done.17.xa_ref = bf16[512,2048]{1,0:T(8,128)(2,1)} collective-permute-done((bf16[512,2048]{1,0:T(8,128)(2,1)S(1)}, bf16[512,2048]{1,0:T(8,128)(2,1)}, u32[]{:S(2)}, u32[]{:S(2)}) %collective-permute-start.17) | collective-permute-done | bytes 2097184 | tf_op jit(solution)/shard_map/ppermute | solution.py:448
  290.4 30.6 %ffn_pair.5 = (bf16[512,2048]{1,0:T(8,128)(2,1)}, bf16[512,2048]{1,0:T(8,128)(2,1)}, bf16[2048,2048]{1,0:T(8,128)(2,1)}, bf16[2048,2048]{1,0:T(8,128)(2,1)}, bf1...) custom-call(s32[1]{0:T(128)} %constant.127.clone.1.place_ref, ...), custom_call_target="tpu_custom_call", output_to_operand_aliasing={{2}: (8, {}), {3}: (9, {}), {4}: (10, {}), {5}: (11, {}), {... | custom-call | flops 1048576 | bytes 65536 | tf_op jit(solution)/shard_map/ffn_pair/pallas_call | solution.py:336
  321.8 3.8 collective-permute-done.23.xb_ref
  326.9 31.1 %ffn_pair.6 = (bf16[512,2048]{1,0:T(8,128)(2,1)}, bf16[512,2048]{1,0:T(8,128)(2,1)}, bf16[2048,2048]{1,0:T(8,128)(2,1)}, bf16[2048,2048]{1,0:T(8,128)(2,1)}, bf1...) custom-call(s32[1]{0:T(128)} %constant.125.clone.1.place_ref, ...), custom_call_target="tpu_custom_call", output_to_operand_aliasing={{2}: (8, {}), {3}: (9, {}), {4}: (10, {}), {5}: (11, {}), {... | custom-call | flops 1048576 | bytes 65536 | tf_op jit(solution)/shard_map/ffn_pair/pallas_call | solution.py:336
  359.0 5.2 collective-permute-done.25
  372.4 30.8 %ffn_pair.7 = (bf16[512,2048]{1,0:T(8,128)(2,1)}, bf16[512,2048]{1,0:T(8,128)(2,1)}, bf16[2048,2048]{1,0:T(8,128)(2,1)}, bf16[2048,2048]{1,0:T(8,128)(2,1)}, bf1...) custom-call(s32[1]{0:T(128)} %constant.128.clone.1.place_ref, ...), custom_call_target="tpu_custom_call", output_to_operand_aliasing={{2}: (8, {}), {3}: (9, {}), {4}: (10, {}), {5}: (11, {}), {... | custom-call | flops 1048576 | bytes 65536 | tf_op jit(solution)/shard_map/ffn_pair/pallas_call | solution.py:336
  403.3 2.8 fusion.17
  414.9 17.1 %convolution_convert_fusion.2 = bf16[704,2048]{1,0:T(8,128)(2,1)} fusion(bf16[4096,704]{1,0:T(8,128)(2,1)S(1)} %bitcast.165, bf16[4096,2048]{1,0:T(8,128)(2,1)} %get-tuple-element.254), kind=kOutput, calls=%fused_computation.37 | convolution fusion | flops 11812601856 | bytes 25427968 | tf_op jit(solution)/shard_map/dot_general | solution.py:435
  432.1 18.9 %convolution_convert_fusion.3 = bf16[704,2048]{1,0:T(8,128)(2,1)} fusion(bf16[4096,704]{1,0:T(8,128)(2,1)} %get-tuple-element.241, bf16[4096,2048]{1,0:T(8,128)(2,1)} %get-tuple-element.242), kind=kOutput, calls=%fused_computation.38 | convolution fusion | flops 11812601856 | bytes 25427968 | tf_op jit(solution)/shard_map/dot_general | solution.py:435
  451.0 4.5 add_convert_fusion.10
  455.6 7.8 add_convert_fusion.1
  464.5 4.0 multiply_reduce_fusion
  468.6 7.1 fusion.66
  475.7 4.5 collective-permute-done.35
  480.2 8.3 %convolution_convert_fusion = bf16[1024,2048]{1,0:T(8,128)(2,1)} fusion(bf16[1024,1024]{1,0:T(8,128)(2,1)S(1)} %copy-done.5, bf16[512,2048]{1,0:T(8,128)(2,1)} %collective-permute-done.35, bf16[512,2048]{1,0:T(8,128)(2,1)} %get-tuple-element.310), kind=kOutput, calls=%fused_computation.35 | convolution fusion | flops 4305453056 | bytes 10485760 | tf_op jit(solution)/shard_map/dot_general | solution.py:435
  488.6 5.2 all-to-all-start.2
  493.8 18.7 %convolution_convert_fusion.1 = bf16[704,2048]{1,0:T(8,128)(2,1)} fusion(bf16[4096,704]{1,0:T(8,128)(2,1)} %get-tuple-element.253, bf16[4096,2048]{1,0:T(8,128)(2,1)} %get-tuple-element.254), kind=kOutput, calls=%fused_computation.36 | convolution fusion | flops 11812601856 | bytes 25427968 | tf_op jit(solution)/shard_map/dot_general | solution.py:435
  516.1 8.0 %fusion.16.g_ref = bf16[1024,1024]{1,0:T(8,128)(2,1)S(1)} fusion(bf16[1024,2048]{1,0:T(8,128)(2,1)} %copy-done.45, bf16[512,2048]{1,0:T(8,128)(2,1)} %collective-permute-done.35, bf16[512,2048]{1,0:T(8,128)(2,1)} %get-tuple-element.310), kind=kOutput, calls=%fused_computation.58 | convolution fusion | flops 4304404480 | bytes 10485760 | tf_op jit(solution)/shard_map/dot_general | solution.py:439
  524.2 12.3 %attend_backward.2 = (bf16[1024,512]{1,0:T(8,128)(2,1)S(1)}, f32[4096,256]{1,0:T(8,128)}) custom-call(s32[2]{0:T(128)S(1)} %copy-done.25, s32[16]{0:T(128)S(1)} %bitcast.150, bf16[4,128,2048]{2,1,0:T(8,128)(2,1)S(1)} %copy-done.7, bf16[1024,1024]{1,0:T(8,128)(2,1)S(1)} %fusion.16.g_ref, bf16[1024,1024]{1,0:T(8,128)(2,1)} %copy-done.4, ...), custom_call_target="tpu_custom_call" | custom-call | flops 1048576 | bytes 65536 | tf_op jit(solution)/shard_map/attend_backward/pallas_call | solution.py:228
  537.6 26.7 %collective-permute-done.36 = bf16[256,2048]{1,0:T(8,128)(2,1)S(1)} collective-permute-done((bf16[256,2048]{1,0:T(8,128)(2,1)}, bf16[256,2048]{1,0:T(8,128)(2,1)S(1)}, u32[]{:S(2)}, u32[]{:S(2)}) %collective-permute-start.36) | collective-permute-done | bytes 1048608 | tf_op jit(solution)/shard_map/ppermute | solution.py:448
  565.2 3.1 fusion.19
  568.7 2.9 fusion.20
  573.1 3.8 convolution_convert_fusion.5
  576.9 4.4 all-to-all-start.3
  581.3 3.3 convert_reduce_fusion
  586.2 3.6 collective-permute-start.42
  589.7 17.8 %collective-permute-start.41 = (bf16[64,2048]{1,0:T(8,128)(2,1)S(1)}, bf16[64,2048]{1,0:T(8,128)(2,1)}, u32[]{:S(2)}, u32[]{:S(2)}) collective-permute-start(bf16[64,2048]{1,0:T(8,128)(2,1)S(1)} %get-tuple-element.327), channel_id=1, source_target_pairs={{0,2},{1,3},{2,0},{3,1},{4,6},{5,7},{6,4},{7,5},{8,10},{9,11},{10,... | collective-permute-start | bytes 786440 | tf_op jit(solution)/shard_map/ppermute | solution.py:448
  607.5 11.7 %attend_backward.3 = (bf16[1024,512]{1,0:T(8,128)(2,1)S(1)}, bf16[2048,256]{1,0:T(8,128)(2,1)S(1)}, bf16[2048,256]{1,0:T(8,128)(2,1)S(1)}) custom-call(s32[2]{0:T(128)S(1)} %copy-done.25, s32[16]{0:T(128)S(1)} %bitcast.151, bf16[4,128,2048]{2,1,0:T(8,128)(2,1)S(1)} %copy-done.7, bf16[1024,1024]{1,0:T(8,128)(2,1)} %copy-done.8, bf16[1024,1024]{1,0:T(8,128)(2,1)} %copy-done.4, ...), custom_call_target="tpu_custom_call" | custom-call | flops 1048576 | bytes 65536 | tf_op jit(solution)/shard_map/attend_backward/pallas_call | solution.py:228
  622.1 17.3 %collective-permute-done.41 = bf16[64,2048]{1,0:T(8,128)(2,1)} collective-permute-done((bf16[64,2048]{1,0:T(8,128)(2,1)S(1)}, bf16[64,2048]{1,0:T(8,128)(2,1)}, u32[]{:S(2)}, u32[]{:S(2)}) %collective-permute-start.41) | collective-permute-done | bytes 262176 | tf_op jit(solution)/shard_map/ppermute | solution.py:448
  655.4 5.9 convolution_convert_fusion.4
  661.4 5.8 collective-permute-done.45
  673.8 3.8 all-to-all-start.4
  685.1 5.9 add_convert_fusion
  691.5 2.9 reduce
  696.1 3.1 collective-permute-start.51
  699.2 17.9 %collective-permute-start.50 = (bf16[2,64,512]{2,1,0:T(8,128)(2,1)}, bf16[2,64,512]{2,1,0:T(8,128)(2,1)}, u32[]{:S(2)}, u32[]{:S(2)}) collective-permute-start(bf16[2,64,512]{2,1,0:T(8,128)(2,1)} %get-tuple-element.345), channel_id=1, source_target_pairs={{0,2},{1,3},{2,0},{3,1},{4,6},{5,7},{6,4},{7,5},{8,10},{9,11},{10,... | collective-permute-start | bytes 393224 | tf_op jit(solution)/shard_map/ppermute | solution.py:448
  717.1 4.7 all-to-all-start.5
  721.8 7.1 select_convert_fusion
  734.2 6.1 fusion.6
  740.4 4.8 fusion.10
  745.2 14.5 %all-to-all-done.5 = bf16[8,256,768]{2,1,0:T(8,128)(2,1)} async-done(((bf16[8,256,768]{2,1,0:T(8,128)(2,1)}), bf16[8,256,768]{2,1,0:T(8,128)(2,1)}, u32[]{:S(2)}, u32[]{:S(2)}) %all-to-all-start.5) | async-done | bytes 3145760 | tf_op jit(solution)/shard_map/all_to_all | solution.py:710
  759.7 3.6 reduce.1
  766.7 7.3 collective-permute-start.53
  775.7 9.9 %collective-permute-done.53 = bf16[2,64,768]{2,1,0:T(8,128)(2,1)} collective-permute-done((bf16[2,64,768]{2,1,0:T(8,128)(2,1)}, bf16[2,64,768]{2,1,0:T(8,128)(2,1)}, u32[]{:S(2)}, u32[]{:S(2)}) %collective-permute-start.53) | collective-permute-done | bytes 196640 | tf_op jit(solution)/shard_map/ppermute | solution.py:448
  (369 shorter events, 175.1 us)
Async XLA Ops:
  7.2 71.7 %all-gather.8.cloned.1.call-start = ((), (), s32[]{:S(2)}) async-start(), calls=%async_computation.13 | async-start | bytes 2969600 | tf_op jit(solution)/shard_map/all_gather | solution.py:562
  13.7 223.8 %all-gather.6.cloned.1.call-start = ((), (), s32[]{:S(2)}) async-start(), calls=%async_computation.12 | async-start | bytes 10813440 | tf_op jit(solution)/shard_map/all_gather | solution.py:590
  18.3 48.9 %collective-permute-start = (bf16[512,2048]{1,0:T(8,128)(2,1)}, bf16[512,2048]{1,0:T(8,128)(2,1)}, u32[]{:S(2)}, u32[]{:S(2)}) collective-permute-start(bf16[512,2048]{1,0:T(8,128)(2,1)} %bitcast_select_fusion.ga_ref), channel_id=1, source_target_pairs={{0,8},{8,0},{16,24},{24,16},{1,9},{9,1},{17,25},{25,17},{2,10},{10... | collective-permute-start | bytes 6291464 | tf_op jit(solution)/shard_map/ppermute | solution.py:448
  21.3 47.4 %collective-permute-start.1 = (bf16[512,2048]{1,0:T(8,128)(2,1)}, bf16[512,2048]{1,0:T(8,128)(2,1)}, u32[]{:S(2)}, u32[]{:S(2)}) collective-permute-start(bf16[512,2048]{1,0:T(8,128)(2,1)} %bitcast_select_fusion.ga_ref), channel_id=1, source_target_pairs={{0,16},{8,24},{16,0},{24,8},{1,17},{9,25},{17,1},{25,9},{2,18},{10... | collective-permute-start | bytes 6291464 | tf_op jit(solution)/shard_map/ppermute | solution.py:448
  22.8 53.6 %collective-permute-start.9 = (bf16[512,2048]{1,0:T(8,128)(2,1)S(1)}, bf16[512,2048]{1,0:T(8,128)(2,1)}, u32[]{:S(2)}, u32[]{:S(2)}) collective-permute-start(bf16[512,2048]{1,0:T(8,128)(2,1)S(1)} %bitcast.166), channel_id=1, source_target_pairs={{0,4},{4,0},{1,5},{5,1},{2,6},{6,2},{3,7},{7,3},{8,12},{12,8},{9,1... | collective-permute-start | bytes 6291464 | tf_op jit(solution)/shard_map/ppermute | solution.py:448
  71.0 28.0 %collective-permute-start.2 = (bf16[256,2048]{1,0:T(8,128)(2,1)}, bf16[256,2048]{1,0:T(8,128)(2,1)}, u32[]{:S(2)}, u32[]{:S(2)}) collective-permute-start(bf16[256,2048]{1,0:T(8,128)(2,1)} %slice.151), channel_id=1, source_target_pairs={{0,16},{8,24},{16,0},{24,8},{1,17},{9,25},{17,1},{25,9},{2,18},{10... | collective-permute-start | bytes 3145736 | tf_op jit(solution)/shard_map/ppermute | solution.py:448
  74.8 26.4 %collective-permute-start.3 = (bf16[256,2048]{1,0:T(8,128)(2,1)}, bf16[256,2048]{1,0:T(8,128)(2,1)}, u32[]{:S(2)}, u32[]{:S(2)}) collective-permute-start(bf16[256,2048]{1,0:T(8,128)(2,1)} %slice.152), channel_id=1, source_target_pairs={{0,8},{8,0},{16,24},{24,16},{1,9},{9,1},{17,25},{25,17},{2,10},{10... | collective-permute-start | bytes 3145736 | tf_op jit(solution)/shard_map/ppermute | solution.py:448
  81.0 31.4 %all-to-all-start = ((bf16[4,4,128,256]{3,2,1,0:T(8,128)(2,1)}), bf16[4,4,128,256]{3,2,1,0:T(8,128)(2,1)}, u32[]{:S(2)}, u32[]{:S(2)}) async-start(bf16[4,4,128,256]{3,2,1,0:T(8,128)(2,1)} %broadcast_in_dim.82), calls=%async_computation | async-start | bytes 2097152 | tf_op jit(solution)/shard_map/all_to_all | solution.py:458
  101.2 31.0 %collective-permute-start.4 = (bf16[2048,256]{1,0:T(8,128)(2,1)}, bf16[2048,256]{1,0:T(8,128)(2,1)}, u32[]{:S(2)}, u32[]{:S(2)}) collective-permute-start(bf16[2048,256]{1,0:T(8,128)(2,1)} %bitcast.12), channel_id=1, source_target_pairs={{0,8},{8,0},{16,24},{24,16},{1,9},{9,1},{17,25},{25,17},{2,10},{10... | collective-permute-start | bytes 3145736 | tf_op jit(solution)/shard_map/ppermute | solution.py:448
  101.7 30.5 %collective-permute-start.5 = (bf16[2048,256]{1,0:T(8,128)(2,1)}, bf16[2048,256]{1,0:T(8,128)(2,1)}, u32[]{:S(2)}, u32[]{:S(2)}) collective-permute-start(bf16[2048,256]{1,0:T(8,128)(2,1)} %bitcast.12), channel_id=1, source_target_pairs={{0,16},{8,24},{16,0},{24,8},{1,17},{9,25},{17,1},{25,9},{2,18},{10... | collective-permute-start | bytes 3145736 | tf_op jit(solution)/shard_map/ppermute | solution.py:448
  132.2 41.0 %collective-permute-start.6 = (bf16[512,2048]{1,0:T(8,128)(2,1)}, bf16[512,2048]{1,0:T(8,128)(2,1)}, u32[]{:S(2)}, u32[]{:S(2)}) collective-permute-start(bf16[512,2048]{1,0:T(8,128)(2,1)} %bitcast_select_fusion.ga_ref), channel_id=1, source_target_pairs={{0,4},{4,0},{1,5},{5,1},{2,6},{6,2},{3,7},{7,3},{8,12},{12,8},{9,1... | collective-permute-start | bytes 6291464 | tf_op jit(solution)/shard_map/ppermute | solution.py:448
  133.5 19.3 %all-to-all-start.1 = ((bf16[4,512,256]{2,1,0:T(8,128)(2,1)}), bf16[4,512,256]{2,1,0:T(8,128)(2,1)}, u32[]{:S(2)}, u32[]{:S(2)}) async-start(bf16[4,512,256]{2,1,0:T(8,128)(2,1)} %broadcast_in_dim.83), calls=%async_computation.1 | async-start | bytes 2097152 | tf_op jit(solution)/shard_map/all_to_all | solution.py:458
  137.8 503.8 %reduce-scatter.4.cloned.1.call-start = ((), (), s32[]{:S(2)}) async-start(), calls=%async_computation.9 | async-start | bytes 3604480 | tf_op jit(solution)/shard_map/reduce_scatter | solution.py:687
  140.0 23.6 %collective-permute-start.11 = (bf16[1024,256]{1,0:T(8,128)(2,1)}, bf16[1024,256]{1,0:T(8,128)(2,1)S(1)}, u32[]{:S(2)}, u32[]{:S(2)}) collective-permute-start(bf16[1024,256]{1,0:T(8,128)(2,1)} %slice.154), channel_id=1, source_target_pairs={{0,8},{8,0},{16,24},{24,16},{1,9},{9,1},{17,25},{25,17},{2,10},{10... | collective-permute-start | bytes 1572872 | tf_op jit(solution)/shard_map/ppermute | solution.py:448
  152.8 20.2 %collective-permute-start.12 = (bf16[2048,256]{1,0:T(8,128)(2,1)}, bf16[2048,256]{1,0:T(8,128)(2,1)}, u32[]{:S(2)}, u32[]{:S(2)}) collective-permute-start(bf16[2048,256]{1,0:T(8,128)(2,1)} %bitcast.19), channel_id=1, source_target_pairs={{0,4},{4,0},{1,5},{5,1},{2,6},{6,2},{3,7},{7,3},{8,12},{12,8},{9,1... | collective-permute-start | bytes 3145736 | tf_op jit(solution)/shard_map/ppermute | solution.py:448
  154.8 14.7 %collective-permute-start.10 = (bf16[1024,256]{1,0:T(8,128)(2,1)}, bf16[1024,256]{1,0:T(8,128)(2,1)}, u32[]{:S(2)}, u32[]{:S(2)}) collective-permute-start(bf16[1024,256]{1,0:T(8,128)(2,1)} %slice.153), channel_id=1, source_target_pairs={{0,16},{8,24},{16,0},{24,8},{1,17},{9,25},{17,1},{25,9},{2,18},{10... | collective-permute-start | bytes 1572872 | tf_op jit(solution)/shard_map/ppermute | solution.py:448
  161.5 21.6 %collective-permute-start.7 = (bf16[512,2048]{1,0:T(8,128)(2,1)}, bf16[512,2048]{1,0:T(8,128)(2,1)S(1)}, u32[]{:S(2)}, u32[]{:S(2)}) collective-permute-start(bf16[512,2048]{1,0:T(8,128)(2,1)} %collective-permute-done.ga_ref), channel_id=1, source_target_pairs={{0,4},{4,0},{1,5},{5,1},{2,6},{6,2},{3,7},{7,3},{8,12},{12,8},{9,1... | collective-permute-start | bytes 6291464 | tf_op jit(solution)/shard_map/ppermute | solution.py:448
  163.5 19.6 %collective-permute-start.8 = (bf16[512,2048]{1,0:T(8,128)(2,1)}, bf16[512,2048]{1,0:T(8,128)(2,1)S(1)}, u32[]{:S(2)}, u32[]{:S(2)}) collective-permute-start(bf16[512,2048]{1,0:T(8,128)(2,1)} %collective-permute-done.1.ga_ref), channel_id=1, source_target_pairs={{0,4},{4,0},{1,5},{5,1},{2,6},{6,2},{3,7},{7,3},{8,12},{12,8},{9,1... | collective-permute-start | bytes 6291464 | tf_op jit(solution)/shard_map/ppermute | solution.py:448
  171.6 26.1 %collective-permute-start.13 = (bf16[1024,512]{1,0:T(8,128)(2,1)S(1)}, bf16[1024,512]{1,0:T(8,128)(2,1)S(1)}, u32[]{:S(2)}, u32[]{:S(2)}) collective-permute-start(bf16[1024,512]{1,0:T(8,128)(2,1)S(1)} %reshape.239), channel_id=1, source_target_pairs={{0,8},{8,0},{16,24},{24,16},{1,9},{9,1},{17,25},{25,17},{2,10},{10... | collective-permute-start | bytes 3145736 | tf_op jit(solution)/shard_map/ppermute | solution.py:448
  173.0 47.0 %collective-permute-start.14 = (bf16[1024,512]{1,0:T(8,128)(2,1)S(1)}, bf16[1024,512]{1,0:T(8,128)(2,1)S(1)}, u32[]{:S(2)}, u32[]{:S(2)}) collective-permute-start(bf16[1024,512]{1,0:T(8,128)(2,1)S(1)} %reshape.239), channel_id=1, source_target_pairs={{0,16},{8,24},{16,0},{24,8},{1,17},{9,25},{17,1},{25,9},{2,18},{10... | collective-permute-start | bytes 3145736 | tf_op jit(solution)/shard_map/ppermute | solution.py:448
  173.3 46.7 %collective-permute-start.15 = (bf16[1024,512]{1,0:T(8,128)(2,1)S(1)}, bf16[1024,512]{1,0:T(8,128)(2,1)S(1)}, u32[]{:S(2)}, u32[]{:S(2)}) collective-permute-start(bf16[1024,512]{1,0:T(8,128)(2,1)S(1)} %reshape.239), channel_id=1, source_target_pairs={{0,24},{8,16},{16,8},{24,0},{1,25},{9,17},{17,9},{25,1},{2,26},{10... | collective-permute-start | bytes 3145736 | tf_op jit(solution)/shard_map/ppermute | solution.py:448
  233.1 4.4 collective-permute-start.19
  233.3 48.0 %collective-permute-start.17 = (bf16[512,2048]{1,0:T(8,128)(2,1)S(1)}, bf16[512,2048]{1,0:T(8,128)(2,1)}, u32[]{:S(2)}, u32[]{:S(2)}) collective-permute-start(bf16[512,2048]{1,0:T(8,128)(2,1)S(1)} %multiply_convert_fusion.xa_ref), channel_id=1, source_target_pairs={{0,8},{8,0},{16,24},{24,16},{1,9},{9,1},{17,25},{25,17},{2,10},{10... | collective-permute-start | bytes 6291464 | tf_op jit(solution)/shard_map/ppermute | solution.py:448
  234.0 47.7 %collective-permute-start.18 = (bf16[512,2048]{1,0:T(8,128)(2,1)S(1)}, bf16[512,2048]{1,0:T(8,128)(2,1)}, u32[]{:S(2)}, u32[]{:S(2)}) collective-permute-start(bf16[512,2048]{1,0:T(8,128)(2,1)S(1)} %multiply_convert_fusion.xa_ref), channel_id=1, source_target_pairs={{0,16},{8,24},{16,0},{24,8},{1,17},{9,25},{17,1},{25,9},{2,18},{10... | collective-permute-start | bytes 6291464 | tf_op jit(solution)/shard_map/ppermute | solution.py:448
  281.7 7.3 collective-permute-start.22
  283.0 38.0 %collective-permute-start.20 = (bf16[256,2048]{1,0:T(8,128)(2,1)S(1)}, bf16[256,2048]{1,0:T(8,128)(2,1)S(1)}, u32[]{:S(2)}, u32[]{:S(2)}) collective-permute-start(bf16[256,2048]{1,0:T(8,128)(2,1)S(1)} %slice.163), channel_id=1, source_target_pairs={{0,16},{8,24},{16,0},{24,8},{1,17},{9,25},{17,1},{25,9},{2,18},{10... | collective-permute-start | bytes 3145736 | tf_op jit(solution)/shard_map/ppermute | solution.py:448
  285.8 35.3 %collective-permute-start.21 = (bf16[256,2048]{1,0:T(8,128)(2,1)S(1)}, bf16[256,2048]{1,0:T(8,128)(2,1)S(1)}, u32[]{:S(2)}, u32[]{:S(2)}) collective-permute-start(bf16[256,2048]{1,0:T(8,128)(2,1)S(1)} %slice.164), channel_id=1, source_target_pairs={{0,8},{8,0},{16,24},{24,16},{1,9},{9,1},{17,25},{25,17},{2,10},{10... | collective-permute-start | bytes 3145736 | tf_op jit(solution)/shard_map/ppermute | solution.py:448
  288.9 32.9 %collective-permute-start.24 = (bf16[512,2048]{1,0:T(8,128)(2,1)S(1)}, bf16[512,2048]{1,0:T(8,128)(2,1)S(1)}, u32[]{:S(2)}, u32[]{:S(2)}) collective-permute-start(bf16[512,2048]{1,0:T(8,128)(2,1)S(1)} %constant_dynamic-update-slice_fusion.9.ga_ref), channel_id=1, source_target_pairs={{0,4},{4,0},{1,5},{5,1},{2,6},{6,2},{3,7},{7,3},{8,12},{12,8},{9,1... | collective-permute-start | bytes 6291464 | tf_op jit(solution)/shard_map/ppermute | solution.py:448
  358.0 6.1 collective-permute-start.25
  358.5 10.5 %collective-permute-start.29 = (bf16[512,2048]{1,0:T(8,128)(2,1)S(1)}, bf16[512,2048]{1,0:T(8,128)(2,1)S(1)}, u32[]{:S(2)}, u32[]{:S(2)}) collective-permute-start(bf16[512,2048]{1,0:T(8,128)(2,1)S(1)} %copy-done.74), channel_id=1, source_target_pairs={{0,4},{4,0},{1,5},{5,1},{2,6},{6,2},{3,7},{7,3},{8,12},{12,8},{9,1... | collective-permute-start | bytes 6291464 | tf_op jit(solution)/shard_map/ppermute | solution.py:448
  358.6 12.5 %collective-permute-start.28 = (bf16[512,2048]{1,0:T(8,128)(2,1)}, bf16[512,2048]{1,0:T(8,128)(2,1)S(1)}, u32[]{:S(2)}, u32[]{:S(2)}) collective-permute-start(bf16[512,2048]{1,0:T(8,128)(2,1)} %collective-permute-done.18.xa_ref), channel_id=1, source_target_pairs={{0,4},{4,0},{1,5},{5,1},{2,6},{6,2},{3,7},{7,3},{8,12},{12,8},{9,1... | collective-permute-start | bytes 6291464 | tf_op jit(solution)/shard_map/ppermute | solution.py:448
  366.8 36.4 %collective-permute-start.26 = (bf16[256,2048]{1,0:T(8,128)(2,1)S(1)}, bf16[256,2048]{1,0:T(8,128)(2,1)S(1)}, u32[]{:S(2)}, u32[]{:S(2)}) collective-permute-start(bf16[256,2048]{1,0:T(8,128)(2,1)S(1)} %get-tuple-element.329), channel_id=1, source_target_pairs={{0,8},{8,0},{16,24},{24,16},{1,9},{9,1},{17,25},{25,17},{2,10},{10... | collective-permute-start | bytes 3145736 | tf_op jit(solution)/shard_map/ppermute | solution.py:448
  368.5 34.7 %collective-permute-start.27 = (bf16[256,2048]{1,0:T(8,128)(2,1)S(1)}, bf16[256,2048]{1,0:T(8,128)(2,1)S(1)}, u32[]{:S(2)}, u32[]{:S(2)}) collective-permute-start(bf16[256,2048]{1,0:T(8,128)(2,1)S(1)} %get-tuple-element.328), channel_id=1, source_target_pairs={{0,16},{8,24},{16,0},{24,8},{1,17},{9,25},{17,1},{25,9},{2,18},{10... | collective-permute-start | bytes 3145736 | tf_op jit(solution)/shard_map/ppermute | solution.py:448
  403.2 4.4 collective-permute-start.30
  412.4 38.6 %collective-permute-start.31 = (bf16[2048,2048]{1,0:T(8,128)(2,1)}, bf16[2048,2048]{1,0:T(8,128)(2,1)}, u32[]{:S(2)}, u32[]{:S(2)}) collective-permute-start(bf16[2048,2048]{1,0:T(8,128)(2,1)} %get-tuple-element.239), channel_id=1, source_target_pairs={{0,4},{4,0},{1,5},{5,1},{2,6},{6,2},{3,7},{7,3},{8,12},{12,8},{9,1... | collective-permute-start | bytes 25165832 | tf_op jit(solution)/shard_map/ppermute | solution.py:448
  412.6 50.9 %collective-permute-start.34 = (bf16[512,2048]{1,0:T(8,128)(2,1)}, bf16[512,2048]{1,0:T(8,128)(2,1)S(1)}, u32[]{:S(2)}, u32[]{:S(2)}) collective-permute-start(bf16[512,2048]{1,0:T(8,128)(2,1)} %get-tuple-element.240), channel_id=1, source_target_pairs={{0,4},{4,0},{1,5},{5,1},{2,6},{6,2},{3,7},{7,3},{8,12},{12,8},{9,1... | collective-permute-start | bytes 6291464 | tf_op jit(solution)/shard_map/ppermute | solution.py:448
  412.9 50.5 %collective-permute-start.32 = (bf16[512,2048]{1,0:T(8,128)(2,1)}, bf16[512,2048]{1,0:T(8,128)(2,1)}, u32[]{:S(2)}, u32[]{:S(2)}) collective-permute-start(bf16[512,2048]{1,0:T(8,128)(2,1)} %fusion.17), channel_id=1, source_target_pairs={{0,8},{8,0},{16,24},{24,16},{1,9},{9,1},{17,25},{25,17},{2,10},{10... | collective-permute-start | bytes 6291464 | tf_op jit(solution)/shard_map/ppermute | solution.py:448
  414.3 49.1 %collective-permute-start.33 = (bf16[512,2048]{1,0:T(8,128)(2,1)}, bf16[512,2048]{1,0:T(8,128)(2,1)}, u32[]{:S(2)}, u32[]{:S(2)}) collective-permute-start(bf16[512,2048]{1,0:T(8,128)(2,1)} %fusion.18), channel_id=1, source_target_pairs={{0,16},{8,24},{16,0},{24,8},{1,17},{9,25},{17,1},{25,9},{2,18},{10... | collective-permute-start | bytes 6291464 | tf_op jit(solution)/shard_map/ppermute | solution.py:448
  432.1 209.6 %reduce-scatter.8.cloned.1.call-start = ((), (), s32[]{:S(2)}) async-start(), calls=%async_computation.11 | async-start | bytes 3604480 | tf_op jit(solution)/shard_map/reduce_scatter | solution.py:687
  475.7 4.5 collective-permute-start.35
  488.6 76.7 %all-to-all-start.2 = ((bf16[4,256,2048]{2,1,0:T(8,128)(2,1)}), bf16[4,256,2048]{2,1,0:T(8,128)(2,1)}, u32[]{:S(2)}, u32[]{:S(2)}) async-start(bf16[4,256,2048]{2,1,0:T(8,128)(2,1)} %bitcast.177), calls=%async_computation.2 | async-start | bytes 8388608 | tf_op jit(solution)/shard_map/all_to_all | solution.py:716
  493.8 147.9 %reduce-scatter.6.cloned.1.call-start = ((), (), s32[]{:S(2)}) async-start(), calls=%async_computation.10 | async-start | bytes 3604480 | tf_op jit(solution)/shard_map/reduce_scatter | solution.py:687
  512.7 51.6 %collective-permute-start.36 = (bf16[256,2048]{1,0:T(8,128)(2,1)}, bf16[256,2048]{1,0:T(8,128)(2,1)S(1)}, u32[]{:S(2)}, u32[]{:S(2)}) collective-permute-start(bf16[256,2048]{1,0:T(8,128)(2,1)} %get-tuple-element.259), channel_id=1, source_target_pairs={{0,8},{8,0},{16,24},{24,16},{1,9},{9,1},{17,25},{25,17},{2,10},{10... | collective-permute-start | bytes 3145736 | tf_op jit(solution)/shard_map/ppermute | solution.py:448
  514.6 50.6 %collective-permute-start.37 = (bf16[256,2048]{1,0:T(8,128)(2,1)}, bf16[256,2048]{1,0:T(8,128)(2,1)}, u32[]{:S(2)}, u32[]{:S(2)}) collective-permute-start(bf16[256,2048]{1,0:T(8,128)(2,1)} %get-tuple-element.260), channel_id=1, source_target_pairs={{0,16},{8,24},{16,0},{24,8},{1,17},{9,25},{17,1},{25,9},{2,18},{10... | collective-permute-start | bytes 3145736 | tf_op jit(solution)/shard_map/ppermute | solution.py:448
  568.3 73.3 %collective-permute-start.38 = (bf16[512,2048]{1,0:T(8,128)(2,1)}, bf16[512,2048]{1,0:T(8,128)(2,1)}, u32[]{:S(2)}, u32[]{:S(2)}) collective-permute-start(bf16[512,2048]{1,0:T(8,128)(2,1)} %fusion.19), channel_id=1, source_target_pairs={{0,8},{8,0},{16,24},{24,16},{1,9},{9,1},{17,25},{25,17},{2,10},{10... | collective-permute-start | bytes 6291464 | tf_op jit(solution)/shard_map/ppermute | solution.py:448
  571.6 70.0 %collective-permute-start.39 = (bf16[512,2048]{1,0:T(8,128)(2,1)}, bf16[512,2048]{1,0:T(8,128)(2,1)}, u32[]{:S(2)}, u32[]{:S(2)}) collective-permute-start(bf16[512,2048]{1,0:T(8,128)(2,1)} %fusion.20), channel_id=1, source_target_pairs={{0,16},{8,24},{16,0},{24,8},{1,17},{9,25},{17,1},{25,9},{2,18},{10... | collective-permute-start | bytes 6291464 | tf_op jit(solution)/shard_map/ppermute | solution.py:448
  576.9 64.7 %all-to-all-start.3 = ((bf16[8,256,512]{2,1,0:T(8,128)(2,1)}), bf16[8,256,512]{2,1,0:T(8,128)(2,1)}, u32[]{:S(2)}, u32[]{:S(2)}) async-start(bf16[8,256,512]{2,1,0:T(8,128)(2,1)} %bitcast.184), calls=%async_computation.6 | async-start | bytes 4194304 | tf_op jit(solution)/shard_map/all_to_all | solution.py:710
  586.2 36.0 %collective-permute-start.42 = (bf16[64,2048]{1,0:T(8,128)(2,1)S(1)}, bf16[64,2048]{1,0:T(8,128)(2,1)}, u32[]{:S(2)}, u32[]{:S(2)}) collective-permute-start(bf16[64,2048]{1,0:T(8,128)(2,1)S(1)} %get-tuple-element.326), channel_id=1, source_target_pairs={{0,3},{1,2},{2,1},{3,0},{4,7},{5,6},{6,5},{7,4},{8,11},{9,10},{10,... | collective-permute-start | bytes 786440 | tf_op jit(solution)/shard_map/ppermute | solution.py:448
  589.7 49.7 %collective-permute-start.41 = (bf16[64,2048]{1,0:T(8,128)(2,1)S(1)}, bf16[64,2048]{1,0:T(8,128)(2,1)}, u32[]{:S(2)}, u32[]{:S(2)}) collective-permute-start(bf16[64,2048]{1,0:T(8,128)(2,1)S(1)} %get-tuple-element.327), channel_id=1, source_target_pairs={{0,2},{1,3},{2,0},{3,1},{4,6},{5,7},{6,4},{7,5},{8,10},{9,11},{10,... | collective-permute-start | bytes 786440 | tf_op jit(solution)/shard_map/ppermute | solution.py:448
  607.5 32.0 %collective-permute-start.40 = (bf16[64,2048]{1,0:T(8,128)(2,1)S(1)}, bf16[64,2048]{1,0:T(8,128)(2,1)}, u32[]{:S(2)}, u32[]{:S(2)}) collective-permute-start(bf16[64,2048]{1,0:T(8,128)(2,1)S(1)} %get-tuple-element.325), channel_id=1, source_target_pairs={{0,1},{1,0},{2,3},{3,2},{4,5},{5,4},{6,7},{7,6},{8,9},{9,8},{10,11... | collective-permute-start | bytes 786440 | tf_op jit(solution)/shard_map/ppermute | solution.py:448
  651.9 9.5 %collective-permute-start.44 = (bf16[512,256]{0,1:T(8,128)(2,1)}, bf16[512,256]{0,1:T(8,128)(2,1)S(1)}, u32[]{:S(2)}, u32[]{:S(2)}) collective-permute-start(bf16[512,256]{0,1:T(8,128)(2,1)} %bitcast.30), channel_id=1, source_target_pairs={{0,8},{8,0},{16,24},{24,16},{1,9},{9,1},{17,25},{25,17},{2,10},{10... | collective-permute-start | bytes 786440 | tf_op jit(solution)/shard_map/ppermute | solution.py:448
  653.3 13.9 %collective-permute-start.45 = (bf16[512,256]{0,1:T(8,128)(2,1)}, bf16[512,256]{0,1:T(8,128)(2,1)S(1)}, u32[]{:S(2)}, u32[]{:S(2)}) collective-permute-start(bf16[512,256]{0,1:T(8,128)(2,1)} %bitcast.31), channel_id=1, source_target_pairs={{0,16},{8,24},{16,0},{24,8},{1,17},{9,25},{17,1},{25,9},{2,18},{10... | collective-permute-start | bytes 786440 | tf_op jit(solution)/shard_map/ppermute | solution.py:448
  654.8 13.1 %collective-permute-start.46 = (bf16[512,256]{0,1:T(8,128)(2,1)}, bf16[512,256]{0,1:T(8,128)(2,1)}, u32[]{:S(2)}, u32[]{:S(2)}) collective-permute-start(bf16[512,256]{0,1:T(8,128)(2,1)} %bitcast.32), channel_id=1, source_target_pairs={{0,24},{8,16},{16,8},{24,0},{1,25},{9,17},{17,9},{25,1},{2,26},{10... | collective-permute-start | bytes 786440 | tf_op jit(solution)/shard_map/ppermute | solution.py:448
  670.0 9.3 %collective-permute-start.47 = (bf16[512,256]{0,1:T(8,128)(2,1)}, bf16[512,256]{0,1:T(8,128)(2,1)}, u32[]{:S(2)}, u32[]{:S(2)}) collective-permute-start(bf16[512,256]{0,1:T(8,128)(2,1)} %pad_maximum_fusion.11), channel_id=1, source_target_pairs={{0,4},{4,0},{1,5},{5,1},{2,6},{6,2},{3,7},{7,3},{8,12},{12,8},{9,1... | collective-permute-start | bytes 786440 | tf_op jit(solution)/shard_map/ppermute | solution.py:448
  673.8 43.3 %all-to-all-start.4 = ((bf16[8,3,176,256]{3,2,1,0:T(8,128)(2,1)}), bf16[8,3,176,256]{3,2,1,0:T(8,128)(2,1)S(1)}, u32[]{:S(2)}, u32[]{:S(2)}) async-start(bf16[8,3,176,256]{3,2,1,0:T(8,128)(2,1)} %copy-done.3), calls=%async_computation.7 | async-start | bytes 4325376 | tf_op jit(solution)/shard_map/all_to_all | solution.py:753
  691.0 43.2 %collective-permute-start.48 = (bf16[512,2048]{1,0:T(8,128)(2,1)}, bf16[512,2048]{1,0:T(8,128)(2,1)}, u32[]{:S(2)}, u32[]{:S(2)}) collective-permute-start(bf16[512,2048]{1,0:T(8,128)(2,1)} %add_convert_fusion), channel_id=1, source_target_pairs={{0,4},{4,0},{1,5},{5,1},{2,6},{6,2},{3,7},{7,3},{8,12},{12,8},{9,1... | collective-permute-start | bytes 6291464 | tf_op jit(solution)/shard_map/ppermute | solution.py:448
  696.1 33.6 %collective-permute-start.51 = (bf16[2,64,512]{2,1,0:T(8,128)(2,1)}, bf16[2,64,512]{2,1,0:T(8,128)(2,1)S(1)}, u32[]{:S(2)}, u32[]{:S(2)}) collective-permute-start(bf16[2,64,512]{2,1,0:T(8,128)(2,1)} %get-tuple-element.344), channel_id=1, source_target_pairs={{0,3},{1,2},{2,1},{3,0},{4,7},{5,6},{6,5},{7,4},{8,11},{9,10},{10,... | collective-permute-start | bytes 393224 | tf_op jit(solution)/shard_map/ppermute | solution.py:448
  699.2 30.5 %collective-permute-start.50 = (bf16[2,64,512]{2,1,0:T(8,128)(2,1)}, bf16[2,64,512]{2,1,0:T(8,128)(2,1)}, u32[]{:S(2)}, u32[]{:S(2)}) collective-permute-start(bf16[2,64,512]{2,1,0:T(8,128)(2,1)} %get-tuple-element.345), channel_id=1, source_target_pairs={{0,2},{1,3},{2,0},{3,1},{4,6},{5,7},{6,4},{7,5},{8,10},{9,11},{10,... | collective-permute-start | bytes 393224 | tf_op jit(solution)/shard_map/ppermute | solution.py:448
  717.1 12.6 %collective-permute-start.49 = (bf16[2,64,512]{2,1,0:T(8,128)(2,1)S(1)}, bf16[2,64,512]{2,1,0:T(8,128)(2,1)}, u32[]{:S(2)}, u32[]{:S(2)}) collective-permute-start(bf16[2,64,512]{2,1,0:T(8,128)(2,1)S(1)} %get-tuple-element.343), channel_id=1, source_target_pairs={{0,1},{1,0},{2,3},{3,2},{4,5},{5,4},{6,7},{7,6},{8,9},{9,8},{10,11... | collective-permute-start | bytes 393224 | tf_op jit(solution)/shard_map/ppermute | solution.py:448
  717.1 42.6 %all-to-all-start.5 = ((bf16[8,256,768]{2,1,0:T(8,128)(2,1)}), bf16[8,256,768]{2,1,0:T(8,128)(2,1)}, u32[]{:S(2)}, u32[]{:S(2)}) async-start(bf16[8,256,768]{2,1,0:T(8,128)(2,1)} %bitcast.169), calls=%async_computation.8 | async-start | bytes 6291456 | tf_op jit(solution)/shard_map/all_to_all | solution.py:710
  765.2 10.5 %collective-permute-start.54 = (bf16[2,64,768]{2,1,0:T(8,128)(2,1)}, bf16[2,64,768]{2,1,0:T(8,128)(2,1)}, u32[]{:S(2)}, u32[]{:S(2)}) collective-permute-start(bf16[2,64,768]{2,1,0:T(8,128)(2,1)} %get-tuple-element.339), channel_id=1, source_target_pairs={{0,3},{1,2},{2,1},{3,0},{4,7},{5,6},{6,5},{7,4},{8,11},{9,10},{10,... | collective-permute-start | bytes 589832 | tf_op jit(solution)/shard_map/ppermute | solution.py:448
  766.7 19.0 %collective-permute-start.53 = (bf16[2,64,768]{2,1,0:T(8,128)(2,1)}, bf16[2,64,768]{2,1,0:T(8,128)(2,1)}, u32[]{:S(2)}, u32[]{:S(2)}) collective-permute-start(bf16[2,64,768]{2,1,0:T(8,128)(2,1)} %get-tuple-element.340), channel_id=1, source_target_pairs={{0,2},{1,3},{2,0},{3,1},{4,6},{5,7},{6,4},{7,5},{8,10},{9,11},{10,... | collective-permute-start | bytes 589832 | tf_op jit(solution)/shard_map/ppermute | solution.py:448
  774.0 11.7 %collective-permute-start.52 = (bf16[2,64,768]{2,1,0:T(8,128)(2,1)S(1)}, bf16[2,64,768]{2,1,0:T(8,128)(2,1)}, u32[]{:S(2)}, u32[]{:S(2)}) collective-permute-start(bf16[2,64,768]{2,1,0:T(8,128)(2,1)S(1)} %get-tuple-element.338), channel_id=1, source_target_pairs={{0,1},{1,0},{2,3},{3,2},{4,5},{5,4},{6,7},{7,6},{8,9},{9,8},{10,11... | collective-permute-start | bytes 589832 | tf_op jit(solution)/shard_map/ppermute | solution.py:448
  775.7 16.3 %collective-permute-start.55 = (bf16[64,1024]{1,0:T(8,128)(2,1)}, bf16[64,1024]{1,0:T(8,128)(2,1)}, u32[]{:S(2)}, u32[]{:S(2)}) collective-permute-start(bf16[64,1024]{1,0:T(8,128)(2,1)} %get-tuple-element.320), channel_id=1, source_target_pairs={{0,4},{4,0},{1,5},{5,1},{2,6},{6,2},{3,7},{7,3},{8,12},{12,8},{9,1... | collective-permute-start | bytes 393224 | tf_op jit(solution)/shard_map/ppermute | solution.py:448
  (80 other events, 938.2 us)
Sparse Core Ops, SparseCore 0:
  13.8 53.4 all-gather.7
  68.9 152.7 all-gather.5
  432.2 69.1 reduce-scatter.3
  503.5 56.0 reduce-scatter.7
  561.7 72.6 reduce-scatter.5

commit v4 on v3

--- a/solution.py
+++ b/solution.py
@@ -409,6 +409,34 @@
     )(first, second)
 
 
+def sum_chips(plane_ref, dealt_ref, *out_refs):
+    rows = out_refs[0].shape[1]
+    for k, out_ref in enumerate(out_refs):
+        start = pl.multiple_of((plane_ref[0] ^ k) * rows, rows)
+        for core in range(2):
+            total = dealt_ref[core, pl.ds(start, rows), :].astype(F32)
+            for place in range(2 + core, dealt_ref.shape[0], 2):
+                total = total + dealt_ref[place, pl.ds(start, rows), :].astype(F32)
+            out_ref[core] = total.astype(BF16)
+
+
+def split_planes(dealt, plane, planes):
+    rows, columns = dealt.shape[1] // planes, dealt.shape[2]
+    return pl.pallas_call(
+        sum_chips,
+        grid_spec=pltpu.PrefetchScalarGridSpec(
+            num_scalar_prefetch=1,
+            grid=(1,),
+            in_specs=[pl.BlockSpec(dealt.shape, lambda i, *_: (0, 0, 0), pipeline_mode=pl.Buffered(1))],
+            out_specs=[pl.BlockSpec((2, rows, columns), lambda i, *_: (0, 0, 0))] * planes,
+        ),
+        out_shape=[jax.ShapeDtypeStruct((2, rows, columns), BF16)] * planes,
+        compiler_params=pltpu.CompilerParams(vmem_limit_bytes=32 * 2**20),
+        cost_estimate=pl.CostEstimate(flops=2**20, bytes_accessed=dealt.size * 3, transcendentals=0),
+        name="sum_chips",
+    )(plane.reshape(1).astype(jnp.int32), dealt)
+
+
 def angles(positions):
     frequency = ROPE_BASE ** (-2.0 * jnp.arange(HALF, dtype=F32) / HD)
     phase_angle = frequency[:, None] * positions.astype(F32)[None, :]
@@ -469,11 +497,12 @@
         return ()
     value, first, second = lax.optimization_barrier(near)
     half = value.shape[0] // 2
-    return exchange(first[:half], "chip", 2), exchange(second[half:], "chip", 1)
+    first, second = lax.optimization_barrier((first[:half], second[half:]))
+    return exchange(first, "chip", 2), exchange(second, "chip", 1)
 
 
 def gather_far(near):
-    halves = send_far(near)
+    halves = lax.optimization_barrier(send_far(near))
     return near + [jnp.concatenate(halves, axis=0)] if halves else near
 
 
@@ -507,9 +536,9 @@
 
 
 def add_half(term, passing, which):
-    start = which * passing.shape[0]
-    half = term[start : start + passing.shape[0]].astype(F32) + passing.astype(F32)
-    return lax.dynamic_update_slice(term, half.astype(BF16), (start, 0))
+    pad = term.shape[0] - passing.shape[0]
+    passing = jnp.pad(passing, ((pad, 0) if which else (0, pad), (0, 0)))
+    return (term.astype(F32) + passing.astype(F32)).astype(BF16)
 
 
 def lay_columns(chunks, chip):
@@ -579,14 +608,13 @@
     live_rows = (own_pos < length)[:, None]
     grad_out = jnp.where(live_rows, cotangent[0], jnp.zeros((), BF16))
     grad_near = after(gather_near(grad_out), pieces)
-    grad_far = send_far(grad_near)
     kv_full = spread_chips(after(kv_piece, grad_near)).swapaxes(0, 1).reshape(model_dim, 2 * HD)
     kv_full = with_layout_constraint(kv_full, Layout((0, 1)))
-    query_near = gather_near(after(query_piece, grad_far))
+    query_near = gather_near(after(query_piece, grad_near))
     query_half = lay_columns(gather_far(query_near), chip)
     grad_others = [swap_core(chunk) for chunk in after(grad_near, query_near)]
-    out_piece = after(out_piece, query_half)
-    out_chunks = [out_piece] + [exchange(out_piece, "chip", k) for k in range(1, chips)]
+    grad_far = send_far(after(grad_near, query_half, grad_others))
+    out_chunks = spread_chips(after(out_piece, query_half))
     ffn_weights = lax.all_gather(pieces, "fsdp", axis=0)
 
     offsets = jnp.arange(blk, dtype=jnp.int32)
@@ -606,22 +634,24 @@
     key_value = matmul(both_normed[:local_len], kv_full)
     key_rot = rotate(key_value[:, :HD], own_cosine, own_sine)
     local_kv = jnp.concatenate([key_rot, key_value[:, HD:]], axis=1).astype(BF16)
-    slot_kv = spread_chips(local_kv).reshape(-1, 2 * HD)
+    slot_kv = after(spread_chips(local_kv), query_half).reshape(-1, 2 * HD)
     slot_kv = jnp.concatenate([slot_kv, swap_core(slot_kv)], axis=0)
 
     heads = wide // HD
     queries = matmul(both_normed, query_half)
-    scalars = after(jnp.stack([own, length]).astype(jnp.int32), grad_others)
+    scalars = jnp.stack([own, length]).astype(jnp.int32)
     attended, lse, turned = attention_forward(
         scalars, order, queries, cosine, sine_vals, slot_kv, blk
     )
 
-    attended, lse, turned, out_chunks = lax.optimization_barrier((attended, lse, turned, out_chunks))
+    attended, lse, turned, out_chunks, grad_far = lax.optimization_barrier(
+        (attended, lse, turned, out_chunks, grad_far)
+    )
     grad_mine = list(grad_near)
     if grad_far:
         grad_mine.append(jnp.concatenate(grad_far, axis=0))
         grad_others.append(swap_core(grad_mine[3]))
-    out_half = lay_columns(out_chunks, chip)
+    out_half = out_chunks.swapaxes(0, 1).reshape(wide, model_dim)
     branch_other = swap_core(matmul(attended[local_len:], out_half).astype(BF16))
     residual = tokens_flat + matmul(attended[:local_len], out_half) + branch_other.astype(F32)
     inverse_two = lax.rsqrt(jnp.mean(residual * residual, axis=1, keepdims=True) + EPSILON)
@@ -650,15 +680,15 @@
         normed_far = after(normed_far, own_first)
         own_last, other_last, kept = pair(3, jnp.concatenate(normed_far, axis=0), kept)
         last = add_cores(own_last, other_last)
-        first = add_cores(own_first, other_first)
-        kept = after(kept, last, first)
+        other_first = swap_core(other_first)
+        kept = after(kept, last, other_first)
         passing = reduce_far(last)
         own_second, other_second, kept = pair(2, normed_near[2], kept)
         passing, own_second, other_second, kept = lax.optimization_barrier(
             (passing, own_second, other_second, kept)
         )
-        first = add_half(first, passing[1], 1)
-        second = add_half(add_cores(own_second, other_second), passing[0], 0)
+        first = add_half(own_first.astype(F32) + other_first.astype(F32), passing[1], 1)
+        second = add_half(own_second.astype(F32) + swap_core(other_second).astype(F32), passing[0], 0)
         kept = after(kept, first, second)
         arrived = [exchange(first, "chip", 1), exchange(second, "chip", 2), back_other]
     else:
@@ -709,10 +739,6 @@
     def deal_rows(terms):
         return lax.all_to_all(terms.reshape(places, planes * (depth // places), -1), ("chip", "core"), 0, 0, tiled=False)
 
-    def by_plane(dealt):
-        total = jnp.sum(dealt.astype(F32).reshape(chips, 2, planes, depth // places, -1), axis=0)
-        return total.swapaxes(0, 1).astype(BF16)
-
     branch_dealt = lax.all_to_all(branch_terms, "chip", 0, 0, tiled=False)
     up_term = contract_rows(*after((dup_all, normed_all), branch_terms)).astype(BF16)
     if chips == 4:
@@ -742,7 +768,7 @@
     )
     kv_parts = with_layout_constraint(add_cores(kv_mine, kv_other), Layout((0, 1)))
     kv_parts = kv_parts.reshape(chips, local_len, 2 * HD)
-    kv_parts = [at(kv_parts, chip ^ k) for k in range(chips)]
+    kv_parts = [with_layout_constraint(at(kv_parts, chip ^ k), Layout((0, 1))) for k in range(chips)]
     kv_arrived = [exchange(kv_parts[k], "chip", k) for k in range(1, chips)]
     out_arrived, ffn_terms, grad_query_b, query_sums_a = after(
         (out_arrived, ffn_terms, grad_query_b, query_sums_a), kv_parts
@@ -750,7 +776,7 @@
     query_terms_b = contract_rows(both_normed, grad_query_b).astype(BF16)
     kv_arrived = after(kv_arrived, query_terms_b)
     ffn_terms = pack_units(after(ffn_terms, query_sums_a), places)
-    ffn_terms = lax.all_to_all(ffn_terms, ("chip", "core"), 0, 0, tiled=False)
+    ffn_terms = lax.all_to_all(after(ffn_terms, kv_arrived), ("chip", "core"), 0, 0, tiled=False)
     kv_total = kv_parts[0].astype(F32)
     for term in kv_arrived:
         kv_total = kv_total + term.astype(F32)
@@ -780,7 +806,8 @@
     last_terms = jnp.concatenate([query_terms_b, kv_grads], axis=1)
     last_terms = with_layout_constraint(last_terms, Layout((0, 1)))
     last_dealt = deal_rows(after(last_terms, ffn_terms))
-    query_sums_a = sum_planes(by_plane(after(query_sums_a, last_terms)), plane)
+    first_planes = split_planes(after(query_sums_a, last_terms), plane, planes)
+    first_arrived = [exchange(first_planes[k], "fsdp", k) for k in range(1, planes)]
     both_query = after(both_query, last_terms)
     other_one = swap_core(normed_one_term(slice(local_len, None)).astype(BF16))
 
@@ -798,10 +825,13 @@
     output = jnp.where(live_rows, residual + ffn_out, 0.0).astype(BF16)
 
     ffn_grads = turn_units(after(ffn_terms, last_terms))
-    last_dealt = after(last_dealt, grad_tokens, output, query_sums_a, ffn_grads)
-    last_planes = by_plane(last_dealt)
-    last_arrived = [exchange(at(last_planes, plane ^ k), "fsdp", k) for k in range(1, planes)]
-    last_sums = at(last_planes, plane).astype(F32)
+    last_dealt = after(last_dealt, grad_tokens, output, ffn_grads)
+    last_planes = split_planes(last_dealt, plane, planes)
+    last_arrived = [exchange(last_planes[k], "fsdp", k) for k in range(1, planes)]
+    query_sums_a = first_planes[0].astype(F32)
+    for term in after(first_arrived, last_planes[0]):
+        query_sums_a = query_sums_a + term.astype(F32)
+    last_sums = last_planes[0].astype(F32)
     for term in last_arrived:
         last_sums = last_sums + term.astype(F32)
     query_sums = jnp.concatenate([query_sums_a, last_sums[:, :, : -2 * HD]], axis=2)

time: 806 us -> 785 us (0.974); the launches traced: 801 us -> 772 us
  Pallas kernels: 161 us -> 209 us
  starting transfers between devices: 113 us -> 78.1 us
  waiting for transfers between devices: 210 us -> 178 us
  other arithmetic: 105 us -> 89.5 us
    ppermute x56 -> x53, starting transfers between devices: 85.7 us -> 46.3 us  [exchange(): return lax.ppermute(value, axis, [(i, i ^ distance) for i in range(size)])]
    ppermute x56 -> x53, waiting for transfers between devices: 181 us -> 146 us  [exchange(): return lax.ppermute(value, axis, [(i, i ^ distance) for i in range(size)])]
    pallas_call x2, Pallas kernels: 24.1 us -> 52 us  [attention_backward(): pl.pallas_call(functools.partial(attend_backward, group, blk, last), grid...]
    pallas_call x1, Pallas kernels: 9.72 us -> 27.1 us  [attention_forward(): pl.pallas_call(functools.partial(attend_forward, heads, blk), grid_spec=p...]
    all_to_all x2, waiting for transfers between devices: 14.5 us -> 30.7 us  [deal_rows(): lax.all_to_all(terms.reshape(places, planes * (depth // places), -1), ('c...]
    all_to_all x2 -> x3, waiting for transfers between devices: 13.8 us -> 1.63 us  [spread_chips(): return lax.all_to_all(copies, 'chip', 0, 0, tiled=False)]
    dynamic_update_slice x4 -> x0, other arithmetic: 11.3 us -> none  [add_half(): return lax.dynamic_update_slice(term, half.astype(BF16), (start, 0))]
    convert_element_type x0 -> x4, other arithmetic: none -> 10.7 us  [add_half(): return (term.astype(F32) + passing.astype(F32)).astype(BF16)]
  transfers between devices with their start and end apart: 67 -> 65, of which waited for: 25 -> 27; matrix products, arithmetic and copies ran while one was open for 31% -> 32% of each run, Pallas kernels for 16% -> 23%
where the time goes in v4:
time: 785 us; the launch traced here: 772 us
  Pallas kernels  209 us (27%)
  waiting for transfers between devices  178 us (23%)
  matrix products  118 us (15%)
  other arithmetic  89.5 us (11%)
  local copies, waits for them, and re-layouts  82.3 us (10%)
  starting transfers between devices  78.1 us (10%)
  between operations  16.4 us (2%)
    ppermute x53, waiting for transfers between devices, exchange(): return lax.ppermute(value, axis, [(i, i ^ distance) for i in range(size)])  146 us
    pallas_call x4, Pallas kernels, ffn_pair(): pl.pallas_call(functools.partial(ffn_rows, count, tiles), grid_spec=pltpu...  123 us
    dot_general x7, matrix products, contract_rows(): lax.dot_general(left, right, (((0,), (0,)), ((), ())), preferred_element_...  74.7 us
    pallas_call x2, Pallas kernels, attention_backward(): pl.pallas_call(functools.partial(attend_backward, group, blk, last), grid...  52 us
    ppermute x53, starting transfers between devices, exchange(): return lax.ppermute(value, axis, [(i, i ^ distance) for i in range(size)])  46.3 us
    unnamed x182, local copies, waits for them, and re-layouts  33.8 us
    all_to_all x2, waiting for transfers between devices, deal_rows(): lax.all_to_all(terms.reshape(places, planes * (depth // places), -1), ('c...  30.7 us
    pallas_call x1, Pallas kernels, attention_forward(): pl.pallas_call(functools.partial(attend_forward, heads, blk), grid_spec=p...  27.1 us
  transfers between devices with their start and end apart: 65, of which 27 were waited for; matrix products, arithmetic and copies ran while one was open for 32% of the time, Pallas kernels for 23%

profile of v4, /device:TPU:0, one launch (start us, length us, event | category | flops | bytes accessed | tf_op | source)
XLA Modules:
  0.0 771.5 jit_solution(3758375836225171420)
XLA Ops:
  10.9 2.7 concatenate.62
  15.2 3.1 bitcast_select_fusion.ga_ref
  18.3 2.9 collective-permute-start.1
  22.8 4.1 constant_dynamic-slice_fusion.2
  30.3 2.9 constant_dynamic-slice_fusion.4
  35.4 3.0 pad_maximum_fusion.4
  40.5 26.6 %collective-permute-done.1.ga_ref = bf16[512,2048]{1,0:T(8,128)(2,1)} collective-permute-done((bf16[512,2048]{1,0:T(8,128)(2,1)}, bf16[512,2048]{1,0:T(8,128)(2,1)}, u32[]{:S(2)}, u32[]{:S(2)}) %collective-permute-start.1) | collective-permute-done | bytes 2097184 | tf_op jit(solution)/shard_map/ppermute | solution.py:476
  73.0 4.3 all-to-all-start
  77.3 3.2 fusion.60
  84.7 6.1 fusion.2
  98.9 4.4 all-to-all-start.1
  103.4 11.5 %collective-permute-done.3 = bf16[2048,256]{1,0:T(8,128)(2,1)} collective-permute-done((bf16[2048,256]{1,0:T(8,128)(2,1)}, bf16[2048,256]{1,0:T(8,128)(2,1)}, u32[]{:S(2)}, u32[]{:S(2)}) %collective-permute-start.3) | collective-permute-done | bytes 1048608 | tf_op jit(solution)/shard_map/ppermute | solution.py:476
  131.8 3.1 collective-permute-done.5
  140.2 5.0 all-to-all-start.2
  152.0 6.3 fusion.63.q_ref
  159.7 27.1 %attend_forward.1 = (bf16[1024,1024]{1,0:T(8,128)(2,1)S(1)}, f32[4,1,2048]{2,1,0:T(1,128)S(1)}, bf16[4,128,2048]{2,1,0:T(8,128)(2,1)S(1)}) custom-call(s32[2]{0:T(128)S(1)} %pad_add_fusion.scal_ref, s32[16]{0:T(128)S(1)} %bitcast.131, f32[1024,1024]{1,0:T(8,128)S(1)} %fusion.63.q_ref, f32[64,1024]{1,0:T(8,128)S(1)} %copy.103.cos_ref, ...), custom_call_target="tpu_custom_call" | custom-call | flops 1048576 | bytes 65536 | tf_op jit(solution)/shard_map/attend_forward/pallas_call | solution.py:110
  189.5 25.0 %collective-permute-done.11 = bf16[256,2048]{1,0:T(8,128)(2,1)} collective-permute-done((bf16[256,2048]{1,0:T(8,128)(2,1)S(1)}, bf16[256,2048]{1,0:T(8,128)(2,1)}, u32[]{:S(2)}, u32[]{:S(2)}) %collective-permute-start.11) | collective-permute-done | bytes 1048608 | tf_op jit(solution)/shard_map/ppermute | solution.py:476
  214.5 4.7 convolution_convert_fusion.6
  219.3 4.1 collective-permute-done.13
  223.5 5.1 multiply_reduce_fusion.2
  235.3 30.8 %ffn_pair.4 = (bf16[512,2048]{1,0:T(8,128)(2,1)}, bf16[512,2048]{1,0:T(8,128)(2,1)}, bf16[2048,2048]{1,0:T(8,128)(2,1)}, bf16[2048,2048]{1,0:T(8,128)(2,1)}, bf1...) custom-call(s32[1]{0:T(128)} %constant.106.clone.1.place_ref, ...), custom_call_target="tpu_custom_call" | custom-call | flops 1048576 | bytes 65536 | tf_op jit(solution)/shard_map/ffn_pair/pallas_call | solution.py:336
  266.2 13.0 %collective-permute-done.14.xa_ref = bf16[512,2048]{1,0:T(8,128)(2,1)} collective-permute-done((bf16[512,2048]{1,0:T(8,128)(2,1)S(1)}, bf16[512,2048]{1,0:T(8,128)(2,1)}, u32[]{:S(2)}, u32[]{:S(2)}) %collective-permute-start.14) | collective-permute-done | bytes 2097184 | tf_op jit(solution)/shard_map/ppermute | solution.py:476
  289.4 30.6 %ffn_pair.5 = (bf16[512,2048]{1,0:T(8,128)(2,1)}, bf16[512,2048]{1,0:T(8,128)(2,1)}, bf16[2048,2048]{1,0:T(8,128)(2,1)}, bf16[2048,2048]{1,0:T(8,128)(2,1)}, bf1...) custom-call(s32[1]{0:T(128)} %constant.107.clone.1.place_ref, ...), custom_call_target="tpu_custom_call", output_to_operand_aliasing={{2}: (8, {}), {3}: (9, {}), {4}: (10, {}), {5}: (11, {}), {... | custom-call | flops 1048576 | bytes 65536 | tf_op jit(solution)/shard_map/ffn_pair/pallas_call | solution.py:336
  320.7 3.8 collective-permute-done.20.xb_ref
  325.8 31.1 %ffn_pair.6 = (bf16[512,2048]{1,0:T(8,128)(2,1)}, bf16[512,2048]{1,0:T(8,128)(2,1)}, bf16[2048,2048]{1,0:T(8,128)(2,1)}, bf16[2048,2048]{1,0:T(8,128)(2,1)}, bf1...) custom-call(s32[1]{0:T(128)} %constant.105.clone.1.place_ref, ...), custom_call_target="tpu_custom_call", output_to_operand_aliasing={{2}: (8, {}), {3}: (9, {}), {4}: (10, {}), {5}: (11, {}), {... | custom-call | flops 1048576 | bytes 65536 | tf_op jit(solution)/shard_map/ffn_pair/pallas_call | solution.py:336
  357.9 3.5 collective-permute-done.22
  368.7 30.7 %ffn_pair.7 = (bf16[512,2048]{1,0:T(8,128)(2,1)}, bf16[512,2048]{1,0:T(8,128)(2,1)}, bf16[2048,2048]{1,0:T(8,128)(2,1)}, bf16[2048,2048]{1,0:T(8,128)(2,1)}, bf1...) custom-call(s32[1]{0:T(128)} %constant.108.clone.1.place_ref, ...), custom_call_target="tpu_custom_call", output_to_operand_aliasing={{2}: (8, {}), {3}: (9, {}), {4}: (10, {}), {5}: (11, {}), {... | custom-call | flops 1048576 | bytes 65536 | tf_op jit(solution)/shard_map/ffn_pair/pallas_call | solution.py:336
  408.8 17.1 %convolution_convert_fusion.2 = bf16[704,2048]{1,0:T(8,128)(2,1)} fusion(bf16[4096,704]{1,0:T(8,128)(2,1)S(1)} %copy-done.28, bf16[4096,2048]{1,0:T(8,128)(2,1)} %get-tuple-element.284), kind=kOutput, calls=%fused_computation.39 | convolution fusion | flops 11812601856 | bytes 25427968 | tf_op jit(solution)/shard_map/dot_general | solution.py:463
  426.0 18.9 %convolution_convert_fusion.3 = bf16[704,2048]{1,0:T(8,128)(2,1)} fusion(bf16[4096,704]{1,0:T(8,128)(2,1)} %get-tuple-element.271, bf16[4096,2048]{1,0:T(8,128)(2,1)} %get-tuple-element.272), kind=kOutput, calls=%fused_computation.40 | convolution fusion | flops 11812601856 | bytes 25427968 | tf_op jit(solution)/shard_map/dot_general | solution.py:463
  444.9 4.4 add_convert_fusion.10
  449.3 7.8 %add_convert_fusion.3 = (bf16[512,2048]{1,0:T(8,128)(2,1)}, bf16[512,2048]{1,0:T(8,128)(2,1)}, bf16[512,2048]{1,0:T(8,128)(2,1)}) fusion(bf16[2048,2048]{1,0:T(8,128)(2,1)} %collective-permute-done.28, bf16[2048,2048]{1,0:T(8,128)(2,1)} %get-tuple-element.268), kind=kLoop, calls=%fused_computation.29 | loop fusion | flops 12582912 | bytes 18874368 | tf_op jit(solution)/shard_map/convert_element_type | solution.py:706
  458.2 4.0 multiply_reduce_fusion
  462.3 7.1 fusion.58
  469.4 4.5 collective-permute-done.32
  473.9 8.4 %convolution_convert_fusion = bf16[1024,2048]{1,0:T(8,128)(2,1)} fusion(bf16[1024,1024]{1,0:T(8,128)(2,1)S(1)} %copy-done.9, bf16[512,2048]{1,0:T(8,128)(2,1)} %collective-permute-done.32, bf16[512,2048]{1,0:T(8,128)(2,1)} %get-tuple-element.352), kind=kOutput, calls=%fused_computation.37 | convolution fusion | flops 4305453056 | bytes 10485760 | tf_op jit(solution)/shard_map/dot_general | solution.py:463
  482.3 5.2 all-to-all-start.3
  487.6 19.2 %convolution_convert_fusion.1 = bf16[704,2048]{1,0:T(8,128)(2,1)} fusion(bf16[4096,704]{1,0:T(8,128)(2,1)} %get-tuple-element.283, bf16[4096,2048]{1,0:T(8,128)(2,1)} %get-tuple-element.284), kind=kOutput, calls=%fused_computation.38 | convolution fusion | flops 11812601856 | bytes 25427968 | tf_op jit(solution)/shard_map/dot_general | solution.py:463
  510.3 8.0 %fusion.16.g_ref = bf16[1024,1024]{1,0:T(8,128)(2,1)S(1)} fusion(bf16[1024,2048]{0,1:T(8,128)(2,1)} %bitcast.21, bf16[512,2048]{1,0:T(8,128)(2,1)} %collective-permute-done.32, bf16[512,2048]{1,0:T(8,128)(2,1)} %get-tuple-element.352), kind=kOutput, calls=%fused_computation.56 | convolution fusion | flops 4304404480 | bytes 10485760 | tf_op jit(solution)/shard_map/dot_general | solution.py:467
  518.3 26.3 %attend_backward.2 = (bf16[1024,512]{1,0:T(8,128)(2,1)S(1)}, f32[4096,256]{1,0:T(8,128)}) custom-call(s32[2]{0:T(128)S(1)} %copy-done.24, s32[16]{0:T(128)S(1)} %bitcast.132, bf16[4,128,2048]{2,1,0:T(8,128)(2,1)S(1)} %copy-done.11, bf16[1024,1024]{1,0:T(8,128)(2,1)S(1)} %fusion.16.g_ref, bf16[1024,1024]{1,0:T(8,128)(2,1)} %copy-done.8, ...), custom_call_target="tpu_custom_call" | custom-call | flops 1048576 | bytes 65536 | tf_op jit(solution)/shard_map/attend_backward/pallas_call | solution.py:228
  545.6 12.2 %collective-permute-done.33 = bf16[256,2048]{1,0:T(8,128)(2,1)S(1)} collective-permute-done((bf16[256,2048]{1,0:T(8,128)(2,1)}, bf16[256,2048]{1,0:T(8,128)(2,1)S(1)}, u32[]{:S(2)}, u32[]{:S(2)}) %collective-permute-start.33) | collective-permute-done | bytes 1048608 | tf_op jit(solution)/shard_map/ppermute | solution.py:476
  558.8 4.0 add_convert_fusion.2
  566.7 3.7 convolution_convert_fusion.5
  570.4 4.4 all-to-all-start.4
  574.8 3.3 convert_reduce_fusion
  579.6 3.7 collective-permute-start.39
  584.1 25.8 %attend_backward.3 = (bf16[1024,512]{1,0:T(8,128)(2,1)S(1)}, bf16[2048,256]{1,0:T(8,128)(2,1)S(1)}, bf16[2048,256]{1,0:T(8,128)(2,1)S(1)}) custom-call(s32[2]{0:T(128)S(1)} %copy-done.24, s32[16]{0:T(128)S(1)} %bitcast.133, bf16[4,128,2048]{2,1,0:T(8,128)(2,1)S(1)} %copy-done.11, bf16[1024,1024]{1,0:T(8,128)(2,1)} %copy-done.12, ...), custom_call_target="tpu_custom_call" | custom-call | flops 1048576 | bytes 65536 | tf_op jit(solution)/shard_map/attend_backward/pallas_call | solution.py:228
  612.7 7.9 %collective-permute-done.38 = bf16[64,2048]{1,0:T(8,128)(2,1)} collective-permute-done((bf16[64,2048]{1,0:T(8,128)(2,1)S(1)}, bf16[64,2048]{1,0:T(8,128)(2,1)}, u32[]{:S(2)}, u32[]{:S(2)}) %collective-permute-start.38) | collective-permute-done | bytes 262176 | tf_op jit(solution)/shard_map/ppermute | solution.py:476
  622.8 13.0 %all-to-all-done.4.dealt_ref = bf16[8,256,512]{2,1,0:T(8,128)(2,1)} async-done(((bf16[8,256,512]{2,1,0:T(8,128)(2,1)}), bf16[8,256,512]{2,1,0:T(8,128)(2,1)}, u32[]{:S(2)}, u32[]{:S(2)}) %all-to-all-start.4) | async-done | bytes 2097184 | tf_op jit(solution)/shard_map/all_to_all | solution.py:740
  636.0 2.8 collective-permute-done.40
  644.0 3.8 convolution_convert_fusion.4
  649.6 4.9 collective-permute-done.42
  662.0 3.8 all-to-all-start.5
  667.5 3.6 convolution_convert_fusion.7
  674.6 6.0 add_convert_fusion
  686.7 2.7 collective-permute-start.47
  689.6 3.8 fusion.30
  694.8 4.4 all-to-all-start.6
  699.3 7.3 select_convert_fusion
  708.9 5.9 fusion.6
  714.8 4.5 fusion.10
  719.4 17.7 %all-to-all-done.6.dealt_ref = bf16[8,256,768]{2,1,0:T(8,128)(2,1)S(1)} async-done(((bf16[8,256,768]{2,1,0:T(8,128)(2,1)}), bf16[8,256,768]{2,1,0:T(8,128)(2,1)S(1)}, u32[]{:S(2)}, u32[]{:S(2)}) %all-to-all-start.6) | async-done | bytes 3145760 | tf_op jit(solution)/shard_map/all_to_all | solution.py:740
  741.3 3.6 collective-permute-start.51
  746.8 4.2 collective-permute-done.51
  751.0 6.8 collective-permute-done.50
  (375 shorter events, 161.6 us)
Async XLA Ops:
  7.2 63.7 %all-gather.8.cloned.1.call-start = ((), (), s32[]{:S(2)}) async-start(), calls=%async_computation.14 | async-start | bytes 2969600 | tf_op jit(solution)/shard_map/all_gather | solution.py:591
  13.7 221.7 %all-gather.6.cloned.1.call-start = ((), (), s32[]{:S(2)}) async-start(), calls=%async_computation.13 | async-start | bytes 10813440 | tf_op jit(solution)/shard_map/all_gather | solution.py:618
  18.3 48.9 %collective-permute-start.1 = (bf16[512,2048]{1,0:T(8,128)(2,1)}, bf16[512,2048]{1,0:T(8,128)(2,1)}, u32[]{:S(2)}, u32[]{:S(2)}) collective-permute-start(bf16[512,2048]{1,0:T(8,128)(2,1)} %bitcast_select_fusion.ga_ref), channel_id=1, source_target_pairs={{0,8},{8,0},{16,24},{24,16},{1,9},{9,1},{17,25},{25,17},{2,10},{10... | collective-permute-start | bytes 6291464 | tf_op jit(solution)/shard_map/ppermute | solution.py:476
  21.2 47.4 %collective-permute-start.2 = (bf16[512,2048]{1,0:T(8,128)(2,1)}, bf16[512,2048]{1,0:T(8,128)(2,1)}, u32[]{:S(2)}, u32[]{:S(2)}) collective-permute-start(bf16[512,2048]{1,0:T(8,128)(2,1)} %bitcast_select_fusion.ga_ref), channel_id=1, source_target_pairs={{0,16},{8,24},{16,0},{24,8},{1,17},{9,25},{17,1},{25,9},{2,18},{10... | collective-permute-start | bytes 6291464 | tf_op jit(solution)/shard_map/ppermute | solution.py:476
  22.8 45.9 %collective-permute-start = (bf16[512,2048]{1,0:T(8,128)(2,1)S(1)}, bf16[512,2048]{1,0:T(8,128)(2,1)}, u32[]{:S(2)}, u32[]{:S(2)}) collective-permute-start(bf16[512,2048]{1,0:T(8,128)(2,1)S(1)} %bitcast.146), channel_id=1, source_target_pairs={{0,4},{4,0},{1,5},{5,1},{2,6},{6,2},{3,7},{7,3},{8,12},{12,8},{9,1... | collective-permute-start | bytes 6291464 | tf_op jit(solution)/shard_map/ppermute | solution.py:476
  73.0 19.4 %all-to-all-start = ((bf16[4,4,128,256]{3,2,1,0:T(8,128)(2,1)}), bf16[4,4,128,256]{3,2,1,0:T(8,128)(2,1)}, u32[]{:S(2)}, u32[]{:S(2)}) async-start(bf16[4,4,128,256]{3,2,1,0:T(8,128)(2,1)} %broadcast_in_dim.85), calls=%async_computation | async-start | bytes 2097152 | tf_op jit(solution)/shard_map/all_to_all | solution.py:486
  80.4 34.4 %collective-permute-start.3 = (bf16[2048,256]{1,0:T(8,128)(2,1)}, bf16[2048,256]{1,0:T(8,128)(2,1)}, u32[]{:S(2)}, u32[]{:S(2)}) collective-permute-start(bf16[2048,256]{1,0:T(8,128)(2,1)} %bitcast.6), channel_id=1, source_target_pairs={{0,8},{8,0},{16,24},{24,16},{1,9},{9,1},{17,25},{25,17},{2,10},{10... | collective-permute-start | bytes 3145736 | tf_op jit(solution)/shard_map/ppermute | solution.py:476
  82.4 34.5 %collective-permute-start.4 = (bf16[2048,256]{1,0:T(8,128)(2,1)}, bf16[2048,256]{1,0:T(8,128)(2,1)}, u32[]{:S(2)}, u32[]{:S(2)}) collective-permute-start(bf16[2048,256]{1,0:T(8,128)(2,1)} %bitcast.6), channel_id=1, source_target_pairs={{0,16},{8,24},{16,0},{24,8},{1,17},{9,25},{17,1},{25,9},{2,18},{10... | collective-permute-start | bytes 3145736 | tf_op jit(solution)/shard_map/ppermute | solution.py:476
  98.9 38.7 %all-to-all-start.1 = ((bf16[4,512,256]{2,1,0:T(8,128)(2,1)}), bf16[4,512,256]{2,1,0:T(8,128)(2,1)}, u32[]{:S(2)}, u32[]{:S(2)}) async-start(bf16[4,512,256]{2,1,0:T(8,128)(2,1)} %broadcast_in_dim.86), calls=%async_computation.1 | async-start | bytes 2097152 | tf_op jit(solution)/shard_map/all_to_all | solution.py:486
  120.7 14.2 %collective-permute-start.5 = (bf16[1024,256]{1,0:T(8,128)(2,1)}, bf16[1024,256]{1,0:T(8,128)(2,1)S(1)}, u32[]{:S(2)}, u32[]{:S(2)}) collective-permute-start(bf16[1024,256]{1,0:T(8,128)(2,1)} %slice.139), channel_id=1, source_target_pairs={{0,16},{8,24},{16,0},{24,8},{1,17},{9,25},{17,1},{25,9},{2,18},{10... | collective-permute-start | bytes 1572872 | tf_op jit(solution)/shard_map/ppermute | solution.py:476
  121.2 13.8 %collective-permute-start.6 = (bf16[1024,256]{1,0:T(8,128)(2,1)}, bf16[1024,256]{1,0:T(8,128)(2,1)}, u32[]{:S(2)}, u32[]{:S(2)}) collective-permute-start(bf16[1024,256]{1,0:T(8,128)(2,1)} %slice.140), channel_id=1, source_target_pairs={{0,8},{8,0},{16,24},{24,16},{1,9},{9,1},{17,25},{25,17},{2,10},{10... | collective-permute-start | bytes 1572872 | tf_op jit(solution)/shard_map/ppermute | solution.py:476
  126.5 19.3 %collective-permute-start.8 = (bf16[512,2048]{1,0:T(8,128)(2,1)}, bf16[512,2048]{1,0:T(8,128)(2,1)}, u32[]{:S(2)}, u32[]{:S(2)}) collective-permute-start(bf16[512,2048]{1,0:T(8,128)(2,1)} %bitcast_select_fusion.ga_ref), channel_id=1, source_target_pairs={{0,4},{4,0},{1,5},{5,1},{2,6},{6,2},{3,7},{7,3},{8,12},{12,8},{9,1... | collective-permute-start | bytes 6291464 | tf_op jit(solution)/shard_map/ppermute | solution.py:476
  126.6 19.2 %collective-permute-start.9 = (bf16[512,2048]{1,0:T(8,128)(2,1)}, bf16[512,2048]{1,0:T(8,128)(2,1)}, u32[]{:S(2)}, u32[]{:S(2)}) collective-permute-start(bf16[512,2048]{1,0:T(8,128)(2,1)} %collective-permute-done.1.ga_ref), channel_id=1, source_target_pairs={{0,4},{4,0},{1,5},{5,1},{2,6},{6,2},{3,7},{7,3},{8,12},{12,8},{9,1... | collective-permute-start | bytes 6291464 | tf_op jit(solution)/shard_map/ppermute | solution.py:476
  127.1 18.7 %collective-permute-start.10 = (bf16[512,2048]{1,0:T(8,128)(2,1)}, bf16[512,2048]{1,0:T(8,128)(2,1)}, u32[]{:S(2)}, u32[]{:S(2)}) collective-permute-start(bf16[512,2048]{1,0:T(8,128)(2,1)} %collective-permute-done.2.ga_ref), channel_id=1, source_target_pairs={{0,4},{4,0},{1,5},{5,1},{2,6},{6,2},{3,7},{7,3},{8,12},{12,8},{9,1... | collective-permute-start | bytes 6291464 | tf_op jit(solution)/shard_map/ppermute | solution.py:476
  140.2 74.3 %all-to-all-start.2 = ((bf16[4,1024,512]{1,2,0:T(8,128)(2,1)}), bf16[4,1024,512]{1,2,0:T(8,128)(2,1)}, u32[]{:S(2)}, u32[]{:S(2)}) async-start(bf16[4,1024,512]{1,2,0:T(8,128)(2,1)} %broadcast_in_dim.87), calls=%async_computation.2 | async-start | bytes 8388608 | tf_op jit(solution)/shard_map/all_to_all | solution.py:486
  145.2 477.6 %reduce-scatter.4.cloned.1.call-start = ((), (), s32[]{:S(2)}) async-start(), calls=%async_computation.10 | async-start | bytes 3604480 | tf_op jit(solution)/shard_map/reduce_scatter | solution.py:717
  145.7 12.6 %collective-permute-start.7 = (bf16[2048,256]{1,0:T(8,128)(2,1)}, bf16[2048,256]{1,0:T(8,128)(2,1)S(1)}, u32[]{:S(2)}, u32[]{:S(2)}) collective-permute-start(bf16[2048,256]{1,0:T(8,128)(2,1)} %bitcast.19), channel_id=1, source_target_pairs={{0,4},{4,0},{1,5},{5,1},{2,6},{6,2},{3,7},{7,3},{8,12},{12,8},{9,1... | collective-permute-start | bytes 3145736 | tf_op jit(solution)/shard_map/ppermute | solution.py:476
  148.6 65.9 %collective-permute-start.11 = (bf16[256,2048]{1,0:T(8,128)(2,1)S(1)}, bf16[256,2048]{1,0:T(8,128)(2,1)}, u32[]{:S(2)}, u32[]{:S(2)}) collective-permute-start(bf16[256,2048]{1,0:T(8,128)(2,1)S(1)} %slice.147), channel_id=1, source_target_pairs={{0,16},{8,24},{16,0},{24,8},{1,17},{9,25},{17,1},{25,9},{2,18},{10... | collective-permute-start | bytes 3145736 | tf_op jit(solution)/shard_map/ppermute | solution.py:476
  150.6 64.0 %collective-permute-start.12 = (bf16[256,2048]{1,0:T(8,128)(2,1)S(1)}, bf16[256,2048]{1,0:T(8,128)(2,1)}, u32[]{:S(2)}, u32[]{:S(2)}) collective-permute-start(bf16[256,2048]{1,0:T(8,128)(2,1)S(1)} %slice.148), channel_id=1, source_target_pairs={{0,8},{8,0},{16,24},{24,16},{1,9},{9,1},{17,25},{25,17},{2,10},{10... | collective-permute-start | bytes 3145736 | tf_op jit(solution)/shard_map/ppermute | solution.py:476
  219.2 4.2 collective-permute-start.13
  231.0 4.4 collective-permute-start.16
  231.2 48.0 %collective-permute-start.14 = (bf16[512,2048]{1,0:T(8,128)(2,1)S(1)}, bf16[512,2048]{1,0:T(8,128)(2,1)}, u32[]{:S(2)}, u32[]{:S(2)}) collective-permute-start(bf16[512,2048]{1,0:T(8,128)(2,1)S(1)} %multiply_convert_fusion.xa_ref), channel_id=1, source_target_pairs={{0,8},{8,0},{16,24},{24,16},{1,9},{9,1},{17,25},{25,17},{2,10},{10... | collective-permute-start | bytes 6291464 | tf_op jit(solution)/shard_map/ppermute | solution.py:476
  232.6 47.7 %collective-permute-start.15 = (bf16[512,2048]{1,0:T(8,128)(2,1)S(1)}, bf16[512,2048]{1,0:T(8,128)(2,1)}, u32[]{:S(2)}, u32[]{:S(2)}) collective-permute-start(bf16[512,2048]{1,0:T(8,128)(2,1)S(1)} %multiply_convert_fusion.xa_ref), channel_id=1, source_target_pairs={{0,16},{8,24},{16,0},{24,8},{1,17},{9,25},{17,1},{25,9},{2,18},{10... | collective-permute-start | bytes 6291464 | tf_op jit(solution)/shard_map/ppermute | solution.py:476
  280.4 7.5 collective-permute-start.19
  283.0 37.0 %collective-permute-start.17 = (bf16[256,2048]{1,0:T(8,128)(2,1)S(1)}, bf16[256,2048]{1,0:T(8,128)(2,1)S(1)}, u32[]{:S(2)}, u32[]{:S(2)}) collective-permute-start(bf16[256,2048]{1,0:T(8,128)(2,1)S(1)} %slice.151), channel_id=1, source_target_pairs={{0,16},{8,24},{16,0},{24,8},{1,17},{9,25},{17,1},{25,9},{2,18},{10... | collective-permute-start | bytes 3145736 | tf_op jit(solution)/shard_map/ppermute | solution.py:476
  283.7 36.3 %collective-permute-start.18 = (bf16[256,2048]{1,0:T(8,128)(2,1)S(1)}, bf16[256,2048]{1,0:T(8,128)(2,1)S(1)}, u32[]{:S(2)}, u32[]{:S(2)}) collective-permute-start(bf16[256,2048]{1,0:T(8,128)(2,1)S(1)} %slice.152), channel_id=1, source_target_pairs={{0,8},{8,0},{16,24},{24,16},{1,9},{9,1},{17,25},{25,17},{2,10},{10... | collective-permute-start | bytes 3145736 | tf_op jit(solution)/shard_map/ppermute | solution.py:476
  287.8 32.9 %collective-permute-start.21 = (bf16[512,2048]{1,0:T(8,128)(2,1)S(1)}, bf16[512,2048]{1,0:T(8,128)(2,1)S(1)}, u32[]{:S(2)}, u32[]{:S(2)}) collective-permute-start(bf16[512,2048]{1,0:T(8,128)(2,1)S(1)} %constant_dynamic-update-slice_fusion.2.ga_ref), channel_id=1, source_target_pairs={{0,4},{4,0},{1,5},{5,1},{2,6},{6,2},{3,7},{7,3},{8,12},{12,8},{9,1... | collective-permute-start | bytes 6291464 | tf_op jit(solution)/shard_map/ppermute | solution.py:476
  320.2 4.2 collective-permute-start.20
  357.0 4.4 collective-permute-start.22
  357.4 10.0 %collective-permute-start.25 = (bf16[512,2048]{1,0:T(8,128)(2,1)}, bf16[512,2048]{1,0:T(8,128)(2,1)S(1)}, u32[]{:S(2)}, u32[]{:S(2)}) collective-permute-start(bf16[512,2048]{1,0:T(8,128)(2,1)} %collective-permute-done.15.xa_ref), channel_id=1, source_target_pairs={{0,4},{4,0},{1,5},{5,1},{2,6},{6,2},{3,7},{7,3},{8,12},{12,8},{9,1... | collective-permute-start | bytes 6291464 | tf_op jit(solution)/shard_map/ppermute | solution.py:476
  357.5 9.6 %collective-permute-start.26 = (bf16[512,2048]{1,0:T(8,128)(2,1)S(1)}, bf16[512,2048]{1,0:T(8,128)(2,1)S(1)}, u32[]{:S(2)}, u32[]{:S(2)}) collective-permute-start(bf16[512,2048]{1,0:T(8,128)(2,1)S(1)} %copy-done.84), channel_id=1, source_target_pairs={{0,4},{4,0},{1,5},{5,1},{2,6},{6,2},{3,7},{7,3},{8,12},{12,8},{9,1... | collective-permute-start | bytes 6291464 | tf_op jit(solution)/shard_map/ppermute | solution.py:476
  363.9 35.5 %collective-permute-start.23 = (bf16[256,2048]{1,0:T(8,128)(2,1)S(1)}, bf16[256,2048]{1,0:T(8,128)(2,1)S(1)}, u32[]{:S(2)}, u32[]{:S(2)}) collective-permute-start(bf16[256,2048]{1,0:T(8,128)(2,1)S(1)} %get-tuple-element.371), channel_id=1, source_target_pairs={{0,8},{8,0},{16,24},{24,16},{1,9},{9,1},{17,25},{25,17},{2,10},{10... | collective-permute-start | bytes 3145736 | tf_op jit(solution)/shard_map/ppermute | solution.py:476
  364.5 34.9 %collective-permute-start.24 = (bf16[256,2048]{1,0:T(8,128)(2,1)S(1)}, bf16[256,2048]{1,0:T(8,128)(2,1)S(1)}, u32[]{:S(2)}, u32[]{:S(2)}) collective-permute-start(bf16[256,2048]{1,0:T(8,128)(2,1)S(1)} %get-tuple-element.370), channel_id=1, source_target_pairs={{0,16},{8,24},{16,0},{24,8},{1,17},{9,25},{17,1},{25,9},{2,18},{10... | collective-permute-start | bytes 3145736 | tf_op jit(solution)/shard_map/ppermute | solution.py:476
  399.4 4.4 collective-permute-start.27
  406.3 38.6 %collective-permute-start.28 = (bf16[2048,2048]{1,0:T(8,128)(2,1)}, bf16[2048,2048]{1,0:T(8,128)(2,1)}, u32[]{:S(2)}, u32[]{:S(2)}) collective-permute-start(bf16[2048,2048]{1,0:T(8,128)(2,1)} %get-tuple-element.269), channel_id=1, source_target_pairs={{0,4},{4,0},{1,5},{5,1},{2,6},{6,2},{3,7},{7,3},{8,12},{12,8},{9,1... | collective-permute-start | bytes 25165832 | tf_op jit(solution)/shard_map/ppermute | solution.py:476
  406.7 50.5 %collective-permute-start.31 = (bf16[512,2048]{1,0:T(8,128)(2,1)}, bf16[512,2048]{1,0:T(8,128)(2,1)S(1)}, u32[]{:S(2)}, u32[]{:S(2)}) collective-permute-start(bf16[512,2048]{1,0:T(8,128)(2,1)} %get-tuple-element.270), channel_id=1, source_target_pairs={{0,4},{4,0},{1,5},{5,1},{2,6},{6,2},{3,7},{7,3},{8,12},{12,8},{9,1... | collective-permute-start | bytes 6291464 | tf_op jit(solution)/shard_map/ppermute | solution.py:476
  406.8 50.3 %collective-permute-start.29 = (bf16[512,2048]{1,0:T(8,128)(2,1)}, bf16[512,2048]{1,0:T(8,128)(2,1)}, u32[]{:S(2)}, u32[]{:S(2)}) collective-permute-start(bf16[512,2048]{1,0:T(8,128)(2,1)} %add_convert_fusion.7), channel_id=1, source_target_pairs={{0,8},{8,0},{16,24},{24,16},{1,9},{9,1},{17,25},{25,17},{2,10},{10... | collective-permute-start | bytes 6291464 | tf_op jit(solution)/shard_map/ppermute | solution.py:476
  407.4 49.8 %collective-permute-start.30 = (bf16[512,2048]{1,0:T(8,128)(2,1)}, bf16[512,2048]{1,0:T(8,128)(2,1)}, u32[]{:S(2)}, u32[]{:S(2)}) collective-permute-start(bf16[512,2048]{1,0:T(8,128)(2,1)} %add_convert_fusion.6), channel_id=1, source_target_pairs={{0,16},{8,24},{16,0},{24,8},{1,17},{9,25},{17,1},{25,9},{2,18},{10... | collective-permute-start | bytes 6291464 | tf_op jit(solution)/shard_map/ppermute | solution.py:476
  425.9 196.9 %reduce-scatter.8.cloned.1.call-start = ((), (), s32[]{:S(2)}) async-start(), calls=%async_computation.12 | async-start | bytes 3604480 | tf_op jit(solution)/shard_map/reduce_scatter | solution.py:717
  469.4 4.5 collective-permute-start.32
  482.3 76.5 %all-to-all-start.3 = ((bf16[4,256,2048]{2,1,0:T(8,128)(2,1)}), bf16[4,256,2048]{2,1,0:T(8,128)(2,1)}, u32[]{:S(2)}, u32[]{:S(2)}) async-start(bf16[4,256,2048]{2,1,0:T(8,128)(2,1)} %bitcast.157), calls=%async_computation.3 | async-start | bytes 8388608 | tf_op jit(solution)/shard_map/all_to_all | solution.py:742
  487.5 148.4 %reduce-scatter.6.cloned.1.call-start = ((), (), s32[]{:S(2)}) async-start(), calls=%async_computation.11 | async-start | bytes 3604480 | tf_op jit(solution)/shard_map/reduce_scatter | solution.py:717
  506.8 51.0 %collective-permute-start.33 = (bf16[256,2048]{1,0:T(8,128)(2,1)}, bf16[256,2048]{1,0:T(8,128)(2,1)S(1)}, u32[]{:S(2)}, u32[]{:S(2)}) collective-permute-start(bf16[256,2048]{1,0:T(8,128)(2,1)} %get-tuple-element.289), channel_id=1, source_target_pairs={{0,8},{8,0},{16,24},{24,16},{1,9},{9,1},{17,25},{25,17},{2,10},{10... | collective-permute-start | bytes 3145736 | tf_op jit(solution)/shard_map/ppermute | solution.py:476
  508.8 50.0 %collective-permute-start.34 = (bf16[256,2048]{1,0:T(8,128)(2,1)}, bf16[256,2048]{1,0:T(8,128)(2,1)}, u32[]{:S(2)}, u32[]{:S(2)}) collective-permute-start(bf16[256,2048]{1,0:T(8,128)(2,1)} %get-tuple-element.290), channel_id=1, source_target_pairs={{0,16},{8,24},{16,0},{24,8},{1,17},{9,25},{17,1},{25,9},{2,18},{10... | collective-permute-start | bytes 3145736 | tf_op jit(solution)/shard_map/ppermute | solution.py:476
  562.9 73.0 %collective-permute-start.35 = (bf16[512,2048]{1,0:T(8,128)(2,1)}, bf16[512,2048]{1,0:T(8,128)(2,1)}, u32[]{:S(2)}, u32[]{:S(2)}) collective-permute-start(bf16[512,2048]{1,0:T(8,128)(2,1)} %add_convert_fusion.2), channel_id=1, source_target_pairs={{0,8},{8,0},{16,24},{24,16},{1,9},{9,1},{17,25},{25,17},{2,10},{10... | collective-permute-start | bytes 6291464 | tf_op jit(solution)/shard_map/ppermute | solution.py:476
  566.6 69.3 %collective-permute-start.36 = (bf16[512,2048]{1,0:T(8,128)(2,1)}, bf16[512,2048]{1,0:T(8,128)(2,1)}, u32[]{:S(2)}, u32[]{:S(2)}) collective-permute-start(bf16[512,2048]{1,0:T(8,128)(2,1)} %add_convert_fusion.1), channel_id=1, source_target_pairs={{0,16},{8,24},{16,0},{24,8},{1,17},{9,25},{17,1},{25,9},{2,18},{10... | collective-permute-start | bytes 6291464 | tf_op jit(solution)/shard_map/ppermute | solution.py:476
  570.4 65.4 %all-to-all-start.4 = ((bf16[8,256,512]{2,1,0:T(8,128)(2,1)}), bf16[8,256,512]{2,1,0:T(8,128)(2,1)}, u32[]{:S(2)}, u32[]{:S(2)}) async-start(bf16[8,256,512]{2,1,0:T(8,128)(2,1)} %bitcast.164), calls=%async_computation.7 | async-start | bytes 4194304 | tf_op jit(solution)/shard_map/all_to_all | solution.py:740
  579.6 33.2 %collective-permute-start.39 = (bf16[64,2048]{1,0:T(8,128)(2,1)S(1)}, bf16[64,2048]{1,0:T(8,128)(2,1)}, u32[]{:S(2)}, u32[]{:S(2)}) collective-permute-start(bf16[64,2048]{1,0:T(8,128)(2,1)S(1)} %get-tuple-element.368), channel_id=1, source_target_pairs={{0,3},{1,2},{2,1},{3,0},{4,7},{5,6},{6,5},{7,4},{8,11},{9,10},{10,... | collective-permute-start | bytes 786440 | tf_op jit(solution)/shard_map/ppermute | solution.py:476
  583.3 37.3 %collective-permute-start.38 = (bf16[64,2048]{1,0:T(8,128)(2,1)S(1)}, bf16[64,2048]{1,0:T(8,128)(2,1)}, u32[]{:S(2)}, u32[]{:S(2)}) collective-permute-start(bf16[64,2048]{1,0:T(8,128)(2,1)S(1)} %get-tuple-element.369), channel_id=1, source_target_pairs={{0,2},{1,3},{2,0},{3,1},{4,6},{5,7},{6,4},{7,5},{8,10},{9,11},{10,... | collective-permute-start | bytes 786440 | tf_op jit(solution)/shard_map/ppermute | solution.py:476
  583.3 37.3 %collective-permute-start.37 = (bf16[64,2048]{1,0:T(8,128)(2,1)S(1)}, bf16[64,2048]{1,0:T(8,128)(2,1)}, u32[]{:S(2)}, u32[]{:S(2)}) collective-permute-start(bf16[64,2048]{1,0:T(8,128)(2,1)S(1)} %get-tuple-element.367), channel_id=1, source_target_pairs={{0,1},{1,0},{2,3},{3,2},{4,5},{5,4},{6,7},{7,6},{8,9},{9,8},{10,11... | collective-permute-start | bytes 786440 | tf_op jit(solution)/shard_map/ppermute | solution.py:476
  640.4 9.2 %collective-permute-start.41 = (bf16[512,256]{1,0:T(8,128)(2,1)S(1)}, bf16[512,256]{1,0:T(8,128)(2,1)S(1)}, u32[]{:S(2)}, u32[]{:S(2)}) collective-permute-start(bf16[512,256]{1,0:T(8,128)(2,1)S(1)} %get-tuple-element.378), channel_id=1, source_target_pairs={{0,8},{8,0},{16,24},{24,16},{1,9},{9,1},{17,25},{25,17},{2,10},{10... | collective-permute-start | bytes 786440 | tf_op jit(solution)/shard_map/ppermute | solution.py:476
  640.7 13.8 %collective-permute-start.42 = (bf16[512,256]{1,0:T(8,128)(2,1)S(1)}, bf16[512,256]{1,0:T(8,128)(2,1)S(1)}, u32[]{:S(2)}, u32[]{:S(2)}) collective-permute-start(bf16[512,256]{1,0:T(8,128)(2,1)S(1)} %get-tuple-element.377), channel_id=1, source_target_pairs={{0,16},{8,24},{16,0},{24,8},{1,17},{9,25},{17,1},{25,9},{2,18},{10... | collective-permute-start | bytes 786440 | tf_op jit(solution)/shard_map/ppermute | solution.py:476
  642.2 12.3 %collective-permute-start.43 = (bf16[512,256]{1,0:T(8,128)(2,1)S(1)}, bf16[512,256]{1,0:T(8,128)(2,1)S(1)}, u32[]{:S(2)}, u32[]{:S(2)}) collective-permute-start(bf16[512,256]{1,0:T(8,128)(2,1)S(1)} %get-tuple-element.376), channel_id=1, source_target_pairs={{0,24},{8,16},{16,8},{24,0},{1,25},{9,17},{17,9},{25,1},{2,26},{10... | collective-permute-start | bytes 786440 | tf_op jit(solution)/shard_map/ppermute | solution.py:476
  656.5 9.3 %collective-permute-start.44 = (bf16[512,256]{1,0:T(8,128)(2,1)}, bf16[512,256]{1,0:T(8,128)(2,1)}, u32[]{:S(2)}, u32[]{:S(2)}) collective-permute-start(bf16[512,256]{1,0:T(8,128)(2,1)} %pad_maximum_fusion.11), channel_id=1, source_target_pairs={{0,4},{4,0},{1,5},{5,1},{2,6},{6,2},{3,7},{7,3},{8,12},{12,8},{9,1... | collective-permute-start | bytes 786440 | tf_op jit(solution)/shard_map/ppermute | solution.py:476
  662.0 31.4 %all-to-all-start.5 = ((bf16[8,3,176,256]{3,2,1,0:T(8,128)(2,1)}), bf16[8,3,176,256]{3,2,1,0:T(8,128)(2,1)S(1)}, u32[]{:S(2)}, u32[]{:S(2)}) async-start(bf16[8,3,176,256]{3,2,1,0:T(8,128)(2,1)} %copy-done.7), calls=%async_computation.8 | async-start | bytes 4325376 | tf_op jit(solution)/shard_map/all_to_all | solution.py:779
  680.6 28.3 %collective-permute-start.45 = (bf16[512,2048]{1,0:T(8,128)(2,1)}, bf16[512,2048]{1,0:T(8,128)(2,1)}, u32[]{:S(2)}, u32[]{:S(2)}) collective-permute-start(bf16[512,2048]{1,0:T(8,128)(2,1)} %add_convert_fusion), channel_id=1, source_target_pairs={{0,4},{4,0},{1,5},{5,1},{2,6},{6,2},{3,7},{7,3},{8,12},{12,8},{9,1... | collective-permute-start | bytes 6291464 | tf_op jit(solution)/shard_map/ppermute | solution.py:476
  682.7 80.0 %collective-permute-start.52 = (bf16[64,1024]{1,0:T(8,128)(2,1)}, bf16[64,1024]{1,0:T(8,128)(2,1)}, u32[]{:S(2)}, u32[]{:S(2)}) collective-permute-start(bf16[64,1024]{1,0:T(8,128)(2,1)} %get-tuple-element.362), channel_id=1, source_target_pairs={{0,4},{4,0},{1,5},{5,1},{2,6},{6,2},{3,7},{7,3},{8,12},{12,8},{9,1... | collective-permute-start | bytes 393224 | tf_op jit(solution)/shard_map/ppermute | solution.py:476
  685.2 56.0 %collective-permute-start.46 = (bf16[2,64,512]{2,1,0:T(8,128)(2,1)}, bf16[2,64,512]{2,1,0:T(8,128)(2,1)}, u32[]{:S(2)}, u32[]{:S(2)}) collective-permute-start(bf16[2,64,512]{2,1,0:T(8,128)(2,1)} %get-tuple-element.322), channel_id=1, source_target_pairs={{0,1},{1,0},{2,3},{3,2},{4,5},{5,4},{6,7},{7,6},{8,9},{9,8},{10,11... | collective-permute-start | bytes 393224 | tf_op jit(solution)/shard_map/ppermute | solution.py:476
  686.7 54.6 %collective-permute-start.47 = (bf16[2,64,512]{2,1,0:T(8,128)(2,1)S(1)}, bf16[2,64,512]{2,1,0:T(8,128)(2,1)}, u32[]{:S(2)}, u32[]{:S(2)}) collective-permute-start(bf16[2,64,512]{2,1,0:T(8,128)(2,1)S(1)} %get-tuple-element.323), channel_id=1, source_target_pairs={{0,2},{1,3},{2,0},{3,1},{4,6},{5,7},{6,4},{7,5},{8,10},{9,11},{10,... | collective-permute-start | bytes 393224 | tf_op jit(solution)/shard_map/ppermute | solution.py:476
  689.3 51.9 %collective-permute-start.48 = (bf16[2,64,512]{2,1,0:T(8,128)(2,1)S(1)}, bf16[2,64,512]{2,1,0:T(8,128)(2,1)}, u32[]{:S(2)}, u32[]{:S(2)}) collective-permute-start(bf16[2,64,512]{2,1,0:T(8,128)(2,1)S(1)} %get-tuple-element.324), channel_id=1, source_target_pairs={{0,3},{1,2},{2,1},{3,0},{4,7},{5,6},{6,5},{7,4},{8,11},{9,10},{10,... | collective-permute-start | bytes 393224 | tf_op jit(solution)/shard_map/ppermute | solution.py:476
  694.8 42.3 %all-to-all-start.6 = ((bf16[8,256,768]{2,1,0:T(8,128)(2,1)}), bf16[8,256,768]{2,1,0:T(8,128)(2,1)S(1)}, u32[]{:S(2)}, u32[]{:S(2)}) async-start(bf16[8,256,768]{2,1,0:T(8,128)(2,1)} %bitcast.149), calls=%async_computation.9 | async-start | bytes 6291456 | tf_op jit(solution)/shard_map/all_to_all | solution.py:740
  741.3 9.7 %collective-permute-start.51 = (bf16[2,64,768]{2,1,0:T(8,128)(2,1)S(1)}, bf16[2,64,768]{2,1,0:T(8,128)(2,1)S(1)}, u32[]{:S(2)}, u32[]{:S(2)}) collective-permute-start(bf16[2,64,768]{2,1,0:T(8,128)(2,1)S(1)} %get-tuple-element.344), channel_id=1, source_target_pairs={{0,3},{1,2},{2,1},{3,0},{4,7},{5,6},{6,5},{7,4},{8,11},{9,10},{10,... | collective-permute-start | bytes 589832 | tf_op jit(solution)/shard_map/ppermute | solution.py:476
  744.9 12.9 %collective-permute-start.50 = (bf16[2,64,768]{2,1,0:T(8,128)(2,1)S(1)}, bf16[2,64,768]{2,1,0:T(8,128)(2,1)S(1)}, u32[]{:S(2)}, u32[]{:S(2)}) collective-permute-start(bf16[2,64,768]{2,1,0:T(8,128)(2,1)S(1)} %get-tuple-element.343), channel_id=1, source_target_pairs={{0,2},{1,3},{2,0},{3,1},{4,6},{5,7},{6,4},{7,5},{8,10},{9,11},{10,... | collective-permute-start | bytes 589832 | tf_op jit(solution)/shard_map/ppermute | solution.py:476
  744.9 12.9 %collective-permute-start.49 = (bf16[2,64,768]{2,1,0:T(8,128)(2,1)S(1)}, bf16[2,64,768]{2,1,0:T(8,128)(2,1)S(1)}, u32[]{:S(2)}, u32[]{:S(2)}) collective-permute-start(bf16[2,64,768]{2,1,0:T(8,128)(2,1)S(1)} %get-tuple-element.342), channel_id=1, source_target_pairs={{0,1},{1,0},{2,3},{3,2},{4,5},{5,4},{6,7},{7,6},{8,9},{9,8},{10,11... | collective-permute-start | bytes 589832 | tf_op jit(solution)/shard_map/ppermute | solution.py:476
  (86 other events, 853.8 us)
Sparse Core Ops, SparseCore 0:
  13.8 53.4 all-gather.7
  68.9 152.7 all-gather.5
  426.1 56.4 reduce-scatter.3
  484.7 56.0 reduce-scatter.7
  542.9 68.6 reduce-scatter.5

commit v5 on v4

--- a/solution.py
+++ b/solution.py
@@ -51,20 +51,30 @@
 
     mine = row_position(order_ref, own, row_block)
 
-    def step(place, masked):
-        start = pl.multiple_of(place * blk, blk)
-        scores = jnp.dot(kv_ref[pl.ds(start, blk), :HD], qt_ref[0], preferred_element_type=F32)
+    def step(places, masked):
+        starts = [pl.multiple_of(place * blk, blk) for place in places]
+        scores = [
+            jnp.dot(kv_ref[pl.ds(start, blk), :HD], qt_ref[0], preferred_element_type=F32)
+            for start in starts
+        ]
         if masked:
-            scores = jnp.where(causal(blk, group), scores, MASKED)
+            scores = [jnp.where(causal(blk, group), part, MASKED) for part in scores]
         old = max_ref[...]
-        new = jnp.maximum(old, jnp.max(scores, axis=0, keepdims=True))
-        weights = jnp.exp2(scores - new)
+        new = old
+        for part in scores:
+            new = jnp.maximum(new, jnp.max(part, axis=0, keepdims=True))
         scale = jnp.exp2(old - new)
+        total = sum_ref[...] * scale
+        acc = acc_ref[...] * scale
+        for start, part in zip(starts, scores):
+            weights = jnp.exp2(part - new)
+            total = total + jnp.sum(weights, axis=0, keepdims=True)
+            acc = acc + jnp.dot(
+                vt_ref[:, pl.ds(start, blk)], weights.astype(BF16), preferred_element_type=F32
+            )
         max_ref[...] = new
-        sum_ref[...] = sum_ref[...] * scale + jnp.sum(weights, axis=0, keepdims=True)
-        acc_ref[...] = acc_ref[...] * scale + jnp.dot(
-            vt_ref[:, pl.ds(start, blk)], weights.astype(BF16), preferred_element_type=F32
-        )
+        sum_ref[...] = total
+        acc_ref[...] = acc
 
     @pl.when(mine * blk < length)
     def _():
@@ -79,13 +89,18 @@
         max_ref[...] = jnp.full(max_ref.shape, MASKED, F32)
         sum_ref[...] = jnp.zeros(sum_ref.shape, F32)
         acc_ref[...] = jnp.zeros(acc_ref.shape, F32)
-        step(place_ref[mine], True)
+        step([place_ref[mine]], True)
 
         def body(j, carried):
-            step(place_ref[j], False)
+            step([place_ref[2 * j], place_ref[2 * j + 1]], False)
             return carried
 
-        lax.fori_loop(0, mine, body, 0)
+        lax.fori_loop(0, mine // 2, body, 0)
+
+        @pl.when(mine % 2 == 1)
+        def _():
+            step([place_ref[mine - 1]], False)
+
         total = sum_ref[...]
         result = acc_ref[...] * (1.0 / total)
         for head in range(group):
@@ -189,10 +204,16 @@
         step(place_ref[mine], True)
 
         def body(j, carried):
-            step(place_ref[j], False)
+            step(place_ref[2 * j], False)
+            step(place_ref[2 * j + 1], False)
             return carried
 
-        lax.fori_loop(0, mine, body, 0)
+        lax.fori_loop(0, mine // 2, body, 0)
+
+        @pl.when(mine % 2 == 1)
+        def _():
+            step(place_ref[mine - 1], False)
+
         cosine, sine = cos_ref[...], sin_ref[...]
         for head in range(group):
             turned = acc_ref[:, head * blk : (head + 1) * blk].astype(BF16).astype(F32)

time: 785 us -> 785 us (level)
  Pallas kernels: 209 us -> 239 us
  waiting for transfers between devices: 178 us -> 149 us
    ppermute x53, waiting for transfers between devices: 146 us -> 119 us  [exchange(): return lax.ppermute(value, axis, [(i, i ^ distance) for i in range(size)])]
    pallas_call x2, Pallas kernels: 52 us -> 71.2 us  [attention_backward(): pl.pallas_call(functools.partial(attend_backward, group, blk, last), grid...]
    pallas_call x1, Pallas kernels: 27.1 us -> 37.1 us  [attention_forward(): pl.pallas_call(functools.partial(attend_forward, heads, blk), grid_spec=p...]
  transfers between devices with their start and end apart: 65 -> 65, of which waited for: 27 -> 26; matrix products, arithmetic and copies ran while one was open for 32% -> 32% of each run, Pallas kernels for 23% -> 27%
where the time goes in v5:
time: 785 us; the launch traced here: 771 us
  Pallas kernels  239 us (30%)
  waiting for transfers between devices  149 us (19%)
  matrix products  118 us (15%)
  other arithmetic  89.6 us (11%)
  local copies, waits for them, and re-layouts  82.3 us (10%)
  starting transfers between devices  78.1 us (10%)
  between operations  16.1 us (2%)
    pallas_call x4, Pallas kernels, ffn_pair(): pl.pallas_call(functools.partial(ffn_rows, count, tiles), grid_spec=pltpu...  123 us
    ppermute x53, waiting for transfers between devices, exchange(): return lax.ppermute(value, axis, [(i, i ^ distance) for i in range(size)])  119 us
    dot_general x7, matrix products, contract_rows(): lax.dot_general(left, right, (((0,), (0,)), ((), ())), preferred_element_...  74.9 us
    pallas_call x2, Pallas kernels, attention_backward(): pl.pallas_call(functools.partial(attend_backward, group, blk, last), grid...  71.2 us
    ppermute x53, starting transfers between devices, exchange(): return lax.ppermute(value, axis, [(i, i ^ distance) for i in range(size)])  46.4 us
    pallas_call x1, Pallas kernels, attention_forward(): pl.pallas_call(functools.partial(attend_forward, heads, blk), grid_spec=p...  37.1 us
    unnamed x182, local copies, waits for them, and re-layouts  33.8 us
    all_to_all x2, waiting for transfers between devices, deal_rows(): lax.all_to_all(terms.reshape(places, planes * (depth // places), -1), ('c...  27.8 us
  transfers between devices with their start and end apart: 65, of which 26 were waited for; matrix products, arithmetic and copies ran while one was open for 32% of the time, Pallas kernels for 27%

profile of v5, /device:TPU:0, one launch (start us, length us, event | category | flops | bytes accessed | tf_op | source)
XLA Modules:
  0.0 771.1 jit_solution(14635004939350176873)
XLA Ops:
  10.9 2.7 concatenate.62
  15.2 3.1 bitcast_select_fusion.ga_ref
  18.3 2.9 collective-permute-start.1
  22.8 4.1 constant_dynamic-slice_fusion.2
  30.3 2.9 constant_dynamic-slice_fusion.4
  35.4 3.0 pad_maximum_fusion.4
  40.5 26.6 %collective-permute-done.1.ga_ref = bf16[512,2048]{1,0:T(8,128)(2,1)} collective-permute-done((bf16[512,2048]{1,0:T(8,128)(2,1)}, bf16[512,2048]{1,0:T(8,128)(2,1)}, u32[]{:S(2)}, u32[]{:S(2)}) %collective-permute-start.1) | collective-permute-done | bytes 2097184 | tf_op jit(solution)/shard_map/ppermute | solution.py:497
  73.0 4.3 all-to-all-start
  77.3 3.2 fusion.60
  84.7 6.1 fusion.2
  98.9 4.3 all-to-all-start.1
  103.2 11.6 %collective-permute-done.3 = bf16[2048,256]{1,0:T(8,128)(2,1)} collective-permute-done((bf16[2048,256]{1,0:T(8,128)(2,1)}, bf16[2048,256]{1,0:T(8,128)(2,1)}, u32[]{:S(2)}, u32[]{:S(2)}) %collective-permute-start.3) | collective-permute-done | bytes 1048608 | tf_op jit(solution)/shard_map/ppermute | solution.py:497
  121.2 2.6 broadcast_in_dim.53
  131.8 3.1 collective-permute-done.5
  140.2 5.0 all-to-all-start.2
  152.2 6.3 fusion.63.q_ref
  159.9 37.1 %attend_forward.1 = (bf16[1024,1024]{1,0:T(8,128)(2,1)S(1)}, f32[4,1,2048]{2,1,0:T(1,128)S(1)}, bf16[4,128,2048]{2,1,0:T(8,128)(2,1)S(1)}) custom-call(s32[2]{0:T(128)S(1)} %pad_add_fusion.scal_ref, s32[16]{0:T(128)S(1)} %bitcast.131, f32[1024,1024]{1,0:T(8,128)S(1)} %fusion.63.q_ref, f32[64,1024]{1,0:T(8,128)S(1)} %copy.103.cos_ref, ...), custom_call_target="tpu_custom_call" | custom-call | flops 1048576 | bytes 65536 | tf_op jit(solution)/shard_map/attend_forward/pallas_call | solution.py:125
  199.8 14.7 %collective-permute-done.11 = bf16[256,2048]{1,0:T(8,128)(2,1)} collective-permute-done((bf16[256,2048]{1,0:T(8,128)(2,1)S(1)}, bf16[256,2048]{1,0:T(8,128)(2,1)}, u32[]{:S(2)}, u32[]{:S(2)}) %collective-permute-start.11) | collective-permute-done | bytes 1048608 | tf_op jit(solution)/shard_map/ppermute | solution.py:497
  214.5 4.7 convolution_convert_fusion.6
  219.3 4.1 collective-permute-done.13
  223.5 5.1 multiply_reduce_fusion.2
  235.3 31.0 %ffn_pair.4 = (bf16[512,2048]{1,0:T(8,128)(2,1)}, bf16[512,2048]{1,0:T(8,128)(2,1)}, bf16[2048,2048]{1,0:T(8,128)(2,1)}, bf16[2048,2048]{1,0:T(8,128)(2,1)}, bf1...) custom-call(s32[1]{0:T(128)} %constant.106.clone.1.place_ref, ...), custom_call_target="tpu_custom_call" | custom-call | flops 1048576 | bytes 65536 | tf_op jit(solution)/shard_map/ffn_pair/pallas_call | solution.py:357
  266.4 12.8 %collective-permute-done.14.xa_ref = bf16[512,2048]{1,0:T(8,128)(2,1)} collective-permute-done((bf16[512,2048]{1,0:T(8,128)(2,1)S(1)}, bf16[512,2048]{1,0:T(8,128)(2,1)}, u32[]{:S(2)}, u32[]{:S(2)}) %collective-permute-start.14) | collective-permute-done | bytes 2097184 | tf_op jit(solution)/shard_map/ppermute | solution.py:497
  289.4 30.6 %ffn_pair.5 = (bf16[512,2048]{1,0:T(8,128)(2,1)}, bf16[512,2048]{1,0:T(8,128)(2,1)}, bf16[2048,2048]{1,0:T(8,128)(2,1)}, bf16[2048,2048]{1,0:T(8,128)(2,1)}, bf1...) custom-call(s32[1]{0:T(128)} %constant.107.clone.1.place_ref, ...), custom_call_target="tpu_custom_call", output_to_operand_aliasing={{2}: (8, {}), {3}: (9, {}), {4}: (10, {}), {5}: (11, {}), {... | custom-call | flops 1048576 | bytes 65536 | tf_op jit(solution)/shard_map/ffn_pair/pallas_call | solution.py:357
  320.7 3.8 collective-permute-done.20.xb_ref
  325.8 30.9 %ffn_pair.6 = (bf16[512,2048]{1,0:T(8,128)(2,1)}, bf16[512,2048]{1,0:T(8,128)(2,1)}, bf16[2048,2048]{1,0:T(8,128)(2,1)}, bf16[2048,2048]{1,0:T(8,128)(2,1)}, bf1...) custom-call(s32[1]{0:T(128)} %constant.105.clone.1.place_ref, ...), custom_call_target="tpu_custom_call", output_to_operand_aliasing={{2}: (8, {}), {3}: (9, {}), {4}: (10, {}), {5}: (11, {}), {... | custom-call | flops 1048576 | bytes 65536 | tf_op jit(solution)/shard_map/ffn_pair/pallas_call | solution.py:357
  357.6 3.5 collective-permute-done.22
  368.4 30.7 %ffn_pair.7 = (bf16[512,2048]{1,0:T(8,128)(2,1)}, bf16[512,2048]{1,0:T(8,128)(2,1)}, bf16[2048,2048]{1,0:T(8,128)(2,1)}, bf16[2048,2048]{1,0:T(8,128)(2,1)}, bf1...) custom-call(s32[1]{0:T(128)} %constant.108.clone.1.place_ref, ...), custom_call_target="tpu_custom_call", output_to_operand_aliasing={{2}: (8, {}), {3}: (9, {}), {4}: (10, {}), {5}: (11, {}), {... | custom-call | flops 1048576 | bytes 65536 | tf_op jit(solution)/shard_map/ffn_pair/pallas_call | solution.py:357
  408.6 17.1 %convolution_convert_fusion.2 = bf16[704,2048]{1,0:T(8,128)(2,1)} fusion(bf16[4096,704]{1,0:T(8,128)(2,1)S(1)} %copy-done.28, bf16[4096,2048]{1,0:T(8,128)(2,1)} %get-tuple-element.284), kind=kOutput, calls=%fused_computation.39 | convolution fusion | flops 11812601856 | bytes 25427968 | tf_op jit(solution)/shard_map/dot_general | solution.py:484
  425.8 19.1 %convolution_convert_fusion.3 = bf16[704,2048]{1,0:T(8,128)(2,1)} fusion(bf16[4096,704]{1,0:T(8,128)(2,1)} %get-tuple-element.271, bf16[4096,2048]{1,0:T(8,128)(2,1)} %get-tuple-element.272), kind=kOutput, calls=%fused_computation.40 | convolution fusion | flops 11812601856 | bytes 25427968 | tf_op jit(solution)/shard_map/dot_general | solution.py:484
  444.8 4.4 add_convert_fusion.10
  449.3 7.8 %add_convert_fusion.3 = (bf16[512,2048]{1,0:T(8,128)(2,1)}, bf16[512,2048]{1,0:T(8,128)(2,1)}, bf16[512,2048]{1,0:T(8,128)(2,1)}) fusion(bf16[2048,2048]{1,0:T(8,128)(2,1)} %collective-permute-done.28, bf16[2048,2048]{1,0:T(8,128)(2,1)} %get-tuple-element.268), kind=kLoop, calls=%fused_computation.29 | loop fusion | flops 12582912 | bytes 18874368 | tf_op jit(solution)/shard_map/convert_element_type | solution.py:727
  458.2 4.0 multiply_reduce_fusion
  462.3 7.1 fusion.58
  469.4 4.5 collective-permute-done.32
  473.9 8.4 %convolution_convert_fusion = bf16[1024,2048]{1,0:T(8,128)(2,1)} fusion(bf16[1024,1024]{1,0:T(8,128)(2,1)S(1)} %copy-done.9, bf16[512,2048]{1,0:T(8,128)(2,1)} %collective-permute-done.32, bf16[512,2048]{1,0:T(8,128)(2,1)} %get-tuple-element.352), kind=kOutput, calls=%fused_computation.37 | convolution fusion | flops 4305453056 | bytes 10485760 | tf_op jit(solution)/shard_map/dot_general | solution.py:484
  482.3 5.0 all-to-all-start.3
  487.3 19.2 %convolution_convert_fusion.1 = bf16[704,2048]{1,0:T(8,128)(2,1)} fusion(bf16[4096,704]{1,0:T(8,128)(2,1)} %get-tuple-element.283, bf16[4096,2048]{1,0:T(8,128)(2,1)} %get-tuple-element.284), kind=kOutput, calls=%fused_computation.38 | convolution fusion | flops 11812601856 | bytes 25427968 | tf_op jit(solution)/shard_map/dot_general | solution.py:484
  510.1 8.0 %fusion.16.g_ref = bf16[1024,1024]{1,0:T(8,128)(2,1)S(1)} fusion(bf16[1024,2048]{0,1:T(8,128)(2,1)} %bitcast.21, bf16[512,2048]{1,0:T(8,128)(2,1)} %collective-permute-done.32, bf16[512,2048]{1,0:T(8,128)(2,1)} %get-tuple-element.352), kind=kOutput, calls=%fused_computation.56 | convolution fusion | flops 4304404480 | bytes 10485760 | tf_op jit(solution)/shard_map/dot_general | solution.py:488
  518.1 35.9 %attend_backward.2 = (bf16[1024,512]{1,0:T(8,128)(2,1)S(1)}, f32[4096,256]{1,0:T(8,128)}) custom-call(s32[2]{0:T(128)S(1)} %copy-done.24, s32[16]{0:T(128)S(1)} %bitcast.132, bf16[4,128,2048]{2,1,0:T(8,128)(2,1)S(1)} %copy-done.11, bf16[1024,1024]{1,0:T(8,128)(2,1)S(1)} %fusion.16.g_ref, bf16[1024,1024]{1,0:T(8,128)(2,1)} %copy-done.8, ...), custom_call_target="tpu_custom_call" | custom-call | flops 1048576 | bytes 65536 | tf_op jit(solution)/shard_map/attend_backward/pallas_call | solution.py:249
  555.0 2.6 collective-permute-done.33
  558.6 4.0 add_convert_fusion.2
  566.5 3.7 convolution_convert_fusion.5
  570.2 4.4 all-to-all-start.4
  574.6 3.3 convert_reduce_fusion
  579.4 3.8 collective-permute-start.39
  583.8 35.3 %attend_backward.3 = (bf16[1024,512]{1,0:T(8,128)(2,1)S(1)}, bf16[2048,256]{1,0:T(8,128)(2,1)S(1)}, bf16[2048,256]{1,0:T(8,128)(2,1)S(1)}) custom-call(s32[2]{0:T(128)S(1)} %copy-done.24, s32[16]{0:T(128)S(1)} %bitcast.133, bf16[4,128,2048]{2,1,0:T(8,128)(2,1)S(1)} %copy-done.11, bf16[1024,1024]{1,0:T(8,128)(2,1)} %copy-done.12, ...), custom_call_target="tpu_custom_call" | custom-call | flops 1048576 | bytes 65536 | tf_op jit(solution)/shard_map/attend_backward/pallas_call | solution.py:249
  624.3 10.1 %all-to-all-done.4.dealt_ref = bf16[8,256,512]{2,1,0:T(8,128)(2,1)} async-done(((bf16[8,256,512]{2,1,0:T(8,128)(2,1)}), bf16[8,256,512]{2,1,0:T(8,128)(2,1)}, u32[]{:S(2)}, u32[]{:S(2)}) %all-to-all-start.4) | async-done | bytes 2097184 | tf_op jit(solution)/shard_map/all_to_all | solution.py:761
  634.6 2.8 collective-permute-done.40
  642.6 3.8 convolution_convert_fusion.4
  648.2 6.0 collective-permute-done.42
  661.7 4.0 all-to-all-start.5
  667.4 3.6 convolution_convert_fusion.7
  674.5 6.0 add_convert_fusion
  686.6 2.7 collective-permute-start.47
  689.5 3.8 fusion.30
  694.7 4.4 all-to-all-start.6
  699.1 7.3 select_convert_fusion
  708.7 5.9 fusion.6
  714.7 4.5 fusion.10
  719.2 17.7 %all-to-all-done.6.dealt_ref = bf16[8,256,768]{2,1,0:T(8,128)(2,1)S(1)} async-done(((bf16[8,256,768]{2,1,0:T(8,128)(2,1)}), bf16[8,256,768]{2,1,0:T(8,128)(2,1)S(1)}, u32[]{:S(2)}, u32[]{:S(2)}) %all-to-all-start.6) | async-done | bytes 3145760 | tf_op jit(solution)/shard_map/all_to_all | solution.py:761
  741.1 3.7 collective-permute-start.51
  746.6 4.2 collective-permute-done.51
  750.8 6.9 collective-permute-done.50
  (375 shorter events, 159.2 us)
Async XLA Ops:
  7.2 63.7 %all-gather.8.cloned.1.call-start = ((), (), s32[]{:S(2)}) async-start(), calls=%async_computation.14 | async-start | bytes 2969600 | tf_op jit(solution)/shard_map/all_gather | solution.py:612
  13.7 221.7 %all-gather.6.cloned.1.call-start = ((), (), s32[]{:S(2)}) async-start(), calls=%async_computation.13 | async-start | bytes 10813440 | tf_op jit(solution)/shard_map/all_gather | solution.py:639
  18.3 48.9 %collective-permute-start.1 = (bf16[512,2048]{1,0:T(8,128)(2,1)}, bf16[512,2048]{1,0:T(8,128)(2,1)}, u32[]{:S(2)}, u32[]{:S(2)}) collective-permute-start(bf16[512,2048]{1,0:T(8,128)(2,1)} %bitcast_select_fusion.ga_ref), channel_id=1, source_target_pairs={{0,8},{8,0},{16,24},{24,16},{1,9},{9,1},{17,25},{25,17},{2,10},{10... | collective-permute-start | bytes 6291464 | tf_op jit(solution)/shard_map/ppermute | solution.py:497
  21.2 47.4 %collective-permute-start.2 = (bf16[512,2048]{1,0:T(8,128)(2,1)}, bf16[512,2048]{1,0:T(8,128)(2,1)}, u32[]{:S(2)}, u32[]{:S(2)}) collective-permute-start(bf16[512,2048]{1,0:T(8,128)(2,1)} %bitcast_select_fusion.ga_ref), channel_id=1, source_target_pairs={{0,16},{8,24},{16,0},{24,8},{1,17},{9,25},{17,1},{25,9},{2,18},{10... | collective-permute-start | bytes 6291464 | tf_op jit(solution)/shard_map/ppermute | solution.py:497
  22.8 45.9 %collective-permute-start = (bf16[512,2048]{1,0:T(8,128)(2,1)S(1)}, bf16[512,2048]{1,0:T(8,128)(2,1)}, u32[]{:S(2)}, u32[]{:S(2)}) collective-permute-start(bf16[512,2048]{1,0:T(8,128)(2,1)S(1)} %bitcast.146), channel_id=1, source_target_pairs={{0,4},{4,0},{1,5},{5,1},{2,6},{6,2},{3,7},{7,3},{8,12},{12,8},{9,1... | collective-permute-start | bytes 6291464 | tf_op jit(solution)/shard_map/ppermute | solution.py:497
  73.0 19.4 %all-to-all-start = ((bf16[4,4,128,256]{3,2,1,0:T(8,128)(2,1)}), bf16[4,4,128,256]{3,2,1,0:T(8,128)(2,1)}, u32[]{:S(2)}, u32[]{:S(2)}) async-start(bf16[4,4,128,256]{3,2,1,0:T(8,128)(2,1)} %broadcast_in_dim.85), calls=%async_computation | async-start | bytes 2097152 | tf_op jit(solution)/shard_map/all_to_all | solution.py:507
  80.4 34.4 %collective-permute-start.3 = (bf16[2048,256]{1,0:T(8,128)(2,1)}, bf16[2048,256]{1,0:T(8,128)(2,1)}, u32[]{:S(2)}, u32[]{:S(2)}) collective-permute-start(bf16[2048,256]{1,0:T(8,128)(2,1)} %bitcast.6), channel_id=1, source_target_pairs={{0,8},{8,0},{16,24},{24,16},{1,9},{9,1},{17,25},{25,17},{2,10},{10... | collective-permute-start | bytes 3145736 | tf_op jit(solution)/shard_map/ppermute | solution.py:497
  82.4 34.5 %collective-permute-start.4 = (bf16[2048,256]{1,0:T(8,128)(2,1)}, bf16[2048,256]{1,0:T(8,128)(2,1)}, u32[]{:S(2)}, u32[]{:S(2)}) collective-permute-start(bf16[2048,256]{1,0:T(8,128)(2,1)} %bitcast.6), channel_id=1, source_target_pairs={{0,16},{8,24},{16,0},{24,8},{1,17},{9,25},{17,1},{25,9},{2,18},{10... | collective-permute-start | bytes 3145736 | tf_op jit(solution)/shard_map/ppermute | solution.py:497
  98.9 38.7 %all-to-all-start.1 = ((bf16[4,512,256]{2,1,0:T(8,128)(2,1)}), bf16[4,512,256]{2,1,0:T(8,128)(2,1)}, u32[]{:S(2)}, u32[]{:S(2)}) async-start(bf16[4,512,256]{2,1,0:T(8,128)(2,1)} %broadcast_in_dim.86), calls=%async_computation.1 | async-start | bytes 2097152 | tf_op jit(solution)/shard_map/all_to_all | solution.py:507
  120.7 14.2 %collective-permute-start.5 = (bf16[1024,256]{1,0:T(8,128)(2,1)}, bf16[1024,256]{1,0:T(8,128)(2,1)S(1)}, u32[]{:S(2)}, u32[]{:S(2)}) collective-permute-start(bf16[1024,256]{1,0:T(8,128)(2,1)} %slice.139), channel_id=1, source_target_pairs={{0,16},{8,24},{16,0},{24,8},{1,17},{9,25},{17,1},{25,9},{2,18},{10... | collective-permute-start | bytes 1572872 | tf_op jit(solution)/shard_map/ppermute | solution.py:497
  121.2 13.8 %collective-permute-start.6 = (bf16[1024,256]{1,0:T(8,128)(2,1)}, bf16[1024,256]{1,0:T(8,128)(2,1)}, u32[]{:S(2)}, u32[]{:S(2)}) collective-permute-start(bf16[1024,256]{1,0:T(8,128)(2,1)} %slice.140), channel_id=1, source_target_pairs={{0,8},{8,0},{16,24},{24,16},{1,9},{9,1},{17,25},{25,17},{2,10},{10... | collective-permute-start | bytes 1572872 | tf_op jit(solution)/shard_map/ppermute | solution.py:497
  126.5 19.5 %collective-permute-start.8 = (bf16[512,2048]{1,0:T(8,128)(2,1)}, bf16[512,2048]{1,0:T(8,128)(2,1)}, u32[]{:S(2)}, u32[]{:S(2)}) collective-permute-start(bf16[512,2048]{1,0:T(8,128)(2,1)} %bitcast_select_fusion.ga_ref), channel_id=1, source_target_pairs={{0,4},{4,0},{1,5},{5,1},{2,6},{6,2},{3,7},{7,3},{8,12},{12,8},{9,1... | collective-permute-start | bytes 6291464 | tf_op jit(solution)/shard_map/ppermute | solution.py:497
  126.6 19.4 %collective-permute-start.9 = (bf16[512,2048]{1,0:T(8,128)(2,1)}, bf16[512,2048]{1,0:T(8,128)(2,1)}, u32[]{:S(2)}, u32[]{:S(2)}) collective-permute-start(bf16[512,2048]{1,0:T(8,128)(2,1)} %collective-permute-done.1.ga_ref), channel_id=1, source_target_pairs={{0,4},{4,0},{1,5},{5,1},{2,6},{6,2},{3,7},{7,3},{8,12},{12,8},{9,1... | collective-permute-start | bytes 6291464 | tf_op jit(solution)/shard_map/ppermute | solution.py:497
  127.1 18.9 %collective-permute-start.10 = (bf16[512,2048]{1,0:T(8,128)(2,1)}, bf16[512,2048]{1,0:T(8,128)(2,1)}, u32[]{:S(2)}, u32[]{:S(2)}) collective-permute-start(bf16[512,2048]{1,0:T(8,128)(2,1)} %collective-permute-done.2.ga_ref), channel_id=1, source_target_pairs={{0,4},{4,0},{1,5},{5,1},{2,6},{6,2},{3,7},{7,3},{8,12},{12,8},{9,1... | collective-permute-start | bytes 6291464 | tf_op jit(solution)/shard_map/ppermute | solution.py:497
  140.2 74.3 %all-to-all-start.2 = ((bf16[4,1024,512]{1,2,0:T(8,128)(2,1)}), bf16[4,1024,512]{1,2,0:T(8,128)(2,1)}, u32[]{:S(2)}, u32[]{:S(2)}) async-start(bf16[4,1024,512]{1,2,0:T(8,128)(2,1)} %broadcast_in_dim.87), calls=%async_computation.2 | async-start | bytes 8388608 | tf_op jit(solution)/shard_map/all_to_all | solution.py:507
  145.2 479.1 %reduce-scatter.4.cloned.1.call-start = ((), (), s32[]{:S(2)}) async-start(), calls=%async_computation.10 | async-start | bytes 3604480 | tf_op jit(solution)/shard_map/reduce_scatter | solution.py:738
  146.0 12.6 %collective-permute-start.7 = (bf16[2048,256]{1,0:T(8,128)(2,1)}, bf16[2048,256]{1,0:T(8,128)(2,1)S(1)}, u32[]{:S(2)}, u32[]{:S(2)}) collective-permute-start(bf16[2048,256]{1,0:T(8,128)(2,1)} %bitcast.19), channel_id=1, source_target_pairs={{0,4},{4,0},{1,5},{5,1},{2,6},{6,2},{3,7},{7,3},{8,12},{12,8},{9,1... | collective-permute-start | bytes 3145736 | tf_op jit(solution)/shard_map/ppermute | solution.py:497
  148.8 65.7 %collective-permute-start.11 = (bf16[256,2048]{1,0:T(8,128)(2,1)S(1)}, bf16[256,2048]{1,0:T(8,128)(2,1)}, u32[]{:S(2)}, u32[]{:S(2)}) collective-permute-start(bf16[256,2048]{1,0:T(8,128)(2,1)S(1)} %slice.147), channel_id=1, source_target_pairs={{0,16},{8,24},{16,0},{24,8},{1,17},{9,25},{17,1},{25,9},{2,18},{10... | collective-permute-start | bytes 3145736 | tf_op jit(solution)/shard_map/ppermute | solution.py:497
  150.8 63.8 %collective-permute-start.12 = (bf16[256,2048]{1,0:T(8,128)(2,1)S(1)}, bf16[256,2048]{1,0:T(8,128)(2,1)}, u32[]{:S(2)}, u32[]{:S(2)}) collective-permute-start(bf16[256,2048]{1,0:T(8,128)(2,1)S(1)} %slice.148), channel_id=1, source_target_pairs={{0,8},{8,0},{16,24},{24,16},{1,9},{9,1},{17,25},{25,17},{2,10},{10... | collective-permute-start | bytes 3145736 | tf_op jit(solution)/shard_map/ppermute | solution.py:497
  219.2 4.2 collective-permute-start.13
  231.0 4.4 collective-permute-start.16
  231.2 48.0 %collective-permute-start.14 = (bf16[512,2048]{1,0:T(8,128)(2,1)S(1)}, bf16[512,2048]{1,0:T(8,128)(2,1)}, u32[]{:S(2)}, u32[]{:S(2)}) collective-permute-start(bf16[512,2048]{1,0:T(8,128)(2,1)S(1)} %multiply_convert_fusion.xa_ref), channel_id=1, source_target_pairs={{0,8},{8,0},{16,24},{24,16},{1,9},{9,1},{17,25},{25,17},{2,10},{10... | collective-permute-start | bytes 6291464 | tf_op jit(solution)/shard_map/ppermute | solution.py:497
  232.6 47.7 %collective-permute-start.15 = (bf16[512,2048]{1,0:T(8,128)(2,1)S(1)}, bf16[512,2048]{1,0:T(8,128)(2,1)}, u32[]{:S(2)}, u32[]{:S(2)}) collective-permute-start(bf16[512,2048]{1,0:T(8,128)(2,1)S(1)} %multiply_convert_fusion.xa_ref), channel_id=1, source_target_pairs={{0,16},{8,24},{16,0},{24,8},{1,17},{9,25},{17,1},{25,9},{2,18},{10... | collective-permute-start | bytes 6291464 | tf_op jit(solution)/shard_map/ppermute | solution.py:497
  280.3 7.5 collective-permute-start.19
  283.0 37.0 %collective-permute-start.17 = (bf16[256,2048]{1,0:T(8,128)(2,1)S(1)}, bf16[256,2048]{1,0:T(8,128)(2,1)S(1)}, u32[]{:S(2)}, u32[]{:S(2)}) collective-permute-start(bf16[256,2048]{1,0:T(8,128)(2,1)S(1)} %slice.151), channel_id=1, source_target_pairs={{0,16},{8,24},{16,0},{24,8},{1,17},{9,25},{17,1},{25,9},{2,18},{10... | collective-permute-start | bytes 3145736 | tf_op jit(solution)/shard_map/ppermute | solution.py:497
  283.7 36.3 %collective-permute-start.18 = (bf16[256,2048]{1,0:T(8,128)(2,1)S(1)}, bf16[256,2048]{1,0:T(8,128)(2,1)S(1)}, u32[]{:S(2)}, u32[]{:S(2)}) collective-permute-start(bf16[256,2048]{1,0:T(8,128)(2,1)S(1)} %slice.152), channel_id=1, source_target_pairs={{0,8},{8,0},{16,24},{24,16},{1,9},{9,1},{17,25},{25,17},{2,10},{10... | collective-permute-start | bytes 3145736 | tf_op jit(solution)/shard_map/ppermute | solution.py:497
  287.8 32.9 %collective-permute-start.21 = (bf16[512,2048]{1,0:T(8,128)(2,1)S(1)}, bf16[512,2048]{1,0:T(8,128)(2,1)S(1)}, u32[]{:S(2)}, u32[]{:S(2)}) collective-permute-start(bf16[512,2048]{1,0:T(8,128)(2,1)S(1)} %constant_dynamic-update-slice_fusion.2.ga_ref), channel_id=1, source_target_pairs={{0,4},{4,0},{1,5},{5,1},{2,6},{6,2},{3,7},{7,3},{8,12},{12,8},{9,1... | collective-permute-start | bytes 6291464 | tf_op jit(solution)/shard_map/ppermute | solution.py:497
  320.2 4.2 collective-permute-start.20
  356.7 4.4 collective-permute-start.22
  357.1 10.0 %collective-permute-start.25 = (bf16[512,2048]{1,0:T(8,128)(2,1)}, bf16[512,2048]{1,0:T(8,128)(2,1)S(1)}, u32[]{:S(2)}, u32[]{:S(2)}) collective-permute-start(bf16[512,2048]{1,0:T(8,128)(2,1)} %collective-permute-done.15.xa_ref), channel_id=1, source_target_pairs={{0,4},{4,0},{1,5},{5,1},{2,6},{6,2},{3,7},{7,3},{8,12},{12,8},{9,1... | collective-permute-start | bytes 6291464 | tf_op jit(solution)/shard_map/ppermute | solution.py:497
  357.3 9.6 %collective-permute-start.26 = (bf16[512,2048]{1,0:T(8,128)(2,1)S(1)}, bf16[512,2048]{1,0:T(8,128)(2,1)S(1)}, u32[]{:S(2)}, u32[]{:S(2)}) collective-permute-start(bf16[512,2048]{1,0:T(8,128)(2,1)S(1)} %copy-done.84), channel_id=1, source_target_pairs={{0,4},{4,0},{1,5},{5,1},{2,6},{6,2},{3,7},{7,3},{8,12},{12,8},{9,1... | collective-permute-start | bytes 6291464 | tf_op jit(solution)/shard_map/ppermute | solution.py:497
  363.6 35.6 %collective-permute-start.23 = (bf16[256,2048]{1,0:T(8,128)(2,1)S(1)}, bf16[256,2048]{1,0:T(8,128)(2,1)S(1)}, u32[]{:S(2)}, u32[]{:S(2)}) collective-permute-start(bf16[256,2048]{1,0:T(8,128)(2,1)S(1)} %get-tuple-element.371), channel_id=1, source_target_pairs={{0,8},{8,0},{16,24},{24,16},{1,9},{9,1},{17,25},{25,17},{2,10},{10... | collective-permute-start | bytes 3145736 | tf_op jit(solution)/shard_map/ppermute | solution.py:497
  364.3 34.9 %collective-permute-start.24 = (bf16[256,2048]{1,0:T(8,128)(2,1)S(1)}, bf16[256,2048]{1,0:T(8,128)(2,1)S(1)}, u32[]{:S(2)}, u32[]{:S(2)}) collective-permute-start(bf16[256,2048]{1,0:T(8,128)(2,1)S(1)} %get-tuple-element.370), channel_id=1, source_target_pairs={{0,16},{8,24},{16,0},{24,8},{1,17},{9,25},{17,1},{25,9},{2,18},{10... | collective-permute-start | bytes 3145736 | tf_op jit(solution)/shard_map/ppermute | solution.py:497
  399.2 4.4 collective-permute-start.27
  406.1 38.8 %collective-permute-start.28 = (bf16[2048,2048]{1,0:T(8,128)(2,1)}, bf16[2048,2048]{1,0:T(8,128)(2,1)}, u32[]{:S(2)}, u32[]{:S(2)}) collective-permute-start(bf16[2048,2048]{1,0:T(8,128)(2,1)} %get-tuple-element.269), channel_id=1, source_target_pairs={{0,4},{4,0},{1,5},{5,1},{2,6},{6,2},{3,7},{7,3},{8,12},{12,8},{9,1... | collective-permute-start | bytes 25165832 | tf_op jit(solution)/shard_map/ppermute | solution.py:497
  406.4 50.6 %collective-permute-start.31 = (bf16[512,2048]{1,0:T(8,128)(2,1)}, bf16[512,2048]{1,0:T(8,128)(2,1)S(1)}, u32[]{:S(2)}, u32[]{:S(2)}) collective-permute-start(bf16[512,2048]{1,0:T(8,128)(2,1)} %get-tuple-element.270), channel_id=1, source_target_pairs={{0,4},{4,0},{1,5},{5,1},{2,6},{6,2},{3,7},{7,3},{8,12},{12,8},{9,1... | collective-permute-start | bytes 6291464 | tf_op jit(solution)/shard_map/ppermute | solution.py:497
  406.6 50.5 %collective-permute-start.29 = (bf16[512,2048]{1,0:T(8,128)(2,1)}, bf16[512,2048]{1,0:T(8,128)(2,1)}, u32[]{:S(2)}, u32[]{:S(2)}) collective-permute-start(bf16[512,2048]{1,0:T(8,128)(2,1)} %add_convert_fusion.7), channel_id=1, source_target_pairs={{0,8},{8,0},{16,24},{24,16},{1,9},{9,1},{17,25},{25,17},{2,10},{10... | collective-permute-start | bytes 6291464 | tf_op jit(solution)/shard_map/ppermute | solution.py:497
  407.2 49.9 %collective-permute-start.30 = (bf16[512,2048]{1,0:T(8,128)(2,1)}, bf16[512,2048]{1,0:T(8,128)(2,1)}, u32[]{:S(2)}, u32[]{:S(2)}) collective-permute-start(bf16[512,2048]{1,0:T(8,128)(2,1)} %add_convert_fusion.6), channel_id=1, source_target_pairs={{0,16},{8,24},{16,0},{24,8},{1,17},{9,25},{17,1},{25,9},{2,18},{10... | collective-permute-start | bytes 6291464 | tf_op jit(solution)/shard_map/ppermute | solution.py:497
  425.7 198.6 %reduce-scatter.8.cloned.1.call-start = ((), (), s32[]{:S(2)}) async-start(), calls=%async_computation.12 | async-start | bytes 3604480 | tf_op jit(solution)/shard_map/reduce_scatter | solution.py:738
  469.4 4.5 collective-permute-start.32
  482.3 76.3 %all-to-all-start.3 = ((bf16[4,256,2048]{2,1,0:T(8,128)(2,1)}), bf16[4,256,2048]{2,1,0:T(8,128)(2,1)}, u32[]{:S(2)}, u32[]{:S(2)}) async-start(bf16[4,256,2048]{2,1,0:T(8,128)(2,1)} %bitcast.157), calls=%async_computation.3 | async-start | bytes 8388608 | tf_op jit(solution)/shard_map/all_to_all | solution.py:763
  487.3 147.2 %reduce-scatter.6.cloned.1.call-start = ((), (), s32[]{:S(2)}) async-start(), calls=%async_computation.11 | async-start | bytes 3604480 | tf_op jit(solution)/shard_map/reduce_scatter | solution.py:738
  506.6 51.0 %collective-permute-start.33 = (bf16[256,2048]{1,0:T(8,128)(2,1)}, bf16[256,2048]{1,0:T(8,128)(2,1)S(1)}, u32[]{:S(2)}, u32[]{:S(2)}) collective-permute-start(bf16[256,2048]{1,0:T(8,128)(2,1)} %get-tuple-element.289), channel_id=1, source_target_pairs={{0,8},{8,0},{16,24},{24,16},{1,9},{9,1},{17,25},{25,17},{2,10},{10... | collective-permute-start | bytes 3145736 | tf_op jit(solution)/shard_map/ppermute | solution.py:497
  508.6 50.0 %collective-permute-start.34 = (bf16[256,2048]{1,0:T(8,128)(2,1)}, bf16[256,2048]{1,0:T(8,128)(2,1)}, u32[]{:S(2)}, u32[]{:S(2)}) collective-permute-start(bf16[256,2048]{1,0:T(8,128)(2,1)} %get-tuple-element.290), channel_id=1, source_target_pairs={{0,16},{8,24},{16,0},{24,8},{1,17},{9,25},{17,1},{25,9},{2,18},{10... | collective-permute-start | bytes 3145736 | tf_op jit(solution)/shard_map/ppermute | solution.py:497
  562.6 71.8 %collective-permute-start.35 = (bf16[512,2048]{1,0:T(8,128)(2,1)}, bf16[512,2048]{1,0:T(8,128)(2,1)}, u32[]{:S(2)}, u32[]{:S(2)}) collective-permute-start(bf16[512,2048]{1,0:T(8,128)(2,1)} %add_convert_fusion.2), channel_id=1, source_target_pairs={{0,8},{8,0},{16,24},{24,16},{1,9},{9,1},{17,25},{25,17},{2,10},{10... | collective-permute-start | bytes 6291464 | tf_op jit(solution)/shard_map/ppermute | solution.py:497
  565.0 69.5 %collective-permute-start.36 = (bf16[512,2048]{1,0:T(8,128)(2,1)}, bf16[512,2048]{1,0:T(8,128)(2,1)}, u32[]{:S(2)}, u32[]{:S(2)}) collective-permute-start(bf16[512,2048]{1,0:T(8,128)(2,1)} %add_convert_fusion.1), channel_id=1, source_target_pairs={{0,16},{8,24},{16,0},{24,8},{1,17},{9,25},{17,1},{25,9},{2,18},{10... | collective-permute-start | bytes 6291464 | tf_op jit(solution)/shard_map/ppermute | solution.py:497
  570.2 64.3 %all-to-all-start.4 = ((bf16[8,256,512]{2,1,0:T(8,128)(2,1)}), bf16[8,256,512]{2,1,0:T(8,128)(2,1)}, u32[]{:S(2)}, u32[]{:S(2)}) async-start(bf16[8,256,512]{2,1,0:T(8,128)(2,1)} %bitcast.164), calls=%async_computation.7 | async-start | bytes 4194304 | tf_op jit(solution)/shard_map/all_to_all | solution.py:761
  579.4 42.7 %collective-permute-start.39 = (bf16[64,2048]{1,0:T(8,128)(2,1)S(1)}, bf16[64,2048]{1,0:T(8,128)(2,1)}, u32[]{:S(2)}, u32[]{:S(2)}) collective-permute-start(bf16[64,2048]{1,0:T(8,128)(2,1)S(1)} %get-tuple-element.368), channel_id=1, source_target_pairs={{0,3},{1,2},{2,1},{3,0},{4,7},{5,6},{6,5},{7,4},{8,11},{9,10},{10,... | collective-permute-start | bytes 786440 | tf_op jit(solution)/shard_map/ppermute | solution.py:497
  583.1 38.9 %collective-permute-start.38 = (bf16[64,2048]{1,0:T(8,128)(2,1)S(1)}, bf16[64,2048]{1,0:T(8,128)(2,1)}, u32[]{:S(2)}, u32[]{:S(2)}) collective-permute-start(bf16[64,2048]{1,0:T(8,128)(2,1)S(1)} %get-tuple-element.369), channel_id=1, source_target_pairs={{0,2},{1,3},{2,0},{3,1},{4,6},{5,7},{6,4},{7,5},{8,10},{9,11},{10,... | collective-permute-start | bytes 786440 | tf_op jit(solution)/shard_map/ppermute | solution.py:497
  583.1 38.9 %collective-permute-start.37 = (bf16[64,2048]{1,0:T(8,128)(2,1)S(1)}, bf16[64,2048]{1,0:T(8,128)(2,1)}, u32[]{:S(2)}, u32[]{:S(2)}) collective-permute-start(bf16[64,2048]{1,0:T(8,128)(2,1)S(1)} %get-tuple-element.367), channel_id=1, source_target_pairs={{0,1},{1,0},{2,3},{3,2},{4,5},{5,4},{6,7},{7,6},{8,9},{9,8},{10,11... | collective-permute-start | bytes 786440 | tf_op jit(solution)/shard_map/ppermute | solution.py:497
  639.0 9.2 %collective-permute-start.41 = (bf16[512,256]{1,0:T(8,128)(2,1)S(1)}, bf16[512,256]{1,0:T(8,128)(2,1)S(1)}, u32[]{:S(2)}, u32[]{:S(2)}) collective-permute-start(bf16[512,256]{1,0:T(8,128)(2,1)S(1)} %get-tuple-element.378), channel_id=1, source_target_pairs={{0,8},{8,0},{16,24},{24,16},{1,9},{9,1},{17,25},{25,17},{2,10},{10... | collective-permute-start | bytes 786440 | tf_op jit(solution)/shard_map/ppermute | solution.py:497
  640.5 13.7 %collective-permute-start.42 = (bf16[512,256]{1,0:T(8,128)(2,1)S(1)}, bf16[512,256]{1,0:T(8,128)(2,1)S(1)}, u32[]{:S(2)}, u32[]{:S(2)}) collective-permute-start(bf16[512,256]{1,0:T(8,128)(2,1)S(1)} %get-tuple-element.377), channel_id=1, source_target_pairs={{0,16},{8,24},{16,0},{24,8},{1,17},{9,25},{17,1},{25,9},{2,18},{10... | collective-permute-start | bytes 786440 | tf_op jit(solution)/shard_map/ppermute | solution.py:497
  642.0 12.2 %collective-permute-start.43 = (bf16[512,256]{1,0:T(8,128)(2,1)S(1)}, bf16[512,256]{1,0:T(8,128)(2,1)S(1)}, u32[]{:S(2)}, u32[]{:S(2)}) collective-permute-start(bf16[512,256]{1,0:T(8,128)(2,1)S(1)} %get-tuple-element.376), channel_id=1, source_target_pairs={{0,24},{8,16},{16,8},{24,0},{1,25},{9,17},{17,9},{25,1},{2,26},{10... | collective-permute-start | bytes 786440 | tf_op jit(solution)/shard_map/ppermute | solution.py:497
  656.2 9.5 %collective-permute-start.44 = (bf16[512,256]{1,0:T(8,128)(2,1)}, bf16[512,256]{1,0:T(8,128)(2,1)}, u32[]{:S(2)}, u32[]{:S(2)}) collective-permute-start(bf16[512,256]{1,0:T(8,128)(2,1)} %pad_maximum_fusion.11), channel_id=1, source_target_pairs={{0,4},{4,0},{1,5},{5,1},{2,6},{6,2},{3,7},{7,3},{8,12},{12,8},{9,1... | collective-permute-start | bytes 786440 | tf_op jit(solution)/shard_map/ppermute | solution.py:497
  661.7 31.6 %all-to-all-start.5 = ((bf16[8,3,176,256]{3,2,1,0:T(8,128)(2,1)}), bf16[8,3,176,256]{3,2,1,0:T(8,128)(2,1)S(1)}, u32[]{:S(2)}, u32[]{:S(2)}) async-start(bf16[8,3,176,256]{3,2,1,0:T(8,128)(2,1)} %copy-done.7), calls=%async_computation.8 | async-start | bytes 4325376 | tf_op jit(solution)/shard_map/all_to_all | solution.py:800
  680.5 28.2 %collective-permute-start.45 = (bf16[512,2048]{1,0:T(8,128)(2,1)}, bf16[512,2048]{1,0:T(8,128)(2,1)}, u32[]{:S(2)}, u32[]{:S(2)}) collective-permute-start(bf16[512,2048]{1,0:T(8,128)(2,1)} %add_convert_fusion), channel_id=1, source_target_pairs={{0,4},{4,0},{1,5},{5,1},{2,6},{6,2},{3,7},{7,3},{8,12},{12,8},{9,1... | collective-permute-start | bytes 6291464 | tf_op jit(solution)/shard_map/ppermute | solution.py:497
  682.6 80.0 %collective-permute-start.52 = (bf16[64,1024]{1,0:T(8,128)(2,1)}, bf16[64,1024]{1,0:T(8,128)(2,1)}, u32[]{:S(2)}, u32[]{:S(2)}) collective-permute-start(bf16[64,1024]{1,0:T(8,128)(2,1)} %get-tuple-element.362), channel_id=1, source_target_pairs={{0,4},{4,0},{1,5},{5,1},{2,6},{6,2},{3,7},{7,3},{8,12},{12,8},{9,1... | collective-permute-start | bytes 393224 | tf_op jit(solution)/shard_map/ppermute | solution.py:497
  685.1 55.9 %collective-permute-start.46 = (bf16[2,64,512]{2,1,0:T(8,128)(2,1)}, bf16[2,64,512]{2,1,0:T(8,128)(2,1)}, u32[]{:S(2)}, u32[]{:S(2)}) collective-permute-start(bf16[2,64,512]{2,1,0:T(8,128)(2,1)} %get-tuple-element.322), channel_id=1, source_target_pairs={{0,1},{1,0},{2,3},{3,2},{4,5},{5,4},{6,7},{7,6},{8,9},{9,8},{10,11... | collective-permute-start | bytes 393224 | tf_op jit(solution)/shard_map/ppermute | solution.py:497
  686.6 54.4 %collective-permute-start.47 = (bf16[2,64,512]{2,1,0:T(8,128)(2,1)S(1)}, bf16[2,64,512]{2,1,0:T(8,128)(2,1)}, u32[]{:S(2)}, u32[]{:S(2)}) collective-permute-start(bf16[2,64,512]{2,1,0:T(8,128)(2,1)S(1)} %get-tuple-element.323), channel_id=1, source_target_pairs={{0,2},{1,3},{2,0},{3,1},{4,6},{5,7},{6,4},{7,5},{8,10},{9,11},{10,... | collective-permute-start | bytes 393224 | tf_op jit(solution)/shard_map/ppermute | solution.py:497
  689.4 51.7 %collective-permute-start.48 = (bf16[2,64,512]{2,1,0:T(8,128)(2,1)S(1)}, bf16[2,64,512]{2,1,0:T(8,128)(2,1)}, u32[]{:S(2)}, u32[]{:S(2)}) collective-permute-start(bf16[2,64,512]{2,1,0:T(8,128)(2,1)S(1)} %get-tuple-element.324), channel_id=1, source_target_pairs={{0,3},{1,2},{2,1},{3,0},{4,7},{5,6},{6,5},{7,4},{8,11},{9,10},{10,... | collective-permute-start | bytes 393224 | tf_op jit(solution)/shard_map/ppermute | solution.py:497
  694.7 42.2 %all-to-all-start.6 = ((bf16[8,256,768]{2,1,0:T(8,128)(2,1)}), bf16[8,256,768]{2,1,0:T(8,128)(2,1)S(1)}, u32[]{:S(2)}, u32[]{:S(2)}) async-start(bf16[8,256,768]{2,1,0:T(8,128)(2,1)} %bitcast.149), calls=%async_computation.9 | async-start | bytes 6291456 | tf_op jit(solution)/shard_map/all_to_all | solution.py:761
  741.1 9.7 %collective-permute-start.51 = (bf16[2,64,768]{2,1,0:T(8,128)(2,1)S(1)}, bf16[2,64,768]{2,1,0:T(8,128)(2,1)S(1)}, u32[]{:S(2)}, u32[]{:S(2)}) collective-permute-start(bf16[2,64,768]{2,1,0:T(8,128)(2,1)S(1)} %get-tuple-element.344), channel_id=1, source_target_pairs={{0,3},{1,2},{2,1},{3,0},{4,7},{5,6},{6,5},{7,4},{8,11},{9,10},{10,... | collective-permute-start | bytes 589832 | tf_op jit(solution)/shard_map/ppermute | solution.py:497
  744.8 12.8 %collective-permute-start.50 = (bf16[2,64,768]{2,1,0:T(8,128)(2,1)S(1)}, bf16[2,64,768]{2,1,0:T(8,128)(2,1)S(1)}, u32[]{:S(2)}, u32[]{:S(2)}) collective-permute-start(bf16[2,64,768]{2,1,0:T(8,128)(2,1)S(1)} %get-tuple-element.343), channel_id=1, source_target_pairs={{0,2},{1,3},{2,0},{3,1},{4,6},{5,7},{6,4},{7,5},{8,10},{9,11},{10,... | collective-permute-start | bytes 589832 | tf_op jit(solution)/shard_map/ppermute | solution.py:497
  744.8 12.8 %collective-permute-start.49 = (bf16[2,64,768]{2,1,0:T(8,128)(2,1)S(1)}, bf16[2,64,768]{2,1,0:T(8,128)(2,1)S(1)}, u32[]{:S(2)}, u32[]{:S(2)}) collective-permute-start(bf16[2,64,768]{2,1,0:T(8,128)(2,1)S(1)} %get-tuple-element.342), channel_id=1, source_target_pairs={{0,1},{1,0},{2,3},{3,2},{4,5},{5,4},{6,7},{7,6},{8,9},{9,8},{10,11... | collective-permute-start | bytes 589832 | tf_op jit(solution)/shard_map/ppermute | solution.py:497
  (86 other events, 847.5 us)
Sparse Core Ops, SparseCore 0:
  13.8 53.4 all-gather.7
  68.9 152.7 all-gather.5
  425.8 56.4 reduce-scatter.3
  484.5 56.0 reduce-scatter.7
  542.7 68.6 reduce-scatter.5

commit v6 on v5

--- a/solution.py
+++ b/solution.py
@@ -368,7 +368,7 @@
         + [shape(pairs * 2 * rows, model_dim)] * 2
         + [shape(pairs * 2 * rows, units)] * 3,
         input_output_aliases={8 + i: 2 + i for i in range(count)},
-        compiler_params=pltpu.CompilerParams(vmem_limit_bytes=52 * 2**20),
+        compiler_params=pltpu.CompilerParams(vmem_limit_bytes=60 * 2**20),
         cost_estimate=pl.CostEstimate(flops=2**20, bytes_accessed=2**16, transcendentals=0),
         name="ffn_pair",
     )(place, xa, xb, ga, gb, weights, weights, weights, *kept)
@@ -452,7 +452,7 @@
             out_specs=[pl.BlockSpec((2, rows, columns), lambda i, *_: (0, 0, 0))] * planes,
         ),
         out_shape=[jax.ShapeDtypeStruct((2, rows, columns), BF16)] * planes,
-        compiler_params=pltpu.CompilerParams(vmem_limit_bytes=32 * 2**20),
+        compiler_params=pltpu.CompilerParams(vmem_limit_bytes=60 * 2**20),
         cost_estimate=pl.CostEstimate(flops=2**20, bytes_accessed=dealt.size * 3, transcendentals=0),
         name="sum_chips",
     )(plane.reshape(1).astype(jnp.int32), dealt)

time: 785 us -> 789 us (level)
  waiting for transfers between devices: 149 us -> 184 us
  Pallas kernels: 239 us -> 207 us
    ppermute x53, waiting for transfers between devices: 119 us -> 152 us  [exchange(): return lax.ppermute(value, axis, [(i, i ^ distance) for i in range(size)])]
    pallas_call x2, Pallas kernels: 71.2 us -> 49.1 us  [attention_backward(): pl.pallas_call(functools.partial(attend_backward, group, blk, last), grid...]
    pallas_call x1, Pallas kernels: 37.1 us -> 24 us  [attention_forward(): pl.pallas_call(functools.partial(attend_forward, heads, blk), grid_spec=p...]
    unnamed x182 -> x172, local copies, waits for them, and re-layouts: 33.8 us -> 30.1 us
  transfers between devices with their start and end apart: 65 -> 65, of which waited for: 26 -> 25; matrix products, arithmetic and copies ran while one was open for 32% -> 33% of each run, Pallas kernels for 27% -> 23%
where the time goes in v6:
time: 789 us; the launch traced here: 777 us
  Pallas kernels  207 us (26%)
  waiting for transfers between devices  184 us (23%)
  matrix products  117 us (15%)
  other arithmetic  93.3 us (12%)
  local copies, waits for them, and re-layouts  83 us (11%)
  starting transfers between devices  77.3 us (10%)
  between operations  16.1 us (2%)
    ppermute x53, waiting for transfers between devices, exchange(): return lax.ppermute(value, axis, [(i, i ^ distance) for i in range(size)])  152 us
    pallas_call x4, Pallas kernels, ffn_pair(): pl.pallas_call(functools.partial(ffn_rows, count, tiles), grid_spec=pltpu...  124 us
    dot_general x7, matrix products, contract_rows(): lax.dot_general(left, right, (((0,), (0,)), ((), ())), preferred_element_...  74.9 us
    pallas_call x2, Pallas kernels, attention_backward(): pl.pallas_call(functools.partial(attend_backward, group, blk, last), grid...  49.1 us
    ppermute x53, starting transfers between devices, exchange(): return lax.ppermute(value, axis, [(i, i ^ distance) for i in range(size)])  45.3 us
    unnamed x172, local copies, waits for them, and re-layouts  30.1 us
    all_to_all x2, waiting for transfers between devices, deal_rows(): lax.all_to_all(terms.reshape(places, planes * (depth // places), -1), ('c...  29.7 us
    pallas_call x1, Pallas kernels, attention_forward(): pl.pallas_call(functools.partial(attend_forward, heads, blk), grid_spec=p...  24 us
  transfers between devices with their start and end apart: 65, of which 25 were waited for; matrix products, arithmetic and copies ran while one was open for 33% of the time, Pallas kernels for 23%

profile of v6, /device:TPU:0, one launch (start us, length us, event | category | flops | bytes accessed | tf_op | source)
XLA Modules:
  0.0 777.2 jit_solution(16234564588541144311)
XLA Ops:
  15.2 3.1 bitcast_select_fusion.ga_ref
  18.3 2.9 collective-permute-start.1
  22.8 4.1 constant_dynamic-slice_fusion.2
  30.3 2.9 constant_dynamic-slice_fusion.4
  35.4 3.0 pad_maximum_fusion.4
  40.6 26.6 %collective-permute-done.1.ga_ref = bf16[512,2048]{1,0:T(8,128)(2,1)} collective-permute-done((bf16[512,2048]{1,0:T(8,128)(2,1)}, bf16[512,2048]{1,0:T(8,128)(2,1)}, u32[]{:S(2)}, u32[]{:S(2)}) %collective-permute-start.1) | collective-permute-done | bytes 2097184 | tf_op jit(solution)/shard_map/ppermute | solution.py:497
  73.0 4.3 all-to-all-start
  77.3 3.2 fusion.60
  84.7 6.1 fusion.2
  98.9 4.3 all-to-all-start.1
  103.2 11.7 %collective-permute-done.3 = bf16[2048,256]{1,0:T(8,128)(2,1)} collective-permute-done((bf16[2048,256]{1,0:T(8,128)(2,1)}, bf16[2048,256]{1,0:T(8,128)(2,1)}, u32[]{:S(2)}, u32[]{:S(2)}) %collective-permute-start.3) | collective-permute-done | bytes 1048608 | tf_op jit(solution)/shard_map/ppermute | solution.py:497
  131.7 3.1 collective-permute-done.5
  140.2 5.0 all-to-all-start.2
  152.3 6.3 fusion.63.q_ref
  160.0 24.0 %attend_forward.1 = (bf16[1024,1024]{1,0:T(8,128)(2,1)S(1)}, f32[4,1,2048]{2,1,0:T(1,128)S(1)}, bf16[4,128,2048]{2,1,0:T(8,128)(2,1)S(1)}) custom-call(s32[2]{0:T(128)S(1)} %pad_add_fusion.scal_ref, s32[16]{0:T(128)S(1)} %bitcast.131, f32[1024,1024]{1,0:T(8,128)S(1)} %fusion.63.q_ref, f32[64,1024]{1,0:T(8,128)S(1)} %copy.103.cos_ref, ...), custom_call_target="tpu_custom_call" | custom-call | flops 1048576 | bytes 65536 | tf_op jit(solution)/shard_map/attend_forward/pallas_call | solution.py:125
  186.6 27.9 %collective-permute-done.11 = bf16[256,2048]{1,0:T(8,128)(2,1)} collective-permute-done((bf16[256,2048]{1,0:T(8,128)(2,1)S(1)}, bf16[256,2048]{1,0:T(8,128)(2,1)}, u32[]{:S(2)}, u32[]{:S(2)}) %collective-permute-start.11) | collective-permute-done | bytes 1048608 | tf_op jit(solution)/shard_map/ppermute | solution.py:497
  214.6 4.7 convolution_convert_fusion.6
  219.4 4.1 collective-permute-done.13
  223.5 5.1 multiply_reduce_fusion.2
  235.4 31.0 %ffn_pair.4 = (bf16[512,2048]{1,0:T(8,128)(2,1)}, bf16[512,2048]{1,0:T(8,128)(2,1)}, bf16[2048,2048]{1,0:T(8,128)(2,1)}, bf16[2048,2048]{1,0:T(8,128)(2,1)}, bf1...) custom-call(s32[1]{0:T(128)} %constant.106.clone.1.place_ref, ...), custom_call_target="tpu_custom_call" | custom-call | flops 1048576 | bytes 65536 | tf_op jit(solution)/shard_map/ffn_pair/pallas_call | solution.py:357
  266.4 12.8 %collective-permute-done.14.xa_ref = bf16[512,2048]{1,0:T(8,128)(2,1)} collective-permute-done((bf16[512,2048]{1,0:T(8,128)(2,1)S(1)}, bf16[512,2048]{1,0:T(8,128)(2,1)}, u32[]{:S(2)}, u32[]{:S(2)}) %collective-permute-start.14) | collective-permute-done | bytes 2097184 | tf_op jit(solution)/shard_map/ppermute | solution.py:497
  289.8 31.1 %ffn_pair.5 = (bf16[512,2048]{1,0:T(8,128)(2,1)}, bf16[512,2048]{1,0:T(8,128)(2,1)}, bf16[2048,2048]{1,0:T(8,128)(2,1)}, bf16[2048,2048]{1,0:T(8,128)(2,1)}, bf1...) custom-call(s32[1]{0:T(128)} %constant.107.clone.1.place_ref, ...), custom_call_target="tpu_custom_call", output_to_operand_aliasing={{2}: (8, {}), {3}: (9, {}), {4}: (10, {}), {5}: (11, {}), {... | custom-call | flops 1048576 | bytes 65536 | tf_op jit(solution)/shard_map/ffn_pair/pallas_call | solution.py:357
  324.9 2.9 collective-permute-done.20.xb_ref
  329.1 30.8 %ffn_pair.6 = (bf16[512,2048]{1,0:T(8,128)(2,1)}, bf16[512,2048]{1,0:T(8,128)(2,1)}, bf16[2048,2048]{1,0:T(8,128)(2,1)}, bf16[2048,2048]{1,0:T(8,128)(2,1)}, bf1...) custom-call(s32[1]{0:T(128)} %constant.105.clone.1.place_ref, ...), custom_call_target="tpu_custom_call", output_to_operand_aliasing={{2}: (8, {}), {3}: (9, {}), {4}: (10, {}), {5}: (11, {}), {... | custom-call | flops 1048576 | bytes 65536 | tf_op jit(solution)/shard_map/ffn_pair/pallas_call | solution.py:357
  360.6 5.5 collective-permute-done.22
  373.3 30.9 %ffn_pair.7 = (bf16[512,2048]{1,0:T(8,128)(2,1)}, bf16[512,2048]{1,0:T(8,128)(2,1)}, bf16[2048,2048]{1,0:T(8,128)(2,1)}, bf16[2048,2048]{1,0:T(8,128)(2,1)}, bf1...) custom-call(s32[1]{0:T(128)} %constant.108.clone.1.place_ref, ...), custom_call_target="tpu_custom_call", output_to_operand_aliasing={{2}: (8, {}), {3}: (9, {}), {4}: (10, {}), {5}: (11, {}), {... | custom-call | flops 1048576 | bytes 65536 | tf_op jit(solution)/shard_map/ffn_pair/pallas_call | solution.py:357
  404.3 4.5 add_convert_fusion.7
  408.8 3.8 add_convert_fusion.6
  415.2 17.1 %convolution_convert_fusion.2 = bf16[704,2048]{1,0:T(8,128)(2,1)} fusion(bf16[4096,704]{1,0:T(8,128)(2,1)S(1)} %copy-done.24, bf16[4096,2048]{1,0:T(8,128)(2,1)} %get-tuple-element.284), kind=kOutput, calls=%fused_computation.39 | convolution fusion | flops 11812601856 | bytes 25427968 | tf_op jit(solution)/shard_map/dot_general | solution.py:484
  432.3 19.1 %convolution_convert_fusion.3 = bf16[704,2048]{1,0:T(8,128)(2,1)} fusion(bf16[4096,704]{1,0:T(8,128)(2,1)} %get-tuple-element.271, bf16[4096,2048]{1,0:T(8,128)(2,1)} %get-tuple-element.272), kind=kOutput, calls=%fused_computation.40 | convolution fusion | flops 11812601856 | bytes 25427968 | tf_op jit(solution)/shard_map/dot_general | solution.py:484
  451.4 4.4 add_convert_fusion.10
  455.8 7.9 %add_convert_fusion.3 = (bf16[512,2048]{1,0:T(8,128)(2,1)}, bf16[512,2048]{1,0:T(8,128)(2,1)}, bf16[512,2048]{1,0:T(8,128)(2,1)}) fusion(bf16[2048,2048]{1,0:T(8,128)(2,1)} %collective-permute-done.28, bf16[2048,2048]{1,0:T(8,128)(2,1)} %get-tuple-element.268), kind=kLoop, calls=%fused_computation.29 | loop fusion | flops 12582912 | bytes 18874368 | tf_op jit(solution)/shard_map/convert_element_type | solution.py:727
  464.7 4.0 multiply_reduce_fusion
  468.8 7.1 fusion.58
  476.0 4.5 collective-permute-done.32
  480.4 8.4 %convolution_convert_fusion = bf16[1024,2048]{1,0:T(8,128)(2,1)} fusion(bf16[1024,1024]{1,0:T(8,128)(2,1)S(1)} %copy-done.5, bf16[512,2048]{1,0:T(8,128)(2,1)} %collective-permute-done.32, bf16[512,2048]{1,0:T(8,128)(2,1)} %get-tuple-element.352), kind=kOutput, calls=%fused_computation.37 | convolution fusion | flops 4305453056 | bytes 10485760 | tf_op jit(solution)/shard_map/dot_general | solution.py:484
  488.8 5.0 all-to-all-start.3
  493.8 19.2 %convolution_convert_fusion.1 = bf16[704,2048]{1,0:T(8,128)(2,1)} fusion(bf16[4096,704]{1,0:T(8,128)(2,1)} %get-tuple-element.283, bf16[4096,2048]{1,0:T(8,128)(2,1)} %get-tuple-element.284), kind=kOutput, calls=%fused_computation.38 | convolution fusion | flops 11812601856 | bytes 25427968 | tf_op jit(solution)/shard_map/dot_general | solution.py:484
  516.6 8.0 %fusion.16.g_ref = bf16[1024,1024]{1,0:T(8,128)(2,1)S(1)} fusion(bf16[1024,2048]{0,1:T(8,128)(2,1)} %bitcast.21, bf16[512,2048]{1,0:T(8,128)(2,1)} %collective-permute-done.32, bf16[512,2048]{1,0:T(8,128)(2,1)} %get-tuple-element.352), kind=kOutput, calls=%fused_computation.56 | convolution fusion | flops 4304404480 | bytes 10485760 | tf_op jit(solution)/shard_map/dot_general | solution.py:488
  524.6 24.9 %attend_backward.2 = (bf16[1024,512]{1,0:T(8,128)(2,1)S(1)}, f32[4096,256]{1,0:T(8,128)}) custom-call(s32[2]{0:T(128)S(1)} %copy-done.20, s32[16]{0:T(128)S(1)} %bitcast.132, bf16[4,128,2048]{2,1,0:T(8,128)(2,1)S(1)} %copy-done.7, bf16[1024,1024]{1,0:T(8,128)(2,1)S(1)} %fusion.16.g_ref, bf16[1024,1024]{1,0:T(8,128)(2,1)} %copy-done.4, ...), custom_call_target="tpu_custom_call" | custom-call | flops 1048576 | bytes 65536 | tf_op jit(solution)/shard_map/attend_backward/pallas_call | solution.py:249
  550.4 13.7 %collective-permute-done.33 = bf16[256,2048]{1,0:T(8,128)(2,1)S(1)} collective-permute-done((bf16[256,2048]{1,0:T(8,128)(2,1)}, bf16[256,2048]{1,0:T(8,128)(2,1)S(1)}, u32[]{:S(2)}, u32[]{:S(2)}) %collective-permute-start.33) | collective-permute-done | bytes 1048608 | tf_op jit(solution)/shard_map/ppermute | solution.py:497
  565.1 4.0 add_convert_fusion.2
  573.0 3.7 convolution_convert_fusion.5
  576.7 4.4 all-to-all-start.4
  581.1 3.3 convert_reduce_fusion
  585.9 3.8 collective-permute-start.39
  590.4 24.2 %attend_backward.3 = (bf16[1024,512]{1,0:T(8,128)(2,1)S(1)}, bf16[2048,256]{1,0:T(8,128)(2,1)S(1)}, bf16[2048,256]{1,0:T(8,128)(2,1)S(1)}) custom-call(s32[2]{0:T(128)S(1)} %copy-done.20, s32[16]{0:T(128)S(1)} %bitcast.133, bf16[4,128,2048]{2,1,0:T(8,128)(2,1)S(1)} %copy-done.7, bf16[1024,1024]{1,0:T(8,128)(2,1)} %copy-done.8, bf16[1024,1024]{1,0:T(8,128)(2,1)} %copy-done.4, ...), custom_call_target="tpu_custom_call" | custom-call | flops 1048576 | bytes 65536 | tf_op jit(solution)/shard_map/attend_backward/pallas_call | solution.py:249
  617.5 9.4 %collective-permute-done.38 = bf16[64,2048]{1,0:T(8,128)(2,1)} collective-permute-done((bf16[64,2048]{1,0:T(8,128)(2,1)S(1)}, bf16[64,2048]{1,0:T(8,128)(2,1)}, u32[]{:S(2)}, u32[]{:S(2)}) %collective-permute-start.38) | collective-permute-done | bytes 262176 | tf_op jit(solution)/shard_map/ppermute | solution.py:497
  629.1 11.9 %all-to-all-done.4.dealt_ref = bf16[8,256,512]{2,1,0:T(8,128)(2,1)} async-done(((bf16[8,256,512]{2,1,0:T(8,128)(2,1)}), bf16[8,256,512]{2,1,0:T(8,128)(2,1)}, u32[]{:S(2)}, u32[]{:S(2)}) %all-to-all-start.4) | async-done | bytes 2097184 | tf_op jit(solution)/shard_map/all_to_all | solution.py:761
  641.1 2.8 collective-permute-done.40
  649.1 3.8 convolution_convert_fusion.4
  654.7 6.0 collective-permute-done.42
  668.2 4.0 all-to-all-start.5
  673.7 3.7 convolution_convert_fusion.7
  680.8 6.0 add_convert_fusion
  699.5 4.6 all-to-all-start.6
  704.1 7.3 select_convert_fusion
  713.7 5.9 fusion.6
  719.7 4.5 fusion.10
  724.2 17.8 %all-to-all-done.6.dealt_ref = bf16[8,256,768]{2,1,0:T(8,128)(2,1)} async-done(((bf16[8,256,768]{2,1,0:T(8,128)(2,1)}), bf16[8,256,768]{2,1,0:T(8,128)(2,1)}, u32[]{:S(2)}, u32[]{:S(2)}) %all-to-all-start.6) | async-done | bytes 3145760 | tf_op jit(solution)/shard_map/all_to_all | solution.py:761
  742.0 3.2 sum_chips.3
  745.2 3.7 collective-permute-start.51
  750.9 4.4 collective-permute-done.51
  755.2 7.4 collective-permute-done.50
  (365 shorter events, 162.4 us)
Async XLA Ops:
  7.2 63.7 %all-gather.8.cloned.1.call-start = ((), (), s32[]{:S(2)}) async-start(), calls=%async_computation.14 | async-start | bytes 2969600 | tf_op jit(solution)/shard_map/all_gather | solution.py:612
  13.7 221.7 %all-gather.6.cloned.1.call-start = ((), (), s32[]{:S(2)}) async-start(), calls=%async_computation.13 | async-start | bytes 10813440 | tf_op jit(solution)/shard_map/all_gather | solution.py:639
  18.3 48.9 %collective-permute-start.1 = (bf16[512,2048]{1,0:T(8,128)(2,1)}, bf16[512,2048]{1,0:T(8,128)(2,1)}, u32[]{:S(2)}, u32[]{:S(2)}) collective-permute-start(bf16[512,2048]{1,0:T(8,128)(2,1)} %bitcast_select_fusion.ga_ref), channel_id=1, source_target_pairs={{0,8},{8,0},{16,24},{24,16},{1,9},{9,1},{17,25},{25,17},{2,10},{10... | collective-permute-start | bytes 6291464 | tf_op jit(solution)/shard_map/ppermute | solution.py:497
  21.3 47.4 %collective-permute-start.2 = (bf16[512,2048]{1,0:T(8,128)(2,1)}, bf16[512,2048]{1,0:T(8,128)(2,1)}, u32[]{:S(2)}, u32[]{:S(2)}) collective-permute-start(bf16[512,2048]{1,0:T(8,128)(2,1)} %bitcast_select_fusion.ga_ref), channel_id=1, source_target_pairs={{0,16},{8,24},{16,0},{24,8},{1,17},{9,25},{17,1},{25,9},{2,18},{10... | collective-permute-start | bytes 6291464 | tf_op jit(solution)/shard_map/ppermute | solution.py:497
  22.8 45.9 %collective-permute-start = (bf16[512,2048]{1,0:T(8,128)(2,1)S(1)}, bf16[512,2048]{1,0:T(8,128)(2,1)}, u32[]{:S(2)}, u32[]{:S(2)}) collective-permute-start(bf16[512,2048]{1,0:T(8,128)(2,1)S(1)} %bitcast.146), channel_id=1, source_target_pairs={{0,4},{4,0},{1,5},{5,1},{2,6},{6,2},{3,7},{7,3},{8,12},{12,8},{9,1... | collective-permute-start | bytes 6291464 | tf_op jit(solution)/shard_map/ppermute | solution.py:497
  73.0 19.4 %all-to-all-start = ((bf16[4,4,128,256]{3,2,1,0:T(8,128)(2,1)}), bf16[4,4,128,256]{3,2,1,0:T(8,128)(2,1)}, u32[]{:S(2)}, u32[]{:S(2)}) async-start(bf16[4,4,128,256]{3,2,1,0:T(8,128)(2,1)} %broadcast_in_dim.85), calls=%async_computation | async-start | bytes 2097152 | tf_op jit(solution)/shard_map/all_to_all | solution.py:507
  80.4 34.4 %collective-permute-start.3 = (bf16[2048,256]{1,0:T(8,128)(2,1)}, bf16[2048,256]{1,0:T(8,128)(2,1)}, u32[]{:S(2)}, u32[]{:S(2)}) collective-permute-start(bf16[2048,256]{1,0:T(8,128)(2,1)} %bitcast.6), channel_id=1, source_target_pairs={{0,8},{8,0},{16,24},{24,16},{1,9},{9,1},{17,25},{25,17},{2,10},{10... | collective-permute-start | bytes 3145736 | tf_op jit(solution)/shard_map/ppermute | solution.py:497
  82.4 34.5 %collective-permute-start.4 = (bf16[2048,256]{1,0:T(8,128)(2,1)}, bf16[2048,256]{1,0:T(8,128)(2,1)}, u32[]{:S(2)}, u32[]{:S(2)}) collective-permute-start(bf16[2048,256]{1,0:T(8,128)(2,1)} %bitcast.6), channel_id=1, source_target_pairs={{0,16},{8,24},{16,0},{24,8},{1,17},{9,25},{17,1},{25,9},{2,18},{10... | collective-permute-start | bytes 3145736 | tf_op jit(solution)/shard_map/ppermute | solution.py:497
  98.9 38.8 %all-to-all-start.1 = ((bf16[4,512,256]{2,1,0:T(8,128)(2,1)}), bf16[4,512,256]{2,1,0:T(8,128)(2,1)}, u32[]{:S(2)}, u32[]{:S(2)}) async-start(bf16[4,512,256]{2,1,0:T(8,128)(2,1)} %broadcast_in_dim.86), calls=%async_computation.1 | async-start | bytes 2097152 | tf_op jit(solution)/shard_map/all_to_all | solution.py:507
  120.6 14.2 %collective-permute-start.5 = (bf16[1024,256]{1,0:T(8,128)(2,1)}, bf16[1024,256]{1,0:T(8,128)(2,1)S(1)}, u32[]{:S(2)}, u32[]{:S(2)}) collective-permute-start(bf16[1024,256]{1,0:T(8,128)(2,1)} %slice.139), channel_id=1, source_target_pairs={{0,16},{8,24},{16,0},{24,8},{1,17},{9,25},{17,1},{25,9},{2,18},{10... | collective-permute-start | bytes 1572872 | tf_op jit(solution)/shard_map/ppermute | solution.py:497
  121.2 13.8 %collective-permute-start.6 = (bf16[1024,256]{1,0:T(8,128)(2,1)}, bf16[1024,256]{1,0:T(8,128)(2,1)}, u32[]{:S(2)}, u32[]{:S(2)}) collective-permute-start(bf16[1024,256]{1,0:T(8,128)(2,1)} %slice.140), channel_id=1, source_target_pairs={{0,8},{8,0},{16,24},{24,16},{1,9},{9,1},{17,25},{25,17},{2,10},{10... | collective-permute-start | bytes 1572872 | tf_op jit(solution)/shard_map/ppermute | solution.py:497
  126.5 19.5 %collective-permute-start.8 = (bf16[512,2048]{1,0:T(8,128)(2,1)}, bf16[512,2048]{1,0:T(8,128)(2,1)}, u32[]{:S(2)}, u32[]{:S(2)}) collective-permute-start(bf16[512,2048]{1,0:T(8,128)(2,1)} %bitcast_select_fusion.ga_ref), channel_id=1, source_target_pairs={{0,4},{4,0},{1,5},{5,1},{2,6},{6,2},{3,7},{7,3},{8,12},{12,8},{9,1... | collective-permute-start | bytes 6291464 | tf_op jit(solution)/shard_map/ppermute | solution.py:497
  126.6 19.5 %collective-permute-start.9 = (bf16[512,2048]{1,0:T(8,128)(2,1)}, bf16[512,2048]{1,0:T(8,128)(2,1)}, u32[]{:S(2)}, u32[]{:S(2)}) collective-permute-start(bf16[512,2048]{1,0:T(8,128)(2,1)} %collective-permute-done.1.ga_ref), channel_id=1, source_target_pairs={{0,4},{4,0},{1,5},{5,1},{2,6},{6,2},{3,7},{7,3},{8,12},{12,8},{9,1... | collective-permute-start | bytes 6291464 | tf_op jit(solution)/shard_map/ppermute | solution.py:497
  127.1 19.0 %collective-permute-start.10 = (bf16[512,2048]{1,0:T(8,128)(2,1)}, bf16[512,2048]{1,0:T(8,128)(2,1)}, u32[]{:S(2)}, u32[]{:S(2)}) collective-permute-start(bf16[512,2048]{1,0:T(8,128)(2,1)} %collective-permute-done.2.ga_ref), channel_id=1, source_target_pairs={{0,4},{4,0},{1,5},{5,1},{2,6},{6,2},{3,7},{7,3},{8,12},{12,8},{9,1... | collective-permute-start | bytes 6291464 | tf_op jit(solution)/shard_map/ppermute | solution.py:497
  140.2 74.3 %all-to-all-start.2 = ((bf16[4,1024,512]{1,2,0:T(8,128)(2,1)}), bf16[4,1024,512]{1,2,0:T(8,128)(2,1)}, u32[]{:S(2)}, u32[]{:S(2)}) async-start(bf16[4,1024,512]{1,2,0:T(8,128)(2,1)} %broadcast_in_dim.87), calls=%async_computation.2 | async-start | bytes 8388608 | tf_op jit(solution)/shard_map/all_to_all | solution.py:507
  145.2 483.8 %reduce-scatter.4.cloned.1.call-start = ((), (), s32[]{:S(2)}) async-start(), calls=%async_computation.10 | async-start | bytes 3604480 | tf_op jit(solution)/shard_map/reduce_scatter | solution.py:738
  146.0 12.6 %collective-permute-start.7 = (bf16[2048,256]{1,0:T(8,128)(2,1)}, bf16[2048,256]{1,0:T(8,128)(2,1)S(1)}, u32[]{:S(2)}, u32[]{:S(2)}) collective-permute-start(bf16[2048,256]{1,0:T(8,128)(2,1)} %bitcast.19), channel_id=1, source_target_pairs={{0,4},{4,0},{1,5},{5,1},{2,6},{6,2},{3,7},{7,3},{8,12},{12,8},{9,1... | collective-permute-start | bytes 3145736 | tf_op jit(solution)/shard_map/ppermute | solution.py:497
  148.8 65.7 %collective-permute-start.11 = (bf16[256,2048]{1,0:T(8,128)(2,1)S(1)}, bf16[256,2048]{1,0:T(8,128)(2,1)}, u32[]{:S(2)}, u32[]{:S(2)}) collective-permute-start(bf16[256,2048]{1,0:T(8,128)(2,1)S(1)} %slice.147), channel_id=1, source_target_pairs={{0,16},{8,24},{16,0},{24,8},{1,17},{9,25},{17,1},{25,9},{2,18},{10... | collective-permute-start | bytes 3145736 | tf_op jit(solution)/shard_map/ppermute | solution.py:497
  150.8 63.8 %collective-permute-start.12 = (bf16[256,2048]{1,0:T(8,128)(2,1)S(1)}, bf16[256,2048]{1,0:T(8,128)(2,1)}, u32[]{:S(2)}, u32[]{:S(2)}) collective-permute-start(bf16[256,2048]{1,0:T(8,128)(2,1)S(1)} %slice.148), channel_id=1, source_target_pairs={{0,8},{8,0},{16,24},{24,16},{1,9},{9,1},{17,25},{25,17},{2,10},{10... | collective-permute-start | bytes 3145736 | tf_op jit(solution)/shard_map/ppermute | solution.py:497
  219.3 4.2 collective-permute-start.13
  231.0 4.4 collective-permute-start.16
  231.2 48.0 %collective-permute-start.14 = (bf16[512,2048]{1,0:T(8,128)(2,1)S(1)}, bf16[512,2048]{1,0:T(8,128)(2,1)}, u32[]{:S(2)}, u32[]{:S(2)}) collective-permute-start(bf16[512,2048]{1,0:T(8,128)(2,1)S(1)} %multiply_convert_fusion.xa_ref), channel_id=1, source_target_pairs={{0,8},{8,0},{16,24},{24,16},{1,9},{9,1},{17,25},{25,17},{2,10},{10... | collective-permute-start | bytes 6291464 | tf_op jit(solution)/shard_map/ppermute | solution.py:497
  232.6 47.7 %collective-permute-start.15 = (bf16[512,2048]{1,0:T(8,128)(2,1)S(1)}, bf16[512,2048]{1,0:T(8,128)(2,1)}, u32[]{:S(2)}, u32[]{:S(2)}) collective-permute-start(bf16[512,2048]{1,0:T(8,128)(2,1)S(1)} %multiply_convert_fusion.xa_ref), channel_id=1, source_target_pairs={{0,16},{8,24},{16,0},{24,8},{1,17},{9,25},{17,1},{25,9},{2,18},{10... | collective-permute-start | bytes 6291464 | tf_op jit(solution)/shard_map/ppermute | solution.py:497
  280.4 9.4 %collective-permute-start.19 = (bf16[512,2048]{1,0:T(8,128)(2,1)}, bf16[512,2048]{1,0:T(8,128)(2,1)}, u32[]{:S(2)}, u32[]{:S(2)}) collective-permute-start(bf16[512,2048]{1,0:T(8,128)(2,1)} %collective-permute-done.14.xa_ref), channel_id=1, source_target_pairs={{0,4},{4,0},{1,5},{5,1},{2,6},{6,2},{3,7},{7,3},{8,12},{12,8},{9,1... | collective-permute-start | bytes 6291464 | tf_op jit(solution)/shard_map/ppermute | solution.py:497
  285.0 36.0 %collective-permute-start.17 = (bf16[256,2048]{1,0:T(8,128)(2,1)}, bf16[256,2048]{1,0:T(8,128)(2,1)}, u32[]{:S(2)}, u32[]{:S(2)}) collective-permute-start(bf16[256,2048]{1,0:T(8,128)(2,1)} %slice.151), channel_id=1, source_target_pairs={{0,16},{8,24},{16,0},{24,8},{1,17},{9,25},{17,1},{25,9},{2,18},{10... | collective-permute-start | bytes 3145736 | tf_op jit(solution)/shard_map/ppermute | solution.py:497
  285.6 35.4 %collective-permute-start.18 = (bf16[256,2048]{1,0:T(8,128)(2,1)}, bf16[256,2048]{1,0:T(8,128)(2,1)}, u32[]{:S(2)}, u32[]{:S(2)}) collective-permute-start(bf16[256,2048]{1,0:T(8,128)(2,1)} %slice.152), channel_id=1, source_target_pairs={{0,8},{8,0},{16,24},{24,16},{1,9},{9,1},{17,25},{25,17},{2,10},{10... | collective-permute-start | bytes 3145736 | tf_op jit(solution)/shard_map/ppermute | solution.py:497
  289.7 33.9 %collective-permute-start.21 = (bf16[512,2048]{1,0:T(8,128)(2,1)S(1)}, bf16[512,2048]{1,0:T(8,128)(2,1)}, u32[]{:S(2)}, u32[]{:S(2)}) collective-permute-start(bf16[512,2048]{1,0:T(8,128)(2,1)S(1)} %constant_dynamic-update-slice_fusion.2.ga_ref), channel_id=1, source_target_pairs={{0,4},{4,0},{1,5},{5,1},{2,6},{6,2},{3,7},{7,3},{8,12},{12,8},{9,1... | collective-permute-start | bytes 6291464 | tf_op jit(solution)/shard_map/ppermute | solution.py:497
  323.6 4.2 collective-permute-start.20
  359.9 6.2 collective-permute-start.22
  360.1 13.2 %collective-permute-start.25 = (bf16[512,2048]{1,0:T(8,128)(2,1)}, bf16[512,2048]{1,0:T(8,128)(2,1)}, u32[]{:S(2)}, u32[]{:S(2)}) collective-permute-start(bf16[512,2048]{1,0:T(8,128)(2,1)} %collective-permute-done.15.xa_ref), channel_id=1, source_target_pairs={{0,4},{4,0},{1,5},{5,1},{2,6},{6,2},{3,7},{7,3},{8,12},{12,8},{9,1... | collective-permute-start | bytes 6291464 | tf_op jit(solution)/shard_map/ppermute | solution.py:497
  360.5 11.4 %collective-permute-start.26 = (bf16[512,2048]{1,0:T(8,128)(2,1)S(1)}, bf16[512,2048]{1,0:T(8,128)(2,1)S(1)}, u32[]{:S(2)}, u32[]{:S(2)}) collective-permute-start(bf16[512,2048]{1,0:T(8,128)(2,1)S(1)} %copy-done.79), channel_id=1, source_target_pairs={{0,4},{4,0},{1,5},{5,1},{2,6},{6,2},{3,7},{7,3},{8,12},{12,8},{9,1... | collective-permute-start | bytes 6291464 | tf_op jit(solution)/shard_map/ppermute | solution.py:497
  370.0 34.2 %collective-permute-start.23 = (bf16[256,2048]{1,0:T(8,128)(2,1)}, bf16[256,2048]{1,0:T(8,128)(2,1)}, u32[]{:S(2)}, u32[]{:S(2)}) collective-permute-start(bf16[256,2048]{1,0:T(8,128)(2,1)} %get-tuple-element.371), channel_id=1, source_target_pairs={{0,8},{8,0},{16,24},{24,16},{1,9},{9,1},{17,25},{25,17},{2,10},{10... | collective-permute-start | bytes 3145736 | tf_op jit(solution)/shard_map/ppermute | solution.py:497
  370.2 34.0 %collective-permute-start.24 = (bf16[256,2048]{1,0:T(8,128)(2,1)}, bf16[256,2048]{1,0:T(8,128)(2,1)}, u32[]{:S(2)}, u32[]{:S(2)}) collective-permute-start(bf16[256,2048]{1,0:T(8,128)(2,1)} %get-tuple-element.370), channel_id=1, source_target_pairs={{0,16},{8,24},{16,0},{24,8},{1,17},{9,25},{17,1},{25,9},{2,18},{10... | collective-permute-start | bytes 3145736 | tf_op jit(solution)/shard_map/ppermute | solution.py:497
  404.2 4.6 collective-permute-start.27
  412.6 38.8 %collective-permute-start.28 = (bf16[2048,2048]{1,0:T(8,128)(2,1)}, bf16[2048,2048]{1,0:T(8,128)(2,1)}, u32[]{:S(2)}, u32[]{:S(2)}) collective-permute-start(bf16[2048,2048]{1,0:T(8,128)(2,1)} %get-tuple-element.269), channel_id=1, source_target_pairs={{0,4},{4,0},{1,5},{5,1},{2,6},{6,2},{3,7},{7,3},{8,12},{12,8},{9,1... | collective-permute-start | bytes 25165832 | tf_op jit(solution)/shard_map/ppermute | solution.py:497
  412.9 50.7 %collective-permute-start.31 = (bf16[512,2048]{1,0:T(8,128)(2,1)}, bf16[512,2048]{1,0:T(8,128)(2,1)S(1)}, u32[]{:S(2)}, u32[]{:S(2)}) collective-permute-start(bf16[512,2048]{1,0:T(8,128)(2,1)} %get-tuple-element.270), channel_id=1, source_target_pairs={{0,4},{4,0},{1,5},{5,1},{2,6},{6,2},{3,7},{7,3},{8,12},{12,8},{9,1... | collective-permute-start | bytes 6291464 | tf_op jit(solution)/shard_map/ppermute | solution.py:497
  413.1 50.6 %collective-permute-start.29 = (bf16[512,2048]{1,0:T(8,128)(2,1)}, bf16[512,2048]{1,0:T(8,128)(2,1)}, u32[]{:S(2)}, u32[]{:S(2)}) collective-permute-start(bf16[512,2048]{1,0:T(8,128)(2,1)} %add_convert_fusion.7), channel_id=1, source_target_pairs={{0,8},{8,0},{16,24},{24,16},{1,9},{9,1},{17,25},{25,17},{2,10},{10... | collective-permute-start | bytes 6291464 | tf_op jit(solution)/shard_map/ppermute | solution.py:497
  413.6 50.0 %collective-permute-start.30 = (bf16[512,2048]{1,0:T(8,128)(2,1)}, bf16[512,2048]{1,0:T(8,128)(2,1)}, u32[]{:S(2)}, u32[]{:S(2)}) collective-permute-start(bf16[512,2048]{1,0:T(8,128)(2,1)} %add_convert_fusion.6), channel_id=1, source_target_pairs={{0,16},{8,24},{16,0},{24,8},{1,17},{9,25},{17,1},{25,9},{2,18},{10... | collective-permute-start | bytes 6291464 | tf_op jit(solution)/shard_map/ppermute | solution.py:497
  432.2 196.8 %reduce-scatter.8.cloned.1.call-start = ((), (), s32[]{:S(2)}) async-start(), calls=%async_computation.12 | async-start | bytes 3604480 | tf_op jit(solution)/shard_map/reduce_scatter | solution.py:738
  475.9 4.5 collective-permute-start.32
  488.8 76.3 %all-to-all-start.3 = ((bf16[4,256,2048]{2,1,0:T(8,128)(2,1)}), bf16[4,256,2048]{2,1,0:T(8,128)(2,1)}, u32[]{:S(2)}, u32[]{:S(2)}) async-start(bf16[4,256,2048]{2,1,0:T(8,128)(2,1)} %bitcast.157), calls=%async_computation.3 | async-start | bytes 8388608 | tf_op jit(solution)/shard_map/all_to_all | solution.py:763
  493.8 147.2 %reduce-scatter.6.cloned.1.call-start = ((), (), s32[]{:S(2)}) async-start(), calls=%async_computation.11 | async-start | bytes 3604480 | tf_op jit(solution)/shard_map/reduce_scatter | solution.py:738
  513.1 51.0 %collective-permute-start.33 = (bf16[256,2048]{1,0:T(8,128)(2,1)}, bf16[256,2048]{1,0:T(8,128)(2,1)S(1)}, u32[]{:S(2)}, u32[]{:S(2)}) collective-permute-start(bf16[256,2048]{1,0:T(8,128)(2,1)} %get-tuple-element.289), channel_id=1, source_target_pairs={{0,8},{8,0},{16,24},{24,16},{1,9},{9,1},{17,25},{25,17},{2,10},{10... | collective-permute-start | bytes 3145736 | tf_op jit(solution)/shard_map/ppermute | solution.py:497
  515.1 50.0 %collective-permute-start.34 = (bf16[256,2048]{1,0:T(8,128)(2,1)}, bf16[256,2048]{1,0:T(8,128)(2,1)}, u32[]{:S(2)}, u32[]{:S(2)}) collective-permute-start(bf16[256,2048]{1,0:T(8,128)(2,1)} %get-tuple-element.290), channel_id=1, source_target_pairs={{0,16},{8,24},{16,0},{24,8},{1,17},{9,25},{17,1},{25,9},{2,18},{10... | collective-permute-start | bytes 3145736 | tf_op jit(solution)/shard_map/ppermute | solution.py:497
  569.1 71.8 %collective-permute-start.35 = (bf16[512,2048]{1,0:T(8,128)(2,1)}, bf16[512,2048]{1,0:T(8,128)(2,1)}, u32[]{:S(2)}, u32[]{:S(2)}) collective-permute-start(bf16[512,2048]{1,0:T(8,128)(2,1)} %add_convert_fusion.2), channel_id=1, source_target_pairs={{0,8},{8,0},{16,24},{24,16},{1,9},{9,1},{17,25},{25,17},{2,10},{10... | collective-permute-start | bytes 6291464 | tf_op jit(solution)/shard_map/ppermute | solution.py:497
  571.5 69.5 %collective-permute-start.36 = (bf16[512,2048]{1,0:T(8,128)(2,1)}, bf16[512,2048]{1,0:T(8,128)(2,1)}, u32[]{:S(2)}, u32[]{:S(2)}) collective-permute-start(bf16[512,2048]{1,0:T(8,128)(2,1)} %add_convert_fusion.1), channel_id=1, source_target_pairs={{0,16},{8,24},{16,0},{24,8},{1,17},{9,25},{17,1},{25,9},{2,18},{10... | collective-permute-start | bytes 6291464 | tf_op jit(solution)/shard_map/ppermute | solution.py:497
  576.7 64.3 %all-to-all-start.4 = ((bf16[8,256,512]{2,1,0:T(8,128)(2,1)}), bf16[8,256,512]{2,1,0:T(8,128)(2,1)}, u32[]{:S(2)}, u32[]{:S(2)}) async-start(bf16[8,256,512]{2,1,0:T(8,128)(2,1)} %bitcast.164), calls=%async_computation.7 | async-start | bytes 4194304 | tf_op jit(solution)/shard_map/all_to_all | solution.py:761
  585.9 31.6 %collective-permute-start.39 = (bf16[64,2048]{1,0:T(8,128)(2,1)S(1)}, bf16[64,2048]{1,0:T(8,128)(2,1)}, u32[]{:S(2)}, u32[]{:S(2)}) collective-permute-start(bf16[64,2048]{1,0:T(8,128)(2,1)S(1)} %get-tuple-element.368), channel_id=1, source_target_pairs={{0,3},{1,2},{2,1},{3,0},{4,7},{5,6},{6,5},{7,4},{8,11},{9,10},{10,... | collective-permute-start | bytes 786440 | tf_op jit(solution)/shard_map/ppermute | solution.py:497
  589.7 37.2 %collective-permute-start.38 = (bf16[64,2048]{1,0:T(8,128)(2,1)S(1)}, bf16[64,2048]{1,0:T(8,128)(2,1)}, u32[]{:S(2)}, u32[]{:S(2)}) collective-permute-start(bf16[64,2048]{1,0:T(8,128)(2,1)S(1)} %get-tuple-element.369), channel_id=1, source_target_pairs={{0,2},{1,3},{2,0},{3,1},{4,6},{5,7},{6,4},{7,5},{8,10},{9,11},{10,... | collective-permute-start | bytes 786440 | tf_op jit(solution)/shard_map/ppermute | solution.py:497
  589.7 37.2 %collective-permute-start.37 = (bf16[64,2048]{1,0:T(8,128)(2,1)S(1)}, bf16[64,2048]{1,0:T(8,128)(2,1)}, u32[]{:S(2)}, u32[]{:S(2)}) collective-permute-start(bf16[64,2048]{1,0:T(8,128)(2,1)S(1)} %get-tuple-element.367), channel_id=1, source_target_pairs={{0,1},{1,0},{2,3},{3,2},{4,5},{5,4},{6,7},{7,6},{8,9},{9,8},{10,11... | collective-permute-start | bytes 786440 | tf_op jit(solution)/shard_map/ppermute | solution.py:497
  645.5 9.2 %collective-permute-start.41 = (bf16[512,256]{1,0:T(8,128)(2,1)S(1)}, bf16[512,256]{1,0:T(8,128)(2,1)S(1)}, u32[]{:S(2)}, u32[]{:S(2)}) collective-permute-start(bf16[512,256]{1,0:T(8,128)(2,1)S(1)} %get-tuple-element.378), channel_id=1, source_target_pairs={{0,8},{8,0},{16,24},{24,16},{1,9},{9,1},{17,25},{25,17},{2,10},{10... | collective-permute-start | bytes 786440 | tf_op jit(solution)/shard_map/ppermute | solution.py:497
  647.0 13.7 %collective-permute-start.42 = (bf16[512,256]{1,0:T(8,128)(2,1)S(1)}, bf16[512,256]{1,0:T(8,128)(2,1)S(1)}, u32[]{:S(2)}, u32[]{:S(2)}) collective-permute-start(bf16[512,256]{1,0:T(8,128)(2,1)S(1)} %get-tuple-element.377), channel_id=1, source_target_pairs={{0,16},{8,24},{16,0},{24,8},{1,17},{9,25},{17,1},{25,9},{2,18},{10... | collective-permute-start | bytes 786440 | tf_op jit(solution)/shard_map/ppermute | solution.py:497
  648.5 12.2 %collective-permute-start.43 = (bf16[512,256]{1,0:T(8,128)(2,1)S(1)}, bf16[512,256]{1,0:T(8,128)(2,1)S(1)}, u32[]{:S(2)}, u32[]{:S(2)}) collective-permute-start(bf16[512,256]{1,0:T(8,128)(2,1)S(1)} %get-tuple-element.376), channel_id=1, source_target_pairs={{0,24},{8,16},{16,8},{24,0},{1,25},{9,17},{17,9},{25,1},{2,26},{10... | collective-permute-start | bytes 786440 | tf_op jit(solution)/shard_map/ppermute | solution.py:497
  662.7 9.5 %collective-permute-start.44 = (bf16[512,256]{1,0:T(8,128)(2,1)}, bf16[512,256]{1,0:T(8,128)(2,1)}, u32[]{:S(2)}, u32[]{:S(2)}) collective-permute-start(bf16[512,256]{1,0:T(8,128)(2,1)} %pad_maximum_fusion.11), channel_id=1, source_target_pairs={{0,4},{4,0},{1,5},{5,1},{2,6},{6,2},{3,7},{7,3},{8,12},{12,8},{9,1... | collective-permute-start | bytes 786440 | tf_op jit(solution)/shard_map/ppermute | solution.py:497
  668.2 31.3 %all-to-all-start.5 = ((bf16[8,3,176,256]{3,2,1,0:T(8,128)(2,1)}), bf16[8,3,176,256]{3,2,1,0:T(8,128)(2,1)S(1)}, u32[]{:S(2)}, u32[]{:S(2)}) async-start(bf16[8,3,176,256]{3,2,1,0:T(8,128)(2,1)} %copy-done.3), calls=%async_computation.8 | async-start | bytes 4325376 | tf_op jit(solution)/shard_map/all_to_all | solution.py:800
  686.9 26.8 %collective-permute-start.45 = (bf16[512,2048]{1,0:T(8,128)(2,1)}, bf16[512,2048]{1,0:T(8,128)(2,1)}, u32[]{:S(2)}, u32[]{:S(2)}) collective-permute-start(bf16[512,2048]{1,0:T(8,128)(2,1)} %add_convert_fusion), channel_id=1, source_target_pairs={{0,4},{4,0},{1,5},{5,1},{2,6},{6,2},{3,7},{7,3},{8,12},{12,8},{9,1... | collective-permute-start | bytes 6291464 | tf_op jit(solution)/shard_map/ppermute | solution.py:497
  689.1 79.4 %collective-permute-start.52 = (bf16[64,1024]{1,0:T(8,128)(2,1)}, bf16[64,1024]{1,0:T(8,128)(2,1)}, u32[]{:S(2)}, u32[]{:S(2)}) collective-permute-start(bf16[64,1024]{1,0:T(8,128)(2,1)} %get-tuple-element.362), channel_id=1, source_target_pairs={{0,4},{4,0},{1,5},{5,1},{2,6},{6,2},{3,7},{7,3},{8,12},{12,8},{9,1... | collective-permute-start | bytes 393224 | tf_op jit(solution)/shard_map/ppermute | solution.py:497
  691.7 53.5 %collective-permute-start.46 = (bf16[2,64,512]{2,1,0:T(8,128)(2,1)}, bf16[2,64,512]{2,1,0:T(8,128)(2,1)}, u32[]{:S(2)}, u32[]{:S(2)}) collective-permute-start(bf16[2,64,512]{2,1,0:T(8,128)(2,1)} %get-tuple-element.322), channel_id=1, source_target_pairs={{0,1},{1,0},{2,3},{3,2},{4,5},{5,4},{6,7},{7,6},{8,9},{9,8},{10,11... | collective-permute-start | bytes 393224 | tf_op jit(solution)/shard_map/ppermute | solution.py:497
  693.1 52.1 %collective-permute-start.47 = (bf16[2,64,512]{2,1,0:T(8,128)(2,1)}, bf16[2,64,512]{2,1,0:T(8,128)(2,1)}, u32[]{:S(2)}, u32[]{:S(2)}) collective-permute-start(bf16[2,64,512]{2,1,0:T(8,128)(2,1)} %get-tuple-element.323), channel_id=1, source_target_pairs={{0,2},{1,3},{2,0},{3,1},{4,6},{5,7},{6,4},{7,5},{8,10},{9,11},{10,... | collective-permute-start | bytes 393224 | tf_op jit(solution)/shard_map/ppermute | solution.py:497
  695.9 49.3 %collective-permute-start.48 = (bf16[2,64,512]{2,1,0:T(8,128)(2,1)}, bf16[2,64,512]{2,1,0:T(8,128)(2,1)}, u32[]{:S(2)}, u32[]{:S(2)}) collective-permute-start(bf16[2,64,512]{2,1,0:T(8,128)(2,1)} %get-tuple-element.324), channel_id=1, source_target_pairs={{0,3},{1,2},{2,1},{3,0},{4,7},{5,6},{6,5},{7,4},{8,11},{9,10},{10,... | collective-permute-start | bytes 393224 | tf_op jit(solution)/shard_map/ppermute | solution.py:497
  699.5 42.5 %all-to-all-start.6 = ((bf16[8,256,768]{2,1,0:T(8,128)(2,1)}), bf16[8,256,768]{2,1,0:T(8,128)(2,1)}, u32[]{:S(2)}, u32[]{:S(2)}) async-start(bf16[8,256,768]{2,1,0:T(8,128)(2,1)} %bitcast.149), calls=%async_computation.9 | async-start | bytes 6291456 | tf_op jit(solution)/shard_map/all_to_all | solution.py:761
  745.2 10.0 %collective-permute-start.51 = (bf16[2,64,768]{2,1,0:T(8,128)(2,1)}, bf16[2,64,768]{2,1,0:T(8,128)(2,1)S(1)}, u32[]{:S(2)}, u32[]{:S(2)}) collective-permute-start(bf16[2,64,768]{2,1,0:T(8,128)(2,1)} %get-tuple-element.344), channel_id=1, source_target_pairs={{0,3},{1,2},{2,1},{3,0},{4,7},{5,6},{6,5},{7,4},{8,11},{9,10},{10,... | collective-permute-start | bytes 589832 | tf_op jit(solution)/shard_map/ppermute | solution.py:497
  748.9 13.7 %collective-permute-start.50 = (bf16[2,64,768]{2,1,0:T(8,128)(2,1)}, bf16[2,64,768]{2,1,0:T(8,128)(2,1)S(1)}, u32[]{:S(2)}, u32[]{:S(2)}) collective-permute-start(bf16[2,64,768]{2,1,0:T(8,128)(2,1)} %get-tuple-element.343), channel_id=1, source_target_pairs={{0,2},{1,3},{2,0},{3,1},{4,6},{5,7},{6,4},{7,5},{8,10},{9,11},{10,... | collective-permute-start | bytes 589832 | tf_op jit(solution)/shard_map/ppermute | solution.py:497
  749.0 13.7 %collective-permute-start.49 = (bf16[2,64,768]{2,1,0:T(8,128)(2,1)}, bf16[2,64,768]{2,1,0:T(8,128)(2,1)S(1)}, u32[]{:S(2)}, u32[]{:S(2)}) collective-permute-start(bf16[2,64,768]{2,1,0:T(8,128)(2,1)} %get-tuple-element.342), channel_id=1, source_target_pairs={{0,1},{1,0},{2,3},{3,2},{4,5},{5,4},{6,7},{7,6},{8,9},{9,8},{10,11... | collective-permute-start | bytes 589832 | tf_op jit(solution)/shard_map/ppermute | solution.py:497
  (81 other events, 831.6 us)
Sparse Core Ops, SparseCore 0:
  13.8 53.4 all-gather.7
  68.9 152.7 all-gather.5
  432.4 56.3 reduce-scatter.3
  491.0 56.0 reduce-scatter.7
  549.2 68.6 reduce-scatter.5
